TPU v7x, 32 devices: a whole 2x2x4 slice. The times are simulated.
32 devices in a mesh: fsdp: 8 (over y, x, core), seq: 4 (over z).
Axes of the slice: x: 2, y: 2, z: 4, core: 2. Of those that a mesh axis runs over, the one named last changes fastest.
Arguments:
- hidden_in: bfloat16 [24, 448, 1024], P('fsdp', 'seq'), may hold values from -6 to 6
- encoded: bfloat16 [24, 1500, 1024], P('fsdp', 'seq'), may hold values from -6 to 6
- out_grad: bfloat16 [24, 448, 1024], P('fsdp', 'seq'), may hold values from -6 to 6
- norm_gain: bfloat16 [3, 1024], P(None, 'fsdp'), may hold values from 0.25 to 1.75
- norm_shift: bfloat16 [3, 1024], P(None, 'fsdp'), may hold values from -3 to 3
- biases: bfloat16 [7, 1024], P(None, 'fsdp'), may hold values from -3 to 3
- self_qkv: bfloat16 [1024, 3072], P('fsdp'), may hold values from -0.1875 to 0.1875
- self_out: bfloat16 [1024, 1024], P('fsdp'), may hold values from -0.5 to 0.5
- cross_q: bfloat16 [1024, 1024], P('fsdp'), may hold values from -0.1875 to 0.1875
- cross_kv: bfloat16 [1024, 2048], P('fsdp'), may hold values from -0.1875 to 0.1875
- cross_out: bfloat16 [1024, 1024], P('fsdp'), may hold values from -0.75 to 0.75
- mlp_in: bfloat16 [1024, 4096], P('fsdp'), may hold values from -0.1875 to 0.1875
- mlp_in_bias: bfloat16 [4096], P('fsdp'), may hold values from -3 to 3
- mlp_out: bfloat16 [4096, 1024], P('fsdp'), may hold values from -0.09375 to 0.09375
Outputs:
- hidden_out: bfloat16 [24, 448, 1024], P('fsdp', 'seq')
- grad_hidden_in: bfloat16 [24, 448, 1024], P('fsdp', 'seq')
- grad_encoded: bfloat16 [24, 1500, 1024], P('fsdp', 'seq')
- grad_norm_gain: float32 [3, 1024], P(None, 'fsdp')
- grad_norm_shift: float32 [3, 1024], P(None, 'fsdp')
- grad_biases: float32 [7, 1024], P(None, 'fsdp')
- grad_self_qkv: float32 [1024, 3072], P('fsdp')
- grad_self_out: float32 [1024, 1024], P('fsdp')
- grad_cross_q: float32 [1024, 1024], P('fsdp')
- grad_cross_kv: float32 [1024, 2048], P('fsdp')
- grad_cross_out: float32 [1024, 1024], P('fsdp')
- grad_mlp_in: float32 [1024, 4096], P('fsdp')
- grad_mlp_in_bias: float32 [4096], P('fsdp')
- grad_mlp_out: float32 [4096, 1024], P('fsdp')
All inputs are finite; a program needn't handle non-finite values.
Results may differ from a plain program's by a relative error of at most 0.018.
Values may be sent and summed in bfloat16 or wider, within the bound.
No kernel may reach another device: no remote copies, remote signals or barrier semaphores. Data moves between devices by JAX's collectives and lax.ppermute only.
A program may use at most 256 MiB of HBM per device.

v0:
```python
import jax
import jax.numpy as jnp
from jax import lax
from jax.sharding import PartitionSpec as P

HD = 64


NORM_EPSILON = 1e-05


def norm_apply(values, gain_row, shift_row):
    average = jnp.mean(values, axis=-1, keepdims=True)
    centred = values - average
    variance = jnp.mean(centred * centred, axis=-1, keepdims=True)
    return centred * lax.rsqrt(variance + NORM_EPSILON) * gain_row + shift_row


def gelu_exact(values):
    return jax.nn.gelu(values, approximate=False)


def project(operand, weight):
    return jnp.einsum("cld,de->cle", operand, weight, preferred_element_type=jnp.float32)


def project_back(operand, weight):
    return jnp.einsum("cle,de->cld", operand, weight, preferred_element_type=jnp.float32)


def weight_grad(operand, incoming):
    return jnp.einsum("cld,cle->de", operand, incoming, preferred_element_type=jnp.float32)


def row_total(values):
    return jnp.sum(values, axis=(0, 1))


def split_heads(block):
    return block.reshape(block.shape[0], -1, HD)


def causal_mask(query_count, key_count):
    return jnp.arange(query_count)[:, None] >= jnp.arange(key_count)[None, :]


def attend_block(query_block, key_block, value_block, causal):
    query_heads = split_heads(query_block)
    key_heads = split_heads(key_block)
    value_heads = split_heads(value_block)
    scores = jnp.einsum("qhd,khd->hqk", query_heads, key_heads, preferred_element_type=jnp.float32)
    if causal:
        allowed = causal_mask(query_block.shape[0], key_block.shape[0])
        scores = jnp.where(allowed[None, :, :], scores, -jnp.inf)
    top_score = jnp.max(scores, axis=-1, keepdims=True)
    raised = jnp.exp(scores - top_score)
    row_sums = jnp.sum(raised, axis=-1, keepdims=True)
    soft_weights = (raised / row_sums).astype(jnp.bfloat16)
    mixed = jnp.einsum(
        "hqk,khd->qhd", soft_weights, value_heads, preferred_element_type=jnp.float32
    )
    log_total = (top_score + jnp.log(row_sums))[:, :, 0]
    return (mixed.reshape(mixed.shape[0], -1).astype(jnp.bfloat16), log_total)


def attend_back(query_block, key_block, value_block, grad_block, log_total, causal):
    query_heads = split_heads(query_block)
    key_heads = split_heads(key_block)
    value_heads = split_heads(value_block)
    grad_heads = split_heads(grad_block)
    scores = jnp.einsum("qhd,khd->hqk", query_heads, key_heads, preferred_element_type=jnp.float32)
    if causal:
        allowed = causal_mask(query_block.shape[0], key_block.shape[0])
        scores = jnp.where(allowed[None, :, :], scores, -jnp.inf)
    soft_weights = jnp.exp(scores - log_total[:, :, None])
    rounded = soft_weights.astype(jnp.bfloat16)
    grad_soft = jnp.einsum(
        "qhd,khd->hqk", grad_heads, value_heads, preferred_element_type=jnp.float32
    )
    grad_value = jnp.einsum("hqk,qhd->khd", rounded, grad_heads, preferred_element_type=jnp.float32)
    row_dot = jnp.sum(grad_soft * soft_weights, axis=-1, keepdims=True)
    grad_scores = (soft_weights * (grad_soft - row_dot)).astype(jnp.bfloat16)
    grad_query = jnp.einsum(
        "hqk,khd->qhd", grad_scores, key_heads, preferred_element_type=jnp.float32
    )
    grad_key = jnp.einsum(
        "hqk,qhd->khd", grad_scores, query_heads, preferred_element_type=jnp.float32
    )
    return (
        grad_query.reshape(grad_query.shape[0], -1).astype(jnp.bfloat16),
        grad_key.reshape(grad_key.shape[0], -1).astype(jnp.bfloat16),
        grad_value.reshape(grad_value.shape[0], -1).astype(jnp.bfloat16),
    )


def self_forward(members):
    return attend_block(members[0], members[1], members[2], True)


def cross_forward(members):
    return attend_block(members[0], members[1], members[2], False)


def self_backward(members):
    return attend_back(members[0], members[1], members[2], members[3], members[4], True)


def cross_backward(members):
    return attend_back(members[0], members[1], members[2], members[3], members[4], False)


def local(
    hidden_in,
    encoded,
    out_grad,
    norm_gain,
    norm_shift,
    biases,
    self_qkv,
    self_out,
    cross_q,
    cross_kv,
    cross_out,
    mlp_in,
    mlp_in_bias,
    mlp_out,
):
    (
        full_gain,
        full_shift,
        full_bias,
        full_qkv,
        full_self_out,
        full_cross_q,
        full_cross_kv,
        full_cross_out,
        full_inner,
        full_inner_bias,
        full_outer,
    ) = (
        lax.all_gather(norm_gain, "fsdp", axis=1, tiled=True),
        lax.all_gather(norm_shift, "fsdp", axis=1, tiled=True),
        lax.all_gather(biases, "fsdp", axis=1, tiled=True),
        lax.all_gather(self_qkv, "fsdp", axis=0, tiled=True),
        lax.all_gather(self_out, "fsdp", axis=0, tiled=True),
        lax.all_gather(cross_q, "fsdp", axis=0, tiled=True),
        lax.all_gather(cross_kv, "fsdp", axis=0, tiled=True),
        lax.all_gather(cross_out, "fsdp", axis=0, tiled=True),
        lax.all_gather(mlp_in, "fsdp", axis=0, tiled=True),
        lax.all_gather(mlp_in_bias, "fsdp", axis=0, tiled=True),
        lax.all_gather(mlp_out, "fsdp", axis=0, tiled=True),
    )
    gain_rows = full_gain.astype(jnp.float32)
    shift_rows = full_shift.astype(jnp.float32)
    bias_rows = full_bias.astype(jnp.float32)
    inner_bias = full_inner_bias.astype(jnp.float32)
    width = hidden_in.shape[2]
    scaling = HD ** (-0.5)
    residual_in = hidden_in.astype(jnp.float32)
    normed_one = norm_apply(residual_in, gain_rows[0], shift_rows[0]).astype(jnp.bfloat16)
    pre_qkv = project(normed_one, full_qkv)
    queries = ((pre_qkv[:, :, :width] + bias_rows[0]) * scaling).astype(jnp.bfloat16)
    key_rows = pre_qkv[:, :, width : 2 * width].astype(jnp.bfloat16)
    value_rows = (pre_qkv[:, :, 2 * width :] + bias_rows[1]).astype(jnp.bfloat16)
    encoded_pre = project(encoded, full_cross_kv)
    cross_keys = encoded_pre[:, :, :width].astype(jnp.bfloat16)
    cross_values = (encoded_pre[:, :, width:] + bias_rows[4]).astype(jnp.bfloat16)
    heads_query, heads_key, heads_value, heads_cross_key, heads_cross_value = (
        lax.all_to_all(queries, "seq", split_axis=2, concat_axis=1, tiled=True),
        lax.all_to_all(key_rows, "seq", split_axis=2, concat_axis=1, tiled=True),
        lax.all_to_all(value_rows, "seq", split_axis=2, concat_axis=1, tiled=True),
        lax.all_to_all(cross_keys, "seq", split_axis=2, concat_axis=1, tiled=True),
        lax.all_to_all(cross_values, "seq", split_axis=2, concat_axis=1, tiled=True),
    )
    self_mix_heads, self_log = lax.map(self_forward, (heads_query, heads_key, heads_value))
    self_mix = lax.all_to_all(self_mix_heads, "seq", split_axis=1, concat_axis=2, tiled=True)
    after_self = residual_in + project(self_mix, full_self_out) + bias_rows[2]
    normed_two = norm_apply(after_self, gain_rows[1], shift_rows[1]).astype(jnp.bfloat16)
    cross_queries = ((project(normed_two, full_cross_q) + bias_rows[3]) * scaling).astype(
        jnp.bfloat16
    )
    heads_cross_query = lax.all_to_all(
        cross_queries, "seq", split_axis=2, concat_axis=1, tiled=True
    )
    cross_mix_heads, cross_log = lax.map(
        cross_forward, (heads_cross_query, heads_cross_key, heads_cross_value)
    )
    cross_mix = lax.all_to_all(cross_mix_heads, "seq", split_axis=1, concat_axis=2, tiled=True)
    after_cross = after_self + project(cross_mix, full_cross_out) + bias_rows[5]
    normed_three = norm_apply(after_cross, gain_rows[2], shift_rows[2]).astype(jnp.bfloat16)
    inner = project(normed_three, full_inner) + inner_bias
    activated = gelu_exact(inner).astype(jnp.bfloat16)
    hidden_out = (after_cross + project(activated, full_outer) + bias_rows[6]).astype(jnp.bfloat16)
    (
        back_gain,
        back_qkv,
        back_self_out,
        back_cross_q,
        back_cross_kv,
        back_cross_out,
        back_inner,
        back_outer,
    ) = (
        lax.all_gather(norm_gain, "fsdp", axis=1, tiled=True),
        lax.all_gather(self_qkv, "fsdp", axis=0, tiled=True),
        lax.all_gather(self_out, "fsdp", axis=0, tiled=True),
        lax.all_gather(cross_q, "fsdp", axis=0, tiled=True),
        lax.all_gather(cross_kv, "fsdp", axis=0, tiled=True),
        lax.all_gather(cross_out, "fsdp", axis=0, tiled=True),
        lax.all_gather(mlp_in, "fsdp", axis=0, tiled=True),
        lax.all_gather(mlp_out, "fsdp", axis=0, tiled=True),
    )
    back_gain_rows = back_gain.astype(jnp.float32)
    grad_top = out_grad.astype(jnp.float32)
    grad_w_outer = weight_grad(activated, out_grad)
    grad_bias_six = row_total(grad_top)
    grad_activated = project_back(out_grad, back_outer)
    gelu_primal, gelu_pull = jax.vjp(gelu_exact, inner)
    grad_inner = gelu_pull(grad_activated)[0]
    grad_inner_low = grad_inner.astype(jnp.bfloat16)
    grad_w_inner = weight_grad(normed_three, grad_inner_low)
    grad_inner_bias = row_total(grad_inner)
    grad_normed_three = project_back(grad_inner_low, back_inner)
    norm_primal, norm_pull = jax.vjp(norm_apply, after_cross, back_gain_rows[2], shift_rows[2])
    from_norm_three, grad_gain_three, grad_shift_three = norm_pull(grad_normed_three)
    grad_after_cross = grad_top + from_norm_three
    grad_cross_low = grad_after_cross.astype(jnp.bfloat16)
    grad_w_cross_out = weight_grad(cross_mix, grad_cross_low)
    grad_bias_five = row_total(grad_after_cross)
    grad_cross_mix = project_back(grad_cross_low, back_cross_out).astype(jnp.bfloat16)
    heads_grad_cross = lax.all_to_all(
        grad_cross_mix, "seq", split_axis=2, concat_axis=1, tiled=True
    )
    grad_cross_query_heads, grad_cross_key_heads, grad_cross_value_heads = lax.map(
        cross_backward,
        (heads_cross_query, heads_cross_key, heads_cross_value, heads_grad_cross, cross_log),
    )
    grad_cross_queries, grad_cross_keys, grad_cross_values = (
        lax.all_to_all(grad_cross_query_heads, "seq", split_axis=1, concat_axis=2, tiled=True),
        lax.all_to_all(grad_cross_key_heads, "seq", split_axis=1, concat_axis=2, tiled=True),
        lax.all_to_all(grad_cross_value_heads, "seq", split_axis=1, concat_axis=2, tiled=True),
    )
    scaled_cross = grad_cross_queries * scaling
    grad_w_cross_q = weight_grad(normed_two, scaled_cross)
    grad_bias_three = row_total(scaled_cross.astype(jnp.float32))
    grad_normed_two = project_back(scaled_cross, back_cross_q)
    grad_pair = jnp.concatenate([grad_cross_keys, grad_cross_values], axis=2)
    grad_w_cross_kv = weight_grad(encoded, grad_pair)
    grad_bias_four = row_total(grad_cross_values.astype(jnp.float32))
    grad_encoded = project_back(grad_pair, back_cross_kv).astype(jnp.bfloat16)
    norm_primal_two, norm_pull_two = jax.vjp(
        norm_apply, after_self, back_gain_rows[1], shift_rows[1]
    )
    from_norm_two, grad_gain_two, grad_shift_two = norm_pull_two(grad_normed_two)
    grad_after_self = grad_after_cross + from_norm_two
    grad_self_low = grad_after_self.astype(jnp.bfloat16)
    grad_w_self_out = weight_grad(self_mix, grad_self_low)
    grad_bias_two = row_total(grad_after_self)
    grad_self_mix = project_back(grad_self_low, back_self_out).astype(jnp.bfloat16)
    heads_grad_self = lax.all_to_all(grad_self_mix, "seq", split_axis=2, concat_axis=1, tiled=True)
    grad_query_heads, grad_key_heads, grad_value_heads = lax.map(
        self_backward, (heads_query, heads_key, heads_value, heads_grad_self, self_log)
    )
    grad_queries, grad_keys, grad_values = (
        lax.all_to_all(grad_query_heads, "seq", split_axis=1, concat_axis=2, tiled=True),
        lax.all_to_all(grad_key_heads, "seq", split_axis=1, concat_axis=2, tiled=True),
        lax.all_to_all(grad_value_heads, "seq", split_axis=1, concat_axis=2, tiled=True),
    )
    scaled_query = grad_queries * scaling
    grad_pre = jnp.concatenate([scaled_query, grad_keys, grad_values], axis=2)
    grad_w_qkv = weight_grad(normed_one, grad_pre)
    grad_bias_zero = row_total(scaled_query.astype(jnp.float32))
    grad_bias_one = row_total(grad_values.astype(jnp.float32))
    grad_normed_one = project_back(grad_pre, back_qkv)
    norm_primal_one, norm_pull_one = jax.vjp(
        norm_apply, residual_in, back_gain_rows[0], shift_rows[0]
    )
    from_norm_one, grad_gain_one, grad_shift_one = norm_pull_one(grad_normed_one)
    grad_hidden_in = (grad_after_self + from_norm_one).astype(jnp.bfloat16)
    grad_gain = jnp.stack([grad_gain_one, grad_gain_two, grad_gain_three])
    grad_shift = jnp.stack([grad_shift_one, grad_shift_two, grad_shift_three])
    grad_bias = jnp.stack(
        [
            grad_bias_zero,
            grad_bias_one,
            grad_bias_two,
            grad_bias_three,
            grad_bias_four,
            grad_bias_five,
            grad_bias_six,
        ]
    )
    (
        part_gain,
        part_shift,
        part_bias,
        part_qkv,
        part_self_out,
        part_cross_q,
        part_cross_kv,
        part_cross_out,
        part_inner,
        part_inner_bias,
        part_outer,
    ) = (
        lax.psum_scatter(grad_gain, "fsdp", scatter_dimension=1, tiled=True),
        lax.psum_scatter(grad_shift, "fsdp", scatter_dimension=1, tiled=True),
        lax.psum_scatter(grad_bias, "fsdp", scatter_dimension=1, tiled=True),
        lax.psum_scatter(grad_w_qkv, "fsdp", scatter_dimension=0, tiled=True),
        lax.psum_scatter(grad_w_self_out, "fsdp", scatter_dimension=0, tiled=True),
        lax.psum_scatter(grad_w_cross_q, "fsdp", scatter_dimension=0, tiled=True),
        lax.psum_scatter(grad_w_cross_kv, "fsdp", scatter_dimension=0, tiled=True),
        lax.psum_scatter(grad_w_cross_out, "fsdp", scatter_dimension=0, tiled=True),
        lax.psum_scatter(grad_w_inner, "fsdp", scatter_dimension=0, tiled=True),
        lax.psum_scatter(grad_inner_bias, "fsdp", scatter_dimension=0, tiled=True),
        lax.psum_scatter(grad_w_outer, "fsdp", scatter_dimension=0, tiled=True),
    )
    (
        total_gain,
        total_shift,
        total_bias,
        total_qkv,
        total_self_out,
        total_cross_q,
        total_cross_kv,
        total_cross_out,
        total_inner,
        total_inner_bias,
        total_outer,
    ) = (
        lax.psum(part_gain.astype(jnp.bfloat16), "seq").astype(jnp.float32),
        lax.psum(part_shift.astype(jnp.bfloat16), "seq").astype(jnp.float32),
        lax.psum(part_bias.astype(jnp.bfloat16), "seq").astype(jnp.float32),
        lax.psum(part_qkv.astype(jnp.bfloat16), "seq").astype(jnp.float32),
        lax.psum(part_self_out.astype(jnp.bfloat16), "seq").astype(jnp.float32),
        lax.psum(part_cross_q.astype(jnp.bfloat16), "seq").astype(jnp.float32),
        lax.psum(part_cross_kv.astype(jnp.bfloat16), "seq").astype(jnp.float32),
        lax.psum(part_cross_out.astype(jnp.bfloat16), "seq").astype(jnp.float32),
        lax.psum(part_inner.astype(jnp.bfloat16), "seq").astype(jnp.float32),
        lax.psum(part_inner_bias.astype(jnp.bfloat16), "seq").astype(jnp.float32),
        lax.psum(part_outer.astype(jnp.bfloat16), "seq").astype(jnp.float32),
    )
    return (
        hidden_out,
        grad_hidden_in,
        grad_encoded,
        total_gain,
        total_shift,
        total_bias,
        total_qkv,
        total_self_out,
        total_cross_q,
        total_cross_kv,
        total_cross_out,
        total_inner,
        total_inner_bias,
        total_outer,
    )


def solution(mesh):
    in_specs = (
        P("fsdp", "seq", None),
        P("fsdp", "seq", None),
        P("fsdp", "seq", None),
        P(None, "fsdp"),
        P(None, "fsdp"),
        P(None, "fsdp"),
        P("fsdp", None),
        P("fsdp", None),
        P("fsdp", None),
        P("fsdp", None),
        P("fsdp", None),
        P("fsdp", None),
        P("fsdp"),
        P("fsdp", None),
    )
    out_specs = (
        P("fsdp", "seq", None),
        P("fsdp", "seq", None),
        P("fsdp", "seq", None),
        P(None, "fsdp"),
        P(None, "fsdp"),
        P(None, "fsdp"),
        P("fsdp", None),
        P("fsdp", None),
        P("fsdp", None),
        P("fsdp", None),
        P("fsdp", None),
        P("fsdp", None),
        P("fsdp"),
        P("fsdp", None),
    )
    return jax.shard_map(local, mesh=mesh, in_specs=in_specs, out_specs=out_specs, check_vma=False)
```

profile of v0, /device:TPU:0, one launch (start us, length us, event | category | flops | bytes accessed | tf_op | source)
XLA Modules:
  0.0 1606.7 jit_solution(17727287539593969022)
XLA Ops:
  10.6 10.5 all_gather.42
  40.8 17.4 %all-gather.9.cloned.1.call-done = bf16[1024,3072]{1,0:T(8,128)(2,1)} async-done(((bf16[128,3072]{1,0:T(8,128)(2,1)}), bf16[1024,3072]{1,0:T(8,128)(2,1)}) %all-gather.9.cloned.1.call-update) | async-done | bytes 6291472 | tf_op jit(solution)/shard_map/all_gather | solution.py:144
  76.8 23.4 %all-to-all-done = bf16[3,112,1024]{1,0,2:T(4,128)(2,1)} async-done(((bf16[3,112,1024]{1,0,2:T(4,128)(2,1)}), bf16[3,112,1024]{1,0,2:T(4,128)(2,1)}, u32[]{:S(2)}, u32[]{:S(2)}) %all-to-all-start) | async-done | bytes 688160 | tf_op jit(solution)/shard_map/all_to_all | solution.py:171
  109.1 20.7 %all-to-all-done.1 = bf16[3,112,1024]{1,0,2:T(4,128)(2,1)} async-done(((bf16[3,112,1024]{1,0,2:T(4,128)(2,1)}), bf16[3,112,1024]{1,0,2:T(4,128)(2,1)}, u32[]{:S(2)}, u32[]{:S(2)}) %all-to-all-start.1) | async-done | bytes 688160 | tf_op jit(solution)/shard_map/all_to_all | solution.py:169
  172.2 16.5 %while.52 = (s32[]{:T(128)}, bf16[3,448,256]{1,2,0:T(8,128)(2,1)}, f32[3,4,448]{2,1,0:T(4,128)S(1)}, bf16[3,448,256]{1,2,0:T(8,128)(2,1)}, bf16[3,448,256]{1,2,0...) while((s32[]{:T(128)}, bf16[3,448,256]{1,2,0:T(8,128)(2,1)}, f32[3,4,448]{2,1,0:T(4,128)S(1)}, ...), condition=%wide.region_5.6_spmd, body=%wide.region_2.5_spmd.sunk | while | flops 213059840 | bytes 13282405 | solution.py:175
  191.0 45.5 %all-to-all-done.4 = bf16[3,375,1024]{1,0,2:T(4,128)(2,1)} async-done(((bf16[3,375,1024]{1,0,2:T(4,128)(2,1)}), bf16[3,375,1024]{1,0,2:T(4,128)(2,1)}, u32[]{:S(2)}, u32[]{:S(2)}) %all-to-all-start.4) | async-done | bytes 2304032 | tf_op jit(solution)/shard_map/all_to_all | solution.py:173
  250.6 12.6 all-to-all-done.3
  278.7 59.4 %all-to-all-done.6 = bf16[3,375,1024]{1,0,2:T(4,128)(2,1)} async-done(((bf16[3,375,1024]{1,0,2:T(4,128)(2,1)}), bf16[3,375,1024]{1,0,2:T(4,128)(2,1)}, u32[]{:S(2)}, u32[]{:S(2)}) %all-to-all-start.6) | async-done | bytes 2304032 | tf_op jit(solution)/shard_map/all_to_all | solution.py:172
  374.2 24.3 %while.53 = (s32[]{:T(128)}, bf16[3,448,256]{1,2,0:T(8,128)(2,1)}, f32[3,4,448]{2,1,0:T(4,128)S(1)}, bf16[3,1500,256]{1,2,0:T(8,128)(2,1)}, bf16[3,448,256]{1,2,...) while((s32[]{:T(128)}, bf16[3,448,256]{1,2,0:T(8,128)(2,1)}, f32[3,4,448]{2,1,0:T(4,128)S(1)}, ...), condition=%wide.region_11.12_spmd, body=%wide.region_8.11_spmd.sunk | while | flops 704368896 | bytes 38333540 | solution.py:185
  415.0 13.3 all-to-all-done.7
  445.7 13.4 multiply_convert_fusion.2
  459.1 12.2 fusion.135
  495.5 20.1 %all-to-all-done.8 = bf16[3,112,1024]{1,0,2:T(4,128)(2,1)} async-done(((bf16[3,112,1024]{1,0,2:T(4,128)(2,1)}), bf16[3,112,1024]{1,0,2:T(4,128)(2,1)}, u32[]{:S(2)}, u32[]{:S(2)}) %all-to-all-start.8) | async-done | bytes 688160 | tf_op jit(solution)/shard_map/all_to_all | solution.py:231
  518.8 83.1 %while.54 = (s32[]{:T(128)}, bf16[3,448,256]{1,2,0:T(8,128)(2,1)}, bf16[3,1500,256]{1,2,0:T(8,128)(2,1)}, bf16[3,1500,256]{1,2,0:T(8,128)(2,1)}, bf16[3,1500,256...) while((s32[]{:T(128)}, bf16[3,448,256]{1,2,0:T(8,128)(2,1)}, ...), condition=%wide.region_18.19_spmd, body=%wide.region_16.18_spmd.sunk | while | flops 1745392896 | bytes 138405184 | solution.py:234
  603.7 25.2 %all_to_all.270 = bf16[3,448,256]{2,0,1:T(4,128)(2,1)S(1)} all-to-all(bf16[3,448,256]{2,0,1:T(4,128)(2,1)S(1)} %copy.249), channel_id=1, replica_groups=mesh['fsdp'=8,'seq'=4] {'seq'}, dimensions={1} | all-to-all | bytes 1376256 | tf_op jit(solution)/shard_map/all_to_all | solution.py:239
  653.5 18.9 %all-to-all-done.10 = bf16[3,112,1024]{1,0,2:T(4,128)(2,1)S(1)} async-done(((bf16[3,112,1024]{1,0,2:T(4,128)(2,1)}), bf16[3,112,1024]{1,0,2:T(4,128)(2,1)S(1)}, u32[]{:S(2)}, u32[]{:S(2)}) %all-to-all-start.10) | async-done | bytes 688160 | tf_op jit(solution)/shard_map/all_to_all | solution.py:260
  687.7 58.0 %all-to-all-done.14 = bf16[3,1500,256]{2,0,1:T(4,128)(2,1)} async-done(((bf16[3,1500,256]{2,0,1:T(4,128)(2,1)}), bf16[3,1500,256]{2,0,1:T(4,128)(2,1)}, u32[]{:S(2)}, u32[]{:S(2)}) %all-to-all-start.14) | async-done | bytes 2304032 | tf_op jit(solution)/shard_map/all_to_all | solution.py:240
  760.8 58.2 %all-to-all-done.15 = bf16[3,1500,256]{2,0,1:T(4,128)(2,1)} async-done(((bf16[3,1500,256]{2,0,1:T(4,128)(2,1)}), bf16[3,1500,256]{2,0,1:T(4,128)(2,1)}, u32[]{:S(2)}, u32[]{:S(2)}) %all-to-all-start.15) | async-done | bytes 2304032 | tf_op jit(solution)/shard_map/all_to_all | solution.py:241
  844.1 49.8 %while.55 = (s32[]{:T(128)}, bf16[3,448,256]{1,2,0:T(8,128)(2,1)}, bf16[3,448,256]{1,2,0:T(8,128)(2,1)}, bf16[3,448,256]{1,2,0:T(8,128)(2,1)}, bf16[3,448,256]{1...) while((s32[]{:T(128)}, bf16[3,448,256]{1,2,0:T(8,128)(2,1)}, ...), condition=%wide.region_23.24_spmd, body=%wide.region_21.23_spmd.sunk | while | flops 523979008 | bytes 43873472 | solution.py:261
  902.3 19.9 %all-to-all-done.11 = bf16[3,448,256]{2,0,1:T(4,128)(2,1)S(1)} async-done(((bf16[3,448,256]{2,0,1:T(4,128)(2,1)}), bf16[3,448,256]{2,0,1:T(4,128)(2,1)S(1)}, u32[]{:S(2)}, u32[]{:S(2)}) %all-to-all-start.11) | async-done | bytes 688160 | tf_op jit(solution)/shard_map/all_to_all | solution.py:265
  928.9 20.1 %all-to-all-done.12 = bf16[3,448,256]{2,0,1:T(4,128)(2,1)S(1)} async-done(((bf16[3,448,256]{2,0,1:T(4,128)(2,1)}), bf16[3,448,256]{2,0,1:T(4,128)(2,1)S(1)}, u32[]{:S(2)}, u32[]{:S(2)}) %all-to-all-start.12) | async-done | bytes 688160 | tf_op jit(solution)/shard_map/all_to_all | solution.py:266
  957.4 18.3 %all-to-all-done.13 = bf16[3,448,256]{2,0,1:T(4,128)(2,1)} async-done(((bf16[3,448,256]{2,0,1:T(4,128)(2,1)}), bf16[3,448,256]{2,0,1:T(4,128)(2,1)}, u32[]{:S(2)}, u32[]{:S(2)}) %all-to-all-start.13) | async-done | bytes 688160 | tf_op jit(solution)/shard_map/all_to_all | solution.py:267
  987.9 16.5 %convolution_bitcast_fusion.1 = f32[1024,4096]{1,0:T(8,128)} fusion(bf16[3,112,4096]{2,1,0:T(8,128)(2,1)} %copy-done.29, f32[3,112,1024]{2,1,0:T(8,128)} %copy-done.10, f32[1024]{0:T(1024)S(1)} %bitcast.466, f32[1024]{0:T(1024)S(1)} %bitcast.464, f32[3,112]{1,0:T(4,128)S(1)} %copy-done.59, f32[3,112]{1,0:T(4,128)S(1)} %copy-done.53), kind=kOutput, calls=%fused_computation.62 | convolution fusion | flops 2820292608 | bytes 20916864 | tf_op jit(solution)/shard_map/cld,cle->de/dot_general | solution.py:32
  1004.9 13.3 convolution_bitcast_fusion
  1038.9 39.2 %reduce-scatter.17.cloned.1.call-done = f32[128,3072]{1,0:T(8,128)} async-done(((f32[1024,3072]{1,0:T(8,128)}), f32[128,3072]{1,0:T(8,128)}) %reduce-scatter.17.cloned.1.call-update) | async-done | bytes 1572880 | tf_op jit(solution)/shard_map/reduce_scatter | solution.py:309
  1080.5 117.2 %reduce-scatter.27.cloned.1.call-done = f32[128,4096]{1,0:T(8,128)} async-done(((f32[1024,4096]{1,0:T(8,128)}), f32[128,4096]{1,0:T(8,128)}) %reduce-scatter.27.cloned.1.call-update) | async-done | bytes 2097168 | tf_op jit(solution)/shard_map/reduce_scatter | solution.py:314
  1200.3 116.7 %reduce-scatter.29.cloned.1.call-done = f32[512,1024]{1,0:T(8,128)} async-done(((f32[4096,1024]{1,0:T(8,128)}), f32[512,1024]{1,0:T(8,128)}) %reduce-scatter.29.cloned.1.call-update) | async-done | bytes 2097168 | tf_op jit(solution)/shard_map/reduce_scatter | solution.py:316
  1321.6 23.4 %all-reduce = bf16[4096]{0:T(1024)(128)(2,1)S(1)} all-reduce(f32[4096]{0:T(1024)S(1)} %copy-done.73), channel_id=11, replica_groups=mesh['fsdp'=8,'seq'=4] {'fsdp'}, use_global_device_ids=true, to_apply=%region_60.61.clone | all-reduce | flops 4096 | bytes 24576
  1355.9 36.8 %reduce-scatter.33.cloned.1.call-done = f32[128,3]{1,0:T(8,128)} async-done(((f32[1024,3]{1,0:T(8,128)}), f32[128,3]{1,0:T(8,128)}) %reduce-scatter.33.cloned.1.call-update) | async-done | bytes 1552
  1403.6 23.2 %reduce-scatter.15.cloned.1.call-done = f32[7,128]{1,0:T(8,128)} async-done(((f32[7,1024]{1,0:T(8,128)}), f32[7,128]{1,0:T(8,128)}) %reduce-scatter.15.cloned.1.call-update) | async-done | bytes 3600 | tf_op jit(solution)/shard_map/reduce_scatter | solution.py:308
  1427.5 11.9 all-reduce.1
  1441.7 146.5 %all-reduce.5.cloned.1.call-done = (bf16[128,2048]{0,1:T(8,128)(2,1)}, bf16[128,3072]{1,0:T(8,128)(2,1)}, bf16[128,1024]{1,0:T(8,128)(2,1)}, bf16[128,1024]{1,0:...) async-done(((bf16[128,2048]{0,1:T(8,128)(2,1)}, bf16[128,3072]{1,0:T(8,128)(2,1)}, bf16[128,1024]{1,0:T(8,128)(2,1)}, ...) | async-done | bytes 4194320 | tf_op jit(solution)/shard_map/psum | solution.py:337
  (565 shorter events, 578.2 us)
Async XLA Ops:
  7.2 51.0 %all-gather.9.cloned.1.call-start = ((), (), s32[]{:S(2)}) async-start(), calls=%async_computation.26 | async-start | bytes 7077888 | tf_op jit(solution)/shard_map/all_gather | solution.py:144
  7.9 126.1 %all-gather.13.cloned.1.call-start = ((), (), s32[]{:S(2)}) async-start(), calls=%async_computation.28 | async-start | bytes 4718592 | tf_op jit(solution)/shard_map/all_gather | solution.py:147
  8.7 261.4 %all-gather.11.cloned.1.call-start = ((), (), s32[]{:S(2)}) async-start(), calls=%async_computation.27 | async-start | bytes 2359296 | tf_op jit(solution)/shard_map/all_gather | solution.py:145
  9.4 264.8 %all-gather.15.cloned.1.call-start = ((), (), s32[]{:S(2)}) async-start(), calls=%async_computation.29 | async-start | bytes 2359296 | tf_op jit(solution)/shard_map/all_gather | solution.py:146
  10.0 420.5 %all-gather.17.cloned.1.call-start = ((), (), s32[]{:S(2)}) async-start(), calls=%async_computation.30 | async-start | bytes 2359296 | tf_op jit(solution)/shard_map/all_gather | solution.py:148
  69.3 30.9 %all-to-all-start = ((bf16[3,112,1024]{1,0,2:T(4,128)(2,1)}), bf16[3,112,1024]{1,0,2:T(4,128)(2,1)}, u32[]{:S(2)}, u32[]{:S(2)}) async-start(bf16[3,112,1024]{1,0,2:T(4,128)(2,1)} %copy.214), calls=%async_computation | async-start | bytes 2097152 | tf_op jit(solution)/shard_map/all_to_all | solution.py:171
  73.9 361.2 %all-gather.19.cloned.1.call-start = ((), (), s32[]{:S(2)}) async-start(), calls=%async_computation.31 | async-start | bytes 9437184 | tf_op jit(solution)/shard_map/all_gather | solution.py:149
  100.1 29.6 %all-to-all-start.1 = ((bf16[3,112,1024]{1,0,2:T(4,128)(2,1)}), bf16[3,112,1024]{1,0,2:T(4,128)(2,1)}, u32[]{:S(2)}, u32[]{:S(2)}) async-start(bf16[3,112,1024]{1,0,2:T(4,128)(2,1)} %copy.217), calls=%async_computation.1 | async-start | bytes 2097152 | tf_op jit(solution)/shard_map/all_to_all | solution.py:169
  129.8 31.6 %all-to-all-start.2 = ((bf16[3,112,1024]{1,0,2:T(4,128)(2,1)}), bf16[3,112,1024]{1,0,2:T(4,128)(2,1)}, u32[]{:S(2)}, u32[]{:S(2)}) async-start(bf16[3,112,1024]{1,0,2:T(4,128)(2,1)} %copy.220), calls=%async_computation.2 | async-start | bytes 2097152 | tf_op jit(solution)/shard_map/all_to_all | solution.py:170
  161.4 75.1 %all-to-all-start.4 = ((bf16[3,375,1024]{1,0,2:T(4,128)(2,1)}), bf16[3,375,1024]{1,0,2:T(4,128)(2,1)}, u32[]{:S(2)}, u32[]{:S(2)}) async-start(bf16[3,375,1024]{1,0,2:T(4,128)(2,1)} %copy.229), calls=%async_computation.4 | async-start | bytes 6291456 | tf_op jit(solution)/shard_map/all_to_all | solution.py:173
  236.5 26.7 %all-to-all-start.3 = ((bf16[3,448,256]{2,0,1:T(4,128)(2,1)}), bf16[3,448,256]{2,0,1:T(4,128)(2,1)}, u32[]{:S(2)}, u32[]{:S(2)}) async-start(bf16[3,448,256]{2,0,1:T(4,128)(2,1)} %copy.226), calls=%async_computation.3 | async-start | bytes 1835008 | tf_op jit(solution)/shard_map/all_to_all | solution.py:176
  263.2 74.9 %all-to-all-start.6 = ((bf16[3,375,1024]{1,0,2:T(4,128)(2,1)}), bf16[3,375,1024]{1,0,2:T(4,128)(2,1)}, u32[]{:S(2)}, u32[]{:S(2)}) async-start(bf16[3,375,1024]{1,0,2:T(4,128)(2,1)} %copy.234), calls=%async_computation.6 | async-start | bytes 6291456 | tf_op jit(solution)/shard_map/all_to_all | solution.py:172
  338.1 32.4 %all-to-all-start.5 = ((bf16[3,112,1024]{1,0,2:T(4,128)(2,1)}), bf16[3,112,1024]{1,0,2:T(4,128)(2,1)S(1)}, u32[]{:S(2)}, u32[]{:S(2)}) async-start(bf16[3,112,1024]{1,0,2:T(4,128)(2,1)} %copy.231), calls=%async_computation.5 | async-start | bytes 2097152 | tf_op jit(solution)/shard_map/all_to_all | solution.py:182
  341.6 117.5 %all-gather.21.cloned.1.call-start = ((), (), s32[]{:S(2)}) async-start(), calls=%async_computation.32 | async-start | bytes 9437184 | tf_op jit(solution)/shard_map/all_gather | solution.py:151
  400.8 27.5 %all-to-all-start.7 = ((bf16[3,448,256]{2,0,1:T(4,128)(2,1)}), bf16[3,448,256]{2,0,1:T(4,128)(2,1)}, u32[]{:S(2)}, u32[]{:S(2)}) async-start(bf16[3,448,256]{2,0,1:T(4,128)(2,1)} %copy.239), calls=%async_computation.7 | async-start | bytes 1835008 | tf_op jit(solution)/shard_map/all_to_all | solution.py:188
  486.0 29.5 %all-to-all-start.8 = ((bf16[3,112,1024]{1,0,2:T(4,128)(2,1)}), bf16[3,112,1024]{1,0,2:T(4,128)(2,1)}, u32[]{:S(2)}, u32[]{:S(2)}) async-start(bf16[3,112,1024]{1,0,2:T(4,128)(2,1)} %copy.242), calls=%async_computation.8 | async-start | bytes 2097152 | tf_op jit(solution)/shard_map/all_to_all | solution.py:231
  490.3 541.0 %reduce-scatter.25.cloned.1.call-start = ((), (), s32[]{:S(2)}) async-start(), calls=%async_computation.38 | async-start | bytes 4718592 | tf_op jit(solution)/shard_map/reduce_scatter | solution.py:313
  495.5 537.7 %reduce-scatter.19.cloned.1.call-start = ((), (), s32[]{:S(2)}) async-start(), calls=%async_computation.35 | async-start | bytes 4718592 | tf_op jit(solution)/shard_map/reduce_scatter | solution.py:310
  644.1 28.3 %all-to-all-start.10 = ((bf16[3,112,1024]{1,0,2:T(4,128)(2,1)}), bf16[3,112,1024]{1,0,2:T(4,128)(2,1)S(1)}, u32[]{:S(2)}, u32[]{:S(2)}) async-start(bf16[3,112,1024]{1,0,2:T(4,128)(2,1)} %copy.252), calls=%async_computation.10 | async-start | bytes 2097152 | tf_op jit(solution)/shard_map/all_to_all | solution.py:260
  672.4 73.3 %all-to-all-start.14 = ((bf16[3,1500,256]{2,0,1:T(4,128)(2,1)}), bf16[3,1500,256]{2,0,1:T(4,128)(2,1)}, u32[]{:S(2)}, u32[]{:S(2)}) async-start(bf16[3,1500,256]{2,0,1:T(4,128)(2,1)} %copy.268), calls=%async_computation.14 | async-start | bytes 6144000 | tf_op jit(solution)/shard_map/all_to_all | solution.py:240
  677.1 357.8 %reduce-scatter.21.cloned.1.call-start = ((), (), s32[]{:S(2)}) async-start(), calls=%async_computation.36 | async-start | bytes 4718592 | tf_op jit(solution)/shard_map/reduce_scatter | solution.py:311
  745.7 73.3 %all-to-all-start.15 = ((bf16[3,1500,256]{2,0,1:T(4,128)(2,1)}), bf16[3,1500,256]{2,0,1:T(4,128)(2,1)}, u32[]{:S(2)}, u32[]{:S(2)}) async-start(bf16[3,1500,256]{2,0,1:T(4,128)(2,1)} %copy.271), calls=%async_computation.15 | async-start | bytes 6144000 | tf_op jit(solution)/shard_map/all_to_all | solution.py:241
  750.3 286.5 %reduce-scatter.23.cloned.1.call-start = ((), (), s32[]{:S(2)}) async-start(), calls=%async_computation.37 | async-start | bytes 9437184 | tf_op jit(solution)/shard_map/reduce_scatter | solution.py:312
  923.1 25.9 %all-to-all-start.12 = ((bf16[3,448,256]{2,0,1:T(4,128)(2,1)}), bf16[3,448,256]{2,0,1:T(4,128)(2,1)S(1)}, u32[]{:S(2)}, u32[]{:S(2)}) async-start(bf16[3,448,256]{2,0,1:T(4,128)(2,1)} %copy.262), calls=%async_computation.12 | async-start | bytes 1835008 | tf_op jit(solution)/shard_map/all_to_all | solution.py:266
  948.9 26.7 %all-to-all-start.13 = ((bf16[3,448,256]{2,0,1:T(4,128)(2,1)}), bf16[3,448,256]{2,0,1:T(4,128)(2,1)}, u32[]{:S(2)}, u32[]{:S(2)}) async-start(bf16[3,448,256]{2,0,1:T(4,128)(2,1)} %copy.265), calls=%async_computation.13 | async-start | bytes 1835008 | tf_op jit(solution)/shard_map/all_to_all | solution.py:267
  953.2 124.9 %reduce-scatter.17.cloned.1.call-start = ((), (), s32[]{:S(2)}) async-start(), calls=%async_computation.34 | async-start | bytes 14155776 | tf_op jit(solution)/shard_map/reduce_scatter | solution.py:309
  987.3 210.3 %reduce-scatter.27.cloned.1.call-start = ((), (), s32[]{:S(2)}) async-start(), calls=%async_computation.39 | async-start | bytes 18874368 | tf_op jit(solution)/shard_map/reduce_scatter | solution.py:314
  1004.4 312.6 %reduce-scatter.29.cloned.1.call-start = ((), (), s32[]{:S(2)}) async-start(), calls=%async_computation.40 | async-start | bytes 18874368 | tf_op jit(solution)/shard_map/reduce_scatter | solution.py:316
  1018.2 336.8 %reduce-scatter.31.cloned.1.call-start = ((), (), s32[]{:S(2)}) async-start(), calls=%async_computation.41 | async-start | bytes 589824
  1028.1 364.6 %reduce-scatter.33.cloned.1.call-start = ((), (), s32[]{:S(2)}) async-start(), calls=%async_computation.42 | async-start | bytes 589824
  1029.2 397.6 %reduce-scatter.15.cloned.1.call-start = ((), (), s32[]{:S(2)}) async-start(), calls=%async_computation.33 | async-start | bytes 36864 | tf_op jit(solution)/shard_map/reduce_scatter | solution.py:308
  1031.3 556.9 %all-reduce.5.cloned.1.call-start = ((), (), s32[]{:S(2)}) async-start(), calls=%async_computation.43 | async-start | bytes 8388608 | tf_op jit(solution)/shard_map/psum | solution.py:337
  (108 other events, 1393.1 us)
Sparse Core Ops, SparseCore 0:
  9.9 48.2 all-gather.8
  60.1 36.7 all-gather.12
  98.7 27.8 all-gather.10
  128.4 27.8 all-gather.14
  158.1 27.8 all-gather.16
  187.7 54.3 all-gather.18
  344.3 54.9 all-gather.20
  495.6 51.8 reduce-scatter.24
  639.9 49.5 reduce-scatter.18
  692.7 51.2 reduce-scatter.20
  841.4 69.4 reduce-scatter.22
  987.4 90.6 reduce-scatter.16
  1081.6 115.9 reduce-scatter.26
  1201.0 115.9 reduce-scatter.28
  1320.5 34.1 reduce-scatter.30
  1358.5 34.1 reduce-scatter.32
  1395.5 31.2 reduce-scatter.14
  1430.9 157.2 all-reduce.4
where the time goes:
time: 1620 us; the launch traced here: 1610 us
  waiting for transfers between devices  889 us (55%)
  matrix products  232 us (14%)
  local copies, waits for them, and re-layouts  229 us (14%)
  blocking collectives  96.7 us (6%)
  other arithmetic  76.6 us (5%)
  starting transfers between devices  66.6 us (4%)
  between operations  16.2 us (1%)
    psum x1, waiting for transfers between devices, local(): lax.psum(part_cross_kv.astype(jnp.bfloat16), 'seq').astype(jnp.float32)  147 us
    reduce_scatter x1, waiting for transfers between devices, local(): lax.psum_scatter(grad_w_inner, 'fsdp', scatter_dimension=0, tiled=True)  117 us
    reduce_scatter x1, waiting for transfers between devices, local(): lax.psum_scatter(grad_w_outer, 'fsdp', scatter_dimension=0, tiled=True)  117 us
    all_to_all x1, waiting for transfers between devices, local(): lax.all_to_all(cross_keys, 'seq', split_axis=2, concat_axis=1, tiled=True)  59.4 us
    all_to_all x1, waiting for transfers between devices, local(): lax.all_to_all(grad_cross_value_heads, 'seq', split_axis=1, concat_axis=2...  58.2 us
    all_to_all x1, waiting for transfers between devices, local(): lax.all_to_all(grad_cross_key_heads, 'seq', split_axis=1, concat_axis=2,...  58 us
    dot_general x7, matrix products, weight_grad(): jnp.einsum('cld,cle->de', operand, incoming, preferred_element_type=jnp.f...  57.2 us
    all_to_all x1, waiting for transfers between devices, local(): lax.all_to_all(cross_values, 'seq', split_axis=2, concat_axis=1, tiled=True)  45.5 us
  transfers between devices with their start and end apart: 33, of which 20 were waited for; matrix products, arithmetic and copies ran while one was open for 28% of the time, Pallas kernels for 0%

commit v1 on v0

v1 whole, which is shorter than its diff:
```python
import functools

import jax
import jax.numpy as jnp
from jax import lax
from jax.experimental import pallas as pl
from jax.experimental.pallas import tpu as pltpu
from jax.sharding import PartitionSpec as P

HD = 64
LANES = 128
NORM_EPSILON = 1e-05
LOW = -1e30
F32 = jnp.float32
BF = jnp.bfloat16
AXES = ("fsdp", "seq")


def two_heads(rows):
    lane = lax.broadcasted_iota(jnp.int32, rows.shape, 1)
    zero = jnp.zeros_like(rows)
    return jnp.concatenate(
        [jnp.where(lane < HD, rows, zero), jnp.where(lane >= HD, rows, zero)], axis=0
    )


def one_row(stacked):
    count = stacked.shape[0] // 2
    lane = lax.broadcasted_iota(jnp.int32, (count, stacked.shape[1]), 1)
    return jnp.where(lane < HD, stacked[:count], stacked[count:])


def over_rows(first, second):
    return lax.dot_general(first, second, (((0,), (0,)), ((), ())), preferred_element_type=F32)


def over_lanes(first, second):
    return lax.dot_general(first, second, (((1,), (1,)), ((), ())), preferred_element_type=F32)


def fill_scores(scores_ref, keys, queries, valid, places):
    size = keys.shape[0]
    scores = over_lanes(keys, queries)
    if places is not None:
        key_place, query_place = places
        scores = jnp.where(key_place <= query_place, scores, LOW)
    scores_ref[...] = scores
    if valid < size:
        first = valid // 8 * 8
        row = lax.broadcasted_iota(jnp.int32, (size - first, queries.shape[0]), 0)
        scores_ref[first:size] = jnp.where(row < valid - first, scores_ref[first:size], LOW)


def forward_kernel(chunk, valid, causal, *refs):
    if causal:
        q_ref, k_ref, v_ref, kp_ref, qp_ref, o_ref, log_ref, s_ref = refs
    else:
        q_ref, k_ref, v_ref, o_ref, log_ref, s_ref = refs
    queries = two_heads(q_ref[...])
    count = k_ref.shape[0] // chunk
    width = queries.shape[0]

    def first(step, top):
        rows = pl.ds(pl.multiple_of(step * chunk, chunk), chunk)
        places = (kp_ref[rows], qp_ref[...]) if causal else None
        part = s_ref.at[rows]
        fill_scores(part, k_ref[rows], queries, valid, places)
        return jnp.maximum(top, jnp.max(part[...], axis=0, keepdims=True))

    top = lax.fori_loop(0, count, first, jnp.full((1, width), LOW, F32))

    def second(step, carry):
        total, mixed = carry
        rows = pl.ds(pl.multiple_of(step * chunk, chunk), chunk)
        raised = jnp.exp(s_ref[rows] - top)
        total = total + jnp.sum(raised, axis=0, keepdims=True)
        mixed = mixed + over_rows(v_ref[rows], raised.astype(BF))
        return total, mixed

    total, mixed = lax.fori_loop(
        0, count, second, (jnp.zeros((1, width), F32), jnp.zeros((LANES, width), F32))
    )
    o_ref[...] = one_row(jnp.transpose(mixed / total)).astype(BF)
    log_ref[...] = (top + jnp.log(total))[None]


def backward_kernel(chunk, valid, causal, *refs):
    if causal:
        q_ref, k_ref, v_ref, o_ref, g_ref, log_ref, kp_ref, qp_ref = refs[:8]
    else:
        q_ref, k_ref, v_ref, o_ref, g_ref, log_ref = refs[:6]
    gq_ref, gk_ref, gv_ref, s_ref = refs[-4:]
    queries = two_heads(q_ref[...])
    grads = two_heads(g_ref[...])
    mixed = o_ref[...].astype(F32)
    product = grads.astype(F32) * jnp.concatenate([mixed, mixed], axis=0)
    row_dot = jnp.sum(jnp.transpose(product), axis=0, keepdims=True)
    log_total = log_ref[0]
    count = k_ref.shape[0] // chunk
    width = queries.shape[0]

    def body(step, grad_queries):
        rows = pl.ds(pl.multiple_of(step * chunk, chunk), chunk)
        places = (kp_ref[rows], qp_ref[...]) if causal else None
        keys = k_ref[rows]
        fill_scores(s_ref, keys, queries, valid, places)
        weights = jnp.exp(s_ref[...] - log_total)
        grad_weights = over_lanes(v_ref[rows], grads)
        grad_scores = (weights * (grad_weights - row_dot)).astype(BF)
        gv_ref[rows] = jnp.dot(weights.astype(BF), grads, preferred_element_type=F32).astype(BF)
        gk_ref[rows] = jnp.dot(grad_scores, queries, preferred_element_type=F32).astype(BF)
        return grad_queries + over_rows(keys, grad_scores)

    grad_queries = lax.fori_loop(0, count, body, jnp.zeros((LANES, width), F32))
    gq_ref[...] = one_row(jnp.transpose(grad_queries)).astype(BF)


def columns(rows):
    return pl.BlockSpec((rows, LANES), lambda pair: (0, pair))


def place_specs(keys, tokens):
    return [
        pl.BlockSpec((keys, 1), lambda pair: (0, 0)),
        pl.BlockSpec((1, 2 * tokens), lambda pair: (0, 0)),
    ]


def attend(queries, keys, values, places, chunk, valid):
    tokens, width = queries.shape
    count = keys.shape[0]
    causal = places is not None
    pairs = width // LANES
    specs = [columns(tokens), columns(count), columns(count)]
    operands = [queries, keys, values]
    if causal:
        specs += place_specs(count, tokens)
        operands += list(places)
    return pl.pallas_call(
        functools.partial(forward_kernel, chunk, valid, causal),
        grid=(pairs,),
        in_specs=specs,
        out_specs=[columns(tokens), pl.BlockSpec((1, 1, 2 * tokens), lambda pair: (pair, 0, 0))],
        out_shape=[
            jax.ShapeDtypeStruct((tokens, width), BF),
            jax.ShapeDtypeStruct((pairs, 1, 2 * tokens), F32),
        ],
        scratch_shapes=[pltpu.VMEM((count, 2 * tokens), F32)],
        compiler_params=pltpu.CompilerParams(vmem_limit_bytes=32 << 20),
        cost_estimate=pl.CostEstimate(
            flops=16 * tokens * count * width,
            transcendentals=tokens * count * width // HD,
            bytes_accessed=4 * (tokens + count) * width,
        ),
        name="attend_causal" if causal else "attend_cross",
    )(*operands)


def attend_back(queries, keys, values, mixed, grads, logs, places, chunk, valid):
    tokens, width = queries.shape
    count = keys.shape[0]
    causal = places is not None
    pairs = width // LANES
    specs = [
        columns(tokens),
        columns(count),
        columns(count),
        columns(tokens),
        columns(tokens),
        pl.BlockSpec((1, 1, 2 * tokens), lambda pair: (pair, 0, 0)),
    ]
    operands = [queries, keys, values, mixed, grads, logs]
    if causal:
        specs += place_specs(count, tokens)
        operands += list(places)
    return pl.pallas_call(
        functools.partial(backward_kernel, chunk, valid, causal),
        grid=(pairs,),
        in_specs=specs,
        out_specs=[columns(tokens), columns(count), columns(count)],
        out_shape=[
            jax.ShapeDtypeStruct((tokens, width), BF),
            jax.ShapeDtypeStruct((count, width), BF),
            jax.ShapeDtypeStruct((count, width), BF),
        ],
        scratch_shapes=[pltpu.VMEM((chunk, 2 * tokens), F32)],
        compiler_params=pltpu.CompilerParams(vmem_limit_bytes=32 << 20),
        cost_estimate=pl.CostEstimate(
            flops=40 * tokens * count * width,
            transcendentals=tokens * count * width // HD,
            bytes_accessed=8 * (tokens + count) * width,
        ),
        name="attend_causal_back" if causal else "attend_cross_back",
    )(*operands)


def product(first, second):
    return jnp.dot(first, second, preferred_element_type=F32)


def product_back(incoming, weight):
    return lax.dot_general(
        incoming, weight, (((1,), (1,)), ((), ())), preferred_element_type=F32
    )


def weight_grad(operand, incoming):
    return lax.dot_general(
        operand, incoming, (((0,), (0,)), ((), ())), preferred_element_type=F32
    ).astype(BF)


def normalized(values):
    average = jnp.mean(values, axis=-1, keepdims=True)
    centred = values - average
    variance = jnp.mean(centred * centred, axis=-1, keepdims=True)
    inverse = lax.rsqrt(variance + NORM_EPSILON)
    return centred * inverse, inverse


def norm_back(incoming, values, gain_row):
    rows, inverse = normalized(values)
    scaled = incoming * gain_row
    average = jnp.mean(scaled, axis=-1, keepdims=True)
    aligned = jnp.mean(scaled * rows, axis=-1, keepdims=True)
    gain_grad = jnp.sum(incoming * rows, axis=0)
    shift_grad = jnp.sum(incoming, axis=0)
    return (scaled - average - rows * aligned) * inverse, gain_grad, shift_grad


def gelu(values):
    return values * (1.0 + lax.erf(values * (0.5**0.5))) * 0.5


def gelu_slope(values):
    return (1.0 + lax.erf(values * (0.5**0.5))) * 0.5 + values * jnp.exp(
        -0.5 * values * values
    ) * (0.5 / jnp.pi) ** 0.5


class Grid:
    def __init__(self, fsdp, seq, clips):
        self.fsdp, self.seq, self.clips = fsdp, seq, clips
        self.here = lax.axis_index("seq")
        self.first = self.first_of(lax.axis_index("fsdp"))

    def first_of(self, group):
        return (group % 2) * (self.seq - self.clips)

    def works(self, group, place):
        return 0 <= place - self.first_of(group) < self.clips

    def turn(self, values, step, to_workers):
        pairs = []
        for group in range(self.fsdp):
            for place in range(self.seq):
                target = (place + step) % self.seq
                worker = target if to_workers else place
                if self.works(group, worker):
                    pairs.append((group * self.seq + place, group * self.seq + target))
        return lax.ppermute(values, AXES, pairs)

    def clip_at(self, place):
        return jnp.clip(place - self.first, 0, self.clips - 1)

    def collect(self, values):
        own = lax.dynamic_index_in_dim(values, self.clip_at(self.here), 0, keepdims=False)
        active = (self.here >= self.first) & (self.here < self.first + self.clips)
        pieces = [jnp.where(active, own, jnp.zeros_like(own))]
        for step in range(1, self.seq):
            target = (self.here + step) % self.seq
            sent = lax.dynamic_index_in_dim(values, self.clip_at(target), 0, keepdims=False)
            pieces.append(self.turn(sent, step, True))
        return pieces

    def hand_back(self, pieces):
        arrived = [pieces[0]]
        for step in range(1, self.seq):
            arrived.append(self.turn(pieces[step], self.seq - step, False))
        stacked = jnp.stack(arrived)
        rows = []
        for clip in range(self.clips):
            step = (clip + self.first - self.here) % self.seq
            rows.append(lax.dynamic_index_in_dim(stacked, step, 0, keepdims=False))
        return jnp.stack(rows)

    def places(self, rows):
        source = (self.here - jnp.arange(self.seq)) % self.seq
        return (source[:, None] * rows + jnp.arange(rows)[None, :]).reshape(-1)

    def seq_sum(self, values):
        if self.seq != 4:
            return lax.psum(values, "seq")

        def chain(moved, links):
            pairs = [
                (group * self.seq + a, group * self.seq + b)
                for group in range(self.fsdp)
                for a, b in links
            ]
            return lax.ppermute(moved, AXES, pairs)

        half = (values.astype(F32) + chain(values, ((0, 1), (3, 2))).astype(F32)).astype(BF)
        whole = (half.astype(F32) + chain(half, ((1, 2), (2, 1))).astype(F32)).astype(BF)
        back = chain(whole, ((1, 0), (2, 3)))
        return jnp.where((self.here == 0) | (self.here == 3), back, whole)


def local(
    mesh_shape,
    hidden_in,
    encoded,
    out_grad,
    norm_gain,
    norm_shift,
    biases,
    self_qkv,
    self_out,
    cross_q,
    cross_kv,
    cross_out,
    mlp_in,
    mlp_in_bias,
    mlp_out,
):
    clips, rows, width = hidden_in.shape
    frames = encoded.shape[1]
    padded = (frames + 15) // 16 * 16
    grid = Grid(mesh_shape["fsdp"], mesh_shape["seq"], clips)
    shard = norm_gain.shape[1]
    norms = norm_gain.shape[0]
    bias_count = biases.shape[0]
    scaling = HD ** (-0.5)

    def gathered(member):
        return lax.all_gather(member, "fsdp", axis=0, tiled=True)

    def reduced(member):
        part = lax.psum_scatter(member, "fsdp", scatter_dimension=0, tiled=True)
        return grid.seq_sum(part).astype(F32)

    residual_in = jnp.concatenate(grid.collect(hidden_in), axis=0).astype(F32)
    small = jnp.concatenate([norm_gain, norm_shift, biases, mlp_in_bias.reshape(-1, shard)], axis=0)
    small = lax.all_gather(small, "fsdp", axis=0)
    vectors = small[:, : 2 * norms + bias_count].swapaxes(0, 1).reshape(-1, width).astype(F32)
    gain, shift, bias = vectors[:norms], vectors[norms : 2 * norms], vectors[2 * norms :]
    inner_bias = small[:, 2 * norms + bias_count :].reshape(1, -1).astype(F32)

    full_qkv = gathered(self_qkv)
    frame_pieces = [
        jnp.pad(piece, ((0, padded - frames), (0, 0)))
        for piece in grid.collect(encoded)
    ]
    frame_rows = jnp.concatenate(frame_pieces, axis=0)
    top = jnp.concatenate(grid.collect(out_grad), axis=0)
    full_self_out = gathered(self_out)
    full_cross_kv = gathered(cross_kv)
    full_cross_q = gathered(cross_q)
    full_cross_out = gathered(cross_out)
    full_inner = gathered(mlp_in)
    full_outer = gathered(mlp_out)

    place = grid.places(rows)
    places = (place[:, None], jnp.concatenate([place, place])[None, :])
    tokens = place.shape[0]

    normed_one = (normalized(residual_in)[0] * gain[0] + shift[0]).astype(BF)
    pre_qkv = product(normed_one, full_qkv)
    queries = ((pre_qkv[:, :width] + bias[0]) * scaling).astype(BF)
    keys = pre_qkv[:, width : 2 * width].astype(BF)
    values = (pre_qkv[:, 2 * width :] + bias[1]).astype(BF)
    self_mix, self_log = attend(queries, keys, values, places, tokens, tokens)
    after_self = residual_in + product(self_mix, full_self_out) + bias[2]
    normed_two = (normalized(after_self)[0] * gain[1] + shift[1]).astype(BF)
    cross_queries = ((product(normed_two, full_cross_q) + bias[3]) * scaling).astype(BF)
    cross_pre = product(frame_rows, full_cross_kv)
    cross_keys = cross_pre[:, :width].astype(BF)
    cross_values = (cross_pre[:, width:] + bias[4]).astype(BF)
    cross_mix, cross_log = attend(cross_queries, cross_keys, cross_values, None, padded, frames)
    after_cross = after_self + product(cross_mix, full_cross_out) + bias[5]
    normed_three = (normalized(after_cross)[0] * gain[2] + shift[2]).astype(BF)
    inner = product(normed_three, full_inner) + inner_bias
    activated = gelu(inner).astype(BF)
    hidden_rows = (after_cross + product(activated, full_outer) + bias[6]).astype(BF)

    top_wide = top.astype(F32)
    grad_w_outer = weight_grad(activated, top)
    grad_bias_six = jnp.sum(top_wide, axis=0)
    grad_inner = product_back(top, full_outer) * gelu_slope(inner)
    grad_inner_low = grad_inner.astype(BF)
    grad_w_inner = weight_grad(normed_three, grad_inner_low)
    grad_inner_bias = jnp.sum(grad_inner, axis=0)
    grad_normed_three = product_back(grad_inner_low, full_inner)
    from_three, gain_three, shift_three = norm_back(grad_normed_three, after_cross, gain[2])
    grad_after_cross = top_wide + from_three
    grad_cross_low = grad_after_cross.astype(BF)
    grad_w_cross_out = weight_grad(cross_mix, grad_cross_low)
    grad_bias_five = jnp.sum(grad_after_cross, axis=0)
    grad_cross_mix = product_back(grad_cross_low, full_cross_out).astype(BF)
    grad_cross_queries, grad_cross_keys, grad_cross_values = attend_back(
        cross_queries,
        cross_keys,
        cross_values,
        cross_mix,
        grad_cross_mix,
        cross_log,
        None,
        padded,
        frames,
    )
    scaled_cross = grad_cross_queries * scaling
    grad_w_cross_q = weight_grad(normed_two, scaled_cross)
    grad_bias_three = jnp.sum(scaled_cross.astype(F32), axis=0)
    grad_normed_two = product_back(scaled_cross, full_cross_q)
    grad_pair = jnp.concatenate([grad_cross_keys, grad_cross_values], axis=1)
    grad_w_cross_kv = weight_grad(frame_rows, grad_pair)
    grad_bias_four = jnp.sum(grad_cross_values.astype(F32), axis=0)
    grad_frames = product_back(grad_pair, full_cross_kv).astype(BF)
    from_two, gain_two, shift_two = norm_back(grad_normed_two, after_self, gain[1])
    grad_after_self = grad_after_cross + from_two
    grad_self_low = grad_after_self.astype(BF)
    grad_w_self_out = weight_grad(self_mix, grad_self_low)
    grad_bias_two = jnp.sum(grad_after_self, axis=0)
    grad_self_mix = product_back(grad_self_low, full_self_out).astype(BF)
    grad_queries, grad_keys, grad_values = attend_back(
        queries, keys, values, self_mix, grad_self_mix, self_log, places, tokens, tokens
    )
    scaled_query = grad_queries * scaling
    grad_pre = jnp.concatenate([scaled_query, grad_keys, grad_values], axis=1)
    grad_w_qkv = weight_grad(normed_one, grad_pre)
    grad_bias_zero = jnp.sum(scaled_query.astype(F32), axis=0)
    grad_bias_one = jnp.sum(grad_values.astype(F32), axis=0)
    grad_normed_one = product_back(grad_pre, full_qkv)
    from_one, gain_one, shift_one = norm_back(grad_normed_one, residual_in, gain[0])
    grad_rows = (grad_after_self + from_one).astype(BF)

    total_outer = reduced(grad_w_outer)
    total_inner = reduced(grad_w_inner)
    total_cross_out = reduced(grad_w_cross_out)
    total_cross_q = reduced(grad_w_cross_q)
    total_cross_kv = reduced(grad_w_cross_kv)
    total_self_out = reduced(grad_w_self_out)
    total_qkv = reduced(grad_w_qkv)

    def token_pieces(member):
        return [member[rows * step : rows * (step + 1)] for step in range(grid.seq)]

    hidden_out = grid.hand_back(token_pieces(hidden_rows))
    grad_encoded = grid.hand_back(
        [grad_frames[padded * step : padded * step + frames] for step in range(grid.seq)]
    )
    grad_hidden_in = grid.hand_back(token_pieces(grad_rows))

    sums = jnp.stack(
        [
            gain_one,
            gain_two,
            gain_three,
            shift_one,
            shift_two,
            shift_three,
            grad_bias_zero,
            grad_bias_one,
            grad_bias_two,
            grad_bias_three,
            grad_bias_four,
            grad_bias_five,
            grad_bias_six,
        ]
    )
    inner_sums = grad_inner_bias.reshape(grid.fsdp, -1, shard)
    packed = jnp.concatenate(
        [sums.reshape(-1, grid.fsdp, shard).swapaxes(0, 1), inner_sums], axis=1
    )
    packed = lax.psum(packed, AXES)
    mine = lax.dynamic_index_in_dim(packed, lax.axis_index("fsdp"), 0, keepdims=False)
    return (
        hidden_out,
        grad_hidden_in,
        grad_encoded,
        mine[:norms],
        mine[norms : 2 * norms],
        mine[2 * norms : 2 * norms + bias_count],
        total_qkv,
        total_self_out,
        total_cross_q,
        total_cross_kv,
        total_cross_out,
        total_inner,
        mine[2 * norms + bias_count :].reshape(-1),
        total_outer,
    )


def solution(mesh):
    rows = P("fsdp", "seq", None)
    wide = P(None, "fsdp")
    tall = P("fsdp", None)
    in_specs = (rows,) * 3 + (wide,) * 3 + (tall,) * 6 + (P("fsdp"), tall)
    out_specs = (rows,) * 3 + (wide,) * 3 + (tall,) * 6 + (P("fsdp"), tall)
    return jax.shard_map(
        functools.partial(local, dict(mesh.shape)),
        mesh=mesh,
        in_specs=in_specs,
        out_specs=out_specs,
        check_vma=False,
    )
```

time: 1620 us -> 1020 us (0.63)
  waiting for transfers between devices: 889 us -> 568 us
  local copies, waits for them, and re-layouts: 229 us -> 31.7 us
  matrix products: 232 us -> 126 us
  Pallas kernels: 0 us -> 93.9 us
  blocking collectives: 96.7 us -> 9.18 us
  starting transfers between devices: 66.6 us -> 133 us
  other arithmetic: 76.6 us -> 39.4 us
    all_to_all x15 -> x0, waiting for transfers between devices: 388 us -> none  [the longest x1 59.4 us: local(): lax.all_to_all(cross_keys, 'seq', split_axis=2, concat_axis=1, tiled=True)]
    ppermute x0 -> x39, waiting for transfers between devices: none -> 137 us  [the longest x21 91.4 us: chain(): return lax.ppermute(moved, AXES, pairs)]
    ppermute x0 -> x39, starting transfers between devices: none -> 132 us  [the longest x18 83.3 us: turn(): return lax.ppermute(values, AXES, pairs)]
    psum x1, waiting for transfers between devices: 147 us -> 23.6 us  [local(): packed = lax.psum(packed, AXES)]
    dot_general x63 -> x21, matrix products: 232 us -> 126 us  [the longest x7 49.9 us: weight_grad(): lax.dot_general(operand, incoming, (((0,), (0,)), ((), ())), preferred_el...]
    all_gather x7, waiting for transfers between devices: 17.5 us -> 115 us  [gathered(): return lax.all_gather(member, 'fsdp', axis=0, tiled=True)]
    pallas_call x0 -> x4, Pallas kernels: none -> 93.9 us  [the longest x2 54.9 us: attend_back(): pl.pallas_call(functools.partial(backward_kernel, chunk, valid, causal),...]
    all_to_all x15 -> x0, starting transfers between devices: 64.4 us -> none  [the longest x1 5.32 us: local(): lax.all_to_all(cross_values, 'seq', split_axis=2, concat_axis=1, tiled=True)]
  transfers between devices with their start and end apart: 33 -> 54, of which waited for: 20 -> 20; matrix products, arithmetic and copies ran while one was open for 28% -> 15% of each run, Pallas kernels for 0% -> 4%
where the time goes in v1:
time: 1020 us
  waiting for transfers between devices  568 us (56%)
  starting transfers between devices  133 us (13%)
  matrix products  126 us (12%)
  Pallas kernels  93.9 us (9%)
  other arithmetic  39.4 us (4%)
  local copies, waits for them, and re-layouts  31.7 us (3%)
  between operations  15.9 us (2%)
    reduce_scatter x7, waiting for transfers between devices, reduced(): part = lax.psum_scatter(member, 'fsdp', scatter_dimension=0, tiled=True)  288 us
    all_gather x7, waiting for transfers between devices, gathered(): return lax.all_gather(member, 'fsdp', axis=0, tiled=True)  115 us
    ppermute x21, waiting for transfers between devices, chain(): return lax.ppermute(moved, AXES, pairs)  91.4 us
    ppermute x18, starting transfers between devices, turn(): return lax.ppermute(values, AXES, pairs)  83.3 us
    pallas_call x2, Pallas kernels, attend_back(): pl.pallas_call(functools.partial(backward_kernel, chunk, valid, causal),...  54.9 us
    dot_general x7, matrix products, weight_grad(): lax.dot_general(operand, incoming, (((0,), (0,)), ((), ())), preferred_el...  49.9 us
    ppermute x21, starting transfers between devices, chain(): return lax.ppermute(moved, AXES, pairs)  49.1 us
    dot_general x7, matrix products, product(): return jnp.dot(first, second, preferred_element_type=F32)  46.2 us
  transfers between devices with their start and end apart: 54, of which 20 were waited for; matrix products, arithmetic and copies ran while one was open for 15% of the time, Pallas kernels for 4%

profile of v1, /device:TPU:0, one launch (start us, length us, event | category | flops | bytes accessed | tf_op | source)
XLA Modules:
  0.0 1018.2 jit_solution(2206352429597066640)
XLA Ops:
  31.0 9.2 all-gather.1
  52.3 30.0 %collective-permute-start.9 = (bf16[112,1024]{1,0:T(8,128)(2,1)}, bf16[112,1024]{1,0:T(8,128)(2,1)}, u32[]{:S(2)}, u32[]{:S(2)}) collective-permute-start(bf16[112,1024]{1,0:T(8,128)(2,1)} %get-tuple-element.79), channel_id=1, source_target_pairs={{0,1},{1,2},{3,0},{4,5},{5,6},{6,7},{8,9},{9,10},{11,8},{12,13},{1... | collective-permute-start | bytes 688136 | tf_op jit(solution)/shard_map/ppermute | solution.py:261
  82.3 11.7 %collective-permute-done.4 = bf16[375,1024]{1,0:T(8,128)(2,1)} collective-permute-done((bf16[375,1024]{1,0:T(8,128)(2,1)}, bf16[375,1024]{1,0:T(8,128)(2,1)}, u32[]{:S(2)}, u32[]{:S(2)}) %collective-permute-start.4) | collective-permute-done | bytes 768032 | tf_op jit(solution)/shard_map/ppermute | solution.py:261
  94.1 13.4 %fusion.62 = f32[1536,2048]{1,0:T(8,128)S(1)} fusion(bf16[1024,2048]{1,0:T(8,128)(2,1)} %all-gather.16.cloned.1.call-done, bf16[375,1024]{1,0:T(8,128)(2,1)} %collective-permute-done.5, bf16[375,1024]{1,0:T(8,128)(2,1)} %collective-permute-done.4, bf16[375,1024]{1,0:T(8,128)(2,1)} %collective-permute-done.3, bf16[375,1024]{1,0:T(8,128)(2,1)S(1)} %copy-done.51), kind=kOutput, calls=%fused_computation.190 | convolution fusion | flops 6473908224 | bytes 19849216 | tf_op jit(solution)/shard_map/dot_general | solution.py:198
  117.3 8.7 attend_causal.1
  133.6 22.8 %all-gather.14.cloned.1.call-done = bf16[1024,1024]{1,0:T(8,128)(2,1)} async-done(((bf16[128,1024]{1,0:T(8,128)(2,1)}), bf16[1024,1024]{1,0:T(8,128)(2,1)}) %all-gather.14.cloned.1.call-update) | async-done | bytes 2097168 | tf_op jit(solution)/shard_map/all_gather | solution.py:336
  159.9 30.3 %attend_cross.1 = (bf16[448,1024]{1,0:T(8,128)(2,1)S(1)}, f32[8,1,896]{2,1,0:T(1,128)S(1)}) custom-call(bf16[448,1024]{1,0:T(8,128)(2,1)S(1)} %multiply_convert_fusion.1.refs_0_, bf16[1536,1024]{1,0:T(8,128)(2,1)S(1)} %slice.240.refs_1_, bf16[1536,1024]{1,0:T(8,128)(2,1)S(1)} %copy-done.3), custom_call_target="tpu_custom_call" | custom-call | flops 11274289152 | bytes 8126464 | tf_op jit(solution)/shard_map/attend_cross/pallas_call | solution.py:139
  196.2 46.1 %all-gather.20.cloned.1.call-done = bf16[1024,4096]{1,0:T(8,128)(2,1)} async-done(((bf16[128,4096]{1,0:T(8,128)(2,1)}), bf16[1024,4096]{1,0:T(8,128)(2,1)}) %all-gather.20.cloned.1.call-update) | async-done | bytes 8388624 | tf_op jit(solution)/shard_map/all_gather | solution.py:336
  242.3 9.9 multiply_convert_fusion
  252.3 46.4 %all-gather.22.cloned.1.call-done = bf16[4096,1024]{1,0:T(8,128)(2,1)} async-done(((bf16[512,1024]{1,0:T(8,128)(2,1)}), bf16[4096,1024]{1,0:T(8,128)(2,1)}) %all-gather.22.cloned.1.call-update) | async-done | bytes 8388624 | tf_op jit(solution)/shard_map/all_gather | solution.py:336
  298.6 10.0 fusion.69
  318.9 42.2 %attend_cross_back.1 = (bf16[448,1024]{1,0:T(8,128)(2,1)S(1)}, bf16[1536,1024]{1,0:T(8,128)(2,1)S(1)}, bf16[1536,1024]{1,0:T(8,128)(2,1)S(1)}) custom-call(bf16[448,1024]{1,0:T(8,128)(2,1)S(1)} %copy-done.19, bf16[1536,1024]{1,0:T(8,128)(2,1)S(1)} %copy-done.2, bf16[1536,1024]{1,0:T(8,128)(2,1)S(1)} %copy-done.4, bf16[448,1024]{1,0:T(8,128)(2,1)S(1)} %copy-done.15, ...), custom_call_target="tpu_custom_call" | custom-call | flops 28185722880 | bytes 16252928 | tf_op jit(solution)/shard_map/attend_cross_back/pallas_call | solution.py:176
  366.7 12.7 %attend_causal_back.1 = (bf16[448,1024]{1,0:T(8,128)(2,1)S(1)}, bf16[448,1024]{1,0:T(8,128)(2,1)S(1)}, bf16[448,1024]{1,0:T(8,128)(2,1)S(1)}) custom-call(bf16[448,1024]{1,0:T(8,128)(2,1)S(1)} %copy-done.13, bf16[448,1024]{1,0:T(8,128)(2,1)S(1)} %copy-done.6, bf16[448,1024]{1,0:T(8,128)(2,1)S(1)} %copy-done.11, bf16[448,1024]{1,0:T(8,128)(2,1)S(1)} %copy-done.17, ...), custom_call_target="tpu_custom_call" | custom-call | flops 8220835840 | bytes 7340032 | tf_op jit(solution)/shard_map/attend_causal_back/pallas_call | solution.py:176
  406.2 9.9 convolution_convert_fusion.3
  417.8 7.5 convolution_convert_fusion.2
  426.8 9.1 convolution_convert_fusion.1
  436.9 10.1 convolution_convert_fusion
  476.1 7.2 convolution_convert_fusion.4
  484.5 23.6 %all-reduce.6.cloned.1.call-done = f32[8,17,128]{2,1,0:T(8,128)} async-done(((f32[8,17,128]{2,1,0:T(8,128)}), f32[8,17,128]{2,1,0:T(8,128)}) %all-reduce.6.cloned.1.call-update) | async-done | bytes 69648 | tf_op jit(solution)/shard_map/psum | solution.py:475
  532.9 23.7 %collective-permute-done.16 = bf16[375,1024]{1,0:T(8,128)(2,1)S(1)} collective-permute-done((bf16[375,1024]{1,0:T(8,128)(2,1)S(1)}, bf16[375,1024]{1,0:T(8,128)(2,1)S(1)}, u32[]{:S(2)}, u32[]{:S(2)}) %collective-permute-start.16) | collective-permute-done | bytes 768032 | tf_op jit(solution)/shard_map/ppermute | solution.py:261
  561.8 11.8 %collective-permute-start.21 = (bf16[128,1024]{1,0:T(8,128)(2,1)}, bf16[128,1024]{1,0:T(8,128)(2,1)S(1)}, u32[]{:S(2)}, u32[]{:S(2)}) collective-permute-start(bf16[128,1024]{1,0:T(8,128)(2,1)} %reduce-scatter.10.cloned.1.call-done), channel_id=1, source_target_pairs={{0,1},{3,2},{4,5},{7,6},{8,9},{11,10},{12,13},{15,14},{16,17},{19,... | collective-permute-start | bytes 786440 | tf_op jit(solution)/shard_map/ppermute | solution.py:301
  575.1 24.3 %reduce-scatter.12.cloned.1.call-done = bf16[128,1024]{1,0:T(8,128)(2,1)} async-done(((bf16[1024,1024]{1,0:T(8,128)(2,1)}), bf16[128,1024]{1,0:T(8,128)(2,1)}) %reduce-scatter.12.cloned.1.call-update) | async-done | bytes 262160 | tf_op jit(solution)/shard_map/reduce_scatter | solution.py:339
  606.1 37.8 %reduce-scatter.16.cloned.1.call-done = bf16[128,1024]{1,0:T(8,128)(2,1)} async-done(((bf16[1024,1024]{1,0:T(8,128)(2,1)}), bf16[128,1024]{1,0:T(8,128)(2,1)}) %reduce-scatter.16.cloned.1.call-update) | async-done | bytes 262160 | tf_op jit(solution)/shard_map/reduce_scatter | solution.py:339
  654.9 44.0 %reduce-scatter.14.cloned.1.call-done = bf16[128,2048]{1,0:T(8,128)(2,1)} async-done(((bf16[1024,2048]{1,0:T(8,128)(2,1)}), bf16[128,2048]{1,0:T(8,128)(2,1)}) %reduce-scatter.14.cloned.1.call-update) | async-done | bytes 524304 | tf_op jit(solution)/shard_map/reduce_scatter | solution.py:339
  706.6 7.3 collective-permute-done.27
  716.3 47.7 %reduce-scatter.8.cloned.1.call-done = bf16[128,3072]{1,0:T(8,128)(2,1)} async-done(((bf16[1024,3072]{1,0:T(8,128)(2,1)}), bf16[128,3072]{1,0:T(8,128)(2,1)}) %reduce-scatter.8.cloned.1.call-update) | async-done | bytes 786448 | tf_op jit(solution)/shard_map/reduce_scatter | solution.py:339
  770.0 69.1 %reduce-scatter.18.cloned.1.call-done = bf16[128,4096]{1,0:T(8,128)(2,1)} async-done(((bf16[1024,4096]{1,0:T(8,128)(2,1)}), bf16[128,4096]{1,0:T(8,128)(2,1)}) %reduce-scatter.18.cloned.1.call-update) | async-done | bytes 1048592 | tf_op jit(solution)/shard_map/reduce_scatter | solution.py:339
  848.2 65.4 %reduce-scatter.20.cloned.1.call-done = bf16[512,1024]{1,0:T(8,128)(2,1)} async-done(((bf16[4096,1024]{1,0:T(8,128)(2,1)}), bf16[512,1024]{1,0:T(8,128)(2,1)}) %reduce-scatter.20.cloned.1.call-update) | async-done | bytes 1048592 | tf_op jit(solution)/shard_map/reduce_scatter | solution.py:339
  920.4 19.4 %collective-permute-done.36 = bf16[512,1024]{1,0:T(8,128)(2,1)S(1)} collective-permute-done((bf16[512,1024]{1,0:T(8,128)(2,1)}, bf16[512,1024]{1,0:T(8,128)(2,1)S(1)}, u32[]{:S(2)}, u32[]{:S(2)}) %collective-permute-start.36) | collective-permute-done | bytes 1048608 | tf_op jit(solution)/shard_map/ppermute | solution.py:301
  946.8 20.2 %collective-permute-done.20 = bf16[128,3072]{1,0:T(8,128)(2,1)S(1)} collective-permute-done((bf16[128,3072]{1,0:T(8,128)(2,1)S(1)}, bf16[128,3072]{1,0:T(8,128)(2,1)S(1)}, u32[]{:S(2)}, u32[]{:S(2)}) %collective-permute-start.20) | collective-permute-done | bytes 786464 | tf_op jit(solution)/shard_map/ppermute | solution.py:301
  968.3 21.2 %collective-permute-done.35 = bf16[128,4096]{1,0:T(8,128)(2,1)S(1)} collective-permute-done((bf16[128,4096]{1,0:T(8,128)(2,1)S(1)}, bf16[128,4096]{1,0:T(8,128)(2,1)S(1)}, u32[]{:S(2)}, u32[]{:S(2)}) %collective-permute-start.35) | collective-permute-done | bytes 1048608 | tf_op jit(solution)/shard_map/ppermute | solution.py:301
  991.0 18.9 %collective-permute-done.38 = bf16[512,1024]{1,0:T(8,128)(2,1)S(1)} collective-permute-done((bf16[512,1024]{1,0:T(8,128)(2,1)S(1)}, bf16[512,1024]{1,0:T(8,128)(2,1)S(1)}, u32[]{:S(2)}, u32[]{:S(2)}) %collective-permute-start.38) | collective-permute-done | bytes 1048608 | tf_op jit(solution)/shard_map/ppermute | solution.py:301
  (345 shorter events, 230.6 us)
Async XLA Ops:
  7.2 86.9 %all-gather.16.cloned.1.call-start = ((), (), s32[]{:S(2)}) async-start(), calls=%async_computation.10 | async-start | bytes 4718592 | tf_op jit(solution)/shard_map/all_gather | solution.py:336
  7.9 102.7 %all-gather.10.cloned.1.call-start = ((), (), s32[]{:S(2)}) async-start(), calls=%async_computation.7 | async-start | bytes 7077888 | tf_op jit(solution)/shard_map/all_gather | solution.py:336
  8.7 120.1 %all-gather.12.cloned.1.call-start = ((), (), s32[]{:S(2)}) async-start(), calls=%async_computation.8 | async-start | bytes 2359296 | tf_op jit(solution)/shard_map/all_gather | solution.py:336
  9.4 147.0 %all-gather.14.cloned.1.call-start = ((), (), s32[]{:S(2)}) async-start(), calls=%async_computation.9 | async-start | bytes 2359296 | tf_op jit(solution)/shard_map/all_gather | solution.py:336
  10.0 182.1 %all-gather.18.cloned.1.call-start = ((), (), s32[]{:S(2)}) async-start(), calls=%async_computation.11 | async-start | bytes 2359296 | tf_op jit(solution)/shard_map/all_gather | solution.py:336
  10.6 231.8 %all-gather.20.cloned.1.call-start = ((), (), s32[]{:S(2)}) async-start(), calls=%async_computation.12 | async-start | bytes 9437184 | tf_op jit(solution)/shard_map/all_gather | solution.py:336
  11.2 287.5 %all-gather.22.cloned.1.call-start = ((), (), s32[]{:S(2)}) async-start(), calls=%async_computation.13 | async-start | bytes 9437184 | tf_op jit(solution)/shard_map/all_gather | solution.py:336
  11.9 496.2 %all-reduce.6.cloned.1.call-start = ((), (), s32[]{:S(2)}) async-start(), calls=%async_computation.14 | async-start | bytes 196608 | tf_op jit(solution)/shard_map/psum | solution.py:475
  26.4 67.6 %collective-permute-start.4 = (bf16[375,1024]{1,0:T(8,128)(2,1)}, bf16[375,1024]{1,0:T(8,128)(2,1)}, u32[]{:S(2)}, u32[]{:S(2)}) collective-permute-start(bf16[375,1024]{1,0:T(8,128)(2,1)} %get-tuple-element.62), channel_id=1, source_target_pairs={{0,2},{2,0},{3,1},{4,6},{5,7},{7,5},{8,10},{10,8},{11,9},{12,14},{... | collective-permute-start | bytes 2304008 | tf_op jit(solution)/shard_map/ppermute | solution.py:261
  45.6 206.7 %collective-permute-start.11 = (bf16[112,1024]{1,0:T(8,128)(2,1)}, bf16[112,1024]{1,0:T(8,128)(2,1)}, u32[]{:S(2)}, u32[]{:S(2)}) collective-permute-start(bf16[112,1024]{1,0:T(8,128)(2,1)} %get-tuple-element.80), channel_id=1, source_target_pairs={{1,0},{2,1},{3,2},{4,7},{6,5},{7,6},{9,8},{10,9},{11,10},{12,15},{... | collective-permute-start | bytes 688136 | tf_op jit(solution)/shard_map/ppermute | solution.py:261
  46.9 205.4 %collective-permute-start.10 = (bf16[112,1024]{1,0:T(8,128)(2,1)}, bf16[112,1024]{1,0:T(8,128)(2,1)}, u32[]{:S(2)}, u32[]{:S(2)}) collective-permute-start(bf16[112,1024]{1,0:T(8,128)(2,1)} %get-tuple-element.81), channel_id=1, source_target_pairs={{0,2},{2,0},{3,1},{4,6},{5,7},{7,5},{8,10},{10,8},{11,9},{12,14},{... | collective-permute-start | bytes 688136 | tf_op jit(solution)/shard_map/ppermute | solution.py:261
  52.3 199.9 %collective-permute-start.9 = (bf16[112,1024]{1,0:T(8,128)(2,1)}, bf16[112,1024]{1,0:T(8,128)(2,1)}, u32[]{:S(2)}, u32[]{:S(2)}) collective-permute-start(bf16[112,1024]{1,0:T(8,128)(2,1)} %get-tuple-element.79), channel_id=1, source_target_pairs={{0,1},{1,2},{3,0},{4,5},{5,6},{6,7},{8,9},{9,10},{11,8},{12,13},{1... | collective-permute-start | bytes 688136 | tf_op jit(solution)/shard_map/ppermute | solution.py:261
  387.1 174.8 %reduce-scatter.10.cloned.1.call-start = ((), (), s32[]{:S(2)}) async-start(), calls=%async_computation.16 | async-start | bytes 2359296 | tf_op jit(solution)/shard_map/reduce_scatter | solution.py:339
  391.7 207.7 %reduce-scatter.12.cloned.1.call-start = ((), (), s32[]{:S(2)}) async-start(), calls=%async_computation.17 | async-start | bytes 2359296 | tf_op jit(solution)/shard_map/reduce_scatter | solution.py:339
  396.3 247.6 %reduce-scatter.16.cloned.1.call-start = ((), (), s32[]{:S(2)}) async-start(), calls=%async_computation.19 | async-start | bytes 2359296 | tf_op jit(solution)/shard_map/reduce_scatter | solution.py:339
  400.8 298.1 %reduce-scatter.14.cloned.1.call-start = ((), (), s32[]{:S(2)}) async-start(), calls=%async_computation.18 | async-start | bytes 4718592 | tf_op jit(solution)/shard_map/reduce_scatter | solution.py:339
  416.2 347.8 %reduce-scatter.8.cloned.1.call-start = ((), (), s32[]{:S(2)}) async-start(), calls=%async_computation.15 | async-start | bytes 7077888 | tf_op jit(solution)/shard_map/reduce_scatter | solution.py:339
  425.3 413.7 %reduce-scatter.18.cloned.1.call-start = ((), (), s32[]{:S(2)}) async-start(), calls=%async_computation.20 | async-start | bytes 9437184 | tf_op jit(solution)/shard_map/reduce_scatter | solution.py:339
  435.9 477.7 %reduce-scatter.20.cloned.1.call-start = ((), (), s32[]{:S(2)}) async-start(), calls=%async_computation.21 | async-start | bytes 9437184 | tf_op jit(solution)/shard_map/reduce_scatter | solution.py:339
  451.6 59.2 %collective-permute-start.14 = (bf16[112,1024]{1,0:T(8,128)(2,1)}, bf16[112,1024]{1,0:T(8,128)(2,1)S(1)}, u32[]{:S(2)}, u32[]{:S(2)}) collective-permute-start(bf16[112,1024]{1,0:T(8,128)(2,1)} %get-tuple-element.68), channel_id=1, source_target_pairs={{0,1},{1,2},{2,3},{5,6},{6,7},{7,4},{8,9},{9,10},{10,11},{13,14},{... | collective-permute-start | bytes 688136 | tf_op jit(solution)/shard_map/ppermute | solution.py:261
  455.3 61.6 %collective-permute-start.13 = (bf16[112,1024]{1,0:T(8,128)(2,1)}, bf16[112,1024]{1,0:T(8,128)(2,1)S(1)}, u32[]{:S(2)}, u32[]{:S(2)}) collective-permute-start(bf16[112,1024]{1,0:T(8,128)(2,1)} %get-tuple-element.69), channel_id=1, source_target_pairs={{0,2},{1,3},{2,0},{5,7},{6,4},{7,5},{8,10},{9,11},{10,8},{13,15},{... | collective-permute-start | bytes 688136 | tf_op jit(solution)/shard_map/ppermute | solution.py:261
  459.6 58.6 %collective-permute-start.12 = (bf16[112,1024]{1,0:T(8,128)(2,1)}, bf16[112,1024]{1,0:T(8,128)(2,1)S(1)}, u32[]{:S(2)}, u32[]{:S(2)}) collective-permute-start(bf16[112,1024]{1,0:T(8,128)(2,1)} %get-tuple-element.70), channel_id=1, source_target_pairs={{0,3},{1,0},{2,1},{5,4},{6,5},{7,6},{8,11},{9,8},{10,9},{13,12},{1... | collective-permute-start | bytes 688136 | tf_op jit(solution)/shard_map/ppermute | solution.py:261
  561.8 85.5 %collective-permute-start.21 = (bf16[128,1024]{1,0:T(8,128)(2,1)}, bf16[128,1024]{1,0:T(8,128)(2,1)S(1)}, u32[]{:S(2)}, u32[]{:S(2)}) collective-permute-start(bf16[128,1024]{1,0:T(8,128)(2,1)} %reduce-scatter.10.cloned.1.call-done), channel_id=1, source_target_pairs={{0,1},{3,2},{4,5},{7,6},{8,9},{11,10},{12,13},{15,14},{16,17},{19,... | collective-permute-start | bytes 786440 | tf_op jit(solution)/shard_map/ppermute | solution.py:301
  648.2 55.6 %collective-permute-start.25 = (bf16[128,1024]{1,0:T(8,128)(2,1)S(1)}, bf16[128,1024]{1,0:T(8,128)(2,1)S(1)}, u32[]{:S(2)}, u32[]{:S(2)}) collective-permute-start(bf16[128,1024]{1,0:T(8,128)(2,1)S(1)} %add_convert_fusion.14), channel_id=1, source_target_pairs={{1,2},{2,1},{5,6},{6,5},{9,10},{10,9},{13,14},{14,13},{17,18},{18,... | collective-permute-start | bytes 786440 | tf_op jit(solution)/shard_map/ppermute | solution.py:301
  703.9 64.4 %collective-permute-start.26 = (bf16[128,1024]{1,0:T(8,128)(2,1)S(1)}, bf16[128,1024]{1,0:T(8,128)(2,1)S(1)}, u32[]{:S(2)}, u32[]{:S(2)}) collective-permute-start(bf16[128,1024]{1,0:T(8,128)(2,1)S(1)} %add_convert_fusion.13), channel_id=1, source_target_pairs={{1,0},{2,3},{5,4},{6,7},{9,8},{10,11},{13,12},{14,15},{17,16},{18,... | collective-permute-start | bytes 786440 | tf_op jit(solution)/shard_map/ppermute | solution.py:301
  705.3 63.8 %collective-permute-start.32 = (bf16[128,1024]{1,0:T(8,128)(2,1)S(1)}, bf16[128,1024]{1,0:T(8,128)(2,1)S(1)}, u32[]{:S(2)}, u32[]{:S(2)}) collective-permute-start(bf16[128,1024]{1,0:T(8,128)(2,1)S(1)} %add_convert_fusion.11), channel_id=1, source_target_pairs={{1,0},{2,3},{5,4},{6,7},{9,8},{10,11},{13,12},{14,15},{17,16},{18,... | collective-permute-start | bytes 786440 | tf_op jit(solution)/shard_map/ppermute | solution.py:301
  714.0 128.6 %collective-permute-start.28 = (bf16[128,2048]{1,0:T(8,128)(2,1)S(1)}, bf16[128,2048]{1,0:T(8,128)(2,1)}, u32[]{:S(2)}, u32[]{:S(2)}) collective-permute-start(bf16[128,2048]{1,0:T(8,128)(2,1)S(1)} %add_convert_fusion.10), channel_id=1, source_target_pairs={{1,2},{2,1},{5,6},{6,5},{9,10},{10,9},{13,14},{14,13},{17,18},{18,... | collective-permute-start | bytes 1572872 | tf_op jit(solution)/shard_map/ppermute | solution.py:301
  764.0 81.1 %collective-permute-start.18 = (bf16[128,3072]{1,0:T(8,128)(2,1)}, bf16[128,3072]{1,0:T(8,128)(2,1)}, u32[]{:S(2)}, u32[]{:S(2)}) collective-permute-start(bf16[128,3072]{1,0:T(8,128)(2,1)} %reduce-scatter.8.cloned.1.call-done), channel_id=1, source_target_pairs={{0,1},{3,2},{4,5},{7,6},{8,9},{11,10},{12,13},{15,14},{16,17},{19,... | collective-permute-start | bytes 2359304 | tf_op jit(solution)/shard_map/ppermute | solution.py:301
  839.0 78.1 %collective-permute-start.33 = (bf16[128,4096]{1,0:T(8,128)(2,1)}, bf16[128,4096]{1,0:T(8,128)(2,1)S(1)}, u32[]{:S(2)}, u32[]{:S(2)}) collective-permute-start(bf16[128,4096]{1,0:T(8,128)(2,1)} %reduce-scatter.18.cloned.1.call-done), channel_id=1, source_target_pairs={{0,1},{3,2},{4,5},{7,6},{8,9},{11,10},{12,13},{15,14},{16,17},{19,... | collective-permute-start | bytes 3145736 | tf_op jit(solution)/shard_map/ppermute | solution.py:301
  843.8 74.5 %collective-permute-start.29 = (bf16[128,2048]{1,0:T(8,128)(2,1)S(1)}, bf16[128,2048]{1,0:T(8,128)(2,1)}, u32[]{:S(2)}, u32[]{:S(2)}) collective-permute-start(bf16[128,2048]{1,0:T(8,128)(2,1)S(1)} %add_convert_fusion.9), channel_id=1, source_target_pairs={{1,0},{2,3},{5,4},{6,7},{9,8},{10,11},{13,12},{14,15},{17,16},{18,... | collective-permute-start | bytes 1572872 | tf_op jit(solution)/shard_map/ppermute | solution.py:301
  846.7 94.2 %collective-permute-start.19 = (bf16[128,3072]{1,0:T(8,128)(2,1)S(1)}, bf16[128,3072]{1,0:T(8,128)(2,1)}, u32[]{:S(2)}, u32[]{:S(2)}) collective-permute-start(bf16[128,3072]{1,0:T(8,128)(2,1)S(1)} %add_convert_fusion.8), channel_id=1, source_target_pairs={{1,2},{2,1},{5,6},{6,5},{9,10},{10,9},{13,14},{14,13},{17,18},{18,... | collective-permute-start | bytes 2359304 | tf_op jit(solution)/shard_map/ppermute | solution.py:301
  945.5 64.4 %collective-permute-start.38 = (bf16[512,1024]{1,0:T(8,128)(2,1)S(1)}, bf16[512,1024]{1,0:T(8,128)(2,1)S(1)}, u32[]{:S(2)}, u32[]{:S(2)}) collective-permute-start(bf16[512,1024]{1,0:T(8,128)(2,1)S(1)} %add_convert_fusion), channel_id=1, source_target_pairs={{1,0},{2,3},{5,4},{6,7},{9,8},{10,11},{13,12},{14,15},{17,16},{18,... | collective-permute-start | bytes 3145736 | tf_op jit(solution)/shard_map/ppermute | solution.py:301
  (95 other events, 1811.9 us)
Sparse Core Ops, SparseCore 0:
  9.9 39.5 all-gather.15
  51.4 45.4 all-gather.9
  98.8 27.9 all-gather.11
  128.5 27.8 all-gather.13
  158.2 27.9 all-gather.17
  187.9 54.3 all-gather.19
  244.2 54.3 all-gather.21
  387.2 120.9 all-reduce.5
  512.0 42.0 reduce-scatter.9
  558.1 41.2 reduce-scatter.11
  602.7 41.1 reduce-scatter.15
  647.5 51.3 reduce-scatter.13
  702.3 61.7 reduce-scatter.7
  767.7 71.2 reduce-scatter.17
  842.4 71.2 reduce-scatter.19

commit v2 on v1

--- a/solution.py
+++ b/solution.py
@@ -2,6 +2,7 @@
 
 import jax
 import jax.numpy as jnp
+import numpy as np
 from jax import lax
 from jax.experimental import pallas as pl
 from jax.experimental.pallas import tpu as pltpu
@@ -156,18 +157,25 @@
     )(*operands)
 
 
-def attend_back(queries, keys, values, mixed, grads, logs, places, chunk, valid):
+def attend_back(
+    queries, keys, values, mixed, grads, logs, places, chunk, valid, part=0, parts=1
+):
     tokens, width = queries.shape
     count = keys.shape[0]
     causal = places is not None
-    pairs = width // LANES
+    pairs = width // LANES // parts
+    first = part * pairs
+
+    def shifted(rows):
+        return pl.BlockSpec((rows, LANES), lambda pair: (0, pair + first))
+
     specs = [
-        columns(tokens),
-        columns(count),
-        columns(count),
-        columns(tokens),
-        columns(tokens),
-        pl.BlockSpec((1, 1, 2 * tokens), lambda pair: (pair, 0, 0)),
+        shifted(tokens),
+        shifted(count),
+        shifted(count),
+        shifted(tokens),
+        shifted(tokens),
+        pl.BlockSpec((1, 1, 2 * tokens), lambda pair: (pair + first, 0, 0)),
     ]
     operands = [queries, keys, values, mixed, grads, logs]
     if causal:
@@ -179,16 +187,16 @@
         in_specs=specs,
         out_specs=[columns(tokens), columns(count), columns(count)],
         out_shape=[
-            jax.ShapeDtypeStruct((tokens, width), BF),
-            jax.ShapeDtypeStruct((count, width), BF),
-            jax.ShapeDtypeStruct((count, width), BF),
+            jax.ShapeDtypeStruct((tokens, width // parts), BF),
+            jax.ShapeDtypeStruct((count, width // parts), BF),
+            jax.ShapeDtypeStruct((count, width // parts), BF),
         ],
         scratch_shapes=[pltpu.VMEM((chunk, 2 * tokens), F32)],
         compiler_params=pltpu.CompilerParams(vmem_limit_bytes=32 << 20),
         cost_estimate=pl.CostEstimate(
-            flops=40 * tokens * count * width,
-            transcendentals=tokens * count * width // HD,
-            bytes_accessed=8 * (tokens + count) * width,
+            flops=40 * tokens * count * width // parts,
+            transcendentals=tokens * count * width // HD // parts,
+            bytes_accessed=8 * (tokens + count) * width // parts,
         ),
         name="attend_causal_back" if causal else "attend_cross_back",
     )(*operands)
@@ -242,7 +250,8 @@
     def __init__(self, fsdp, seq, clips):
         self.fsdp, self.seq, self.clips = fsdp, seq, clips
         self.here = lax.axis_index("seq")
-        self.first = self.first_of(lax.axis_index("fsdp"))
+        self.group = lax.axis_index("fsdp")
+        self.first = self.first_of(self.group)
 
     def first_of(self, group):
         return (group % 2) * (self.seq - self.clips)
@@ -288,22 +297,125 @@
         source = (self.here - jnp.arange(self.seq)) % self.seq
         return (source[:, None] * rows + jnp.arange(rows)[None, :]).reshape(-1)
 
+    def chain(self, values, links):
+        pairs = [
+            (group * self.seq + a, group * self.seq + b)
+            for group in range(self.fsdp)
+            for a, b in links
+        ]
+        return lax.ppermute(values, AXES, pairs)
+
     def seq_sum(self, values):
         if self.seq != 4:
             return lax.psum(values, "seq")
-
-        def chain(moved, links):
-            pairs = [
-                (group * self.seq + a, group * self.seq + b)
-                for group in range(self.fsdp)
-                for a, b in links
-            ]
-            return lax.ppermute(moved, AXES, pairs)
-
-        half = (values.astype(F32) + chain(values, ((0, 1), (3, 2))).astype(F32)).astype(BF)
-        whole = (half.astype(F32) + chain(half, ((1, 2), (2, 1))).astype(F32)).astype(BF)
-        back = chain(whole, ((1, 0), (2, 3)))
+        half = plus(values, self.chain(values, ((0, 1), (3, 2))))
+        whole = plus(half, self.chain(half, ((1, 2), (2, 1))))
+        back = self.chain(whole, ((1, 0), (2, 3)))
         return jnp.where((self.here == 0) | (self.here == 3), back, whole)
+
+    def flip(self, values, bits):
+        return lax.ppermute(values, "fsdp", [(f, f ^ bits) for f in range(self.fsdp)])
+
+    def spread_far(self, shard, by_x, by_y):
+        half = shard.shape[0] // 2
+        return self.flip(by_y[:half], 2), self.flip(by_x[half:], 4)
+
+    def spread_core(self, shard, by_x, by_y, far_x, far_y):
+        mine = jnp.stack([shard, by_x, by_y, jnp.concatenate([far_x, far_y], axis=0)])
+        return mine, self.flip(mine, 1)
+
+    def fold_parts(self, members):
+        parts = [m.reshape(4, 2, m.shape[0] // 8, m.shape[1]) for m in members]
+        core = self.group % 2
+        sent = jnp.concatenate([pick(p, 1 - core, 1) for p in parts], axis=2)
+        kept = jnp.concatenate([pick(p, core, 1) for p in parts], axis=2)
+        return kept, self.flip(sent, 1)
+
+    def fold_far(self, kept, arrived):
+        sums = plus(kept, arrived)
+        half = sums.shape[1] // 2
+        far = pick(sums, (self.group // 2) ^ 3, 0)
+        return sums, self.flip(far[:half], 2), self.flip(far[half:], 4)
+
+    def fold_near(self, sums, from_x, from_y):
+        chip, half = self.group // 2, sums.shape[1] // 2
+        to_x, to_y = pick(sums, chip ^ 1, 0), pick(sums, chip ^ 2, 0)
+        to_x = jnp.concatenate([to_x[:half], plus(to_x[half:], from_y)], axis=0)
+        to_y = jnp.concatenate([plus(to_y[:half], from_x), to_y[half:]], axis=0)
+        return pick(sums, chip, 0), self.flip(to_x, 2), self.flip(to_y, 4)
+
+    def hop_one(self, values):
+        return values, self.chain(values, ((0, 1), (3, 2)))
+
+    def hop_two(self, values, arrived):
+        half = plus(values, arrived)
+        return half, self.chain(half, ((1, 2), (2, 1)))
+
+    def hop_three(self, half, arrived):
+        whole = plus(half, arrived)
+        return whole, self.chain(whole, ((1, 0), (2, 3)))
+
+    def hop_end(self, whole, back):
+        return jnp.where((self.here == 0) | (self.here == 3), back, whole).astype(F32)
+
+
+def plus3(first, second, third):
+    return (first.astype(F32) + second.astype(F32) + third.astype(F32)).astype(BF)
+
+
+def pick(values, index, axis):
+    return lax.dynamic_index_in_dim(values, index, axis, keepdims=False)
+
+
+def plus(first, second):
+    return (first.astype(F32) + second.astype(F32)).astype(BF)
+
+
+def tied(*members):
+    return lax.optimization_barrier(members)
+
+
+def assemble_kernel(widths, group_ref, mine_ref, other_ref, *outs):
+    slot = pl.program_id(0) * 2 + pl.program_id(1)
+
+    def store(source_ref):
+        start = 0
+        for out, width in zip(outs, widths):
+            out[...] = source_ref[0, :, start : start + width]
+            start += width
+
+    pl.when(slot % 2 == 0)(lambda: store(mine_ref))
+    pl.when(slot % 2 == 1)(lambda: store(other_ref))
+
+
+def assemble(group, mine, other, widths):
+    rows, total = mine.shape[1], mine.shape[2]
+    cut = 2
+    step_rows = rows // cut
+    source = pl.BlockSpec((1, step_rows, total), lambda chip, core, part, group: (chip, part, 0))
+    return pl.pallas_call(
+        functools.partial(assemble_kernel, widths),
+        grid_spec=pltpu.PrefetchScalarGridSpec(
+            num_scalar_prefetch=1,
+            grid=(4, 2, cut),
+            in_specs=[source, source],
+            out_specs=[
+                pl.BlockSpec(
+                    (step_rows, width),
+                    lambda chip, core, part, group: (
+                        (group[0] ^ (2 * chip + core)) * cut + part,
+                        0,
+                    ),
+                )
+                for width in widths
+            ],
+        ),
+        out_shape=[jax.ShapeDtypeStruct((8 * rows, width), BF) for width in widths],
+        cost_estimate=pl.CostEstimate(
+            flops=0, transcendentals=0, bytes_accessed=32 * rows * total
+        ),
+        name="assemble",
+    )(group.reshape(1), mine, other)
 
 
 def local(
@@ -331,125 +443,177 @@
     norms = norm_gain.shape[0]
     bias_count = biases.shape[0]
     scaling = HD ** (-0.5)
-
-    def gathered(member):
-        return lax.all_gather(member, "fsdp", axis=0, tiled=True)
-
-    def reduced(member):
-        part = lax.psum_scatter(member, "fsdp", scatter_dimension=0, tiled=True)
-        return grid.seq_sum(part).astype(F32)
-
-    residual_in = jnp.concatenate(grid.collect(hidden_in), axis=0).astype(F32)
+    swift = grid.fsdp == 8 and grid.seq == 4
+
+    def gathered(*members):
+        widths = [member.shape[1] for member in members]
+        joined = jnp.concatenate(members, axis=1)
+        joined = lax.all_gather(joined, "fsdp", axis=0, tiled=True)
+        return jnp.split(joined, np.cumsum(widths)[:-1].tolist(), axis=1)
+
+    def scattered(member):
+        return lax.psum_scatter(member, "fsdp", scatter_dimension=0, tiled=True)
+
+    token_pieces = grid.collect(hidden_in)
     small = jnp.concatenate([norm_gain, norm_shift, biases, mlp_in_bias.reshape(-1, shard)], axis=0)
     small = lax.all_gather(small, "fsdp", axis=0)
     vectors = small[:, : 2 * norms + bias_count].swapaxes(0, 1).reshape(-1, width).astype(F32)
     gain, shift, bias = vectors[:norms], vectors[norms : 2 * norms], vectors[2 * norms :]
     inner_bias = small[:, 2 * norms + bias_count :].reshape(1, -1).astype(F32)
 
-    full_qkv = gathered(self_qkv)
-    frame_pieces = [
-        jnp.pad(piece, ((0, padded - frames), (0, 0)))
-        for piece in grid.collect(encoded)
-    ]
-    frame_rows = jnp.concatenate(frame_pieces, axis=0)
-    top = jnp.concatenate(grid.collect(out_grad), axis=0)
-    full_self_out = gathered(self_out)
-    full_cross_kv = gathered(cross_kv)
-    full_cross_q = gathered(cross_q)
-    full_cross_out = gathered(cross_out)
-    full_inner = gathered(mlp_in)
-    full_outer = gathered(mlp_out)
+    full_qkv, full_self_out = gathered(self_qkv, self_out)
+    cross_widths = (cross_kv.shape[1], cross_q.shape[1], cross_out.shape[1])
+    cross_shard = jnp.concatenate([cross_kv, cross_q, cross_out], axis=1)
+    if swift:
+        cross_x, cross_y = grid.flip(cross_shard, 2), grid.flip(cross_shard, 4)
+    residual_in = jnp.concatenate(token_pieces, axis=0).astype(F32)
+    normed_one = (normalized(residual_in)[0] * gain[0] + shift[0]).astype(BF)
+    late_in = jnp.concatenate([encoded, out_grad], axis=1)
+    late_in, normed_one = tied(late_in, normed_one)
+    late = grid.collect(late_in)
+    full_inner = gathered(mlp_in)[0]
+
+    if swift:
+        normed_one, cross_x, cross_y = tied(normed_one, cross_x, cross_y)
+        cross_far = grid.spread_far(cross_shard, cross_x, cross_y)
+    else:
+        full_cross_kv, full_cross_q, full_cross_out = gathered(cross_kv, cross_q, cross_out)
+        full_outer = gathered(mlp_out)[0]
 
     place = grid.places(rows)
     places = (place[:, None], jnp.concatenate([place, place])[None, :])
     tokens = place.shape[0]
 
-    normed_one = (normalized(residual_in)[0] * gain[0] + shift[0]).astype(BF)
     pre_qkv = product(normed_one, full_qkv)
     queries = ((pre_qkv[:, :width] + bias[0]) * scaling).astype(BF)
     keys = pre_qkv[:, width : 2 * width].astype(BF)
     values = (pre_qkv[:, 2 * width :] + bias[1]).astype(BF)
     self_mix, self_log = attend(queries, keys, values, places, tokens, tokens)
+    if swift:
+        self_mix, far_x, far_y = tied(self_mix, *cross_far)
+        cross_mine, cross_other = grid.spread_core(cross_shard, cross_x, cross_y, far_x, far_y)
     after_self = residual_in + product(self_mix, full_self_out) + bias[2]
     normed_two = (normalized(after_self)[0] * gain[1] + shift[1]).astype(BF)
+    if swift:
+        cross_other, mlp_out = tied(cross_other, mlp_out)
+        outer_x, outer_y = grid.flip(mlp_out, 2), grid.flip(mlp_out, 4)
+        full_cross_kv, full_cross_q, full_cross_out = assemble(
+            grid.group, cross_mine, cross_other, cross_widths
+        )
     cross_queries = ((product(normed_two, full_cross_q) + bias[3]) * scaling).astype(BF)
+    frame_rows = jnp.concatenate(
+        [jnp.pad(piece[:frames], ((0, padded - frames), (0, 0))) for piece in late], axis=0
+    )
+    top = jnp.concatenate([piece[frames:] for piece in late], axis=0)
     cross_pre = product(frame_rows, full_cross_kv)
     cross_keys = cross_pre[:, :width].astype(BF)
     cross_values = (cross_pre[:, width:] + bias[4]).astype(BF)
+    if swift:
+        cross_queries, outer_x, outer_y = tied(cross_queries, outer_x, outer_y)
+        outer_far = grid.spread_far(mlp_out, outer_x, outer_y)
     cross_mix, cross_log = attend(cross_queries, cross_keys, cross_values, None, padded, frames)
+    if swift:
+        cross_mix, far_x, far_y = tied(cross_mix, *outer_far)
+        outer_mine, outer_other = grid.spread_core(mlp_out, outer_x, outer_y, far_x, far_y)
     after_cross = after_self + product(cross_mix, full_cross_out) + bias[5]
     normed_three = (normalized(after_cross)[0] * gain[2] + shift[2]).astype(BF)
     inner = product(normed_three, full_inner) + inner_bias
     activated = gelu(inner).astype(BF)
-    hidden_rows = (after_cross + product(activated, full_outer) + bias[6]).astype(BF)
 
     top_wide = top.astype(F32)
     grad_w_outer = weight_grad(activated, top)
+    grad_w_outer, top = tied(grad_w_outer, top)
+    part_outer = scattered(grad_w_outer)
     grad_bias_six = jnp.sum(top_wide, axis=0)
+    if swift:
+        (full_outer,) = assemble(grid.group, outer_mine, outer_other, (mlp_out.shape[1],))
     grad_inner = product_back(top, full_outer) * gelu_slope(inner)
     grad_inner_low = grad_inner.astype(BF)
     grad_w_inner = weight_grad(normed_three, grad_inner_low)
+    grad_w_inner, grad_inner_low = tied(grad_w_inner, grad_inner_low)
     grad_inner_bias = jnp.sum(grad_inner, axis=0)
+    if swift:
+        inner_kept, inner_core = grid.fold_parts([grad_w_inner])
+    else:
+        part_inner = scattered(grad_w_inner)
     grad_normed_three = product_back(grad_inner_low, full_inner)
     from_three, gain_three, shift_three = norm_back(grad_normed_three, after_cross, gain[2])
     grad_after_cross = top_wide + from_three
     grad_cross_low = grad_after_cross.astype(BF)
+    grad_bias_five = jnp.sum(grad_after_cross, axis=0)
+    if swift:
+        grad_cross_low, inner_core = tied(grad_cross_low, inner_core)
+        inner_sums, inner_x, inner_y = grid.fold_far(inner_kept, inner_core)
     grad_w_cross_out = weight_grad(cross_mix, grad_cross_low)
-    grad_bias_five = jnp.sum(grad_after_cross, axis=0)
     grad_cross_mix = product_back(grad_cross_low, full_cross_out).astype(BF)
-    grad_cross_queries, grad_cross_keys, grad_cross_values = attend_back(
-        cross_queries,
-        cross_keys,
-        cross_values,
-        cross_mix,
-        grad_cross_mix,
-        cross_log,
-        None,
-        padded,
-        frames,
-    )
+
+    def cross_back(half, count, grads):
+        return attend_back(
+            cross_queries,
+            cross_keys,
+            cross_values,
+            cross_mix,
+            grads,
+            cross_log,
+            None,
+            padded,
+            frames,
+            half,
+            count,
+        )
+
+    first_half = cross_back(0, 2, grad_cross_mix)
+    if swift:
+        grad_cross_mix, inner_x, inner_y, *first_half = tied(
+            grad_cross_mix, inner_x, inner_y, *first_half
+        )
+        inner_own, inner_near_x, inner_near_y = grid.fold_near(inner_sums, inner_x, inner_y)
+    second_half = cross_back(1, 2, grad_cross_mix)
+    if swift:
+        part_outer, *second_half = tied(part_outer, *second_half)
+        outer_sum, outer_in = grid.hop_one(part_outer)
+    grad_cross_queries = jnp.concatenate([first_half[0], second_half[0]], axis=1)
+    grad_pair = jnp.concatenate(
+        [first_half[1], second_half[1], first_half[2], second_half[2]], axis=1
+    )
+    grad_cross_values = grad_pair[:, width:]
+    grad_w_cross_kv = weight_grad(frame_rows, grad_pair)
     scaled_cross = grad_cross_queries * scaling
+    scaled_cross, grad_w_cross_kv = tied(scaled_cross, grad_w_cross_kv)
+    part_kv = scattered(grad_w_cross_kv)
+    grad_bias_four = jnp.sum(grad_cross_values.astype(F32), axis=0)
     grad_w_cross_q = weight_grad(normed_two, scaled_cross)
     grad_bias_three = jnp.sum(scaled_cross.astype(F32), axis=0)
     grad_normed_two = product_back(scaled_cross, full_cross_q)
-    grad_pair = jnp.concatenate([grad_cross_keys, grad_cross_values], axis=1)
-    grad_w_cross_kv = weight_grad(frame_rows, grad_pair)
-    grad_bias_four = jnp.sum(grad_cross_values.astype(F32), axis=0)
-    grad_frames = product_back(grad_pair, full_cross_kv).astype(BF)
     from_two, gain_two, shift_two = norm_back(grad_normed_two, after_self, gain[1])
     grad_after_self = grad_after_cross + from_two
     grad_self_low = grad_after_self.astype(BF)
     grad_w_self_out = weight_grad(self_mix, grad_self_low)
     grad_bias_two = jnp.sum(grad_after_self, axis=0)
     grad_self_mix = product_back(grad_self_low, full_self_out).astype(BF)
+    middle = [grad_w_cross_out, grad_w_cross_q, grad_w_self_out]
+    if swift:
+        grad_self_mix, inner_near_x, inner_near_y, outer_in, *middle = tied(
+            grad_self_mix, inner_near_x, inner_near_y, outer_in, *middle
+        )
+        part_inner = plus3(inner_own, inner_near_x, inner_near_y)
+        inner_sum, inner_in = grid.hop_one(part_inner)
+        outer_sum, outer_in = grid.hop_two(outer_sum, outer_in)
+        middle_kept, middle_core = grid.fold_parts(middle)
     grad_queries, grad_keys, grad_values = attend_back(
         queries, keys, values, self_mix, grad_self_mix, self_log, places, tokens, tokens
     )
+    if swift:
+        grad_queries, middle_core = tied(grad_queries, middle_core)
+        middle_sums, middle_x, middle_y = grid.fold_far(middle_kept, middle_core)
     scaled_query = grad_queries * scaling
     grad_pre = jnp.concatenate([scaled_query, grad_keys, grad_values], axis=1)
+    grad_normed_one = product_back(grad_pre, full_qkv)
     grad_w_qkv = weight_grad(normed_one, grad_pre)
     grad_bias_zero = jnp.sum(scaled_query.astype(F32), axis=0)
     grad_bias_one = jnp.sum(grad_values.astype(F32), axis=0)
-    grad_normed_one = product_back(grad_pre, full_qkv)
     from_one, gain_one, shift_one = norm_back(grad_normed_one, residual_in, gain[0])
     grad_rows = (grad_after_self + from_one).astype(BF)
-
-    total_outer = reduced(grad_w_outer)
-    total_inner = reduced(grad_w_inner)
-    total_cross_out = reduced(grad_w_cross_out)
-    total_cross_q = reduced(grad_w_cross_q)
-    total_cross_kv = reduced(grad_w_cross_kv)
-    total_self_out = reduced(grad_w_self_out)
-    total_qkv = reduced(grad_w_qkv)
-
-    def token_pieces(member):
-        return [member[rows * step : rows * (step + 1)] for step in range(grid.seq)]
-
-    hidden_out = grid.hand_back(token_pieces(hidden_rows))
-    grad_encoded = grid.hand_back(
-        [grad_frames[padded * step : padded * step + frames] for step in range(grid.seq)]
-    )
-    grad_hidden_in = grid.hand_back(token_pieces(grad_rows))
 
     sums = jnp.stack(
         [
@@ -468,12 +632,71 @@
             grad_bias_six,
         ]
     )
-    inner_sums = grad_inner_bias.reshape(grid.fsdp, -1, shard)
+    inner_sums_row = grad_inner_bias.reshape(grid.fsdp, -1, shard)
     packed = jnp.concatenate(
-        [sums.reshape(-1, grid.fsdp, shard).swapaxes(0, 1), inner_sums], axis=1
-    )
-    packed = lax.psum(packed, AXES)
-    mine = lax.dynamic_index_in_dim(packed, lax.axis_index("fsdp"), 0, keepdims=False)
+        [sums.reshape(-1, grid.fsdp, shard).swapaxes(0, 1), inner_sums_row], axis=1
+    )
+    kinds = packed.shape[1]
+    packed = packed.reshape(grid.fsdp, -1).astype(BF)
+    span = grad_w_qkv.shape[1]
+    lines = -(-packed.shape[1] // span)
+    filled = -(-lines // 16) * 16
+    packed = jnp.pad(packed, ((0, 0), (0, filled * span - packed.shape[1])))
+    packed = packed.reshape(grid.fsdp, filled, span)
+    shard_rows = grad_w_qkv.shape[0] // grid.fsdp
+    joined = jnp.concatenate([grad_w_qkv.reshape(grid.fsdp, shard_rows, span), packed], axis=1)
+    joined = joined.reshape(-1, span)
+    if swift:
+        joined, inner_in, outer_in, middle_x, middle_y = tied(
+            joined, inner_in, outer_in, middle_x, middle_y
+        )
+        inner_sum, inner_in = grid.hop_two(inner_sum, inner_in)
+        outer_sum, outer_in = grid.hop_three(outer_sum, outer_in)
+        middle_own, middle_x, middle_y = grid.fold_near(middle_sums, middle_x, middle_y)
+        last_kept, last_core = grid.fold_parts([joined])
+    grad_frames = product_back(grad_pair, full_cross_kv).astype(BF)
+    hidden_rows = (after_cross + product(activated, full_outer) + bias[6]).astype(BF)
+    if swift:
+        grad_frames, hidden_rows, inner_in, outer_in, middle_x, middle_y, last_core = tied(
+            grad_frames, hidden_rows, inner_in, outer_in, middle_x, middle_y, last_core
+        )
+        last_sums, last_x, last_y = grid.fold_far(last_kept, last_core)
+        inner_sum, inner_in = grid.hop_three(inner_sum, inner_in)
+        total_outer = grid.hop_end(outer_sum, outer_in)
+        part_middle = plus3(middle_own, middle_x, middle_y)
+        part_middle = jnp.concatenate([part_middle, part_kv], axis=1)
+        last_own, last_x, last_y = grid.fold_near(last_sums, last_x, last_y)
+        part_last = plus3(last_own, last_x, last_y)
+        total_inner = grid.hop_end(inner_sum, inner_in)
+    else:
+        part_middle = scattered(jnp.concatenate(middle, axis=1))
+        part_middle = jnp.concatenate([part_middle, part_kv], axis=1)
+        part_last = scattered(joined)
+        total_outer = grid.seq_sum(part_outer).astype(F32)
+        total_inner = grid.seq_sum(part_inner).astype(F32)
+    total_middle = grid.seq_sum(part_middle).astype(F32)
+    total_cross_out, total_cross_q, total_self_out, total_cross_kv = jnp.split(
+        total_middle, (width, 2 * width, 3 * width), axis=1
+    )
+    total = grid.seq_sum(part_last).astype(F32)
+    total_qkv = total[:shard_rows]
+    mine = total[shard_rows:].reshape(-1)[: kinds * shard].reshape(kinds, shard)
+
+    late_rows = [
+        jnp.concatenate(
+            [
+                grad_frames[padded * step : padded * step + frames],
+                hidden_rows[rows * step : rows * (step + 1)],
+            ],
+            axis=0,
+        )
+        for step in range(grid.seq)
+    ]
+    late_rows = grid.hand_back(late_rows)
+    grad_encoded, hidden_out = late_rows[:, :frames], late_rows[:, frames:]
+    grad_hidden_in = grid.hand_back(
+        [grad_rows[rows * step : rows * (step + 1)] for step in range(grid.seq)]
+    )
     return (
         hidden_out,
         grad_hidden_in,

time: 1020 us -> 718 us (0.70)
  waiting for transfers between devices: 568 us -> 187 us
  other arithmetic: 39.4 us -> 92.1 us
  starting transfers between devices: 133 us -> 86.6 us
  local copies, waits for them, and re-layouts: 31.7 us -> 61.3 us
  Pallas kernels: 93.9 us -> 123 us
  blocking collectives: 9.18 us -> 27.5 us
  matrix products: 126 us -> 115 us
    reduce_scatter x7 -> x2, waiting for transfers between devices: 288 us -> 0.01 us  [scattered(): return lax.psum_scatter(member, 'fsdp', scatter_dimension=0, tiled=True)]
    all_gather x7 -> x2, waiting for transfers between devices: 115 us -> 22.9 us  [gathered(): joined = lax.all_gather(joined, 'fsdp', axis=0, tiled=True)]
    ppermute x18 -> x12, starting transfers between devices: 83.3 us -> 44.6 us  [turn(): return lax.ppermute(values, AXES, pairs)]
    pallas_call x0 -> x2, Pallas kernels: none -> 30.1 us  [assemble(): pl.pallas_call(functools.partial(assemble_kernel, widths), grid_spec=pltp...]
    ppermute x18 -> x12, waiting for transfers between devices: 45.3 us -> 70.3 us  [turn(): return lax.ppermute(values, AXES, pairs)]
    psum x1 -> x0, waiting for transfers between devices: 23.6 us -> none  [local(): packed = lax.psum(packed, AXES)]
    concatenate x1 -> x15, other arithmetic: 0.66 us -> 23.4 us  [the longest x1 6.37 us: local(): jnp.concatenate([grad_w_qkv.reshape(grid.fsdp, shard_rows, span), packed]...]
    all_gather x1, blocking collectives: 9.18 us -> 27.5 us  [local(): small = lax.all_gather(small, 'fsdp', axis=0)]
  transfers between devices with their start and end apart: 54 -> 53, of which waited for: 20 -> 16; matrix products, arithmetic and copies ran while one was open for 15% -> 33% of each run, Pallas kernels for 4% -> 17%
where the time goes in v2:
time: 718 us; the launch traced here: 709 us
  waiting for transfers between devices  187 us (26%)
  Pallas kernels  123 us (17%)
  matrix products  115 us (16%)
  other arithmetic  92.1 us (13%)
  starting transfers between devices  86.6 us (12%)
  local copies, waits for them, and re-layouts  61.3 us (9%)
  blocking collectives  27.5 us (4%)
  between operations  16.4 us (2%)
    ppermute x12, waiting for transfers between devices, chain(): return lax.ppermute(values, AXES, pairs)  73 us
    ppermute x12, waiting for transfers between devices, turn(): return lax.ppermute(values, AXES, pairs)  70.3 us
    pallas_call x3, Pallas kernels, attend_back(): pl.pallas_call(functools.partial(backward_kernel, chunk, valid, causal),...  53.8 us
    ppermute x12, starting transfers between devices, turn(): return lax.ppermute(values, AXES, pairs)  44.6 us
    dot_general x7, matrix products, product_back(): lax.dot_general(incoming, weight, (((1,), (1,)), ((), ())), preferred_ele...  44.2 us
    pallas_call x2, Pallas kernels, attend(): pl.pallas_call(functools.partial(forward_kernel, chunk, valid, causal), g...  38.8 us
    dot_general x7, matrix products, product(): return jnp.dot(first, second, preferred_element_type=F32)  35.4 us
    dot_general x7, matrix products, weight_grad(): lax.dot_general(operand, incoming, (((0,), (0,)), ((), ())), preferred_el...  35.1 us
  transfers between devices with their start and end apart: 53, of which 16 were waited for; matrix products, arithmetic and copies ran while one was open for 33% of the time, Pallas kernels for 17%

profile of v2, /device:TPU:0, one launch (start us, length us, event | category | flops | bytes accessed | tf_op | source)
XLA Modules:
  0.0 708.7 jit_solution(12210048102356761898)
XLA Ops:
  22.0 5.6 collective-permute-start.1
  27.8 27.5 %all-gather.1 = bf16[8,17,128]{2,1,0:T(8,128)(2,1)S(1)} all-gather(bf16[1,17,128]{2,1,0:T(8,128)(2,1)S(1)} %maximum_bitcast_fusion.4), channel_id=2, replica_groups=mesh['fsdp'=8,'seq'=4] {'fsdp'}, dimensions={0}, use_global_device_ids=true | all-gather | bytes 39168 | tf_op jit(solution)/shard_map/all_gather | solution.py:459
  66.0 22.8 %all-gather.5.cloned.1.call-done = bf16[1024,4096]{1,0:T(8,128)(2,1)} async-done(((bf16[128,4096]{1,0:T(8,128)(2,1)}), bf16[1024,4096]{1,0:T(8,128)(2,1)}) %all-gather.5.cloned.1.call-update) | async-done | bytes 8388624 | tf_op jit(solution)/shard_map/all_gather | solution.py:451
  95.1 8.7 %attend_causal.1 = (bf16[448,1024]{1,0:T(8,128)(2,1)S(1)}, f32[8,1,896]{2,1,0:T(1,128)S(1)}) custom-call(bf16[448,1024]{1,0:T(8,128)(2,1)S(1)} %get-tuple-element.175.refs_0_, bf16[448,1024]{1,0:T(8,128)(2,1)S(1)} %slice.463.refs_1_, bf16[448,1024]{1,0:T(8,128)(2,1)S(1)} %get-tuple-element.174.refs_2_, s32[448,1]{1,0:T(8,128)S(1)} %add.484.refs_3_.refs_6_, ...), custom_call_target="tpu_custom_call" | custom-call | flops 3288334336 | bytes 3670016 | tf_op jit(solution)/shard_map/attend_causal/pallas_call | solution.py:140
  121.3 6.5 collective-permute-done.5
  130.0 51.4 %collective-permute-done.4 = bf16[487,1024]{1,0:T(8,128)(2,1)} collective-permute-done((bf16[487,1024]{1,0:T(8,128)(2,1)}, bf16[487,1024]{1,0:T(8,128)(2,1)}, u32[]{:S(2)}, u32[]{:S(2)}) %collective-permute-start.4) | collective-permute-done | bytes 997408 | tf_op jit(solution)/shard_map/ppermute | solution.py:270
  195.5 14.8 %assemble.2 = (bf16[1024,2048]{1,0:T(8,128)(2,1)}, bf16[1024,1024]{1,0:T(8,128)(2,1)}, bf16[1024,1024]{1,0:T(8,128)(2,1)}) custom-call(s32[1]{0:T(128)} %bitcast.18.group_ref, bf16[4,128,4096]{2,1,0:T(8,128)(2,1)} %pad_maximum_fusion.1.mine_ref, bf16[4,128,4096]{2,1,0:T(8,128)(2,1)} %collective-permute-done.10.other_ref), custom_call_target="tpu_custom_call" | custom-call | bytes 16777216 | tf_op jit(solution)/shard_map/assemble/pallas_call | solution.py:396
  210.3 10.4 %fusion.53 = f32[1536,2048]{1,0:T(8,128)S(1)} fusion(bf16[1024,2048]{1,0:T(8,128)(2,1)} %get-tuple-element.98, bf16[384,1024]{1,0:T(8,128)(2,1)} %get-tuple-element.259, bf16[384,1024]{1,0:T(8,128)(2,1)} %get-tuple-element.258, bf16[384,1024]{1,0:T(8,128)(2,1)} %get-tuple-element.257, bf16[384,1024]{1,0:T(8,128)(2,1)} %get-tuple-element.256), kind=kOutput, calls=%fused_computation.159 | convolution fusion | flops 6455033856 | bytes 19922944 | tf_op jit(solution)/shard_map/dot_general | solution.py:206
  229.8 30.1 %attend_cross.1 = (bf16[448,1024]{1,0:T(8,128)(2,1)S(1)}, f32[8,1,896]{2,1,0:T(1,128)S(1)}) custom-call(bf16[448,1024]{1,0:T(8,128)(2,1)S(1)} %multiply_convert_fusion.1.refs_0_, bf16[1536,1024]{1,0:T(8,128)(2,1)S(1)} %slice.462.refs_1_, bf16[1536,1024]{1,0:T(8,128)(2,1)S(1)} %fusion.7.refs_2_), custom_call_target="tpu_custom_call" | custom-call | flops 11274289152 | bytes 8126464 | tf_op jit(solution)/shard_map/attend_cross/pallas_call | solution.py:140
  267.8 9.7 %multiply_convert_fusion = (bf16[448,4096]{1,0:T(8,128)(2,1)S(1)}, f32[448,4096]{1,0:T(8,128)}) fusion(f32[4096]{0:T(1024)S(1)} %convert.98, bf16[1024,4096]{1,0:T(8,128)(2,1)} %all-gather.7.cloned.1.call-done, f32[448,1024]{1,0:T(8,128)} %copy-done.36, f32[1024]{0:T(1024)S(1)} %bitcast.260, f32[1024]{0:T(1024)S(1)} %bitcast.250, ...), kind=kOutput, calls=%fused_computation.10 | convolution fusion | flops 3771400192 | bytes 21261824 | tf_op jit(solution)/shard_map/dot_general | solution.py:206
  279.3 7.1 convolution_convert_fusion.1
  286.4 15.3 %assemble.3 = bf16[4096,1024]{1,0:T(8,128)(2,1)} custom-call(s32[1]{0:T(128)} %bitcast.18.group_ref, bf16[4,512,1024]{2,1,0:T(8,128)(2,1)} %pad_maximum_fusion.2.mine_ref, bf16[4,512,1024]{2,1,0:T(8,128)(2,1)} %collective-permute-done.15.other_ref), custom_call_target="tpu_custom_call" | custom-call | bytes 16777216 | tf_op jit(solution)/shard_map/assemble/pallas_call | solution.py:396
  301.7 10.0 %fusion.66 = (bf16[4096]{0:T(1024)(128)(2,1)S(1)}, bf16[448,4096]{1,0:T(8,128)(2,1)S(1)}) fusion(f32[448,4096]{1,0:T(8,128)} %get-tuple-element.265, f32[4096]{0:T(1024)S(1)} %convert.98, bf16[448,1024]{1,0:T(8,128)(2,1)} %pad_maximum_fusion.20, bf16[4096,1024]{1,0:T(8,128)(2,1)} %assemble.3), kind=kOutput, calls=%fused_computation.248 | convolution fusion | flops 3780112384 | bytes 20340736 | tf_op jit(solution)/shard_map/dot_general | solution.py:210
  322.1 9.8 %multiply_reduce_fusion = (bf16[1024]{0:T(1024)(128)(2,1)S(1)}, f32[448]{0:T(512)S(1)}, f32[448]{0:T(512)S(1)}, bf16[1024]{0:T(1024)(128)(2,1)S(1)}, f32[448,1024]{1,0:T(8,128)S(1)}) fusion(f32[448,1024]{1,0:T(8,128)} %copy-done.36, f32[448]{0:T(512)S(1)} %add_rsqrt_fusion, f32[448]{0:T(512)S(1)} %broadcast_multiply_fusion.7, f32[1024]{0:T(1024)S(1)} %bitcast.252, ...), kind=kOutput, calls=%fused_computation.79 | convolution fusion | flops 3762222080 | bytes 15744000 | tf_op jit(solution)/shard_map/dot_general | solution.py:210
  345.8 20.5 %attend_cross_back.2 = (bf16[448,512]{1,0:T(8,128)(2,1)S(1)}, bf16[1536,512]{1,0:T(8,128)(2,1)S(1)}, bf16[1536,512]{1,0:T(8,128)(2,1)S(1)}) custom-call(bf16[448,1024]{1,0:T(8,128)(2,1)S(1)} %multiply_convert_fusion.1.refs_0_, bf16[1536,1024]{1,0:T(8,128)(2,1)S(1)} %copy-done.1, bf16[1536,1024]{1,0:T(8,128)(2,1)S(1)} %copy-done.3, ...), custom_call_target="tpu_custom_call" | custom-call | flops 14092861440 | bytes 8126464 | tf_op jit(solution)/shard_map/attend_cross_back/pallas_call | solution.py:184
  375.1 20.6 %attend_cross_back.3 = (bf16[448,512]{1,0:T(8,128)(2,1)S(1)}, bf16[1536,512]{1,0:T(8,128)(2,1)S(1)}, bf16[1536,512]{1,0:T(8,128)(2,1)S(1)}) custom-call(bf16[448,1024]{1,0:T(8,128)(2,1)S(1)} %copy-done.24, bf16[1536,1024]{1,0:T(8,128)(2,1)S(1)} %copy-done.1, bf16[1536,1024]{1,0:T(8,128)(2,1)S(1)} %copy-done.3, bf16[448,1024]{1,0:T(8,128)(2,1)S(1)} %copy-done.19, ...), custom_call_target="tpu_custom_call" | custom-call | flops 14092861440 | bytes 8126464 | tf_op jit(solution)/shard_map/attend_cross_back/pallas_call | solution.py:184
  406.3 11.7 %convolution_convert_fusion.3 = bf16[1024,2048]{1,0:T(8,128)(2,1)} fusion(bf16[1536,2048]{1,0:T(8,128)(2,1)} %constant_dynamic-update-slice_fusion.3, bf16[384,1024]{1,0:T(8,128)(2,1)S(1)} %copy-done.86, bf16[384,1024]{1,0:T(8,128)(2,1)S(1)} %copy-done.85, bf16[384,1024]{1,0:T(8,128)(2,1)S(1)} %copy-done.84, bf16[384,1024]{1,0:T(8,128)(2,1)S(1)} %copy-done.83), kind=kOutput, calls=%fused_computation.28 | convolution fusion | flops 6457131008 | bytes 13631488 | tf_op jit(solution)/shard_map/dot_general | solution.py:216
  449.8 12.7 %attend_causal_back.1 = (bf16[448,1024]{1,0:T(8,128)(2,1)S(1)}, bf16[448,1024]{1,0:T(8,128)(2,1)S(1)}, bf16[448,1024]{1,0:T(8,128)(2,1)S(1)}) custom-call(bf16[448,1024]{1,0:T(8,128)(2,1)S(1)} %copy-done.10, bf16[448,1024]{1,0:T(8,128)(2,1)S(1)} %copy-done.6, bf16[448,1024]{1,0:T(8,128)(2,1)S(1)} %copy-done.8, bf16[448,1024]{1,0:T(8,128)(2,1)S(1)} %copy-done.22, ...), custom_call_target="tpu_custom_call" | custom-call | flops 8220835840 | bytes 7340032 | tf_op jit(solution)/shard_map/attend_causal_back/pallas_call | solution.py:184
  473.2 6.5 fusion.27
  491.2 5.8 convolution_convert_fusion.2
  497.0 6.4 pad_maximum_fusion
  522.8 8.8 %convolution_convert_fusion.4 = bf16[1536,1024]{1,0:T(8,128)(2,1)S(1)} fusion(bf16[1536,2048]{1,0:T(8,128)(2,1)} %constant_dynamic-update-slice_fusion.3, bf16[1024,2048]{1,0:T(8,128)(2,1)S(1)} %copy-done.111), kind=kOutput, calls=%fused_computation.29 | convolution fusion | flops 6444023808 | bytes 13631488 | tf_op jit(solution)/shard_map/dot_general | solution.py:210
  539.2 7.9 %collective-permute-done.28 = bf16[512,1024]{1,0:T(8,128)(2,1)S(1)} collective-permute-done((bf16[512,1024]{1,0:T(8,128)(2,1)S(1)}, bf16[512,1024]{1,0:T(8,128)(2,1)S(1)}, u32[]{:S(2)}, u32[]{:S(2)}) %collective-permute-start.28) | collective-permute-done | bytes 1048608 | tf_op jit(solution)/shard_map/ppermute | solution.py:306
  555.3 6.6 collective-permute-start.33
  567.6 7.7 %collective-permute-done.38 = bf16[72,3072]{1,0:T(8,128)(2,1)S(1)} collective-permute-done((bf16[72,3072]{1,0:T(8,128)(2,1)S(1)}, bf16[72,3072]{1,0:T(8,128)(2,1)S(1)}, u32[]{:S(2)}, u32[]{:S(2)}) %collective-permute-start.38) | collective-permute-done | bytes 442400 | tf_op jit(solution)/shard_map/ppermute | solution.py:317
  584.4 6.6 collective-permute-done.41
  591.1 8.2 %collective-permute-start.34 = (bf16[487,1024]{1,0:T(8,128)(2,1)S(1)}, bf16[487,1024]{1,0:T(8,128)(2,1)S(1)}, u32[]{:S(2)}, u32[]{:S(2)}) collective-permute-start(bf16[487,1024]{1,0:T(8,128)(2,1)S(1)} %pad_maximum_fusion.18), channel_id=1, source_target_pairs={{0,1},{1,2},{2,3},{5,6},{6,7},{7,4},{8,9},{9,10},{10,11},{13,14},{... | collective-permute-start | bytes 2992136 | tf_op jit(solution)/shard_map/ppermute | solution.py:270
  602.5 8.0 %collective-permute-done.45 = bf16[128,5120]{1,0:T(8,128)(2,1)S(1)} collective-permute-done((bf16[128,5120]{1,0:T(8,128)(2,1)S(1)}, bf16[128,5120]{1,0:T(8,128)(2,1)S(1)}, u32[]{:S(2)}, u32[]{:S(2)}) %collective-permute-start.45) | collective-permute-done | bytes 1310752 | tf_op jit(solution)/shard_map/ppermute | solution.py:306
  616.0 7.3 %collective-permute-done.33 = bf16[487,1024]{1,0:T(8,128)(2,1)} collective-permute-done((bf16[487,1024]{1,0:T(8,128)(2,1)}, bf16[487,1024]{1,0:T(8,128)(2,1)}, u32[]{:S(2)}, u32[]{:S(2)}) %collective-permute-start.33) | collective-permute-done | bytes 997408 | tf_op jit(solution)/shard_map/ppermute | solution.py:270
  633.4 6.8 collective-permute-done.42
  646.5 36.7 %collective-permute-done.47 = bf16[128,5120]{1,0:T(8,128)(2,1)S(1)} collective-permute-done((bf16[128,5120]{1,0:T(8,128)(2,1)S(1)}, bf16[128,5120]{1,0:T(8,128)(2,1)S(1)}, u32[]{:S(2)}, u32[]{:S(2)}) %collective-permute-start.47) | collective-permute-done | bytes 1310752 | tf_op jit(solution)/shard_map/ppermute | solution.py:306
  685.5 12.9 %collective-permute-done.44 = bf16[144,3072]{1,0:T(8,128)(2,1)S(1)} collective-permute-done((bf16[144,3072]{1,0:T(8,128)(2,1)S(1)}, bf16[144,3072]{1,0:T(8,128)(2,1)S(1)}, u32[]{:S(2)}, u32[]{:S(2)}) %collective-permute-start.44) | collective-permute-done | bytes 884768 | tf_op jit(solution)/shard_map/ppermute | solution.py:306
  (496 shorter events, 261.1 us)
Async XLA Ops:
  7.2 81.6 %all-gather.5.cloned.1.call-start = ((), (), s32[]{:S(2)}) async-start(), calls=%async_computation.2 | async-start | bytes 9437184 | tf_op jit(solution)/shard_map/all_gather | solution.py:451
  9.6 258.1 %all-gather.7.cloned.1.call-start = ((), (), s32[]{:S(2)}) async-start(), calls=%async_computation.3 | async-start | bytes 9437184 | tf_op jit(solution)/shard_map/all_gather | solution.py:451
  12.0 49.2 %collective-permute-start.7 = (bf16[128,4096]{1,0:T(8,128)(2,1)}, bf16[128,4096]{1,0:T(8,128)(2,1)S(1)}, u32[]{:S(2)}, u32[]{:S(2)}) collective-permute-start(bf16[128,4096]{1,0:T(8,128)(2,1)} %constant_dynamic-update-slice_fusion), channel_id=1, source_target_pairs={{0,16},{4,20},{8,24},{12,28},{16,0},{20,4},{24,8},{28,12},{1,17},{... | collective-permute-start | bytes 3145736 | tf_op jit(solution)/shard_map/ppermute | solution.py:317
  15.0 46.3 %collective-permute-start.6 = (bf16[128,4096]{1,0:T(8,128)(2,1)}, bf16[128,4096]{1,0:T(8,128)(2,1)}, u32[]{:S(2)}, u32[]{:S(2)}) collective-permute-start(bf16[128,4096]{1,0:T(8,128)(2,1)} %constant_dynamic-update-slice_fusion), channel_id=1, source_target_pairs={{0,8},{4,12},{8,0},{12,4},{16,24},{20,28},{24,16},{28,20},{1,9},{5... | collective-permute-start | bytes 3145736 | tf_op jit(solution)/shard_map/ppermute | solution.py:317
  17.2 42.9 %collective-permute-start = (bf16[112,1024]{1,0:T(8,128)(2,1)}, bf16[112,1024]{1,0:T(8,128)(2,1)S(1)}, u32[]{:S(2)}, u32[]{:S(2)}) collective-permute-start(bf16[112,1024]{1,0:T(8,128)(2,1)} %get-tuple-element.238), channel_id=1, source_target_pairs={{0,1},{1,2},{3,0},{4,5},{5,6},{6,7},{8,9},{9,10},{11,8},{12,13},{1... | collective-permute-start | bytes 688136 | tf_op jit(solution)/shard_map/ppermute | solution.py:270
  20.7 39.4 %collective-permute-start.2 = (bf16[112,1024]{1,0:T(8,128)(2,1)S(1)}, bf16[112,1024]{1,0:T(8,128)(2,1)S(1)}, u32[]{:S(2)}, u32[]{:S(2)}) collective-permute-start(bf16[112,1024]{1,0:T(8,128)(2,1)S(1)} %get-tuple-element.239), channel_id=1, source_target_pairs={{1,0},{2,1},{3,2},{4,7},{6,5},{7,6},{9,8},{10,9},{11,10},{12,15},{... | collective-permute-start | bytes 688136 | tf_op jit(solution)/shard_map/ppermute | solution.py:270
  22.0 38.1 %collective-permute-start.1 = (bf16[112,1024]{1,0:T(8,128)(2,1)S(1)}, bf16[112,1024]{1,0:T(8,128)(2,1)S(1)}, u32[]{:S(2)}, u32[]{:S(2)}) collective-permute-start(bf16[112,1024]{1,0:T(8,128)(2,1)S(1)} %get-tuple-element.240), channel_id=1, source_target_pairs={{0,2},{2,0},{3,1},{4,6},{5,7},{7,5},{8,10},{10,8},{11,9},{12,14},{... | collective-permute-start | bytes 688136 | tf_op jit(solution)/shard_map/ppermute | solution.py:270
  27.6 370.0 %reduce-scatter.3.cloned.1.call-start = ((), (), s32[]{:S(2)}) async-start(), calls=%async_computation.4 | async-start | bytes 9437184 | tf_op jit(solution)/shard_map/reduce_scatter | solution.py:455
  64.0 39.8 %collective-permute-start.9 = (bf16[64,4096]{1,0:T(8,128)(2,1)}, bf16[64,4096]{1,0:T(8,128)(2,1)}, u32[]{:S(2)}, u32[]{:S(2)}) collective-permute-start(bf16[64,4096]{1,0:T(8,128)(2,1)} %slice.327), channel_id=1, source_target_pairs={{0,16},{4,20},{8,24},{12,28},{16,0},{20,4},{24,8},{28,12},{1,17},{... | collective-permute-start | bytes 1572872 | tf_op jit(solution)/shard_map/ppermute | solution.py:317
  64.5 39.3 %collective-permute-start.8 = (bf16[64,4096]{1,0:T(8,128)(2,1)}, bf16[64,4096]{1,0:T(8,128)(2,1)}, u32[]{:S(2)}, u32[]{:S(2)}) collective-permute-start(bf16[64,4096]{1,0:T(8,128)(2,1)} %slice.326), channel_id=1, source_target_pairs={{0,8},{4,12},{8,0},{12,4},{16,24},{20,28},{24,16},{28,20},{1,9},{5... | collective-permute-start | bytes 1572872 | tf_op jit(solution)/shard_map/ppermute | solution.py:317
  109.3 83.7 %collective-permute-start.10 = (bf16[4,128,4096]{2,1,0:T(8,128)(2,1)}, bf16[4,128,4096]{2,1,0:T(8,128)(2,1)}, u32[]{:S(2)}, u32[]{:S(2)}) collective-permute-start(bf16[4,128,4096]{2,1,0:T(8,128)(2,1)} %pad_maximum_fusion.1.mine_ref), channel_id=1, source_target_pairs={{0,4},{4,0},{8,12},{12,8},{16,20},{20,16},{24,28},{28,24},{1,5},{5... | collective-permute-start | bytes 12582920 | tf_op jit(solution)/shard_map/ppermute | solution.py:317
  112.5 68.8 %collective-permute-start.4 = (bf16[487,1024]{1,0:T(8,128)(2,1)}, bf16[487,1024]{1,0:T(8,128)(2,1)}, u32[]{:S(2)}, u32[]{:S(2)}) collective-permute-start(bf16[487,1024]{1,0:T(8,128)(2,1)} %get-tuple-element.203), channel_id=1, source_target_pairs={{0,2},{2,0},{3,1},{4,6},{5,7},{7,5},{8,10},{10,8},{11,9},{12,14},{... | collective-permute-start | bytes 2992136 | tf_op jit(solution)/shard_map/ppermute | solution.py:270
  117.9 65.7 %collective-permute-start.3 = (bf16[487,1024]{1,0:T(8,128)(2,1)}, bf16[487,1024]{1,0:T(8,128)(2,1)}, u32[]{:S(2)}, u32[]{:S(2)}) collective-permute-start(bf16[487,1024]{1,0:T(8,128)(2,1)} %get-tuple-element.204), channel_id=1, source_target_pairs={{0,1},{1,2},{3,0},{4,5},{5,6},{6,7},{8,9},{9,10},{11,8},{12,13},{1... | collective-permute-start | bytes 2992136 | tf_op jit(solution)/shard_map/ppermute | solution.py:270
  193.0 33.2 %collective-permute-start.12 = (bf16[512,1024]{1,0:T(8,128)(2,1)}, bf16[512,1024]{1,0:T(8,128)(2,1)S(1)}, u32[]{:S(2)}, u32[]{:S(2)}) collective-permute-start(bf16[512,1024]{1,0:T(8,128)(2,1)} %param.27), channel_id=1, source_target_pairs={{0,16},{4,20},{8,24},{12,28},{16,0},{20,4},{24,8},{28,12},{1,17},{... | collective-permute-start | bytes 3145736 | tf_op jit(solution)/shard_map/ppermute | solution.py:317
  193.8 32.4 %collective-permute-start.11 = (bf16[512,1024]{1,0:T(8,128)(2,1)}, bf16[512,1024]{1,0:T(8,128)(2,1)}, u32[]{:S(2)}, u32[]{:S(2)}) collective-permute-start(bf16[512,1024]{1,0:T(8,128)(2,1)} %param.27), channel_id=1, source_target_pairs={{0,8},{4,12},{8,0},{12,4},{16,24},{20,28},{24,16},{28,20},{1,9},{5... | collective-permute-start | bytes 3145736 | tf_op jit(solution)/shard_map/ppermute | solution.py:317
  227.7 32.2 %collective-permute-start.14 = (bf16[256,1024]{1,0:T(8,128)(2,1)S(1)}, bf16[256,1024]{1,0:T(8,128)(2,1)S(1)}, u32[]{:S(2)}, u32[]{:S(2)}) collective-permute-start(bf16[256,1024]{1,0:T(8,128)(2,1)S(1)} %slice.340), channel_id=1, source_target_pairs={{0,16},{4,20},{8,24},{12,28},{16,0},{20,4},{24,8},{28,12},{1,17},{... | collective-permute-start | bytes 1572872 | tf_op jit(solution)/shard_map/ppermute | solution.py:317
  229.8 30.2 %collective-permute-start.13 = (bf16[256,1024]{1,0:T(8,128)(2,1)S(1)}, bf16[256,1024]{1,0:T(8,128)(2,1)S(1)}, u32[]{:S(2)}, u32[]{:S(2)}) collective-permute-start(bf16[256,1024]{1,0:T(8,128)(2,1)S(1)} %slice.339), channel_id=1, source_target_pairs={{0,8},{4,12},{8,0},{12,4},{16,24},{20,28},{24,16},{28,20},{1,9},{5... | collective-permute-start | bytes 1572872 | tf_op jit(solution)/shard_map/ppermute | solution.py:317
  286.3 293.3 %reduce-scatter.5.cloned.1.call-start = ((), (), s32[]{:S(2)}) async-start(), calls=%async_computation.5 | async-start | bytes 4718592 | tf_op jit(solution)/shard_map/reduce_scatter | solution.py:455
  370.3 60.9 %collective-permute-start.19 = (bf16[128,4096]{1,0:T(8,128)(2,1)}, bf16[128,4096]{1,0:T(8,128)(2,1)}, u32[]{:S(2)}, u32[]{:S(2)}) collective-permute-start(bf16[128,4096]{1,0:T(8,128)(2,1)} %pad_maximum_fusion.14), channel_id=1, source_target_pairs={{0,8},{4,12},{8,0},{12,4},{16,24},{20,28},{24,16},{28,20},{1,9},{5... | collective-permute-start | bytes 3145736 | tf_op jit(solution)/shard_map/ppermute | solution.py:317
  373.1 58.2 %collective-permute-start.20 = (bf16[128,4096]{1,0:T(8,128)(2,1)}, bf16[128,4096]{1,0:T(8,128)(2,1)}, u32[]{:S(2)}, u32[]{:S(2)}) collective-permute-start(bf16[128,4096]{1,0:T(8,128)(2,1)} %pad_maximum_fusion.15), channel_id=1, source_target_pairs={{0,16},{4,20},{8,24},{12,28},{16,0},{20,4},{24,8},{28,12},{1,17},{... | collective-permute-start | bytes 3145736 | tf_op jit(solution)/shard_map/ppermute | solution.py:317
  397.6 33.7 %collective-permute-start.21 = (bf16[512,1024]{1,0:T(8,128)(2,1)}, bf16[512,1024]{1,0:T(8,128)(2,1)}, u32[]{:S(2)}, u32[]{:S(2)}) collective-permute-start(bf16[512,1024]{1,0:T(8,128)(2,1)} %reduce-scatter.3.cloned.1.call-done), channel_id=1, source_target_pairs={{0,1},{3,2},{4,5},{7,6},{8,9},{11,10},{12,13},{15,14},{16,17},{19,... | collective-permute-start | bytes 3145736 | tf_op jit(solution)/shard_map/ppermute | solution.py:306
  436.7 36.1 %collective-permute-start.22 = (bf16[4,128,3072]{2,1,0:T(8,128)(2,1)}, bf16[4,128,3072]{2,1,0:T(8,128)(2,1)}, u32[]{:S(2)}, u32[]{:S(2)}) collective-permute-start(bf16[4,128,3072]{2,1,0:T(8,128)(2,1)} %pad_maximum_fusion.5), channel_id=1, source_target_pairs={{0,4},{4,0},{8,12},{12,8},{16,20},{20,16},{24,28},{28,24},{1,5},{5... | collective-permute-start | bytes 9437192 | tf_op jit(solution)/shard_map/ppermute | solution.py:317
  466.1 37.2 %collective-permute-start.23 = (bf16[128,4096]{1,0:T(8,128)(2,1)}, bf16[128,4096]{1,0:T(8,128)(2,1)}, u32[]{:S(2)}, u32[]{:S(2)}) collective-permute-start(bf16[128,4096]{1,0:T(8,128)(2,1)} %fusion.19), channel_id=1, source_target_pairs={{0,1},{3,2},{4,5},{7,6},{8,9},{11,10},{12,13},{15,14},{16,17},{19,... | collective-permute-start | bytes 3145736 | tf_op jit(solution)/shard_map/ppermute | solution.py:306
  471.1 36.5 %collective-permute-start.24 = (bf16[512,1024]{1,0:T(8,128)(2,1)}, bf16[512,1024]{1,0:T(8,128)(2,1)}, u32[]{:S(2)}, u32[]{:S(2)}) collective-permute-start(bf16[512,1024]{1,0:T(8,128)(2,1)} %add_convert_fusion.6), channel_id=1, source_target_pairs={{1,2},{2,1},{5,6},{6,5},{9,10},{10,9},{13,14},{14,13},{17,18},{18,... | collective-permute-start | bytes 3145736 | tf_op jit(solution)/shard_map/ppermute | solution.py:306
  481.4 38.5 %collective-permute-start.37 = (bf16[112,1024]{1,0:T(8,128)(2,1)}, bf16[112,1024]{1,0:T(8,128)(2,1)}, u32[]{:S(2)}, u32[]{:S(2)}) collective-permute-start(bf16[112,1024]{1,0:T(8,128)(2,1)} %get-tuple-element.228), channel_id=1, source_target_pairs={{0,1},{1,2},{2,3},{5,6},{6,7},{7,4},{8,9},{9,10},{10,11},{13,14},{... | collective-permute-start | bytes 688136 | tf_op jit(solution)/shard_map/ppermute | solution.py:270
  513.8 33.3 %collective-permute-start.31 = (bf16[4,144,3072]{2,1,0:T(8,128)(2,1)S(1)}, bf16[4,144,3072]{2,1,0:T(8,128)(2,1)S(1)}, u32[]{:S(2)}, u32[]{:S(2)}) collective-permute-start(bf16[4,144,3072]{2,1,0:T(8,128)(2,1)S(1)} %dynamic-slice_bitcast_fusion.1), channel_id=1, source_target_pairs={{0,4},{4,0},{8,12},{12,8},{16,20},{20,16},{24,28},{28,24},{1,5},{5... | collective-permute-start | bytes 10616840 | tf_op jit(solution)/shard_map/ppermute | solution.py:317
  551.6 63.7 %collective-permute-start.32 = (bf16[487,1024]{1,0:T(8,128)(2,1)}, bf16[487,1024]{1,0:T(8,128)(2,1)}, u32[]{:S(2)}, u32[]{:S(2)}) collective-permute-start(bf16[487,1024]{1,0:T(8,128)(2,1)} %pad_maximum_fusion.16), channel_id=1, source_target_pairs={{0,3},{1,0},{2,1},{5,4},{6,5},{7,6},{8,11},{9,8},{10,9},{13,12},{1... | collective-permute-start | bytes 2992136 | tf_op jit(solution)/shard_map/ppermute | solution.py:270
  555.3 68.0 %collective-permute-start.33 = (bf16[487,1024]{1,0:T(8,128)(2,1)}, bf16[487,1024]{1,0:T(8,128)(2,1)}, u32[]{:S(2)}, u32[]{:S(2)}) collective-permute-start(bf16[487,1024]{1,0:T(8,128)(2,1)} %pad_maximum_fusion.17), channel_id=1, source_target_pairs={{0,2},{1,3},{2,0},{5,7},{6,4},{7,5},{8,10},{9,11},{10,8},{13,15},{... | collective-permute-start | bytes 2992136 | tf_op jit(solution)/shard_map/ppermute | solution.py:270
  591.1 37.5 %collective-permute-start.34 = (bf16[487,1024]{1,0:T(8,128)(2,1)S(1)}, bf16[487,1024]{1,0:T(8,128)(2,1)S(1)}, u32[]{:S(2)}, u32[]{:S(2)}) collective-permute-start(bf16[487,1024]{1,0:T(8,128)(2,1)S(1)} %pad_maximum_fusion.18), channel_id=1, source_target_pairs={{0,1},{1,2},{2,3},{5,6},{6,7},{7,4},{8,9},{9,10},{10,11},{13,14},{... | collective-permute-start | bytes 2992136 | tf_op jit(solution)/shard_map/ppermute | solution.py:270
  599.3 44.2 %collective-permute-start.48 = (bf16[128,4096]{1,0:T(8,128)(2,1)S(1)}, bf16[128,4096]{1,0:T(8,128)(2,1)S(1)}, u32[]{:S(2)}, u32[]{:S(2)}) collective-permute-start(bf16[128,4096]{1,0:T(8,128)(2,1)S(1)} %copy-done.50), channel_id=1, source_target_pairs={{1,0},{2,3},{5,4},{6,7},{9,8},{10,11},{13,12},{14,15},{17,16},{18,... | collective-permute-start | bytes 3145736 | tf_op jit(solution)/shard_map/ppermute | solution.py:306
  641.5 41.7 %collective-permute-start.47 = (bf16[128,5120]{1,0:T(8,128)(2,1)S(1)}, bf16[128,5120]{1,0:T(8,128)(2,1)S(1)}, u32[]{:S(2)}, u32[]{:S(2)}) collective-permute-start(bf16[128,5120]{1,0:T(8,128)(2,1)S(1)} %add_convert_fusion.1), channel_id=1, source_target_pairs={{1,0},{2,3},{5,4},{6,7},{9,8},{10,11},{13,12},{14,15},{17,16},{18,... | collective-permute-start | bytes 3932168 | tf_op jit(solution)/shard_map/ppermute | solution.py:306
  645.2 53.2 %collective-permute-start.44 = (bf16[144,3072]{1,0:T(8,128)(2,1)S(1)}, bf16[144,3072]{1,0:T(8,128)(2,1)S(1)}, u32[]{:S(2)}, u32[]{:S(2)}) collective-permute-start(bf16[144,3072]{1,0:T(8,128)(2,1)S(1)} %add_convert_fusion.10), channel_id=1, source_target_pairs={{1,0},{2,3},{5,4},{6,7},{9,8},{10,11},{13,12},{14,15},{17,16},{18,... | collective-permute-start | bytes 2654216 | tf_op jit(solution)/shard_map/ppermute | solution.py:306
  (143 other events, 1893.4 us)
Sparse Core Ops, SparseCore 0:
  10.5 78.2 all-gather.4
  90.7 55.0 all-gather.6
  286.5 81.8 reduce-scatter.2
  444.2 50.6 reduce-scatter.4

commit v3 on v1

v3 whole, which is shorter than its diff:
```python
import functools

import jax
import jax.numpy as jnp
import numpy as np
from jax import lax
from jax.experimental import pallas as pl
from jax.experimental.pallas import tpu as pltpu
from jax.sharding import PartitionSpec as P

HD = 64
LANES = 128
NORM_EPSILON = 1e-05
LOW = -1e30
F32 = jnp.float32
BF = jnp.bfloat16
AXES = ("fsdp", "seq")


def two_heads(rows):
    lane = lax.broadcasted_iota(jnp.int32, rows.shape, 1)
    zero = jnp.zeros_like(rows)
    return jnp.concatenate(
        [jnp.where(lane < HD, rows, zero), jnp.where(lane >= HD, rows, zero)], axis=0
    )


def one_row(stacked):
    count = stacked.shape[0] // 2
    lane = lax.broadcasted_iota(jnp.int32, (count, stacked.shape[1]), 1)
    return jnp.where(lane < HD, stacked[:count], stacked[count:])


def over_rows(first, second):
    return lax.dot_general(first, second, (((0,), (0,)), ((), ())), preferred_element_type=F32)


def over_lanes(first, second):
    return lax.dot_general(first, second, (((1,), (1,)), ((), ())), preferred_element_type=F32)


def fill_scores(scores_ref, keys, queries, valid, places):
    size = keys.shape[0]
    scores = over_lanes(keys, queries)
    if places is not None:
        key_place, query_place = places
        scores = jnp.where(key_place <= query_place, scores, LOW)
    scores_ref[...] = scores
    if valid < size:
        first = valid // 8 * 8
        row = lax.broadcasted_iota(jnp.int32, (size - first, queries.shape[0]), 0)
        scores_ref[first:size] = jnp.where(row < valid - first, scores_ref[first:size], LOW)


def forward_kernel(chunk, valid, causal, *refs):
    if causal:
        q_ref, k_ref, v_ref, kp_ref, qp_ref, o_ref, log_ref, s_ref = refs
    else:
        q_ref, k_ref, v_ref, o_ref, log_ref, s_ref = refs
    queries = two_heads(q_ref[...])
    count = k_ref.shape[0] // chunk
    width = queries.shape[0]

    def first(step, top):
        rows = pl.ds(pl.multiple_of(step * chunk, chunk), chunk)
        places = (kp_ref[rows], qp_ref[...]) if causal else None
        part = s_ref.at[rows]
        fill_scores(part, k_ref[rows], queries, valid, places)
        return jnp.maximum(top, jnp.max(part[...], axis=0, keepdims=True))

    top = lax.fori_loop(0, count, first, jnp.full((1, width), LOW, F32))

    def second(step, carry):
        total, mixed = carry
        rows = pl.ds(pl.multiple_of(step * chunk, chunk), chunk)
        raised = jnp.exp(s_ref[rows] - top)
        total = total + jnp.sum(raised, axis=0, keepdims=True)
        mixed = mixed + over_rows(v_ref[rows], raised.astype(BF))
        return total, mixed

    total, mixed = lax.fori_loop(
        0, count, second, (jnp.zeros((1, width), F32), jnp.zeros((LANES, width), F32))
    )
    o_ref[...] = one_row(jnp.transpose(mixed / total)).astype(BF)
    log_ref[...] = (top + jnp.log(total))[None]


def backward_kernel(chunk, valid, causal, *refs):
    q_ref, k_ref, v_ref, o_ref, g_ref, log_ref = refs[:6]
    if causal:
        kp_ref, qp_ref = refs[6:8]
        joint_ref, s_ref, gk_ref, gv_ref = refs[-4:]
    else:
        gq_ref, joint_ref, s_ref, gv_ref = refs[-4:]
        gk_ref = joint_ref
    phase = pl.program_id(1)

    @pl.when(phase == 0)
    def _():
        queries = two_heads(q_ref[...])
        grads = two_heads(g_ref[...])
        mixed = o_ref[...].astype(F32)
        product = grads.astype(F32) * jnp.concatenate([mixed, mixed], axis=0)
        row_dot = jnp.sum(jnp.transpose(product), axis=0, keepdims=True)
        log_total = log_ref[0]
        width = queries.shape[0]

        def body(step, grad_queries):
            rows = pl.ds(pl.multiple_of(step * chunk, chunk), chunk)
            places = (kp_ref[rows], qp_ref[...]) if causal else None
            keys = k_ref[rows]
            fill_scores(s_ref, keys, queries, valid, places)
            weights = jnp.exp(s_ref[...] - log_total)
            grad_weights = over_lanes(v_ref[rows], grads)
            grad_scores = (weights * (grad_weights - row_dot)).astype(BF)
            gv_ref[rows] = jnp.dot(
                weights.astype(BF), grads, preferred_element_type=F32
            ).astype(BF)
            gk_ref[rows] = jnp.dot(grad_scores, queries, preferred_element_type=F32).astype(BF)
            return grad_queries + over_rows(keys, grad_scores)

        steps = k_ref.shape[0] // chunk
        grad_queries = lax.fori_loop(0, steps, body, jnp.zeros((LANES, width), F32))
        grad_queries = one_row(jnp.transpose(grad_queries)).astype(BF) * BF(HD**-0.5)
        (joint_ref if causal else gq_ref)[...] = grad_queries

    if causal:

        @pl.when(phase == 1)
        def _():
            joint_ref[...] = gk_ref[...]

    @pl.when(phase == (2 if causal else 1))
    def _():
        joint_ref[...] = gv_ref[...]


def columns(rows, first=0):
    return pl.BlockSpec((rows, LANES), lambda pair, *phase: (0, pair + first))


def place_specs(keys, tokens):
    return [
        pl.BlockSpec((keys, 1), lambda pair, *phase: (0, 0)),
        pl.BlockSpec((1, 2 * tokens), lambda pair, *phase: (0, 0)),
    ]


def log_spec(tokens, first=0):
    return pl.BlockSpec((1, 1, 2 * tokens), lambda pair, *phase: (pair + first, 0, 0))


def attend(sources, places, chunk, valid, width):
    tokens, count = sources[0][0].shape[0], sources[1][0].shape[0]
    causal = places is not None
    pairs = width // LANES
    specs = [columns(member.shape[0], first) for member, first in sources]
    operands = [member for member, _ in sources]
    if causal:
        specs += place_specs(count, tokens)
        operands += list(places)
    return pl.pallas_call(
        functools.partial(forward_kernel, chunk, valid, causal),
        grid=(pairs,),
        in_specs=specs,
        out_specs=[columns(tokens), log_spec(tokens)],
        out_shape=[
            jax.ShapeDtypeStruct((tokens, width), BF),
            jax.ShapeDtypeStruct((pairs, 1, 2 * tokens), F32),
        ],
        scratch_shapes=[pltpu.VMEM((count, 2 * tokens), F32)],
        compiler_params=pltpu.CompilerParams(vmem_limit_bytes=32 << 20),
        cost_estimate=pl.CostEstimate(
            flops=16 * tokens * count * width,
            transcendentals=tokens * count * width // HD,
            bytes_accessed=4 * (tokens + count) * width,
        ),
        name="attend_causal" if causal else "attend_cross",
    )(*operands)


def attend_back(
    sources, mixed, grads, logs, places, chunk, valid, width, part=0, parts=1, before=()
):
    tokens, count = sources[0][0].shape[0], sources[1][0].shape[0]
    causal = places is not None
    pairs = width // LANES
    count_here = pairs // parts
    low = part * count_here
    specs = [columns(member.shape[0], first + low) for member, first in sources]
    specs += [columns(tokens, low), columns(tokens, low), log_spec(tokens, low)]
    operands = [member for member, _ in sources] + [mixed, grads, logs]
    joint_spec = pl.BlockSpec(
        (count, LANES), lambda pair, phase: (0, pair + low + pairs * phase)
    )
    if causal:
        specs += place_specs(count, tokens)
        operands += list(places)
        out_specs = [joint_spec]
        out_shape = [jax.ShapeDtypeStruct((count, 3 * width), BF)]
    else:
        out_specs = [columns(tokens, low), joint_spec]
        out_shape = [
            jax.ShapeDtypeStruct((tokens, width), BF),
            jax.ShapeDtypeStruct((count, 2 * width), BF),
        ]
    aliases = {len(operands) + i: i for i in range(len(before))}
    specs += [pl.BlockSpec(memory_space=pl.ANY)] * len(before)
    operands += list(before)
    kept = [pltpu.VMEM((count, LANES), BF)] * (2 if causal else 1)
    return pl.pallas_call(
        functools.partial(backward_kernel, chunk, valid, causal),
        grid=(count_here, 3 if causal else 2),
        in_specs=specs,
        out_specs=out_specs,
        out_shape=out_shape,
        scratch_shapes=[pltpu.VMEM((chunk, 2 * tokens), F32)] + kept,
        input_output_aliases=aliases,
        compiler_params=pltpu.CompilerParams(vmem_limit_bytes=32 << 20),
        cost_estimate=pl.CostEstimate(
            flops=40 * tokens * count * width // parts,
            transcendentals=tokens * count * width // HD // parts,
            bytes_accessed=8 * (tokens + count) * width // parts,
        ),
        name="attend_causal_back" if causal else "attend_cross_back",
    )(*operands)


def product(first, second):
    return jnp.dot(first, second, preferred_element_type=F32)


def product_back(incoming, weight):
    return lax.dot_general(
        incoming, weight, (((1,), (1,)), ((), ())), preferred_element_type=F32
    )


def weight_grad(operand, incoming):
    return lax.dot_general(
        operand, incoming, (((0,), (0,)), ((), ())), preferred_element_type=F32
    ).astype(BF)


def normalized(values):
    average = jnp.mean(values, axis=-1, keepdims=True)
    centred = values - average
    variance = jnp.mean(centred * centred, axis=-1, keepdims=True)
    inverse = lax.rsqrt(variance + NORM_EPSILON)
    return centred * inverse, inverse


def norm_back(incoming, values, gain_row):
    rows, inverse = normalized(values)
    scaled = incoming * gain_row
    average = jnp.mean(scaled, axis=-1, keepdims=True)
    aligned = jnp.mean(scaled * rows, axis=-1, keepdims=True)
    gain_grad = jnp.sum(incoming * rows, axis=0)
    shift_grad = jnp.sum(incoming, axis=0)
    return (scaled - average - rows * aligned) * inverse, gain_grad, shift_grad


def gelu(values):
    return values * (1.0 + lax.erf(values * (0.5**0.5))) * 0.5


def gelu_slope(values):
    return (1.0 + lax.erf(values * (0.5**0.5))) * 0.5 + values * jnp.exp(
        -0.5 * values * values
    ) * (0.5 / jnp.pi) ** 0.5


class Grid:
    def __init__(self, fsdp, seq, clips):
        self.fsdp, self.seq, self.clips = fsdp, seq, clips
        self.here = lax.axis_index("seq")
        self.group = lax.axis_index("fsdp")
        self.first = self.first_of(self.group)

    def first_of(self, group):
        return (group % 2) * (self.seq - self.clips)

    def works(self, group, place):
        return 0 <= place - self.first_of(group) < self.clips

    def turn(self, values, step, to_workers):
        pairs = []
        for group in range(self.fsdp):
            for place in range(self.seq):
                target = (place + step) % self.seq
                worker = target if to_workers else place
                if self.works(group, worker):
                    pairs.append((group * self.seq + place, group * self.seq + target))
        return lax.ppermute(values, AXES, pairs)

    def clip_at(self, place):
        return jnp.clip(place - self.first, 0, self.clips - 1)

    def collect(self, values, steps):
        pieces = {}
        for step in steps:
            target = (self.here + step) % self.seq
            sent = lax.dynamic_index_in_dim(values, self.clip_at(target), 0, keepdims=False)
            if step == 0:
                active = (self.here >= self.first) & (self.here < self.first + self.clips)
                pieces[step] = jnp.where(active, sent, jnp.zeros_like(sent))
            else:
                pieces[step] = self.turn(sent, step, True)
        return pieces

    def hand_back(self, rows):
        parts = rows.reshape(self.seq, -1, rows.shape[1])
        moved = lax.all_to_all(parts, "seq", split_axis=0, concat_axis=0, tiled=True)
        return lax.dynamic_slice_in_dim(moved, self.first, self.clips, 0)

    def chain(self, values, links):
        pairs = [
            (group * self.seq + a, group * self.seq + b)
            for group in range(self.fsdp)
            for a, b in links
        ]
        return lax.ppermute(values, AXES, pairs)

    def flip(self, values, bits):
        return lax.ppermute(values, "fsdp", [(f, f ^ bits) for f in range(self.fsdp)])

    def spread_far(self, shard, by_x, by_y):
        half = shard.shape[0] // 2
        return self.flip(by_y[:half], 2), self.flip(by_x[half:], 4)

    def spread_core(self, shard, by_x, by_y, far_x, far_y):
        mine = jnp.stack([shard, by_x, by_y, jnp.concatenate([far_x, far_y], axis=0)])
        return mine, self.flip(mine, 1)

    def fold_core(self, *members):
        core = self.group % 2
        parts = [m.reshape(4, 2, m.shape[0] // 8, m.shape[1]) for m in members]
        sent = jnp.concatenate([pick(p, 1 - core, 1) for p in parts], axis=2)
        kept = jnp.concatenate([pick(p, core, 1) for p in parts], axis=2)
        return kept, self.flip(sent, 1)

    def fold_chips(self, kept, arrived):
        sums = plus(kept, arrived)
        chip = self.group // 2
        moved = [self.flip(pick(sums, chip ^ bits, 0), 2 * bits) for bits in (1, 2, 3)]
        return pick(sums, chip, 0), moved

    def hop_one(self, values):
        return values, self.chain(values, ((0, 1), (3, 2)))

    def hop_two(self, values, arrived):
        half = plus(values, arrived)
        return half, self.chain(half, ((1, 2), (2, 1)))

    def hop_three(self, half, arrived):
        whole = plus(half, arrived)
        return whole, self.chain(whole, ((1, 0), (2, 3)))

    def hop_end(self, whole, back):
        return jnp.where((self.here == 0) | (self.here == 3), back, whole).astype(F32)

    def seq_sum(self, values):
        if self.seq != 4:
            return lax.psum(values, "seq").astype(F32)
        return self.hop_end(*self.hop_three(*self.hop_two(*self.hop_one(values))))


def pick(values, index, axis):
    return lax.dynamic_index_in_dim(values, index, axis, keepdims=False)


def plus(first, second):
    return (first.astype(F32) + second.astype(F32)).astype(first.dtype)


def plus_all(first, others):
    total = first.astype(F32)
    for other in others:
        total = total + other.astype(F32)
    return total.astype(first.dtype)


def tied(*members):
    return lax.optimization_barrier(members)


def place_kernel(parts, here_ref, *refs):
    count = len(refs) - len(parts)
    pieces, outs = refs[:count], refs[count:]

    def store(piece):
        for out, (low, high, padded) in zip(outs, parts):
            out[: high - low] = piece[low:high]
            if padded > high - low:
                out[high - low :] = jnp.zeros((padded - high + low, out.shape[1]), out.dtype)

    for step, piece in enumerate(pieces):
        pl.when(pl.program_id(0) == step)(functools.partial(store, piece))


def place(here, pieces, parts):
    count = len(pieces)
    rows, width = pieces[0].shape
    return pl.pallas_call(
        functools.partial(place_kernel, parts),
        grid_spec=pltpu.PrefetchScalarGridSpec(
            num_scalar_prefetch=1,
            grid=(count,),
            in_specs=[pl.BlockSpec((rows, width), lambda step, here: (0, 0))] * count,
            out_specs=[
                pl.BlockSpec((padded, width), lambda step, here: ((here[0] - step) % count, 0))
                for _, _, padded in parts
            ],
        ),
        out_shape=[
            jax.ShapeDtypeStruct((count * padded, width), BF) for _, _, padded in parts
        ],
        compiler_params=pltpu.CompilerParams(vmem_limit_bytes=24 << 20),
        cost_estimate=pl.CostEstimate(
            flops=0, transcendentals=0, bytes_accessed=4 * count * rows * width
        ),
        name="place",
    )(here.reshape(1), *pieces)


def assemble_kernel(widths, rows, group_ref, mine_ref, other_ref, *outs):
    flipped = group_ref[0] % 2

    def store(first_ref, second_ref):
        start = 0
        for out, width in zip(outs, widths):
            out[:rows] = first_ref[0, :, start : start + width]
            out[rows:] = second_ref[0, :, start : start + width]
            start += width

    pl.when(flipped == 0)(lambda: store(mine_ref, other_ref))
    pl.when(flipped == 1)(lambda: store(other_ref, mine_ref))


def assemble(group, mine, other, widths):
    rows, total = mine.shape[1], mine.shape[2]
    source = pl.BlockSpec((1, rows, total), lambda chip, group: (chip, 0, 0))
    return pl.pallas_call(
        functools.partial(assemble_kernel, widths, rows),
        grid_spec=pltpu.PrefetchScalarGridSpec(
            num_scalar_prefetch=1,
            grid=(4,),
            in_specs=[source, source],
            out_specs=[
                pl.BlockSpec((2 * rows, width), lambda chip, group: ((group[0] // 2) ^ chip, 0))
                for width in widths
            ],
        ),
        out_shape=[jax.ShapeDtypeStruct((8 * rows, width), BF) for width in widths],
        compiler_params=pltpu.CompilerParams(vmem_limit_bytes=16 << 20),
        cost_estimate=pl.CostEstimate(
            flops=0, transcendentals=0, bytes_accessed=32 * rows * total
        ),
        name="assemble",
    )(group.reshape(1), mine, other)


def local(
    mesh_shape,
    hidden_in,
    encoded,
    out_grad,
    norm_gain,
    norm_shift,
    biases,
    self_qkv,
    self_out,
    cross_q,
    cross_kv,
    cross_out,
    mlp_in,
    mlp_in_bias,
    mlp_out,
):
    clips, rows, width = hidden_in.shape
    frames = encoded.shape[1]
    padded = (frames + 15) // 16 * 16
    grid = Grid(mesh_shape["fsdp"], mesh_shape["seq"], clips)
    shard = norm_gain.shape[1]
    norms = norm_gain.shape[0]
    bias_count = biases.shape[0]
    scaling = HD ** (-0.5)
    swift = grid.fsdp == 8 and grid.seq == 4 and self_qkv.shape[0] >= 32

    def gathered(*members):
        widths = [member.shape[1] for member in members]
        joined = jnp.concatenate(members, axis=1)
        joined = lax.all_gather(joined, "fsdp", axis=0, tiled=True)
        return jnp.split(joined, np.cumsum(widths)[:-1].tolist(), axis=1)

    def scattered(member):
        return lax.psum_scatter(member, "fsdp", scatter_dimension=0, tiled=True)

    tokens_in = jnp.concatenate([hidden_in, encoded], axis=1)
    pieces = grid.collect(tokens_in, (0, 1, 3) if swift else range(grid.seq))
    small = jnp.concatenate([norm_gain, norm_shift, biases, mlp_in_bias.reshape(-1, shard)], axis=0)
    kinds = small.shape[0]
    shard_rows = self_qkv.shape[0]
    if swift:
        small = jnp.pad(small, ((0, shard_rows - kinds), (0, 0)))
        first_shard = jnp.concatenate([self_qkv, small], axis=1)
        first_widths = (self_qkv.shape[1], shard)
        first_x, first_y = grid.flip(first_shard, 2), grid.flip(first_shard, 4)
    full_self_out, full_cross_q, full_cross_kv = gathered(self_out, cross_q, cross_kv)
    full_cross_out, full_inner = gathered(cross_out, mlp_in)
    if swift:
        first_x, first_y, pieces[1], pieces[3], tokens_in = tied(
            first_x, first_y, pieces[1], pieces[3], tokens_in
        )
        pieces.update(grid.collect(tokens_in, (2,)))
        far_x, far_y = grid.spread_far(first_shard, first_x, first_y)
        far_x, far_y, pieces[2] = tied(far_x, far_y, pieces[2])
        mine, other = grid.spread_core(first_shard, first_x, first_y, far_x, far_y)
        other, mlp_out = tied(other, mlp_out)
        outer_x, outer_y = grid.flip(mlp_out, 2), grid.flip(mlp_out, 4)
        full_qkv, small = assemble(grid.group, mine, other, first_widths)
        small = small.reshape(grid.fsdp, shard_rows, shard)[:, :kinds]
    else:
        (full_qkv,) = gathered(self_qkv)
        small = lax.all_gather(small, "fsdp", axis=0)
        (full_outer,) = gathered(mlp_out)
    vectors = small[:, : 2 * norms + bias_count].swapaxes(0, 1).reshape(-1, width).astype(F32)
    gain, shift, bias = vectors[:norms], vectors[norms : 2 * norms], vectors[2 * norms :]
    inner_bias = small[:, 2 * norms + bias_count :].reshape(1, -1).astype(F32)
    none = jnp.zeros((width,), F32)

    token_rows, frame_rows = place(
        grid.here,
        [pieces[step] for step in range(grid.seq)],
        ((0, rows, rows), (rows, rows + frames, padded)),
    )
    residual_in = token_rows.astype(F32)
    normed_one = (normalized(residual_in)[0] * gain[0] + shift[0]).astype(BF)
    tokens = grid.seq * rows
    line = jnp.arange(tokens)
    places = (line[:, None], jnp.concatenate([line, line])[None, :])
    blocks = width // LANES

    qkv_bias = jnp.concatenate([bias[0], none, bias[1]])
    qkv_scale = jnp.concatenate([none + scaling, none + 1.0, none + 1.0])
    qkv = ((product(normed_one, full_qkv) + qkv_bias) * qkv_scale).astype(BF)
    self_sources = ((qkv, 0), (qkv, blocks), (qkv, 2 * blocks))
    self_mix, self_log = attend(self_sources, places, tokens, tokens, width)
    after_self = residual_in + product(self_mix, full_self_out) + bias[2]
    normed_two = (normalized(after_self)[0] * gain[1] + shift[1]).astype(BF)
    cross_queries = ((product(normed_two, full_cross_q) + bias[3]) * scaling).astype(BF)
    out_grad, cross_queries = tied(out_grad, cross_queries)
    top_pieces = list(grid.collect(out_grad, range(grid.seq)).values())
    kv_bias = jnp.concatenate([none, bias[4]])
    cross_pair = (product(frame_rows, full_cross_kv) + kv_bias).astype(BF)
    cross_sources = ((cross_queries, 0), (cross_pair, 0), (cross_pair, blocks))
    cross_mix, cross_log = attend(cross_sources, None, padded, frames, width)
    if swift:
        cross_mix, outer_x, outer_y, *top_pieces = tied(cross_mix, outer_x, outer_y, *top_pieces)
        far_x, far_y = grid.spread_far(mlp_out, outer_x, outer_y)
    (top,) = place(grid.here, top_pieces, ((0, rows, rows),))
    after_cross = after_self + product(cross_mix, full_cross_out) + bias[5]
    normed_three = (normalized(after_cross)[0] * gain[2] + shift[2]).astype(BF)
    inner = product(normed_three, full_inner) + inner_bias
    activated = gelu(inner).astype(BF)
    if swift:
        activated, far_x, far_y = tied(activated, far_x, far_y)
        mine, other = grid.spread_core(mlp_out, outer_x, outer_y, far_x, far_y)

    top_wide = top.astype(F32)
    grad_w_outer = weight_grad(activated, top)
    if swift:
        grad_w_outer, top, other = tied(grad_w_outer, top, other)
        (full_outer,) = assemble(grid.group, mine, other, (mlp_out.shape[1],))
    part_outer = scattered(grad_w_outer)
    grad_bias_six = jnp.sum(top_wide, axis=0)
    grad_inner = product_back(top, full_outer) * gelu_slope(inner)
    grad_inner_low = grad_inner.astype(BF)
    grad_w_inner = weight_grad(normed_three, grad_inner_low)
    grad_w_inner, grad_inner_low = tied(grad_w_inner, grad_inner_low)
    part_inner = scattered(grad_w_inner)
    grad_inner_bias = jnp.sum(grad_inner, axis=0)
    grad_normed_three = product_back(grad_inner_low, full_inner)
    from_three, gain_three, shift_three = norm_back(grad_normed_three, after_cross, gain[2])
    grad_after_cross = top_wide + from_three
    grad_cross_low = grad_after_cross.astype(BF)
    grad_bias_five = jnp.sum(grad_after_cross, axis=0)
    grad_w_cross_out = weight_grad(cross_mix, grad_cross_low)
    grad_cross_mix = product_back(grad_cross_low, full_cross_out).astype(BF)

    cross_back = functools.partial(
        attend_back,
        cross_sources,
        cross_mix,
        logs=cross_log,
        places=None,
        chunk=padded,
        valid=frames,
        width=width,
        parts=2,
    )
    first_part = cross_back(grads=grad_cross_mix)
    if swift:
        grad_cross_mix, part_outer, *first_part = tied(grad_cross_mix, part_outer, *first_part)
        outer_sum, outer_in = grid.hop_one(part_outer)
    grad_cross_queries, grad_pair = cross_back(
        grads=grad_cross_mix, part=1, before=tuple(first_part)
    )
    if swift:
        grad_cross_queries, grad_pair, outer_in = tied(grad_cross_queries, grad_pair, outer_in)
        outer_sum, outer_in = grid.hop_two(outer_sum, outer_in)
    grad_frames = product_back(grad_pair, full_cross_kv).astype(BF)
    grad_frames, grad_pair = tied(grad_frames, grad_pair)
    grad_encoded = grid.hand_back(grad_frames)
    grad_w_cross_kv = weight_grad(frame_rows, grad_pair)
    if swift:
        grad_w_cross_kv, grad_cross_queries, outer_in = tied(
            grad_w_cross_kv, grad_cross_queries, outer_in
        )
        outer_sum, outer_in = grid.hop_three(outer_sum, outer_in)
    part_kv = scattered(grad_w_cross_kv)
    grad_bias_four = jnp.sum(grad_pair[:, width:].astype(F32), axis=0)
    grad_w_cross_q = weight_grad(normed_two, grad_cross_queries)
    grad_bias_three = jnp.sum(grad_cross_queries.astype(F32), axis=0)
    grad_normed_two = product_back(grad_cross_queries, full_cross_q)
    from_two, gain_two, shift_two = norm_back(grad_normed_two, after_self, gain[1])
    grad_after_self = grad_after_cross + from_two
    grad_self_low = grad_after_self.astype(BF)
    grad_w_self_out = weight_grad(self_mix, grad_self_low)
    grad_bias_two = jnp.sum(grad_after_self, axis=0)
    grad_self_mix = product_back(grad_self_low, full_self_out).astype(BF)
    middle = [grad_w_cross_out, grad_w_cross_q, grad_w_self_out]
    if swift:
        grad_self_mix, *middle = tied(grad_self_mix, *middle)
        middle_kept, middle_core = grid.fold_core(*middle)
    (grad_pre,) = attend_back(
        self_sources, self_mix, grad_self_mix, self_log, places, tokens, tokens, width
    )
    if swift:
        grad_pre, middle_core, part_inner = tied(grad_pre, middle_core, part_inner)
        middle_own, middle_near = grid.fold_chips(middle_kept, middle_core)
        inner_sum, inner_in = grid.hop_one(part_inner)
    grad_normed_one = product_back(grad_pre, full_qkv)
    grad_w_qkv = weight_grad(normed_one, grad_pre)
    pre_sums = jnp.sum(grad_pre.astype(F32), axis=0)
    from_one, gain_one, shift_one = norm_back(grad_normed_one, residual_in, gain[0])
    grad_rows = (grad_after_self + from_one).astype(BF)

    sums = jnp.stack(
        [
            gain_one,
            gain_two,
            gain_three,
            shift_one,
            shift_two,
            shift_three,
            pre_sums[:width],
            pre_sums[2 * width :],
            grad_bias_two,
            grad_bias_three,
            grad_bias_four,
            grad_bias_five,
            grad_bias_six,
        ]
    )
    inner_sums = grad_inner_bias.reshape(grid.fsdp, -1, shard)
    packed = jnp.concatenate(
        [sums.reshape(-1, grid.fsdp, shard).swapaxes(0, 1), inner_sums], axis=1
    )
    if swift:
        packed = jnp.pad(packed.astype(BF), ((0, 0), (0, shard_rows - kinds), (0, 0)))
        packed = packed.reshape(-1, shard)
        last_kept, last_core = grid.fold_core(grad_w_qkv, packed)
        last_kept, activated, grad_rows = tied(last_kept, activated, grad_rows)
    hidden_rows = (after_cross + product(activated, full_outer) + bias[6]).astype(BF)
    leaving = jnp.concatenate(
        [
            grad_rows.reshape(grid.seq, rows, width),
            hidden_rows.reshape(grid.seq, rows, width),
        ],
        axis=1,
    ).reshape(-1, width)
    if swift:
        last_core, leaving, inner_in, outer_in = tied(last_core, leaving, inner_in, outer_in)
        last_own, last_near = grid.fold_chips(last_kept, last_core)
        inner_sum, inner_in = grid.hop_two(inner_sum, inner_in)
    leaving = grid.hand_back(leaving)
    if swift:
        part_middle = jnp.concatenate([plus_all(middle_own, middle_near), part_kv], axis=1)
        middle_sum, middle_in = grid.hop_one(part_middle)
        middle_in, inner_in, grad_encoded, *last_near = tied(
            middle_in, inner_in, grad_encoded, *last_near
        )
        part_last = plus_all(last_own, last_near)
        half = 12 * LANES
        last_one, one_in = grid.hop_one(part_last[:, :half])
        last_two, two_in = grid.hop_one(part_last[:, half:])
        inner_sum, inner_in = grid.hop_three(inner_sum, inner_in)
        middle_sum, middle_in = grid.hop_two(middle_sum, middle_in)
        total_outer = grid.hop_end(outer_sum, outer_in)
        last_one, one_in = grid.hop_two(last_one, one_in)
        last_two, two_in = grid.hop_two(last_two, two_in)
        middle_sum, middle_in = grid.hop_three(middle_sum, middle_in)
        total_inner = grid.hop_end(inner_sum, inner_in)
        last_one, one_in = grid.hop_three(last_one, one_in)
        last_two, two_in = grid.hop_three(last_two, two_in)
        total_middle = grid.hop_end(middle_sum, middle_in)
        total_last = jnp.concatenate(
            [grid.hop_end(last_one, one_in), grid.hop_end(last_two, two_in)], axis=1
        )
        total_qkv = total_last[:, : grad_w_qkv.shape[1]]
        mine = total_last[:kinds, grad_w_qkv.shape[1] :]
    else:
        part_middle = jnp.concatenate(
            [scattered(jnp.concatenate(middle, axis=1)), part_kv], axis=1
        )
        total_outer = grid.seq_sum(part_outer)
        total_inner = grid.seq_sum(part_inner)
        total_middle = grid.seq_sum(part_middle)
        total_qkv = grid.seq_sum(scattered(grad_w_qkv))
        mine = pick(lax.psum(packed, AXES), grid.group, 0)
    total_cross_out, total_cross_q, total_self_out, total_cross_kv = jnp.split(
        total_middle, (width, 2 * width, 3 * width), axis=1
    )

    grad_encoded = grad_encoded[:, :frames]
    grad_hidden_in, hidden_out = leaving[:, :rows], leaving[:, rows:]
    return (
        hidden_out,
        grad_hidden_in,
        grad_encoded,
        mine[:norms],
        mine[norms : 2 * norms],
        mine[2 * norms : 2 * norms + bias_count],
        total_qkv,
        total_self_out,
        total_cross_q,
        total_cross_kv,
        total_cross_out,
        total_inner,
        mine[2 * norms + bias_count :].reshape(-1),
        total_outer,
    )


def solution(mesh):
    rows = P("fsdp", "seq", None)
    wide = P(None, "fsdp")
    tall = P("fsdp", None)
    in_specs = (rows,) * 3 + (wide,) * 3 + (tall,) * 6 + (P("fsdp"), tall)
    out_specs = (rows,) * 3 + (wide,) * 3 + (tall,) * 6 + (P("fsdp"), tall)
    return jax.shard_map(
        functools.partial(local, dict(mesh.shape)),
        mesh=mesh,
        in_specs=in_specs,
        out_specs=out_specs,
        check_vma=False,
    )
```

time: 1020 us -> 617 us (0.60)
  waiting for transfers between devices: 568 us -> 181 us
  starting transfers between devices: 133 us -> 77.7 us
  local copies, waits for them, and re-layouts: 31.7 us -> 60.8 us
  other arithmetic: 39.4 us -> 55.9 us
  matrix products: 126 us -> 114 us
    reduce_scatter x7 -> x3, waiting for transfers between devices: 288 us -> 1.31 us  [scattered(): return lax.psum_scatter(member, 'fsdp', scatter_dimension=0, tiled=True)]
    all_gather x7 -> x2, waiting for transfers between devices: 115 us -> 0.01 us  [gathered(): joined = lax.all_gather(joined, 'fsdp', axis=0, tiled=True)]
    ppermute x21 -> x33, waiting for transfers between devices: 91.4 us -> 166 us  [the longest x18 87.8 us: flip(): lax.ppermute(values, 'fsdp', [(f, f ^ bits) for f in range(self.fsdp)])]
    ppermute x18 -> x6, starting transfers between devices: 83.3 us -> 18.5 us  [turn(): return lax.ppermute(values, AXES, pairs)]
    ppermute x18 -> x6, waiting for transfers between devices: 45.3 us -> 14.1 us  [turn(): return lax.ppermute(values, AXES, pairs)]
    psum x1 -> x0, waiting for transfers between devices: 23.6 us -> none  [local(): packed = lax.psum(packed, AXES)]
    dot_general x7, matrix products: 30.1 us -> 51.4 us  [product_back(): lax.dot_general(incoming, weight, (((1,), (1,)), ((), ())), preferred_ele...]
    dot_general x7, matrix products: 49.9 us -> 32.7 us  [weight_grad(): lax.dot_general(operand, incoming, (((0,), (0,)), ((), ())), preferred_el...]
  transfers between devices with their start and end apart: 54 -> 46, of which waited for: 20 -> 18; matrix products, arithmetic and copies ran while one was open for 15% -> 30% of each run, Pallas kernels for 4% -> 17%
where the time goes in v3:
time: 617 us; the launch traced here: 609 us
  waiting for transfers between devices  181 us (29%)
  matrix products  114 us (18%)
  Pallas kernels  103 us (17%)
  starting transfers between devices  77.7 us (13%)
  local copies, waits for them, and re-layouts  60.8 us (10%)
  other arithmetic  55.9 us (9%)
  between operations  15.8 us (3%)
    ppermute x18, waiting for transfers between devices, flip(): lax.ppermute(values, 'fsdp', [(f, f ^ bits) for f in range(self.fsdp)])  87.8 us
    ppermute x15, waiting for transfers between devices, chain(): return lax.ppermute(values, AXES, pairs)  78.1 us
    pallas_call x3, Pallas kernels, attend_back(): pl.pallas_call(functools.partial(backward_kernel, chunk, valid, causal),...  57.6 us
    dot_general x7, matrix products, product_back(): lax.dot_general(incoming, weight, (((1,), (1,)), ((), ())), preferred_ele...  51.4 us
    pallas_call x2, Pallas kernels, attend(): pl.pallas_call(functools.partial(forward_kernel, chunk, valid, causal), g...  39 us
    unnamed x170, local copies, waits for them, and re-layouts  36.9 us
    dot_general x7, matrix products, weight_grad(): lax.dot_general(operand, incoming, (((0,), (0,)), ((), ())), preferred_el...  32.7 us
    ppermute x15, starting transfers between devices, chain(): return lax.ppermute(values, AXES, pairs)  30 us
  transfers between devices with their start and end apart: 46, of which 18 were waited for; matrix products, arithmetic and copies ran while one was open for 30% of the time, Pallas kernels for 17%

profile of v3, /device:TPU:0, one launch (start us, length us, event | category | flops | bytes accessed | tf_op | source)
XLA Modules:
  0.0 608.6 jit_solution(9891757094057499213)
XLA Ops:
  17.0 5.6 collective-permute-start.2
  27.1 25.7 %collective-permute-done.1 = bf16[128,3200]{1,0:T(8,128)(2,1)} collective-permute-done((bf16[128,3200]{1,0:T(8,128)(2,1)}, bf16[128,3200]{1,0:T(8,128)(2,1)}, u32[]{:S(2)}, u32[]{:S(2)}) %collective-permute-start.1) | collective-permute-done | bytes 819232 | tf_op jit(solution)/shard_map/ppermute | solution.py:325
  57.2 4.4 collective-permute-start.6
  66.8 17.6 %collective-permute-done.5 = bf16[64,3200]{1,0:T(8,128)(2,1)S(1)} collective-permute-done((bf16[64,3200]{1,0:T(8,128)(2,1)S(1)}, bf16[64,3200]{1,0:T(8,128)(2,1)S(1)}, u32[]{:S(2)}, u32[]{:S(2)}) %collective-permute-start.5) | collective-permute-done | bytes 409632 | tf_op jit(solution)/shard_map/ppermute | solution.py:325
  84.8 10.9 %collective-permute-done.6.refs_2_ = bf16[487,1024]{1,0:T(8,128)(2,1)S(1)} collective-permute-done((bf16[487,1024]{1,0:T(8,128)(2,1)S(1)}, bf16[487,1024]{1,0:T(8,128)(2,1)S(1)}, u32[]{:S(2)}, u32[]{:S(2)}) %collective-permute-start.6) | collective-permute-done | bytes 997408 | tf_op jit(solution)/shard_map/ppermute | solution.py:294
  113.4 8.7 %attend_causal.1 = (bf16[448,1024]{1,0:T(8,128)(2,1)S(1)}, f32[8,1,896]{2,1,0:T(1,128)S(1)}) custom-call(bf16[448,3072]{1,0:T(8,128)(2,1)S(1)} %multiply_convert_fusion.1.refs_0_.refs_1_.refs_2_, bf16[448,3072]{1,0:T(8,128)(2,1)S(1)} %multiply_convert_fusion.1.refs_0_.refs_1_.refs_2_, bf16[448,3072]{1,0:T(8,128)(2,1)S(1)} %multiply_convert_fusion.1.refs_0_.refs_1_.refs_2_, ...), custom_call_target="tpu_custom_call" | custom-call | flops 3288334336 | bytes 3670016 | tf_op jit(solution)/shard_map/attend_causal/pallas_call | solution.py:162
  137.0 7.1 %add_convert_fusion.refs_1_.refs_2_ = bf16[1536,2048]{1,0:T(8,128)(2,1)S(1)} fusion(bf16[1536,1024]{1,0:T(8,128)(2,1)S(1)} %copy-done.12, f32[2048]{0:T(1024)S(1)} %concatenate.64, bf16[1024,4096]{1,0:T(8,128)(2,1)S(1)} %copy-done.71), kind=kOutput, calls=%fused_computation | convolution fusion | flops 6448742400 | bytes 13639680 | tf_op jit(solution)/shard_map/dot_general | solution.py:230
  144.2 30.2 %attend_cross.1 = (bf16[448,1024]{1,0:T(8,128)(2,1)S(1)}, f32[8,1,896]{2,1,0:T(1,128)S(1)}) custom-call(bf16[448,1024]{1,0:T(8,128)(2,1)S(1)} %multiply_convert_fusion.2.refs_0_, bf16[1536,2048]{1,0:T(8,128)(2,1)S(1)} %add_convert_fusion.refs_1_.refs_2_, bf16[1536,2048]{1,0:T(8,128)(2,1)S(1)} %add_convert_fusion.refs_1_.refs_2_), custom_call_target="tpu_custom_call" | custom-call | flops 11274289152 | bytes 8126464 | tf_op jit(solution)/shard_map/attend_cross/pallas_call | solution.py:162
  183.9 7.0 %multiply_convert_fusion = (bf16[448,4096]{1,0:T(8,128)(2,1)S(1)}, f32[448,4096]{1,0:T(8,128)}) fusion(f32[4096]{0:T(1024)S(1)} %convert.79, bf16[1024,5120]{1,0:T(8,128)(2,1)S(1)} %copy-done.70, f32[448,1024]{1,0:T(8,128)S(1)} %get-tuple-element.222, f32[1024]{0:T(1024)S(1)} %bitcast.187, f32[1024]{0:T(1024)S(1)} %bitcast.177, f32[448]{0:T(512)S(1)} %add_rsqrt_fusion, ...), kind=kOutput, calls=%fused_computation.13 | convolution fusion | flops 3771400192 | bytes 21262336 | tf_op jit(solution)/shard_map/dot_general | solution.py:230
  196.9 6.8 %convolution_convert_fusion.1 = bf16[4096,1024]{1,0:T(8,128)(2,1)} fusion(bf16[448,4096]{1,0:T(8,128)(2,1)S(1)} %get-tuple-element.139, bf16[448,1024]{1,0:T(8,128)(2,1)S(1)} %place.3), kind=kOutput, calls=%fused_computation.3 | convolution fusion | flops 3762290688 | bytes 12976128 | tf_op jit(solution)/shard_map/dot_general | solution.py:240
  208.7 10.8 %fusion.73 = (bf16[448,4096]{1,0:T(8,128)(2,1)S(1)}, bf16[4096]{0:T(1024)(128)(2,1)S(1)}) fusion(f32[448,4096]{1,0:T(8,128)} %get-tuple-element.224, f32[4096]{0:T(1024)S(1)} %convert.79, bf16[448,1024]{1,0:T(8,128)(2,1)S(1)} %place.3, bf16[4096,1024]{1,0:T(8,128)(2,1)S(1)} %assemble.3), kind=kOutput, calls=%fused_computation.190 | convolution fusion | flops 3780112384 | bytes 20340736 | tf_op jit(solution)/shard_map/dot_general | solution.py:234
  221.5 7.3 %convolution_convert_fusion = bf16[1024,4096]{1,0:T(8,128)(2,1)} fusion(bf16[448,4096]{1,0:T(8,128)(2,1)S(1)} %get-tuple-element.115, f32[448,1024]{1,0:T(8,128)S(1)} %copy-done.33, f32[1024]{0:T(1024)S(1)} %bitcast.188, f32[1024]{0:T(1024)S(1)} %bitcast.178, f32[448]{0:T(512)S(1)} %add_rsqrt_fusion, f32[448]{0:T(512)S(1)} %broadcast_multiply_fusion.6), kind=kOutput, calls=%fused_computation.2 | convolution fusion | flops 3764584448 | bytes 13905408 | tf_op jit(solution)/shard_map/dot_general | solution.py:240
  228.8 10.0 %multiply_reduce_fusion = (bf16[1024]{0:T(1024)(128)(2,1)S(1)}, f32[448]{0:T(512)S(1)}, f32[448]{0:T(512)S(1)}, bf16[1024]{0:T(1024)(128)(2,1)S(1)}, f32[448,1024]{1,0:T(8,128)S(1)}) fusion(f32[448,1024]{1,0:T(8,128)} %copy-done.32, f32[448]{0:T(512)S(1)} %add_rsqrt_fusion, f32[448]{0:T(512)S(1)} %broadcast_multiply_fusion.6, f32[1024]{0:T(1024)S(1)} %bitcast.179, ...), kind=kOutput, calls=%fused_computation.73 | convolution fusion | flops 3762222080 | bytes 15744000 | tf_op jit(solution)/shard_map/dot_general | solution.py:234
  249.9 21.8 %attend_cross_back.2 = (bf16[448,1024]{1,0:T(8,128)(2,1)S(1)}, bf16[1536,2048]{1,0:T(8,128)(2,1)S(1)}) custom-call(bf16[448,1024]{1,0:T(8,128)(2,1)S(1)} %copy-done.23, bf16[1536,2048]{1,0:T(8,128)(2,1)S(1)} %copy-done.26, bf16[1536,2048]{1,0:T(8,128)(2,1)S(1)} %copy-done.26, bf16[448,1024]{1,0:T(8,128)(2,1)S(1)} %copy-done.20, ...), custom_call_target="tpu_custom_call" | custom-call | flops 14092861440 | bytes 8126464 | tf_op jit(solution)/shard_map/attend_cross_back/pallas_call | solution.py:211
  287.4 21.4 %attend_cross_back.3 = (bf16[448,1024]{1,0:T(8,128)(2,1)S(1)}, bf16[1536,2048]{1,0:T(8,128)(2,1)S(1)}) custom-call(bf16[448,1024]{1,0:T(8,128)(2,1)S(1)} %copy-done.24, bf16[1536,2048]{1,0:T(8,128)(2,1)S(1)} %copy-done.27, bf16[1536,2048]{1,0:T(8,128)(2,1)S(1)} %copy-done.27, ...), custom_call_target="tpu_custom_call", output_to_operand_aliasing={{0}: (6, {}), {1}: (7, {})} | custom-call | flops 14092861440 | bytes 8126464 | tf_op jit(solution)/shard_map/attend_cross_back/pallas_call | solution.py:211
  310.9 12.0 %convolution_convert_fusion.4 = bf16[1536,1024]{1,0:T(8,128)(2,1)} fusion(bf16[1536,2048]{1,0:T(8,128)(2,1)S(1)} %get-tuple-element.127, bf16[1024,4096]{1,0:T(8,128)(2,1)} %all-gather.3.cloned.1.call-done), kind=kOutput, calls=%fused_computation.21 | convolution fusion | flops 6444023808 | bytes 13631488 | tf_op jit(solution)/shard_map/dot_general | solution.py:234
  323.0 8.8 %convolution_convert_fusion.3 = bf16[1024,2048]{1,0:T(8,128)(2,1)} fusion(bf16[1536,1024]{1,0:T(8,128)(2,1)S(1)} %copy-done.13, bf16[1536,2048]{1,0:T(8,128)(2,1)S(1)} %get-tuple-element.127), kind=kOutput, calls=%fused_computation.20 | convolution fusion | flops 6444548096 | bytes 13631488 | tf_op jit(solution)/shard_map/dot_general | solution.py:240
  348.4 5.4 all-to-all-start.1
  363.9 14.5 %attend_causal_back.1 = bf16[448,3072]{1,0:T(8,128)(2,1)S(1)} custom-call(bf16[448,3072]{1,0:T(8,128)(2,1)S(1)} %copy-done.15, bf16[448,3072]{1,0:T(8,128)(2,1)S(1)} %copy-done.15, bf16[448,3072]{1,0:T(8,128)(2,1)S(1)} %copy-done.15, bf16[448,1024]{1,0:T(8,128)(2,1)S(1)} %copy-done.18, bf16[448,1024]{1,0:T(8,128)(2,1)S(1)} %fusion.51.refs_4_, ...), custom_call_target="tpu_custom_call" | custom-call | flops 8220835840 | bytes 7340032 | tf_op jit(solution)/shard_map/attend_causal_back/pallas_call | solution.py:211
  380.0 8.3 %fusion.32 = (f32[448]{0:T(512)S(1)}, bf16[1024]{0:T(1024)(128)(2,1)S(1)}, f32[448]{0:T(512)S(1)}, bf16[1024]{0:T(1024)(128)(2,1)S(1)}, f32[448,1024]{1,0:T(8,128)}) fusion(bf16[448,1024]{1,0:T(8,128)(2,1)S(1)} %copy-done.2, f32[1024]{0:T(1024)S(1)} %bitcast.167, f32[448]{0:T(512)S(1)} %copy-done.60, f32[448]{0:T(512)S(1)} %copy-done.56, ...), kind=kOutput, calls=%fused_computation.64 | convolution fusion | flops 2823156736 | bytes 11811840 | tf_op jit(solution)/shard_map/dot_general | solution.py:234
  416.8 5.1 collective-permute-done.22
  425.6 13.9 %collective-permute-done.24 = bf16[128,3072]{1,0:T(8,128)(2,1)S(1)} collective-permute-done((bf16[128,3072]{1,0:T(8,128)(2,1)S(1)}, bf16[128,3072]{1,0:T(8,128)(2,1)S(1)}, u32[]{:S(2)}, u32[]{:S(2)}) %collective-permute-start.24) | collective-permute-done | bytes 786464 | tf_op jit(solution)/shard_map/ppermute | solution.py:325
  442.5 5.8 collective-permute-start.25
  462.3 5.4 all-to-all-start
  470.4 7.5 %collective-permute-done.29 = bf16[128,3200]{1,0:T(8,128)(2,1)} collective-permute-done((bf16[128,3200]{1,0:T(8,128)(2,1)}, bf16[128,3200]{1,0:T(8,128)(2,1)}, u32[]{:S(2)}, u32[]{:S(2)}) %collective-permute-start.29) | collective-permute-done | bytes 819232 | tf_op jit(solution)/shard_map/ppermute | solution.py:325
  477.9 15.4 %collective-permute-done.28 = bf16[128,3200]{1,0:T(8,128)(2,1)} collective-permute-done((bf16[128,3200]{1,0:T(8,128)(2,1)}, bf16[128,3200]{1,0:T(8,128)(2,1)}, u32[]{:S(2)}, u32[]{:S(2)}) %collective-permute-start.28) | collective-permute-done | bytes 819232 | tf_op jit(solution)/shard_map/ppermute | solution.py:325
  508.0 6.7 %collective-permute-done.33 = bf16[128,1536]{1,0:T(8,128)(2,1)S(1)} collective-permute-done((bf16[128,1536]{1,0:T(8,128)(2,1)S(1)}, bf16[128,1536]{1,0:T(8,128)(2,1)S(1)}, u32[]{:S(2)}, u32[]{:S(2)}) %collective-permute-start.33) | collective-permute-done | bytes 393248 | tf_op jit(solution)/shard_map/ppermute | solution.py:322
  515.4 7.1 %collective-permute-done.30 = bf16[128,1664]{1,0:T(8,128)(2,1)S(1)} collective-permute-done((bf16[128,1664]{1,0:T(8,128)(2,1)S(1)}, bf16[128,1664]{1,0:T(8,128)(2,1)S(1)}, u32[]{:S(2)}, u32[]{:S(2)}) %collective-permute-start.30) | collective-permute-done | bytes 426016 | tf_op jit(solution)/shard_map/ppermute | solution.py:322
  526.2 11.1 %collective-permute-done.38 = bf16[128,4096]{1,0:T(8,128)(2,1)S(1)} collective-permute-done((bf16[128,4096]{1,0:T(8,128)(2,1)S(1)}, bf16[128,4096]{1,0:T(8,128)(2,1)S(1)}, u32[]{:S(2)}, u32[]{:S(2)}) %collective-permute-start.38) | collective-permute-done | bytes 1048608 | tf_op jit(solution)/shard_map/ppermute | solution.py:322
  538.7 23.9 %collective-permute-done.35 = bf16[128,1536]{1,0:T(8,128)(2,1)S(1)} collective-permute-done((bf16[128,1536]{1,0:T(8,128)(2,1)S(1)}, bf16[128,1536]{1,0:T(8,128)(2,1)S(1)}, u32[]{:S(2)}, u32[]{:S(2)}) %collective-permute-start.35) | collective-permute-done | bytes 393248 | tf_op jit(solution)/shard_map/ppermute | solution.py:322
  564.3 9.4 %collective-permute-done.32 = bf16[128,1664]{1,0:T(8,128)(2,1)S(1)} collective-permute-done((bf16[128,1664]{1,0:T(8,128)(2,1)S(1)}, bf16[128,1664]{1,0:T(8,128)(2,1)S(1)}, u32[]{:S(2)}, u32[]{:S(2)}) %collective-permute-start.32) | collective-permute-done | bytes 426016 | tf_op jit(solution)/shard_map/ppermute | solution.py:322
  579.4 19.9 %collective-permute-done.37 = bf16[128,5120]{1,0:T(8,128)(2,1)S(1)} collective-permute-done((bf16[128,5120]{1,0:T(8,128)(2,1)S(1)}, bf16[128,5120]{1,0:T(8,128)(2,1)S(1)}, u32[]{:S(2)}, u32[]{:S(2)}) %collective-permute-start.37) | collective-permute-done | bytes 1310752 | tf_op jit(solution)/shard_map/ppermute | solution.py:322
  (362 shorter events, 217.3 us)
Async XLA Ops:
  7.2 116.5 %all-gather.3.cloned.1.call-start = ((), (), s32[]{:S(2)}) async-start(), calls=%async_computation.5 | async-start | bytes 9437184 | tf_op jit(solution)/shard_map/all_gather | solution.py:493
  9.6 168.5 %all-gather.5.cloned.1.call-start = ((), (), s32[]{:S(2)}) async-start(), calls=%async_computation.6 | async-start | bytes 11796480 | tf_op jit(solution)/shard_map/all_gather | solution.py:493
  11.9 263.7 %reduce-scatter.4.cloned.1.call-start = ((), (), s32[]{:S(2)}) async-start(), calls=%async_computation.7 | async-start | bytes 9437184 | tf_op jit(solution)/shard_map/reduce_scatter | solution.py:497
  15.7 37.1 %collective-permute-start.3 = (bf16[487,1024]{1,0:T(8,128)(2,1)}, bf16[487,1024]{1,0:T(8,128)(2,1)S(1)}, u32[]{:S(2)}, u32[]{:S(2)}) collective-permute-start(bf16[487,1024]{1,0:T(8,128)(2,1)} %get-tuple-element.182), channel_id=1, source_target_pairs={{1,0},{2,1},{3,2},{4,7},{6,5},{7,6},{9,8},{10,9},{11,10},{12,15},{... | collective-permute-start | bytes 2992136 | tf_op jit(solution)/shard_map/ppermute | solution.py:294
  17.0 38.9 %collective-permute-start.2 = (bf16[487,1024]{1,0:T(8,128)(2,1)}, bf16[487,1024]{1,0:T(8,128)(2,1)}, u32[]{:S(2)}, u32[]{:S(2)}) collective-permute-start(bf16[487,1024]{1,0:T(8,128)(2,1)} %get-tuple-element.183), channel_id=1, source_target_pairs={{0,1},{1,2},{3,0},{4,5},{5,6},{6,7},{8,9},{9,10},{11,8},{12,13},{1... | collective-permute-start | bytes 2992136 | tf_op jit(solution)/shard_map/ppermute | solution.py:294
  23.6 29.2 %collective-permute-start.1 = (bf16[128,3200]{1,0:T(8,128)(2,1)}, bf16[128,3200]{1,0:T(8,128)(2,1)}, u32[]{:S(2)}, u32[]{:S(2)}) collective-permute-start(bf16[128,3200]{1,0:T(8,128)(2,1)} %get-tuple-element.199), channel_id=1, source_target_pairs={{0,16},{4,20},{8,24},{12,28},{16,0},{20,4},{24,8},{28,12},{1,17},{... | collective-permute-start | bytes 2457608 | tf_op jit(solution)/shard_map/ppermute | solution.py:325
  57.2 38.5 %collective-permute-start.6 = (bf16[487,1024]{1,0:T(8,128)(2,1)S(1)}, bf16[487,1024]{1,0:T(8,128)(2,1)S(1)}, u32[]{:S(2)}, u32[]{:S(2)}) collective-permute-start(bf16[487,1024]{1,0:T(8,128)(2,1)S(1)} %dynamic-slice_bitcast_fusion.8), channel_id=1, source_target_pairs={{0,2},{2,0},{3,1},{4,6},{5,7},{7,5},{8,10},{10,8},{11,9},{12,14},{... | collective-permute-start | bytes 2992136 | tf_op jit(solution)/shard_map/ppermute | solution.py:294
  103.6 70.9 %collective-permute-start.9 = (bf16[512,1024]{1,0:T(8,128)(2,1)}, bf16[512,1024]{1,0:T(8,128)(2,1)}, u32[]{:S(2)}, u32[]{:S(2)}) collective-permute-start(bf16[512,1024]{1,0:T(8,128)(2,1)} %param.27), channel_id=1, source_target_pairs={{0,16},{4,20},{8,24},{12,28},{16,0},{20,4},{24,8},{28,12},{1,17},{... | collective-permute-start | bytes 3145736 | tf_op jit(solution)/shard_map/ppermute | solution.py:325
  105.1 69.4 %collective-permute-start.8 = (bf16[512,1024]{1,0:T(8,128)(2,1)}, bf16[512,1024]{1,0:T(8,128)(2,1)}, u32[]{:S(2)}, u32[]{:S(2)}) collective-permute-start(bf16[512,1024]{1,0:T(8,128)(2,1)} %param.27), channel_id=1, source_target_pairs={{0,8},{4,12},{8,0},{12,4},{16,24},{20,28},{24,16},{28,20},{1,9},{5... | collective-permute-start | bytes 3145736 | tf_op jit(solution)/shard_map/ppermute | solution.py:325
  129.7 44.8 %collective-permute-start.12 = (bf16[112,1024]{1,0:T(8,128)(2,1)S(1)}, bf16[112,1024]{1,0:T(8,128)(2,1)S(1)}, u32[]{:S(2)}, u32[]{:S(2)}) collective-permute-start(bf16[112,1024]{1,0:T(8,128)(2,1)S(1)} %get-tuple-element.200), channel_id=1, source_target_pairs={{1,0},{2,1},{3,2},{4,7},{6,5},{7,6},{9,8},{10,9},{11,10},{12,15},{... | collective-permute-start | bytes 688136 | tf_op jit(solution)/shard_map/ppermute | solution.py:294
  131.0 43.5 %collective-permute-start.11 = (bf16[112,1024]{1,0:T(8,128)(2,1)S(1)}, bf16[112,1024]{1,0:T(8,128)(2,1)S(1)}, u32[]{:S(2)}, u32[]{:S(2)}) collective-permute-start(bf16[112,1024]{1,0:T(8,128)(2,1)S(1)} %get-tuple-element.201), channel_id=1, source_target_pairs={{0,2},{2,0},{3,1},{4,6},{5,7},{7,5},{8,10},{10,8},{11,9},{12,14},{... | collective-permute-start | bytes 688136 | tf_op jit(solution)/shard_map/ppermute | solution.py:294
  132.9 41.6 %collective-permute-start.10 = (bf16[112,1024]{1,0:T(8,128)(2,1)S(1)}, bf16[112,1024]{1,0:T(8,128)(2,1)S(1)}, u32[]{:S(2)}, u32[]{:S(2)}) collective-permute-start(bf16[112,1024]{1,0:T(8,128)(2,1)S(1)} %get-tuple-element.202), channel_id=1, source_target_pairs={{0,1},{1,2},{3,0},{4,5},{5,6},{6,7},{8,9},{9,10},{11,8},{12,13},{1... | collective-permute-start | bytes 688136 | tf_op jit(solution)/shard_map/ppermute | solution.py:294
  204.2 175.8 %reduce-scatter.6.cloned.1.call-start = ((), (), s32[]{:S(2)}) async-start(), calls=%async_computation.8 | async-start | bytes 9437184 | tf_op jit(solution)/shard_map/reduce_scatter | solution.py:497
  275.6 33.1 %collective-permute-start.16 = (bf16[512,1024]{1,0:T(8,128)(2,1)}, bf16[512,1024]{1,0:T(8,128)(2,1)S(1)}, u32[]{:S(2)}, u32[]{:S(2)}) collective-permute-start(bf16[512,1024]{1,0:T(8,128)(2,1)} %reduce-scatter.4.cloned.1.call-done), channel_id=1, source_target_pairs={{0,1},{3,2},{4,5},{7,6},{8,9},{11,10},{12,13},{15,14},{16,17},{19,... | collective-permute-start | bytes 3145736 | tf_op jit(solution)/shard_map/ppermute | solution.py:322
  348.1 32.0 %collective-permute-start.18 = (bf16[4,128,3072]{2,1,0:T(8,128)(2,1)}, bf16[4,128,3072]{2,1,0:T(8,128)(2,1)}, u32[]{:S(2)}, u32[]{:S(2)}) collective-permute-start(bf16[4,128,3072]{2,1,0:T(8,128)(2,1)} %pad_maximum_fusion.4), channel_id=1, source_target_pairs={{0,4},{4,0},{8,12},{12,8},{16,20},{20,16},{24,28},{28,24},{1,5},{5... | collective-permute-start | bytes 9437192 | tf_op jit(solution)/shard_map/ppermute | solution.py:325
  348.4 110.7 %all-to-all-start.1 = ((bf16[4,384,1024]{2,1,0:T(8,128)(2,1)}), bf16[4,384,1024]{2,1,0:T(8,128)(2,1)}, u32[]{:S(2)}, u32[]{:S(2)}) async-start(bf16[4,384,1024]{2,1,0:T(8,128)(2,1)} %bitcast.158), calls=%async_computation.4 | async-start | bytes 6291456 | tf_op jit(solution)/shard_map/all_to_all | solution.py:313
  353.9 86.2 %reduce-scatter.8.cloned.1.call-start = ((), (), s32[]{:S(2)}) async-start(), calls=%async_computation.9 | async-start | bytes 4718592 | tf_op jit(solution)/shard_map/reduce_scatter | solution.py:497
  359.4 88.9 %collective-permute-start.21 = (bf16[512,1024]{1,0:T(8,128)(2,1)}, bf16[512,1024]{1,0:T(8,128)(2,1)}, u32[]{:S(2)}, u32[]{:S(2)}) collective-permute-start(bf16[512,1024]{1,0:T(8,128)(2,1)} %add_convert_fusion.7), channel_id=1, source_target_pairs={{1,0},{2,3},{5,4},{6,7},{9,8},{10,11},{13,12},{14,15},{17,16},{18,... | collective-permute-start | bytes 3145736 | tf_op jit(solution)/shard_map/ppermute | solution.py:322
  394.1 27.9 %collective-permute-start.22 = (bf16[128,3072]{1,0:T(8,128)(2,1)S(1)}, bf16[128,3072]{1,0:T(8,128)(2,1)S(1)}, u32[]{:S(2)}, u32[]{:S(2)}) collective-permute-start(bf16[128,3072]{1,0:T(8,128)(2,1)S(1)} %get-tuple-element.179), channel_id=1, source_target_pairs={{0,8},{4,12},{8,0},{12,4},{16,24},{20,28},{24,16},{28,20},{1,9},{5... | collective-permute-start | bytes 2359304 | tf_op jit(solution)/shard_map/ppermute | solution.py:325
  395.4 44.1 %collective-permute-start.24 = (bf16[128,3072]{1,0:T(8,128)(2,1)S(1)}, bf16[128,3072]{1,0:T(8,128)(2,1)S(1)}, u32[]{:S(2)}, u32[]{:S(2)}) collective-permute-start(bf16[128,3072]{1,0:T(8,128)(2,1)S(1)} %get-tuple-element.180), channel_id=1, source_target_pairs={{0,24},{4,28},{8,16},{12,20},{16,8},{20,12},{24,0},{28,4},{1,25},{... | collective-permute-start | bytes 2359304 | tf_op jit(solution)/shard_map/ppermute | solution.py:325
  396.9 42.6 %collective-permute-start.23 = (bf16[128,3072]{1,0:T(8,128)(2,1)S(1)}, bf16[128,3072]{1,0:T(8,128)(2,1)S(1)}, u32[]{:S(2)}, u32[]{:S(2)}) collective-permute-start(bf16[128,3072]{1,0:T(8,128)(2,1)S(1)} %get-tuple-element.181), channel_id=1, source_target_pairs={{0,16},{4,20},{8,24},{12,28},{16,0},{20,4},{24,8},{28,12},{1,17},{... | collective-permute-start | bytes 2359304 | tf_op jit(solution)/shard_map/ppermute | solution.py:325
  404.4 43.9 %collective-permute-start.19 = (bf16[4,128,3200]{2,1,0:T(8,128)(2,1)}, bf16[4,128,3200]{2,1,0:T(8,128)(2,1)}, u32[]{:S(2)}, u32[]{:S(2)}) collective-permute-start(bf16[4,128,3200]{2,1,0:T(8,128)(2,1)} %pad_maximum_fusion.2), channel_id=1, source_target_pairs={{0,4},{4,0},{8,12},{12,8},{16,20},{20,16},{24,28},{28,24},{1,5},{5... | collective-permute-start | bytes 9830408 | tf_op jit(solution)/shard_map/ppermute | solution.py:325
  442.5 50.8 %collective-permute-start.25 = (bf16[128,5120]{1,0:T(8,128)(2,1)}, bf16[128,5120]{1,0:T(8,128)(2,1)}, u32[]{:S(2)}, u32[]{:S(2)}) collective-permute-start(bf16[128,5120]{1,0:T(8,128)(2,1)} %pad_maximum_fusion.8), channel_id=1, source_target_pairs={{0,1},{3,2},{4,5},{7,6},{8,9},{11,10},{12,13},{15,14},{16,17},{19,... | collective-permute-start | bytes 3932168 | tf_op jit(solution)/shard_map/ppermute | solution.py:322
  449.6 43.7 %collective-permute-start.26 = (bf16[128,4096]{1,0:T(8,128)(2,1)}, bf16[128,4096]{1,0:T(8,128)(2,1)}, u32[]{:S(2)}, u32[]{:S(2)}) collective-permute-start(bf16[128,4096]{1,0:T(8,128)(2,1)} %add_convert_fusion.6), channel_id=1, source_target_pairs={{1,2},{2,1},{5,6},{6,5},{9,10},{10,9},{13,14},{14,13},{17,18},{18,... | collective-permute-start | bytes 3145736 | tf_op jit(solution)/shard_map/ppermute | solution.py:322
  457.0 36.3 %collective-permute-start.28 = (bf16[128,3200]{1,0:T(8,128)(2,1)}, bf16[128,3200]{1,0:T(8,128)(2,1)}, u32[]{:S(2)}, u32[]{:S(2)}) collective-permute-start(bf16[128,3200]{1,0:T(8,128)(2,1)} %get-tuple-element.177), channel_id=1, source_target_pairs={{0,16},{4,20},{8,24},{12,28},{16,0},{20,4},{24,8},{28,12},{1,17},{... | collective-permute-start | bytes 2457608 | tf_op jit(solution)/shard_map/ppermute | solution.py:325
  459.0 34.3 %collective-permute-start.27 = (bf16[128,3200]{1,0:T(8,128)(2,1)}, bf16[128,3200]{1,0:T(8,128)(2,1)}, u32[]{:S(2)}, u32[]{:S(2)}) collective-permute-start(bf16[128,3200]{1,0:T(8,128)(2,1)} %get-tuple-element.178), channel_id=1, source_target_pairs={{0,8},{4,12},{8,0},{12,4},{16,24},{20,28},{24,16},{28,20},{1,9},{5... | collective-permute-start | bytes 2457608 | tf_op jit(solution)/shard_map/ppermute | solution.py:325
  462.3 114.5 %all-to-all-start = ((bf16[4,224,1024]{2,1,0:T(8,128)(2,1)}), bf16[4,224,1024]{2,1,0:T(8,128)(2,1)}, u32[]{:S(2)}, u32[]{:S(2)}) async-start(bf16[4,224,1024]{2,1,0:T(8,128)(2,1)} %pad_maximum_fusion.5), calls=%async_computation.2 | async-start | bytes 3670016 | tf_op jit(solution)/shard_map/all_to_all | solution.py:313
  504.3 33.0 %collective-permute-start.38 = (bf16[128,4096]{1,0:T(8,128)(2,1)S(1)}, bf16[128,4096]{1,0:T(8,128)(2,1)S(1)}, u32[]{:S(2)}, u32[]{:S(2)}) collective-permute-start(bf16[128,4096]{1,0:T(8,128)(2,1)S(1)} %add_convert_fusion.5), channel_id=1, source_target_pairs={{1,0},{2,3},{5,4},{6,7},{9,8},{10,11},{13,12},{14,15},{17,16},{18,... | collective-permute-start | bytes 3145736 | tf_op jit(solution)/shard_map/ppermute | solution.py:322
  507.2 55.5 %collective-permute-start.36 = (bf16[128,5120]{1,0:T(8,128)(2,1)S(1)}, bf16[128,5120]{1,0:T(8,128)(2,1)S(1)}, u32[]{:S(2)}, u32[]{:S(2)}) collective-permute-start(bf16[128,5120]{1,0:T(8,128)(2,1)S(1)} %add_convert_fusion.4), channel_id=1, source_target_pairs={{1,2},{2,1},{5,6},{6,5},{9,10},{10,9},{13,14},{14,13},{17,18},{18,... | collective-permute-start | bytes 3932168 | tf_op jit(solution)/shard_map/ppermute | solution.py:322
  523.4 39.2 %collective-permute-start.35 = (bf16[128,1536]{1,0:T(8,128)(2,1)S(1)}, bf16[128,1536]{1,0:T(8,128)(2,1)S(1)}, u32[]{:S(2)}, u32[]{:S(2)}) collective-permute-start(bf16[128,1536]{1,0:T(8,128)(2,1)S(1)} %add_convert_fusion.14), channel_id=1, source_target_pairs={{1,0},{2,3},{5,4},{6,7},{9,8},{10,11},{13,12},{14,15},{17,16},{18,... | collective-permute-start | bytes 1179656 | tf_op jit(solution)/shard_map/ppermute | solution.py:322
  524.9 48.8 %collective-permute-start.32 = (bf16[128,1664]{1,0:T(8,128)(2,1)S(1)}, bf16[128,1664]{1,0:T(8,128)(2,1)S(1)}, u32[]{:S(2)}, u32[]{:S(2)}) collective-permute-start(bf16[128,1664]{1,0:T(8,128)(2,1)S(1)} %add_convert_fusion.12), channel_id=1, source_target_pairs={{1,0},{2,3},{5,4},{6,7},{9,8},{10,11},{13,12},{14,15},{17,16},{18,... | collective-permute-start | bytes 1277960 | tf_op jit(solution)/shard_map/ppermute | solution.py:322
  563.0 36.2 %collective-permute-start.37 = (bf16[128,5120]{1,0:T(8,128)(2,1)S(1)}, bf16[128,5120]{1,0:T(8,128)(2,1)S(1)}, u32[]{:S(2)}, u32[]{:S(2)}) collective-permute-start(bf16[128,5120]{1,0:T(8,128)(2,1)S(1)} %add_convert_fusion.3), channel_id=1, source_target_pairs={{1,0},{2,3},{5,4},{6,7},{9,8},{10,11},{13,12},{14,15},{17,16},{18,... | collective-permute-start | bytes 3932168 | tf_op jit(solution)/shard_map/ppermute | solution.py:322
  (92 other events, 814.1 us)
Sparse Core Ops, SparseCore 0:
  10.5 76.2 all-gather.2
  89.2 78.1 all-gather.4
  204.3 71.2 reduce-scatter.3
  279.4 71.2 reduce-scatter.5
  361.0 61.6 reduce-scatter.7

commit v4 on v3

--- a/solution.py
+++ b/solution.py
@@ -39,100 +39,103 @@
     return lax.dot_general(first, second, (((1,), (1,)), ((), ())), preferred_element_type=F32)
 
 
-def fill_scores(scores_ref, keys, queries, valid, places):
-    size = keys.shape[0]
+def chunk_scores(keys, queries, places, step):
     scores = over_lanes(keys, queries)
     if places is not None:
-        key_place, query_place = places
-        scores = jnp.where(key_place <= query_place, scores, LOW)
-    scores_ref[...] = scores
-    if valid < size:
-        first = valid // 8 * 8
-        row = lax.broadcasted_iota(jnp.int32, (size - first, queries.shape[0]), 0)
-        scores_ref[first:size] = jnp.where(row < valid - first, scores_ref[first:size], LOW)
+        key_ref, query_ref = places
+        rows = slice(step * keys.shape[0], (step + 1) * keys.shape[0])
+        scores = jnp.where(key_ref[rows] <= query_ref[...], scores, LOW)
+    return scores
+
+
+def tail_kept(values, valid, other):
+    size = values.shape[0]
+    if valid == size:
+        return values
+    first = valid // 8 * 8
+    row = lax.broadcasted_iota(jnp.int32, (size - first, values.shape[1]), 0)
+    tail = jnp.where(row < valid - first, values[first:], other)
+    return jnp.concatenate([values[:first], tail], axis=0)
 
 
 def forward_kernel(chunk, valid, causal, *refs):
-    if causal:
-        q_ref, k_ref, v_ref, kp_ref, qp_ref, o_ref, log_ref, s_ref = refs
-    else:
-        q_ref, k_ref, v_ref, o_ref, log_ref, s_ref = refs
+    q_ref, k_ref, v_ref = refs[:3]
+    places = refs[3:5] if causal else None
+    o_ref, log_ref, s_ref = refs[-3:]
     queries = two_heads(q_ref[...])
-    count = k_ref.shape[0] // chunk
     width = queries.shape[0]
-
-    def first(step, top):
-        rows = pl.ds(pl.multiple_of(step * chunk, chunk), chunk)
-        places = (kp_ref[rows], qp_ref[...]) if causal else None
-        part = s_ref.at[rows]
-        fill_scores(part, k_ref[rows], queries, valid, places)
-        return jnp.maximum(top, jnp.max(part[...], axis=0, keepdims=True))
-
-    top = lax.fori_loop(0, count, first, jnp.full((1, width), LOW, F32))
-
-    def second(step, carry):
-        total, mixed = carry
-        rows = pl.ds(pl.multiple_of(step * chunk, chunk), chunk)
+    strips = [slice(low, low + chunk) for low in range(0, k_ref.shape[0], chunk)]
+    top = jnp.full((1, width), LOW, F32)
+    for step, rows in enumerate(strips):
+        scores = tail_kept(chunk_scores(k_ref[rows], queries, places, step), valid, LOW)
+        s_ref[rows] = scores
+        top = jnp.maximum(top, jnp.max(scores, axis=0, keepdims=True))
+    total, mixed = jnp.zeros((1, width), F32), jnp.zeros((LANES, width), F32)
+    for rows in strips:
         raised = jnp.exp(s_ref[rows] - top)
         total = total + jnp.sum(raised, axis=0, keepdims=True)
         mixed = mixed + over_rows(v_ref[rows], raised.astype(BF))
-        return total, mixed
-
-    total, mixed = lax.fori_loop(
-        0, count, second, (jnp.zeros((1, width), F32), jnp.zeros((LANES, width), F32))
-    )
     o_ref[...] = one_row(jnp.transpose(mixed / total)).astype(BF)
     log_ref[...] = (top + jnp.log(total))[None]
 
 
-def backward_kernel(chunk, valid, causal, *refs):
-    q_ref, k_ref, v_ref, o_ref, g_ref, log_ref = refs[:6]
-    if causal:
-        kp_ref, qp_ref = refs[6:8]
-        joint_ref, s_ref, gk_ref, gv_ref = refs[-4:]
-    else:
-        gq_ref, joint_ref, s_ref, gv_ref = refs[-4:]
-        gk_ref = joint_ref
+def pair_back(chunk, valid, places, refs, store_key, store_value):
+    q_ref, k_ref, v_ref, o_ref, g_ref, log_ref = refs
+    queries = two_heads(q_ref[...])
+    grads = two_heads(g_ref[...])
+    mixed = o_ref[...].astype(F32)
+    product = grads.astype(F32) * jnp.concatenate([mixed, mixed], axis=0)
+    row_dot = jnp.sum(jnp.transpose(product), axis=0, keepdims=True)
+    log_total = log_ref[0]
+    grad_queries = jnp.zeros((LANES, queries.shape[0]), F32)
+    for step, low in enumerate(range(0, k_ref.shape[0], chunk)):
+        rows = slice(low, low + chunk)
+        keys = k_ref[rows]
+        scores = chunk_scores(keys, queries, places, step)
+        weights = jnp.exp(tail_kept(scores, valid, LOW) - log_total)
+        grad_weights = over_lanes(v_ref[rows], grads)
+        grad_scores = (weights * (grad_weights - row_dot)).astype(BF)
+        store_value(rows, jnp.dot(weights.astype(BF), grads, preferred_element_type=F32))
+        store_key(rows, jnp.dot(grad_scores, queries, preferred_element_type=F32))
+        grad_queries = grad_queries + over_rows(keys, grad_scores)
+    return one_row(jnp.transpose(grad_queries)).astype(BF) * BF(HD**-0.5)
+
+
+def cross_back_kernel(chunk, valid, *refs):
+    gq_ref, joint_ref, gv_ref = refs[-3:]
     phase = pl.program_id(1)
 
     @pl.when(phase == 0)
     def _():
-        queries = two_heads(q_ref[...])
-        grads = two_heads(g_ref[...])
-        mixed = o_ref[...].astype(F32)
-        product = grads.astype(F32) * jnp.concatenate([mixed, mixed], axis=0)
-        row_dot = jnp.sum(jnp.transpose(product), axis=0, keepdims=True)
-        log_total = log_ref[0]
-        width = queries.shape[0]
-
-        def body(step, grad_queries):
-            rows = pl.ds(pl.multiple_of(step * chunk, chunk), chunk)
-            places = (kp_ref[rows], qp_ref[...]) if causal else None
-            keys = k_ref[rows]
-            fill_scores(s_ref, keys, queries, valid, places)
-            weights = jnp.exp(s_ref[...] - log_total)
-            grad_weights = over_lanes(v_ref[rows], grads)
-            grad_scores = (weights * (grad_weights - row_dot)).astype(BF)
-            gv_ref[rows] = jnp.dot(
-                weights.astype(BF), grads, preferred_element_type=F32
-            ).astype(BF)
-            gk_ref[rows] = jnp.dot(grad_scores, queries, preferred_element_type=F32).astype(BF)
-            return grad_queries + over_rows(keys, grad_scores)
-
-        steps = k_ref.shape[0] // chunk
-        grad_queries = lax.fori_loop(0, steps, body, jnp.zeros((LANES, width), F32))
-        grad_queries = one_row(jnp.transpose(grad_queries)).astype(BF) * BF(HD**-0.5)
-        (joint_ref if causal else gq_ref)[...] = grad_queries
-
-    if causal:
-
-        @pl.when(phase == 1)
-        def _():
-            joint_ref[...] = gk_ref[...]
-
-    @pl.when(phase == (2 if causal else 1))
+        def store_key(rows, part):
+            joint_ref[rows] = part.astype(BF)
+
+        def store_value(rows, part):
+            gv_ref[rows] = part.astype(BF)
+
+        gq_ref[...] = pair_back(chunk, valid, None, refs[:6], store_key, store_value)
+
+    @pl.when(phase == 1)
     def _():
         joint_ref[...] = gv_ref[...]
+
+
+def causal_back_kernel(chunk, width, *refs):
+    joint_ref = refs[-1]
+
+    def lanes(part):
+        start = part * width + pl.program_id(0) * LANES
+        return pl.ds(pl.multiple_of(start, LANES), LANES)
+
+    def store_key(rows, part):
+        joint_ref[rows, lanes(1)] = part.astype(BF)
+
+    def store_value(rows, part):
+        joint_ref[rows, lanes(2)] = part.astype(BF)
+
+    joint_ref[:, lanes(0)] = pair_back(
+        chunk, chunk, refs[6:8], refs[:6], store_key, store_value
+    )
 
 
 def columns(rows, first=0):
@@ -190,31 +193,36 @@
     specs = [columns(member.shape[0], first + low) for member, first in sources]
     specs += [columns(tokens, low), columns(tokens, low), log_spec(tokens, low)]
     operands = [member for member, _ in sources] + [mixed, grads, logs]
-    joint_spec = pl.BlockSpec(
-        (count, LANES), lambda pair, phase: (0, pair + low + pairs * phase)
-    )
     if causal:
         specs += place_specs(count, tokens)
         operands += list(places)
-        out_specs = [joint_spec]
+        kernel = functools.partial(causal_back_kernel, chunk, width)
+        grid = (count_here,)
+        out_specs = [pl.BlockSpec((count, 3 * width), lambda pair: (0, 0))]
         out_shape = [jax.ShapeDtypeStruct((count, 3 * width), BF)]
+        kept = []
     else:
-        out_specs = [columns(tokens, low), joint_spec]
+        kernel = functools.partial(cross_back_kernel, chunk, valid)
+        grid = (count_here, 2)
+        out_specs = [
+            columns(tokens, low),
+            pl.BlockSpec((count, LANES), lambda pair, phase: (0, pair + low + pairs * phase)),
+        ]
         out_shape = [
             jax.ShapeDtypeStruct((tokens, width), BF),
             jax.ShapeDtypeStruct((count, 2 * width), BF),
         ]
+        kept = [pltpu.VMEM((count, LANES), BF)]
     aliases = {len(operands) + i: i for i in range(len(before))}
     specs += [pl.BlockSpec(memory_space=pl.ANY)] * len(before)
     operands += list(before)
-    kept = [pltpu.VMEM((count, LANES), BF)] * (2 if causal else 1)
     return pl.pallas_call(
-        functools.partial(backward_kernel, chunk, valid, causal),
-        grid=(count_here, 3 if causal else 2),
+        kernel,
+        grid=grid,
         in_specs=specs,
         out_specs=out_specs,
         out_shape=out_shape,
-        scratch_shapes=[pltpu.VMEM((chunk, 2 * tokens), F32)] + kept,
+        scratch_shapes=kept,
         input_output_aliases=aliases,
         compiler_params=pltpu.CompilerParams(vmem_limit_bytes=32 << 20),
         cost_estimate=pl.CostEstimate(
@@ -681,15 +689,15 @@
         axis=1,
     ).reshape(-1, width)
     if swift:
-        last_core, leaving, inner_in, outer_in = tied(last_core, leaving, inner_in, outer_in)
+        last_core, leaving = tied(last_core, leaving)
         last_own, last_near = grid.fold_chips(last_kept, last_core)
         inner_sum, inner_in = grid.hop_two(inner_sum, inner_in)
     leaving = grid.hand_back(leaving)
     if swift:
         part_middle = jnp.concatenate([plus_all(middle_own, middle_near), part_kv], axis=1)
         middle_sum, middle_in = grid.hop_one(part_middle)
-        middle_in, inner_in, grad_encoded, *last_near = tied(
-            middle_in, inner_in, grad_encoded, *last_near
+        middle_in, inner_in, outer_in, grad_encoded, *last_near = tied(
+            middle_in, inner_in, outer_in, grad_encoded, *last_near
         )
         part_last = plus_all(last_own, last_near)
         half = 12 * LANES

time: 617 us -> 601 us (0.974)
  Pallas kernels: 103 us -> 84.3 us
    pallas_call x3, Pallas kernels: 57.6 us -> 48.1 us  [attend_back(): pl.pallas_call(kernel, grid=grid, in_specs=specs, out_specs=out_specs, ou...]
    pallas_call x2, Pallas kernels: 39 us -> 29.7 us  [attend(): pl.pallas_call(functools.partial(forward_kernel, chunk, valid, causal), g...]
    unnamed x170 -> x166, local copies, waits for them, and re-layouts: 36.9 us -> 34 us
  transfers between devices with their start and end apart: 46 -> 46, of which waited for: 18 -> 19; matrix products, arithmetic and copies ran while one was open for 30% -> 32% of each run, Pallas kernels for 17% -> 14%
where the time goes in v4:
time: 601 us; the launch traced here: 593 us
  waiting for transfers between devices  185 us (31%)
  matrix products  115 us (19%)
  Pallas kernels  84.3 us (14%)
  starting transfers between devices  74.3 us (12%)
  local copies, waits for them, and re-layouts  61.4 us (10%)
  other arithmetic  56.9 us (9%)
  between operations  16 us (3%)
    ppermute x18, waiting for transfers between devices, flip(): lax.ppermute(values, 'fsdp', [(f, f ^ bits) for f in range(self.fsdp)])  91.7 us
    ppermute x15, waiting for transfers between devices, chain(): return lax.ppermute(values, AXES, pairs)  74.2 us
    dot_general x7, matrix products, product_back(): lax.dot_general(incoming, weight, (((1,), (1,)), ((), ())), preferred_ele...  51.3 us
    pallas_call x3, Pallas kernels, attend_back(): pl.pallas_call(kernel, grid=grid, in_specs=specs, out_specs=out_specs, ou...  48.1 us
    dot_general x7, matrix products, weight_grad(): lax.dot_general(operand, incoming, (((0,), (0,)), ((), ())), preferred_el...  34.1 us
    unnamed x166, local copies, waits for them, and re-layouts  34 us
    dot_general x7, matrix products, product(): return jnp.dot(first, second, preferred_element_type=F32)  29.8 us
    pallas_call x2, Pallas kernels, attend(): pl.pallas_call(functools.partial(forward_kernel, chunk, valid, causal), g...  29.7 us
  transfers between devices with their start and end apart: 46, of which 19 were waited for; matrix products, arithmetic and copies ran while one was open for 32% of the time, Pallas kernels for 14%

profile of v4, /device:TPU:0, one launch (start us, length us, event | category | flops | bytes accessed | tf_op | source)
XLA Modules:
  0.0 593.2 jit_solution(17425913974209991351)
XLA Ops:
  17.0 5.6 collective-permute-start.2
  27.1 25.7 %collective-permute-done.1 = bf16[128,3200]{1,0:T(8,128)(2,1)} collective-permute-done((bf16[128,3200]{1,0:T(8,128)(2,1)}, bf16[128,3200]{1,0:T(8,128)(2,1)}, u32[]{:S(2)}, u32[]{:S(2)}) %collective-permute-start.1) | collective-permute-done | bytes 819232 | tf_op jit(solution)/shard_map/ppermute | solution.py:333
  66.8 17.6 %collective-permute-done.5 = bf16[64,3200]{1,0:T(8,128)(2,1)S(1)} collective-permute-done((bf16[64,3200]{1,0:T(8,128)(2,1)S(1)}, bf16[64,3200]{1,0:T(8,128)(2,1)S(1)}, u32[]{:S(2)}, u32[]{:S(2)}) %collective-permute-start.5) | collective-permute-done | bytes 409632 | tf_op jit(solution)/shard_map/ppermute | solution.py:333
  84.8 10.9 %collective-permute-done.6.refs_2_ = bf16[487,1024]{1,0:T(8,128)(2,1)S(1)} collective-permute-done((bf16[487,1024]{1,0:T(8,128)(2,1)S(1)}, bf16[487,1024]{1,0:T(8,128)(2,1)S(1)}, u32[]{:S(2)}, u32[]{:S(2)}) %collective-permute-start.6) | collective-permute-done | bytes 997408 | tf_op jit(solution)/shard_map/ppermute | solution.py:302
  113.5 8.8 %attend_causal.1 = (bf16[448,1024]{1,0:T(8,128)(2,1)S(1)}, f32[8,1,896]{2,1,0:T(1,128)S(1)}) custom-call(bf16[448,3072]{1,0:T(8,128)(2,1)S(1)} %multiply_convert_fusion.1.refs_0_.refs_1_.refs_2_, bf16[448,3072]{1,0:T(8,128)(2,1)S(1)} %multiply_convert_fusion.1.refs_0_.refs_1_.refs_2_, bf16[448,3072]{1,0:T(8,128)(2,1)S(1)} %multiply_convert_fusion.1.refs_0_.refs_1_.refs_2_, ...), custom_call_target="tpu_custom_call" | custom-call | flops 3288334336 | bytes 3670016 | tf_op jit(solution)/shard_map/attend_causal/pallas_call | solution.py:165
  137.1 7.1 %add_convert_fusion.refs_1_.refs_2_ = bf16[1536,2048]{1,0:T(8,128)(2,1)S(1)} fusion(bf16[1536,1024]{1,0:T(8,128)(2,1)S(1)} %copy-done.12, f32[2048]{0:T(1024)S(1)} %concatenate.64, bf16[1024,4096]{1,0:T(8,128)(2,1)S(1)} %copy-done.69), kind=kOutput, calls=%fused_computation | convolution fusion | flops 6448742400 | bytes 13639680 | tf_op jit(solution)/shard_map/dot_general | solution.py:238
  144.2 20.9 %attend_cross.1 = (bf16[448,1024]{1,0:T(8,128)(2,1)S(1)}, f32[8,1,896]{2,1,0:T(1,128)S(1)}) custom-call(bf16[448,1024]{1,0:T(8,128)(2,1)S(1)} %multiply_convert_fusion.2.refs_0_, bf16[1536,2048]{1,0:T(8,128)(2,1)S(1)} %add_convert_fusion.refs_1_.refs_2_, bf16[1536,2048]{1,0:T(8,128)(2,1)S(1)} %add_convert_fusion.refs_1_.refs_2_), custom_call_target="tpu_custom_call" | custom-call | flops 11274289152 | bytes 8126464 | tf_op jit(solution)/shard_map/attend_cross/pallas_call | solution.py:165
  174.8 7.1 %multiply_convert_fusion = (bf16[448,4096]{1,0:T(8,128)(2,1)S(1)}, f32[448,4096]{1,0:T(8,128)}) fusion(f32[4096]{0:T(1024)S(1)} %convert.79, bf16[1024,5120]{1,0:T(8,128)(2,1)S(1)} %copy-done.68, f32[448,1024]{1,0:T(8,128)S(1)} %get-tuple-element.220, f32[1024]{0:T(1024)S(1)} %bitcast.187, f32[1024]{0:T(1024)S(1)} %bitcast.177, f32[448]{0:T(512)S(1)} %add_rsqrt_fusion, ...), kind=kOutput, calls=%fused_computation.13 | convolution fusion | flops 3771400192 | bytes 21262336 | tf_op jit(solution)/shard_map/dot_general | solution.py:238
  187.8 6.8 %convolution_convert_fusion.1 = bf16[4096,1024]{1,0:T(8,128)(2,1)} fusion(bf16[448,4096]{1,0:T(8,128)(2,1)S(1)} %get-tuple-element.138, bf16[448,1024]{1,0:T(8,128)(2,1)S(1)} %place.3), kind=kOutput, calls=%fused_computation.3 | convolution fusion | flops 3762290688 | bytes 12976128 | tf_op jit(solution)/shard_map/dot_general | solution.py:248
  199.6 10.8 %fusion.73 = (bf16[448,4096]{1,0:T(8,128)(2,1)S(1)}, bf16[4096]{0:T(1024)(128)(2,1)S(1)}) fusion(f32[448,4096]{1,0:T(8,128)} %get-tuple-element.222, f32[4096]{0:T(1024)S(1)} %convert.79, bf16[448,1024]{1,0:T(8,128)(2,1)S(1)} %place.3, bf16[4096,1024]{1,0:T(8,128)(2,1)S(1)} %assemble.3), kind=kOutput, calls=%fused_computation.190 | convolution fusion | flops 3780112384 | bytes 20340736 | tf_op jit(solution)/shard_map/dot_general | solution.py:242
  212.4 7.4 %convolution_convert_fusion = bf16[1024,4096]{1,0:T(8,128)(2,1)} fusion(bf16[448,4096]{1,0:T(8,128)(2,1)S(1)} %get-tuple-element.114, f32[448,1024]{1,0:T(8,128)S(1)} %copy-done.32, f32[1024]{0:T(1024)S(1)} %bitcast.188, f32[1024]{0:T(1024)S(1)} %bitcast.178, f32[448]{0:T(512)S(1)} %add_rsqrt_fusion, f32[448]{0:T(512)S(1)} %broadcast_multiply_fusion.6), kind=kOutput, calls=%fused_computation.2 | convolution fusion | flops 3764584448 | bytes 13905408 | tf_op jit(solution)/shard_map/dot_general | solution.py:248
  219.7 9.9 %multiply_reduce_fusion = (bf16[1024]{0:T(1024)(128)(2,1)S(1)}, f32[448]{0:T(512)S(1)}, f32[448]{0:T(512)S(1)}, bf16[1024]{0:T(1024)(128)(2,1)S(1)}, f32[448,1024]{1,0:T(8,128)S(1)}) fusion(f32[448,1024]{1,0:T(8,128)} %copy-done.31, f32[448]{0:T(512)S(1)} %add_rsqrt_fusion, f32[448]{0:T(512)S(1)} %broadcast_multiply_fusion.6, f32[1024]{0:T(1024)S(1)} %bitcast.179, ...), kind=kOutput, calls=%fused_computation.73 | convolution fusion | flops 3762222080 | bytes 15744000 | tf_op jit(solution)/shard_map/dot_general | solution.py:242
  240.9 18.0 %attend_cross_back.2 = (bf16[448,1024]{1,0:T(8,128)(2,1)S(1)}, bf16[1536,2048]{1,0:T(8,128)(2,1)S(1)}) custom-call(bf16[448,1024]{1,0:T(8,128)(2,1)S(1)} %copy-done.23, bf16[1536,2048]{1,0:T(8,128)(2,1)S(1)} %copy-done.26, bf16[1536,2048]{1,0:T(8,128)(2,1)S(1)} %copy-done.26, bf16[448,1024]{1,0:T(8,128)(2,1)S(1)} %copy-done.20, ...), custom_call_target="tpu_custom_call" | custom-call | flops 14092861440 | bytes 8126464 | tf_op jit(solution)/shard_map/attend_cross_back/pallas_call | solution.py:219
  261.5 5.0 reduce-scatter.4.cloned.1.call-done
  278.3 17.6 %attend_cross_back.3 = (bf16[448,1024]{1,0:T(8,128)(2,1)S(1)}, bf16[1536,2048]{1,0:T(8,128)(2,1)S(1)}) custom-call(bf16[448,1024]{1,0:T(8,128)(2,1)S(1)} %copy-done.24, bf16[1536,2048]{1,0:T(8,128)(2,1)S(1)} %copy-done.27, bf16[1536,2048]{1,0:T(8,128)(2,1)S(1)} %copy-done.27, ...), custom_call_target="tpu_custom_call", output_to_operand_aliasing={{0}: (6, {}), {1}: (7, {})} | custom-call | flops 14092861440 | bytes 8126464 | tf_op jit(solution)/shard_map/attend_cross_back/pallas_call | solution.py:219
  298.1 11.7 %convolution_convert_fusion.4 = bf16[1536,1024]{1,0:T(8,128)(2,1)} fusion(bf16[1536,2048]{1,0:T(8,128)(2,1)S(1)} %get-tuple-element.126, bf16[1024,4096]{1,0:T(8,128)(2,1)} %all-gather.3.cloned.1.call-done), kind=kOutput, calls=%fused_computation.21 | convolution fusion | flops 6444023808 | bytes 13631488 | tf_op jit(solution)/shard_map/dot_general | solution.py:242
  309.9 8.9 %convolution_convert_fusion.3 = bf16[1024,2048]{1,0:T(8,128)(2,1)} fusion(bf16[1536,1024]{1,0:T(8,128)(2,1)S(1)} %copy-done.13, bf16[1536,2048]{1,0:T(8,128)(2,1)S(1)} %get-tuple-element.126), kind=kOutput, calls=%fused_computation.20 | convolution fusion | flops 6444548096 | bytes 13631488 | tf_op jit(solution)/shard_map/dot_general | solution.py:248
  335.2 5.8 all-to-all-start.1
  347.0 12.4 %attend_causal_back.1 = bf16[448,3072]{1,0:T(8,128)(2,1)S(1)} custom-call(bf16[448,3072]{1,0:T(8,128)(2,1)S(1)} %copy-done.15, bf16[448,3072]{1,0:T(8,128)(2,1)S(1)} %copy-done.15, bf16[448,3072]{1,0:T(8,128)(2,1)S(1)} %copy-done.15, bf16[448,1024]{1,0:T(8,128)(2,1)S(1)} %copy-done.18, bf16[448,1024]{1,0:T(8,128)(2,1)S(1)} %fusion.51.refs_4_, ...), custom_call_target="tpu_custom_call" | custom-call | flops 8220835840 | bytes 7340032 | tf_op jit(solution)/shard_map/attend_causal_back/pallas_call | solution.py:219
  361.0 8.3 %fusion.32 = (f32[448]{0:T(512)S(1)}, bf16[1024]{0:T(1024)(128)(2,1)S(1)}, f32[448]{0:T(512)S(1)}, bf16[1024]{0:T(1024)(128)(2,1)S(1)}, f32[448,1024]{1,0:T(8,128)}) fusion(bf16[448,1024]{1,0:T(8,128)(2,1)S(1)} %copy-done.2, f32[1024]{0:T(1024)S(1)} %bitcast.167, f32[448]{0:T(512)S(1)} %copy-done.58, f32[448]{0:T(512)S(1)} %copy-done.54, ...), kind=kOutput, calls=%fused_computation.64 | convolution fusion | flops 2823156736 | bytes 11811840 | tf_op jit(solution)/shard_map/dot_general | solution.py:242
  372.0 4.4 collective-permute-start.24
  386.4 5.7 convolution_convert_fusion.2
  408.8 15.7 %collective-permute-done.22 = bf16[128,3072]{1,0:T(8,128)(2,1)} collective-permute-done((bf16[128,3072]{1,0:T(8,128)(2,1)}, bf16[128,3072]{1,0:T(8,128)(2,1)}, u32[]{:S(2)}, u32[]{:S(2)}) %collective-permute-start.22) | collective-permute-done | bytes 786464 | tf_op jit(solution)/shard_map/ppermute | solution.py:333
  434.1 4.5 collective-permute-start.23
  449.2 4.4 all-to-all-start
  453.6 12.5 %collective-permute-done.29 = bf16[128,3200]{1,0:T(8,128)(2,1)S(1)} collective-permute-done((bf16[128,3200]{1,0:T(8,128)(2,1)}, bf16[128,3200]{1,0:T(8,128)(2,1)S(1)}, u32[]{:S(2)}, u32[]{:S(2)}) %collective-permute-start.29) | collective-permute-done | bytes 819232 | tf_op jit(solution)/shard_map/ppermute | solution.py:333
  466.1 15.2 %collective-permute-done.28 = bf16[128,3200]{1,0:T(8,128)(2,1)} collective-permute-done((bf16[128,3200]{1,0:T(8,128)(2,1)}, bf16[128,3200]{1,0:T(8,128)(2,1)}, u32[]{:S(2)}, u32[]{:S(2)}) %collective-permute-start.28) | collective-permute-done | bytes 819232 | tf_op jit(solution)/shard_map/ppermute | solution.py:333
  496.3 8.6 %collective-permute-done.33 = bf16[128,1536]{1,0:T(8,128)(2,1)S(1)} collective-permute-done((bf16[128,1536]{1,0:T(8,128)(2,1)S(1)}, bf16[128,1536]{1,0:T(8,128)(2,1)S(1)}, u32[]{:S(2)}, u32[]{:S(2)}) %collective-permute-start.33) | collective-permute-done | bytes 393248 | tf_op jit(solution)/shard_map/ppermute | solution.py:330
  505.6 6.2 %collective-permute-done.30 = bf16[128,1664]{1,0:T(8,128)(2,1)S(1)} collective-permute-done((bf16[128,1664]{1,0:T(8,128)(2,1)S(1)}, bf16[128,1664]{1,0:T(8,128)(2,1)S(1)}, u32[]{:S(2)}, u32[]{:S(2)}) %collective-permute-start.30) | collective-permute-done | bytes 426016 | tf_op jit(solution)/shard_map/ppermute | solution.py:330
  518.0 27.8 %collective-permute-done.35 = bf16[128,1536]{1,0:T(8,128)(2,1)S(1)} collective-permute-done((bf16[128,1536]{1,0:T(8,128)(2,1)S(1)}, bf16[128,1536]{1,0:T(8,128)(2,1)S(1)}, u32[]{:S(2)}, u32[]{:S(2)}) %collective-permute-start.35) | collective-permute-done | bytes 393248 | tf_op jit(solution)/shard_map/ppermute | solution.py:330
  547.5 10.0 %collective-permute-done.32 = bf16[128,1664]{1,0:T(8,128)(2,1)S(1)} collective-permute-done((bf16[128,1664]{1,0:T(8,128)(2,1)S(1)}, bf16[128,1664]{1,0:T(8,128)(2,1)S(1)}, u32[]{:S(2)}, u32[]{:S(2)}) %collective-permute-start.32) | collective-permute-done | bytes 426016 | tf_op jit(solution)/shard_map/ppermute | solution.py:330
  563.2 20.5 %collective-permute-done.37 = bf16[128,5120]{1,0:T(8,128)(2,1)S(1)} collective-permute-done((bf16[128,5120]{1,0:T(8,128)(2,1)S(1)}, bf16[128,5120]{1,0:T(8,128)(2,1)S(1)}, u32[]{:S(2)}, u32[]{:S(2)}) %collective-permute-start.37) | collective-permute-done | bytes 1310752 | tf_op jit(solution)/shard_map/ppermute | solution.py:330
  (358 shorter events, 215.2 us)
Async XLA Ops:
  7.2 116.6 %all-gather.3.cloned.1.call-start = ((), (), s32[]{:S(2)}) async-start(), calls=%async_computation.5 | async-start | bytes 9437184 | tf_op jit(solution)/shard_map/all_gather | solution.py:501
  9.6 159.3 %all-gather.5.cloned.1.call-start = ((), (), s32[]{:S(2)}) async-start(), calls=%async_computation.6 | async-start | bytes 11796480 | tf_op jit(solution)/shard_map/all_gather | solution.py:501
  11.9 254.6 %reduce-scatter.4.cloned.1.call-start = ((), (), s32[]{:S(2)}) async-start(), calls=%async_computation.7 | async-start | bytes 9437184 | tf_op jit(solution)/shard_map/reduce_scatter | solution.py:505
  15.7 37.1 %collective-permute-start.3 = (bf16[487,1024]{1,0:T(8,128)(2,1)}, bf16[487,1024]{1,0:T(8,128)(2,1)S(1)}, u32[]{:S(2)}, u32[]{:S(2)}) collective-permute-start(bf16[487,1024]{1,0:T(8,128)(2,1)} %get-tuple-element.180), channel_id=1, source_target_pairs={{1,0},{2,1},{3,2},{4,7},{6,5},{7,6},{9,8},{10,9},{11,10},{12,15},{... | collective-permute-start | bytes 2992136 | tf_op jit(solution)/shard_map/ppermute | solution.py:302
  17.0 38.9 %collective-permute-start.2 = (bf16[487,1024]{1,0:T(8,128)(2,1)}, bf16[487,1024]{1,0:T(8,128)(2,1)}, u32[]{:S(2)}, u32[]{:S(2)}) collective-permute-start(bf16[487,1024]{1,0:T(8,128)(2,1)} %get-tuple-element.181), channel_id=1, source_target_pairs={{0,1},{1,2},{3,0},{4,5},{5,6},{6,7},{8,9},{9,10},{11,8},{12,13},{1... | collective-permute-start | bytes 2992136 | tf_op jit(solution)/shard_map/ppermute | solution.py:302
  23.7 29.2 %collective-permute-start.1 = (bf16[128,3200]{1,0:T(8,128)(2,1)}, bf16[128,3200]{1,0:T(8,128)(2,1)}, u32[]{:S(2)}, u32[]{:S(2)}) collective-permute-start(bf16[128,3200]{1,0:T(8,128)(2,1)} %get-tuple-element.197), channel_id=1, source_target_pairs={{0,16},{4,20},{8,24},{12,28},{16,0},{20,4},{24,8},{28,12},{1,17},{... | collective-permute-start | bytes 2457608 | tf_op jit(solution)/shard_map/ppermute | solution.py:333
  25.6 27.2 %collective-permute-start = (bf16[128,3200]{1,0:T(8,128)(2,1)}, bf16[128,3200]{1,0:T(8,128)(2,1)}, u32[]{:S(2)}, u32[]{:S(2)}) collective-permute-start(bf16[128,3200]{1,0:T(8,128)(2,1)} %get-tuple-element.197), channel_id=1, source_target_pairs={{0,8},{4,12},{8,0},{12,4},{16,24},{20,28},{24,16},{28,20},{1,9},{5... | collective-permute-start | bytes 2457608 | tf_op jit(solution)/shard_map/ppermute | solution.py:333
  57.2 38.5 %collective-permute-start.6 = (bf16[487,1024]{1,0:T(8,128)(2,1)S(1)}, bf16[487,1024]{1,0:T(8,128)(2,1)S(1)}, u32[]{:S(2)}, u32[]{:S(2)}) collective-permute-start(bf16[487,1024]{1,0:T(8,128)(2,1)S(1)} %dynamic-slice_bitcast_fusion.8), channel_id=1, source_target_pairs={{0,2},{2,0},{3,1},{4,6},{5,7},{7,5},{8,10},{10,8},{11,9},{12,14},{... | collective-permute-start | bytes 2992136 | tf_op jit(solution)/shard_map/ppermute | solution.py:302
  103.6 61.6 %collective-permute-start.9 = (bf16[512,1024]{1,0:T(8,128)(2,1)}, bf16[512,1024]{1,0:T(8,128)(2,1)}, u32[]{:S(2)}, u32[]{:S(2)}) collective-permute-start(bf16[512,1024]{1,0:T(8,128)(2,1)} %param.27), channel_id=1, source_target_pairs={{0,16},{4,20},{8,24},{12,28},{16,0},{20,4},{24,8},{28,12},{1,17},{... | collective-permute-start | bytes 3145736 | tf_op jit(solution)/shard_map/ppermute | solution.py:333
  105.1 60.1 %collective-permute-start.8 = (bf16[512,1024]{1,0:T(8,128)(2,1)}, bf16[512,1024]{1,0:T(8,128)(2,1)}, u32[]{:S(2)}, u32[]{:S(2)}) collective-permute-start(bf16[512,1024]{1,0:T(8,128)(2,1)} %param.27), channel_id=1, source_target_pairs={{0,8},{4,12},{8,0},{12,4},{16,24},{20,28},{24,16},{28,20},{1,9},{5... | collective-permute-start | bytes 3145736 | tf_op jit(solution)/shard_map/ppermute | solution.py:333
  129.7 35.5 %collective-permute-start.12 = (bf16[112,1024]{1,0:T(8,128)(2,1)S(1)}, bf16[112,1024]{1,0:T(8,128)(2,1)S(1)}, u32[]{:S(2)}, u32[]{:S(2)}) collective-permute-start(bf16[112,1024]{1,0:T(8,128)(2,1)S(1)} %get-tuple-element.198), channel_id=1, source_target_pairs={{1,0},{2,1},{3,2},{4,7},{6,5},{7,6},{9,8},{10,9},{11,10},{12,15},{... | collective-permute-start | bytes 688136 | tf_op jit(solution)/shard_map/ppermute | solution.py:302
  131.0 34.2 %collective-permute-start.11 = (bf16[112,1024]{1,0:T(8,128)(2,1)S(1)}, bf16[112,1024]{1,0:T(8,128)(2,1)S(1)}, u32[]{:S(2)}, u32[]{:S(2)}) collective-permute-start(bf16[112,1024]{1,0:T(8,128)(2,1)S(1)} %get-tuple-element.199), channel_id=1, source_target_pairs={{0,2},{2,0},{3,1},{4,6},{5,7},{7,5},{8,10},{10,8},{11,9},{12,14},{... | collective-permute-start | bytes 688136 | tf_op jit(solution)/shard_map/ppermute | solution.py:302
  133.0 32.3 %collective-permute-start.10 = (bf16[112,1024]{1,0:T(8,128)(2,1)S(1)}, bf16[112,1024]{1,0:T(8,128)(2,1)S(1)}, u32[]{:S(2)}, u32[]{:S(2)}) collective-permute-start(bf16[112,1024]{1,0:T(8,128)(2,1)S(1)} %get-tuple-element.200), channel_id=1, source_target_pairs={{0,1},{1,2},{3,0},{4,5},{5,6},{6,7},{8,9},{9,10},{11,8},{12,13},{1... | collective-permute-start | bytes 688136 | tf_op jit(solution)/shard_map/ppermute | solution.py:302
  195.1 165.9 %reduce-scatter.6.cloned.1.call-start = ((), (), s32[]{:S(2)}) async-start(), calls=%async_computation.8 | async-start | bytes 9437184 | tf_op jit(solution)/shard_map/reduce_scatter | solution.py:505
  266.5 29.4 %collective-permute-start.16 = (bf16[512,1024]{1,0:T(8,128)(2,1)}, bf16[512,1024]{1,0:T(8,128)(2,1)S(1)}, u32[]{:S(2)}, u32[]{:S(2)}) collective-permute-start(bf16[512,1024]{1,0:T(8,128)(2,1)} %reduce-scatter.4.cloned.1.call-done), channel_id=1, source_target_pairs={{0,1},{3,2},{4,5},{7,6},{8,9},{11,10},{12,13},{15,14},{16,17},{19,... | collective-permute-start | bytes 3145736 | tf_op jit(solution)/shard_map/ppermute | solution.py:330
  335.2 112.1 %all-to-all-start.1 = ((bf16[4,384,1024]{2,1,0:T(8,128)(2,1)}), bf16[4,384,1024]{2,1,0:T(8,128)(2,1)}, u32[]{:S(2)}, u32[]{:S(2)}) async-start(bf16[4,384,1024]{2,1,0:T(8,128)(2,1)} %bitcast.158), calls=%async_computation.4 | async-start | bytes 6291456 | tf_op jit(solution)/shard_map/all_to_all | solution.py:321
  341.1 90.6 %reduce-scatter.8.cloned.1.call-start = ((), (), s32[]{:S(2)}) async-start(), calls=%async_computation.9 | async-start | bytes 4718592 | tf_op jit(solution)/shard_map/reduce_scatter | solution.py:505
  372.0 56.8 %collective-permute-start.24 = (bf16[128,4096]{1,0:T(8,128)(2,1)}, bf16[128,4096]{1,0:T(8,128)(2,1)S(1)}, u32[]{:S(2)}, u32[]{:S(2)}) collective-permute-start(bf16[128,4096]{1,0:T(8,128)(2,1)} %reduce-scatter.6.cloned.1.call-done), channel_id=1, source_target_pairs={{0,1},{3,2},{4,5},{7,6},{8,9},{11,10},{12,13},{15,14},{16,17},{19,... | collective-permute-start | bytes 3145736 | tf_op jit(solution)/shard_map/ppermute | solution.py:330
  381.2 26.3 %collective-permute-start.20 = (bf16[128,3072]{1,0:T(8,128)(2,1)}, bf16[128,3072]{1,0:T(8,128)(2,1)}, u32[]{:S(2)}, u32[]{:S(2)}) collective-permute-start(bf16[128,3072]{1,0:T(8,128)(2,1)} %get-tuple-element.177), channel_id=1, source_target_pairs={{0,8},{4,12},{8,0},{12,4},{16,24},{20,28},{24,16},{28,20},{1,9},{5... | collective-permute-start | bytes 2359304 | tf_op jit(solution)/shard_map/ppermute | solution.py:333
  382.5 41.9 %collective-permute-start.22 = (bf16[128,3072]{1,0:T(8,128)(2,1)}, bf16[128,3072]{1,0:T(8,128)(2,1)}, u32[]{:S(2)}, u32[]{:S(2)}) collective-permute-start(bf16[128,3072]{1,0:T(8,128)(2,1)} %get-tuple-element.178), channel_id=1, source_target_pairs={{0,24},{4,28},{8,16},{12,20},{16,8},{20,12},{24,0},{28,4},{1,25},{... | collective-permute-start | bytes 2359304 | tf_op jit(solution)/shard_map/ppermute | solution.py:333
  384.0 41.8 %collective-permute-start.21 = (bf16[128,3072]{1,0:T(8,128)(2,1)}, bf16[128,3072]{1,0:T(8,128)(2,1)}, u32[]{:S(2)}, u32[]{:S(2)}) collective-permute-start(bf16[128,3072]{1,0:T(8,128)(2,1)} %get-tuple-element.179), channel_id=1, source_target_pairs={{0,16},{4,20},{8,24},{12,28},{16,0},{20,4},{24,8},{28,12},{1,17},{... | collective-permute-start | bytes 2359304 | tf_op jit(solution)/shard_map/ppermute | solution.py:333
  398.2 40.5 %collective-permute-start.19 = (bf16[4,128,3200]{2,1,0:T(8,128)(2,1)}, bf16[4,128,3200]{2,1,0:T(8,128)(2,1)}, u32[]{:S(2)}, u32[]{:S(2)}) collective-permute-start(bf16[4,128,3200]{2,1,0:T(8,128)(2,1)} %pad_maximum_fusion.2), channel_id=1, source_target_pairs={{0,4},{4,0},{8,12},{12,8},{16,20},{20,16},{24,28},{28,24},{1,5},{5... | collective-permute-start | bytes 9830408 | tf_op jit(solution)/shard_map/ppermute | solution.py:333
  407.5 38.9 %collective-permute-start.26 = (bf16[512,1024]{1,0:T(8,128)(2,1)}, bf16[512,1024]{1,0:T(8,128)(2,1)}, u32[]{:S(2)}, u32[]{:S(2)}) collective-permute-start(bf16[512,1024]{1,0:T(8,128)(2,1)} %add_convert_fusion.6), channel_id=1, source_target_pairs={{1,0},{2,3},{5,4},{6,7},{9,8},{10,11},{13,12},{14,15},{17,16},{18,... | collective-permute-start | bytes 3145736 | tf_op jit(solution)/shard_map/ppermute | solution.py:330
  434.1 47.1 %collective-permute-start.23 = (bf16[128,5120]{1,0:T(8,128)(2,1)}, bf16[128,5120]{1,0:T(8,128)(2,1)}, u32[]{:S(2)}, u32[]{:S(2)}) collective-permute-start(bf16[128,5120]{1,0:T(8,128)(2,1)} %pad_maximum_fusion.8), channel_id=1, source_target_pairs={{0,1},{3,2},{4,5},{7,6},{8,9},{11,10},{12,13},{15,14},{16,17},{19,... | collective-permute-start | bytes 3932168 | tf_op jit(solution)/shard_map/ppermute | solution.py:330
  445.2 36.0 %collective-permute-start.28 = (bf16[128,3200]{1,0:T(8,128)(2,1)}, bf16[128,3200]{1,0:T(8,128)(2,1)}, u32[]{:S(2)}, u32[]{:S(2)}) collective-permute-start(bf16[128,3200]{1,0:T(8,128)(2,1)} %get-tuple-element.175), channel_id=1, source_target_pairs={{0,16},{4,20},{8,24},{12,28},{16,0},{20,4},{24,8},{28,12},{1,17},{... | collective-permute-start | bytes 2457608 | tf_op jit(solution)/shard_map/ppermute | solution.py:333
  446.4 34.9 %collective-permute-start.27 = (bf16[128,3200]{1,0:T(8,128)(2,1)}, bf16[128,3200]{1,0:T(8,128)(2,1)}, u32[]{:S(2)}, u32[]{:S(2)}) collective-permute-start(bf16[128,3200]{1,0:T(8,128)(2,1)} %get-tuple-element.176), channel_id=1, source_target_pairs={{0,8},{4,12},{8,0},{12,4},{16,24},{20,28},{24,16},{28,20},{1,9},{5... | collective-permute-start | bytes 2457608 | tf_op jit(solution)/shard_map/ppermute | solution.py:333
  449.2 111.4 %all-to-all-start = ((bf16[4,224,1024]{2,1,0:T(8,128)(2,1)}), bf16[4,224,1024]{2,1,0:T(8,128)(2,1)}, u32[]{:S(2)}, u32[]{:S(2)}) async-start(bf16[4,224,1024]{2,1,0:T(8,128)(2,1)} %pad_maximum_fusion.5), calls=%async_computation.2 | async-start | bytes 3670016 | tf_op jit(solution)/shard_map/all_to_all | solution.py:321
  489.5 27.0 %collective-permute-start.38 = (bf16[128,4096]{1,0:T(8,128)(2,1)S(1)}, bf16[128,4096]{1,0:T(8,128)(2,1)S(1)}, u32[]{:S(2)}, u32[]{:S(2)}) collective-permute-start(bf16[128,4096]{1,0:T(8,128)(2,1)S(1)} %add_convert_fusion.5), channel_id=1, source_target_pairs={{1,0},{2,3},{5,4},{6,7},{9,8},{10,11},{13,12},{14,15},{17,16},{18,... | collective-permute-start | bytes 3145736 | tf_op jit(solution)/shard_map/ppermute | solution.py:330
  492.8 53.0 %collective-permute-start.36 = (bf16[128,5120]{1,0:T(8,128)(2,1)S(1)}, bf16[128,5120]{1,0:T(8,128)(2,1)S(1)}, u32[]{:S(2)}, u32[]{:S(2)}) collective-permute-start(bf16[128,5120]{1,0:T(8,128)(2,1)S(1)} %add_convert_fusion.4), channel_id=1, source_target_pairs={{1,2},{2,1},{5,6},{6,5},{9,10},{10,9},{13,14},{14,13},{17,18},{18,... | collective-permute-start | bytes 3932168 | tf_op jit(solution)/shard_map/ppermute | solution.py:330
  512.7 33.1 %collective-permute-start.35 = (bf16[128,1536]{1,0:T(8,128)(2,1)S(1)}, bf16[128,1536]{1,0:T(8,128)(2,1)S(1)}, u32[]{:S(2)}, u32[]{:S(2)}) collective-permute-start(bf16[128,1536]{1,0:T(8,128)(2,1)S(1)} %add_convert_fusion.14), channel_id=1, source_target_pairs={{1,0},{2,3},{5,4},{6,7},{9,8},{10,11},{13,12},{14,15},{17,16},{18,... | collective-permute-start | bytes 1179656 | tf_op jit(solution)/shard_map/ppermute | solution.py:330
  514.1 43.4 %collective-permute-start.32 = (bf16[128,1664]{1,0:T(8,128)(2,1)S(1)}, bf16[128,1664]{1,0:T(8,128)(2,1)S(1)}, u32[]{:S(2)}, u32[]{:S(2)}) collective-permute-start(bf16[128,1664]{1,0:T(8,128)(2,1)S(1)} %add_convert_fusion.12), channel_id=1, source_target_pairs={{1,0},{2,3},{5,4},{6,7},{9,8},{10,11},{13,12},{14,15},{17,16},{18,... | collective-permute-start | bytes 1277960 | tf_op jit(solution)/shard_map/ppermute | solution.py:330
  546.2 37.5 %collective-permute-start.37 = (bf16[128,5120]{1,0:T(8,128)(2,1)S(1)}, bf16[128,5120]{1,0:T(8,128)(2,1)S(1)}, u32[]{:S(2)}, u32[]{:S(2)}) collective-permute-start(bf16[128,5120]{1,0:T(8,128)(2,1)S(1)} %add_convert_fusion.3), channel_id=1, source_target_pairs={{1,0},{2,3},{5,4},{6,7},{9,8},{10,11},{13,12},{14,15},{17,16},{18,... | collective-permute-start | bytes 3932168 | tf_op jit(solution)/shard_map/ppermute | solution.py:330
  (90 other events, 799.5 us)
Sparse Core Ops, SparseCore 0:
  10.5 76.2 all-gather.2
  89.2 78.1 all-gather.4
  195.2 71.2 reduce-scatter.3
  270.2 71.2 reduce-scatter.5
  344.9 57.9 reduce-scatter.7

commit v5 on v4

--- a/solution.py
+++ b/solution.py
@@ -101,39 +101,30 @@
     return one_row(jnp.transpose(grad_queries)).astype(BF) * BF(HD**-0.5)
 
 
-def cross_back_kernel(chunk, valid, *refs):
-    gq_ref, joint_ref, gv_ref = refs[-3:]
-    phase = pl.program_id(1)
-
-    @pl.when(phase == 0)
-    def _():
-        def store_key(rows, part):
-            joint_ref[rows] = part.astype(BF)
-
-        def store_value(rows, part):
-            gv_ref[rows] = part.astype(BF)
-
-        gq_ref[...] = pair_back(chunk, valid, None, refs[:6], store_key, store_value)
-
-    @pl.when(phase == 1)
-    def _():
-        joint_ref[...] = gv_ref[...]
+def joint_stores(joint_ref, width, first):
+    def lanes(part):
+        start = (part + first) * width + pl.program_id(0) * LANES
+        return pl.ds(pl.multiple_of(start, LANES), LANES)
+
+    def store_key(rows, part):
+        joint_ref[rows, lanes(0)] = part.astype(BF)
+
+    def store_value(rows, part):
+        joint_ref[rows, lanes(1)] = part.astype(BF)
+
+    return lanes, store_key, store_value
+
+
+def cross_back_kernel(chunk, valid, width, *refs):
+    gq_ref, joint_ref = refs[-2:]
+    _, store_key, store_value = joint_stores(joint_ref, width, 0)
+    gq_ref[...] = pair_back(chunk, valid, None, refs[:6], store_key, store_value)
 
 
 def causal_back_kernel(chunk, width, *refs):
     joint_ref = refs[-1]
-
-    def lanes(part):
-        start = part * width + pl.program_id(0) * LANES
-        return pl.ds(pl.multiple_of(start, LANES), LANES)
-
-    def store_key(rows, part):
-        joint_ref[rows, lanes(1)] = part.astype(BF)
-
-    def store_value(rows, part):
-        joint_ref[rows, lanes(2)] = part.astype(BF)
-
-    joint_ref[:, lanes(0)] = pair_back(
+    lanes, store_key, store_value = joint_stores(joint_ref, width, 1)
+    joint_ref[:, lanes(-1)] = pair_back(
         chunk, chunk, refs[6:8], refs[:6], store_key, store_value
     )
 
@@ -182,53 +173,35 @@
     )(*operands)
 
 
-def attend_back(
-    sources, mixed, grads, logs, places, chunk, valid, width, part=0, parts=1, before=()
-):
+def attend_back(sources, mixed, grads, logs, places, chunk, valid, width):
     tokens, count = sources[0][0].shape[0], sources[1][0].shape[0]
     causal = places is not None
     pairs = width // LANES
-    count_here = pairs // parts
-    low = part * count_here
-    specs = [columns(member.shape[0], first + low) for member, first in sources]
-    specs += [columns(tokens, low), columns(tokens, low), log_spec(tokens, low)]
+    specs = [columns(member.shape[0], first) for member, first in sources]
+    specs += [columns(tokens), columns(tokens), log_spec(tokens)]
     operands = [member for member, _ in sources] + [mixed, grads, logs]
+    parts = 3 if causal else 2
+    out_specs = [pl.BlockSpec((count, parts * width), lambda pair: (0, 0))]
+    out_shape = [jax.ShapeDtypeStruct((count, parts * width), BF)]
     if causal:
         specs += place_specs(count, tokens)
         operands += list(places)
         kernel = functools.partial(causal_back_kernel, chunk, width)
-        grid = (count_here,)
-        out_specs = [pl.BlockSpec((count, 3 * width), lambda pair: (0, 0))]
-        out_shape = [jax.ShapeDtypeStruct((count, 3 * width), BF)]
-        kept = []
     else:
-        kernel = functools.partial(cross_back_kernel, chunk, valid)
-        grid = (count_here, 2)
-        out_specs = [
-            columns(tokens, low),
-            pl.BlockSpec((count, LANES), lambda pair, phase: (0, pair + low + pairs * phase)),
-        ]
-        out_shape = [
-            jax.ShapeDtypeStruct((tokens, width), BF),
-            jax.ShapeDtypeStruct((count, 2 * width), BF),
-        ]
-        kept = [pltpu.VMEM((count, LANES), BF)]
-    aliases = {len(operands) + i: i for i in range(len(before))}
-    specs += [pl.BlockSpec(memory_space=pl.ANY)] * len(before)
-    operands += list(before)
+        kernel = functools.partial(cross_back_kernel, chunk, valid, width)
+        out_specs = [columns(tokens)] + out_specs
+        out_shape = [jax.ShapeDtypeStruct((tokens, width), BF)] + out_shape
     return pl.pallas_call(
         kernel,
-        grid=grid,
+        grid=(pairs,),
         in_specs=specs,
         out_specs=out_specs,
         out_shape=out_shape,
-        scratch_shapes=kept,
-        input_output_aliases=aliases,
-        compiler_params=pltpu.CompilerParams(vmem_limit_bytes=32 << 20),
+        compiler_params=pltpu.CompilerParams(vmem_limit_bytes=40 << 20),
         cost_estimate=pl.CostEstimate(
-            flops=40 * tokens * count * width // parts,
-            transcendentals=tokens * count * width // HD // parts,
-            bytes_accessed=8 * (tokens + count) * width // parts,
+            flops=40 * tokens * count * width,
+            transcendentals=tokens * count * width // HD,
+            bytes_accessed=8 * (tokens + count) * width,
         ),
         name="attend_causal_back" if causal else "attend_cross_back",
     )(*operands)
@@ -390,6 +363,34 @@
 
 def tied(*members):
     return lax.optimization_barrier(members)
+
+
+def join_kernel(*refs):
+    start = 0
+    for member in refs[:-1]:
+        refs[-1][:, start : start + member.shape[1]] = member[...]
+        start += member.shape[1]
+
+
+def join(*members):
+    rows, step = members[0].shape[0], 128
+    widths = [member.shape[1] for member in members]
+
+    def strip(width):
+        return pl.BlockSpec((step, width), lambda i: (i, 0))
+
+    return pl.pallas_call(
+        join_kernel,
+        grid=(rows // step,),
+        in_specs=[strip(width) for width in widths],
+        out_specs=strip(sum(widths)),
+        out_shape=jax.ShapeDtypeStruct((rows, sum(widths)), BF),
+        compiler_params=pltpu.CompilerParams(vmem_limit_bytes=16 << 20),
+        cost_estimate=pl.CostEstimate(
+            flops=0, transcendentals=0, bytes_accessed=4 * rows * sum(widths)
+        ),
+        name="join",
+    )(*members)
 
 
 def place_kernel(parts, here_ref, *refs):
@@ -596,27 +597,14 @@
     grad_w_cross_out = weight_grad(cross_mix, grad_cross_low)
     grad_cross_mix = product_back(grad_cross_low, full_cross_out).astype(BF)
 
-    cross_back = functools.partial(
-        attend_back,
-        cross_sources,
-        cross_mix,
-        logs=cross_log,
-        places=None,
-        chunk=padded,
-        valid=frames,
-        width=width,
-        parts=2,
-    )
-    first_part = cross_back(grads=grad_cross_mix)
-    if swift:
-        grad_cross_mix, part_outer, *first_part = tied(grad_cross_mix, part_outer, *first_part)
+    grad_cross_queries, grad_pair = attend_back(
+        cross_sources, cross_mix, grad_cross_mix, cross_log, None, padded, frames, width
+    )
+    if swift:
+        part_outer, grad_cross_queries, grad_pair = tied(
+            part_outer, grad_cross_queries, grad_pair
+        )
         outer_sum, outer_in = grid.hop_one(part_outer)
-    grad_cross_queries, grad_pair = cross_back(
-        grads=grad_cross_mix, part=1, before=tuple(first_part)
-    )
-    if swift:
-        grad_cross_queries, grad_pair, outer_in = tied(grad_cross_queries, grad_pair, outer_in)
-        outer_sum, outer_in = grid.hop_two(outer_sum, outer_in)
     grad_frames = product_back(grad_pair, full_cross_kv).astype(BF)
     grad_frames, grad_pair = tied(grad_frames, grad_pair)
     grad_encoded = grid.hand_back(grad_frames)
@@ -625,8 +613,7 @@
         grad_w_cross_kv, grad_cross_queries, outer_in = tied(
             grad_w_cross_kv, grad_cross_queries, outer_in
         )
-        outer_sum, outer_in = grid.hop_three(outer_sum, outer_in)
-    part_kv = scattered(grad_w_cross_kv)
+        outer_sum, outer_in = grid.hop_two(outer_sum, outer_in)
     grad_bias_four = jnp.sum(grad_pair[:, width:].astype(F32), axis=0)
     grad_w_cross_q = weight_grad(normed_two, grad_cross_queries)
     grad_bias_three = jnp.sum(grad_cross_queries.astype(F32), axis=0)
@@ -637,16 +624,14 @@
     grad_w_self_out = weight_grad(self_mix, grad_self_low)
     grad_bias_two = jnp.sum(grad_after_self, axis=0)
     grad_self_mix = product_back(grad_self_low, full_self_out).astype(BF)
-    middle = [grad_w_cross_out, grad_w_cross_q, grad_w_self_out]
-    if swift:
-        grad_self_mix, *middle = tied(grad_self_mix, *middle)
-        middle_kept, middle_core = grid.fold_core(*middle)
+    grad_w_middle = join(grad_w_cross_out, grad_w_cross_q, grad_w_self_out, grad_w_cross_kv)
+    grad_w_middle, grad_self_mix = tied(grad_w_middle, grad_self_mix)
+    part_middle = scattered(grad_w_middle)
     (grad_pre,) = attend_back(
         self_sources, self_mix, grad_self_mix, self_log, places, tokens, tokens, width
     )
     if swift:
-        grad_pre, middle_core, part_inner = tied(grad_pre, middle_core, part_inner)
-        middle_own, middle_near = grid.fold_chips(middle_kept, middle_core)
+        grad_pre, part_inner = tied(grad_pre, part_inner)
         inner_sum, inner_in = grid.hop_one(part_inner)
     grad_normed_one = product_back(grad_pre, full_qkv)
     grad_w_qkv = weight_grad(normed_one, grad_pre)
@@ -694,34 +679,28 @@
         inner_sum, inner_in = grid.hop_two(inner_sum, inner_in)
     leaving = grid.hand_back(leaving)
     if swift:
-        part_middle = jnp.concatenate([plus_all(middle_own, middle_near), part_kv], axis=1)
-        middle_sum, middle_in = grid.hop_one(part_middle)
-        middle_in, inner_in, outer_in, grad_encoded, *last_near = tied(
-            middle_in, inner_in, outer_in, grad_encoded, *last_near
+        inner_in, outer_in, grad_encoded, leaving, *last_near = tied(
+            inner_in, outer_in, grad_encoded, leaving, *last_near
         )
         part_last = plus_all(last_own, last_near)
-        half = 12 * LANES
-        last_one, one_in = grid.hop_one(part_last[:, :half])
-        last_two, two_in = grid.hop_one(part_last[:, half:])
+        last_sum, last_in = grid.hop_one(part_last)
+        outer_sum, outer_in = grid.hop_three(outer_sum, outer_in)
         inner_sum, inner_in = grid.hop_three(inner_sum, inner_in)
+        last_in, part_middle = tied(last_in, part_middle)
+        middle_sum, middle_in = grid.hop_one(part_middle)
+        last_sum, last_in = grid.hop_two(last_sum, last_in)
+        last_in, middle_in = tied(last_in, middle_in)
         middle_sum, middle_in = grid.hop_two(middle_sum, middle_in)
+        last_sum, last_in = grid.hop_three(last_sum, last_in)
+        outer_in, inner_in, middle_in = tied(outer_in, inner_in, middle_in)
+        middle_sum, middle_in = grid.hop_three(middle_sum, middle_in)
         total_outer = grid.hop_end(outer_sum, outer_in)
-        last_one, one_in = grid.hop_two(last_one, one_in)
-        last_two, two_in = grid.hop_two(last_two, two_in)
-        middle_sum, middle_in = grid.hop_three(middle_sum, middle_in)
         total_inner = grid.hop_end(inner_sum, inner_in)
-        last_one, one_in = grid.hop_three(last_one, one_in)
-        last_two, two_in = grid.hop_three(last_two, two_in)
+        total_last = grid.hop_end(last_sum, last_in)
         total_middle = grid.hop_end(middle_sum, middle_in)
-        total_last = jnp.concatenate(
-            [grid.hop_end(last_one, one_in), grid.hop_end(last_two, two_in)], axis=1
-        )
         total_qkv = total_last[:, : grad_w_qkv.shape[1]]
         mine = total_last[:kinds, grad_w_qkv.shape[1] :]
     else:
-        part_middle = jnp.concatenate(
-            [scattered(jnp.concatenate(middle, axis=1)), part_kv], axis=1
-        )
         total_outer = grid.seq_sum(part_outer)
         total_inner = grid.seq_sum(part_inner)
         total_middle = grid.seq_sum(part_middle)

time: 601 us -> 587 us (0.977)
  local copies, waits for them, and re-layouts: 61.4 us -> 50.1 us
  starting transfers between devices: 74.3 us -> 85.1 us
  other arithmetic: 56.9 us -> 48.5 us
  waiting for transfers between devices: 185 us -> 193 us
    ppermute x18 -> x14, waiting for transfers between devices: 91.7 us -> 64.2 us  [flip(): lax.ppermute(values, 'fsdp', [(f, f ^ bits) for f in range(self.fsdp)])]
    all_to_all x2, waiting for transfers between devices: 0.01 us -> 23.7 us  [hand_back(): lax.all_to_all(parts, 'seq', split_axis=0, concat_axis=0, tiled=True)]
    ppermute x15 -> x12, waiting for transfers between devices: 74.2 us -> 90.5 us  [chain(): return lax.ppermute(values, AXES, pairs)]
    reduce_scatter x3, starting transfers between devices: 0.3 us -> 11.7 us  [scattered(): return lax.psum_scatter(member, 'fsdp', scatter_dimension=0, tiled=True)]
    squeeze x7 -> x3, local copies, waits for them, and re-layouts: 10.3 us -> 2.01 us  [pick(): return lax.dynamic_index_in_dim(values, index, axis, keepdims=False)]
    unnamed x166 -> x140, local copies, waits for them, and re-layouts: 34 us -> 28.6 us
    ppermute x15 -> x12, starting transfers between devices: 27.3 us -> 31.3 us  [chain(): return lax.ppermute(values, AXES, pairs)]
    ppermute x18 -> x14, starting transfers between devices: 17.8 us -> 14.3 us  [flip(): lax.ppermute(values, 'fsdp', [(f, f ^ bits) for f in range(self.fsdp)])]
  transfers between devices with their start and end apart: 46 -> 39, of which waited for: 19 -> 16; matrix products, arithmetic and copies ran while one was open for 32% -> 29% of each run, Pallas kernels for 14% -> 14%
where the time goes in v5:
time: 587 us; the launch traced here: 584 us
  waiting for transfers between devices  193 us (33%)
  matrix products  110 us (19%)
  starting transfers between devices  85.1 us (14%)
  Pallas kernels  82 us (14%)
  local copies, waits for them, and re-layouts  50.1 us (9%)
  other arithmetic  48.5 us (8%)
  between operations  15.5 us (3%)
    ppermute x12, waiting for transfers between devices, chain(): return lax.ppermute(values, AXES, pairs)  90.5 us
    ppermute x14, waiting for transfers between devices, flip(): lax.ppermute(values, 'fsdp', [(f, f ^ bits) for f in range(self.fsdp)])  64.2 us
    dot_general x7, matrix products, product_back(): lax.dot_general(incoming, weight, (((1,), (1,)), ((), ())), preferred_ele...  47.5 us
    pallas_call x2, Pallas kernels, attend_back(): pl.pallas_call(kernel, grid=(pairs,), in_specs=specs, out_specs=out_specs...  44 us
    dot_general x7, matrix products, weight_grad(): lax.dot_general(operand, incoming, (((0,), (0,)), ((), ())), preferred_el...  32.6 us
    ppermute x12, starting transfers between devices, chain(): return lax.ppermute(values, AXES, pairs)  31.3 us
    dot_general x7, matrix products, product(): return jnp.dot(first, second, preferred_element_type=F32)  29.8 us
    pallas_call x2, Pallas kernels, attend(): pl.pallas_call(functools.partial(forward_kernel, chunk, valid, causal), g...  29.7 us
  transfers between devices with their start and end apart: 39, of which 16 were waited for; matrix products, arithmetic and copies ran while one was open for 29% of the time, Pallas kernels for 14%

profile of v5, /device:TPU:0, one launch (start us, length us, event | category | flops | bytes accessed | tf_op | source)
XLA Modules:
  0.0 583.7 jit_solution(1812326832220968763)
XLA Ops:
  17.0 5.6 collective-permute-start.2
  27.1 25.7 %collective-permute-done.1 = bf16[128,3200]{1,0:T(8,128)(2,1)} collective-permute-done((bf16[128,3200]{1,0:T(8,128)(2,1)}, bf16[128,3200]{1,0:T(8,128)(2,1)}, u32[]{:S(2)}, u32[]{:S(2)}) %collective-permute-start.1) | collective-permute-done | bytes 819232 | tf_op jit(solution)/shard_map/ppermute | solution.py:306
  66.8 17.6 %collective-permute-done.5 = bf16[64,3200]{1,0:T(8,128)(2,1)S(1)} collective-permute-done((bf16[64,3200]{1,0:T(8,128)(2,1)S(1)}, bf16[64,3200]{1,0:T(8,128)(2,1)S(1)}, u32[]{:S(2)}, u32[]{:S(2)}) %collective-permute-start.5) | collective-permute-done | bytes 409632 | tf_op jit(solution)/shard_map/ppermute | solution.py:306
  84.8 10.9 %collective-permute-done.6.refs_2_ = bf16[487,1024]{1,0:T(8,128)(2,1)S(1)} collective-permute-done((bf16[487,1024]{1,0:T(8,128)(2,1)S(1)}, bf16[487,1024]{1,0:T(8,128)(2,1)S(1)}, u32[]{:S(2)}, u32[]{:S(2)}) %collective-permute-start.6) | collective-permute-done | bytes 997408 | tf_op jit(solution)/shard_map/ppermute | solution.py:275
  113.4 8.8 %attend_causal.1 = (bf16[448,1024]{1,0:T(8,128)(2,1)S(1)}, f32[8,1,896]{2,1,0:T(1,128)S(1)}) custom-call(bf16[448,3072]{1,0:T(8,128)(2,1)S(1)} %multiply_convert_fusion.1.refs_0_.refs_1_.refs_2_, bf16[448,3072]{1,0:T(8,128)(2,1)S(1)} %multiply_convert_fusion.1.refs_0_.refs_1_.refs_2_, bf16[448,3072]{1,0:T(8,128)(2,1)S(1)} %multiply_convert_fusion.1.refs_0_.refs_1_.refs_2_, ...), custom_call_target="tpu_custom_call" | custom-call | flops 3288334336 | bytes 3670016 | tf_op jit(solution)/shard_map/attend_causal/pallas_call | solution.py:156
  137.2 7.2 %add_convert_fusion.refs_1_.refs_2_ = bf16[1536,2048]{1,0:T(8,128)(2,1)S(1)} fusion(bf16[1536,1024]{1,0:T(8,128)(2,1)S(1)} %copy-done.11, f32[2048]{0:T(1024)S(1)} %concatenate.52, bf16[1024,4096]{1,0:T(8,128)(2,1)S(1)} %copy-done.56), kind=kOutput, calls=%fused_computation | convolution fusion | flops 6448742400 | bytes 13639680 | tf_op jit(solution)/shard_map/dot_general | solution.py:211
  144.4 20.9 %attend_cross.1 = (bf16[448,1024]{1,0:T(8,128)(2,1)S(1)}, f32[8,1,896]{2,1,0:T(1,128)S(1)}) custom-call(bf16[448,1024]{1,0:T(8,128)(2,1)S(1)} %multiply_convert_fusion.2.refs_0_, bf16[1536,2048]{1,0:T(8,128)(2,1)S(1)} %add_convert_fusion.refs_1_.refs_2_, bf16[1536,2048]{1,0:T(8,128)(2,1)S(1)} %add_convert_fusion.refs_1_.refs_2_), custom_call_target="tpu_custom_call" | custom-call | flops 11274289152 | bytes 8126464 | tf_op jit(solution)/shard_map/attend_cross/pallas_call | solution.py:156
  174.9 7.0 %multiply_convert_fusion = (bf16[448,4096]{1,0:T(8,128)(2,1)S(1)}, f32[448,4096]{1,0:T(8,128)}) fusion(f32[4096]{0:T(1024)S(1)} %convert.78, bf16[1024,5120]{1,0:T(8,128)(2,1)S(1)} %copy-done.55, f32[448,1024]{1,0:T(8,128)S(1)} %get-tuple-element.207, f32[1024]{0:T(1024)S(1)} %bitcast.160, f32[1024]{0:T(1024)S(1)} %bitcast.150, f32[448]{0:T(512)S(1)} %add_rsqrt_fusion, ...), kind=kOutput, calls=%fused_computation.13 | convolution fusion | flops 3771400192 | bytes 21262336 | tf_op jit(solution)/shard_map/dot_general | solution.py:211
  187.9 6.9 %convolution_convert_fusion.1 = bf16[4096,1024]{1,0:T(8,128)(2,1)} fusion(bf16[448,4096]{1,0:T(8,128)(2,1)S(1)} %get-tuple-element.131, bf16[448,1024]{1,0:T(8,128)(2,1)S(1)} %place.3), kind=kOutput, calls=%fused_computation.3 | convolution fusion | flops 3762290688 | bytes 12976128 | tf_op jit(solution)/shard_map/dot_general | solution.py:221
  195.2 11.6 %reduce-scatter.6.cloned.1.call-start = ((), (), s32[]{:S(2)}) async-start(), calls=%async_computation.8 | async-start | bytes 9437184 | tf_op jit(solution)/shard_map/reduce_scatter | solution.py:506
  206.8 5.1 assemble.3
  211.9 10.3 %fusion.70 = (bf16[4096]{0:T(1024)(128)(2,1)S(1)}, bf16[448,4096]{1,0:T(8,128)(2,1)S(1)}) fusion(f32[448,4096]{1,0:T(8,128)} %get-tuple-element.209, f32[4096]{0:T(1024)S(1)} %convert.78, bf16[448,1024]{1,0:T(8,128)(2,1)S(1)} %place.3, bf16[4096,1024]{1,0:T(8,128)(2,1)S(1)} %assemble.3), kind=kOutput, calls=%fused_computation.169 | convolution fusion | flops 3780112384 | bytes 20340736 | tf_op jit(solution)/shard_map/dot_general | solution.py:215
  224.1 7.1 %convolution_convert_fusion = bf16[1024,4096]{1,0:T(8,128)(2,1)} fusion(bf16[448,4096]{1,0:T(8,128)(2,1)S(1)} %get-tuple-element.112, f32[448,1024]{1,0:T(8,128)S(1)} %copy-done.26, f32[1024]{0:T(1024)S(1)} %bitcast.161, f32[1024]{0:T(1024)S(1)} %bitcast.151, f32[448]{0:T(512)S(1)} %add_rsqrt_fusion, f32[448]{0:T(512)S(1)} %broadcast_multiply_fusion.6), kind=kOutput, calls=%fused_computation.2 | convolution fusion | flops 3764584448 | bytes 13905408 | tf_op jit(solution)/shard_map/dot_general | solution.py:221
  231.5 8.4 %multiply_reduce_fusion = (bf16[1024]{0:T(1024)(128)(2,1)S(1)}, f32[448]{0:T(512)S(1)}, f32[448]{0:T(512)S(1)}, bf16[1024]{0:T(1024)(128)(2,1)S(1)}, f32[448,1024]{1,0:T(8,128)S(1)}) fusion(f32[448,1024]{1,0:T(8,128)S(1)} %copy-done.26, f32[448]{0:T(512)S(1)} %add_rsqrt_fusion, f32[448]{0:T(512)S(1)} %broadcast_multiply_fusion.6, f32[1024]{0:T(1024)S(1)} %bitcast.152, ...), kind=kOutput, calls=%fused_computation.71 | convolution fusion | flops 3762222080 | bytes 15744000 | tf_op jit(solution)/shard_map/dot_general | solution.py:215
  245.3 31.9 %attend_cross_back.1 = (bf16[448,1024]{1,0:T(8,128)(2,1)S(1)}, bf16[1536,2048]{1,0:T(8,128)(2,1)S(1)}) custom-call(bf16[448,1024]{1,0:T(8,128)(2,1)S(1)} %copy-done.20, bf16[1536,2048]{1,0:T(8,128)(2,1)} %copy-done.21, bf16[1536,2048]{1,0:T(8,128)(2,1)} %copy-done.21, bf16[448,1024]{1,0:T(8,128)(2,1)S(1)} %copy-done.18, ...), custom_call_target="tpu_custom_call" | custom-call | flops 28185722880 | bytes 16252928 | tf_op jit(solution)/shard_map/attend_cross_back/pallas_call | solution.py:194
  285.0 11.6 %convolution_convert_fusion.4 = bf16[1536,1024]{1,0:T(8,128)(2,1)} fusion(bf16[1536,2048]{1,0:T(8,128)(2,1)} %copy-done.6, bf16[1024,4096]{1,0:T(8,128)(2,1)} %all-gather.3.cloned.1.call-done), kind=kOutput, calls=%fused_computation.20 | convolution fusion | flops 6444023808 | bytes 13631488 | tf_op jit(solution)/shard_map/dot_general | solution.py:215
  296.6 4.6 all-to-all-start
  301.3 10.6 %convolution_convert_fusion.3.refs_3_ = bf16[1024,2048]{1,0:T(8,128)(2,1)S(1)} fusion(bf16[1536,1024]{1,0:T(8,128)(2,1)} %copy-done.10, bf16[1536,2048]{1,0:T(8,128)(2,1)} %copy-done.6), kind=kOutput, calls=%fused_computation.19 | convolution fusion | flops 6444548096 | bytes 13631488 | tf_op jit(solution)/shard_map/dot_general | solution.py:221
  332.1 12.1 %attend_causal_back.1 = bf16[448,3072]{1,0:T(8,128)(2,1)S(1)} custom-call(bf16[448,3072]{1,0:T(8,128)(2,1)S(1)} %copy-done.13, bf16[448,3072]{1,0:T(8,128)(2,1)S(1)} %copy-done.13, bf16[448,3072]{1,0:T(8,128)(2,1)S(1)} %copy-done.13, bf16[448,1024]{1,0:T(8,128)(2,1)S(1)} %copy-done.16, bf16[448,1024]{1,0:T(8,128)(2,1)S(1)} %fusion.48.refs_4_, ...), custom_call_target="tpu_custom_call" | custom-call | flops 8220835840 | bytes 7340032 | tf_op jit(solution)/shard_map/attend_causal_back/pallas_call | solution.py:194
  348.3 7.7 %fusion.32 = (f32[448]{0:T(512)S(1)}, bf16[1024]{0:T(1024)(128)(2,1)S(1)}, f32[448]{0:T(512)S(1)}, bf16[1024]{0:T(1024)(128)(2,1)S(1)}, f32[448,1024]{1,0:T(8,128)S(1)}) fusion(bf16[448,1024]{1,0:T(8,128)(2,1)S(1)} %copy-done.3, f32[1024]{0:T(1024)S(1)} %bitcast.140, f32[448]{0:T(512)S(1)} %copy-done.45, f32[448]{0:T(512)S(1)} %copy-done.41, ...), kind=kOutput, calls=%fused_computation.62 | convolution fusion | flops 2823156736 | bytes 11811840 | tf_op jit(solution)/shard_map/dot_general | solution.py:215
  367.4 6.4 %collective-permute-start.17 = (bf16[128,4096]{1,0:T(8,128)(2,1)}, bf16[128,4096]{1,0:T(8,128)(2,1)}, u32[]{:S(2)}, u32[]{:S(2)}) collective-permute-start(bf16[128,4096]{1,0:T(8,128)(2,1)} %reduce-scatter.6.cloned.1.call-done), channel_id=1, source_target_pairs={{0,1},{3,2},{4,5},{7,6},{8,9},{11,10},{12,13},{15,14},{16,17},{19,... | collective-permute-start | bytes 3145736 | tf_op jit(solution)/shard_map/ppermute | solution.py:303
  383.3 4.5 all-to-all-start.1
  387.8 9.0 %collective-permute-done.17 = bf16[128,4096]{1,0:T(8,128)(2,1)} collective-permute-done((bf16[128,4096]{1,0:T(8,128)(2,1)}, bf16[128,4096]{1,0:T(8,128)(2,1)}, u32[]{:S(2)}, u32[]{:S(2)}) %collective-permute-start.17) | collective-permute-done | bytes 1048608 | tf_op jit(solution)/shard_map/ppermute | solution.py:303
  411.5 23.7 %all-to-all-done.1 = bf16[4,224,1024]{2,1,0:T(8,128)(2,1)} async-done(((bf16[4,224,1024]{2,1,0:T(8,128)(2,1)}), bf16[4,224,1024]{2,1,0:T(8,128)(2,1)}, u32[]{:S(2)}, u32[]{:S(2)}) %all-to-all-start.1) | async-done | bytes 1835040 | tf_op jit(solution)/shard_map/all_to_all | solution.py:294
  437.7 4.9 collective-permute-done.23
  442.5 13.2 %collective-permute-done.22 = bf16[128,3200]{1,0:T(8,128)(2,1)} collective-permute-done((bf16[128,3200]{1,0:T(8,128)(2,1)}, bf16[128,3200]{1,0:T(8,128)(2,1)}, u32[]{:S(2)}, u32[]{:S(2)}) %collective-permute-start.22) | collective-permute-done | bytes 819232 | tf_op jit(solution)/shard_map/ppermute | solution.py:306
  459.2 6.0 %collective-permute-start.24 = (bf16[128,3200]{1,0:T(8,128)(2,1)}, bf16[128,3200]{1,0:T(8,128)(2,1)}, u32[]{:S(2)}, u32[]{:S(2)}) collective-permute-start(bf16[128,3200]{1,0:T(8,128)(2,1)} %fusion.41), channel_id=1, source_target_pairs={{0,1},{3,2},{4,5},{7,6},{8,9},{11,10},{12,13},{15,14},{16,17},{19,... | collective-permute-start | bytes 2457608 | tf_op jit(solution)/shard_map/ppermute | solution.py:303
  468.5 13.1 %collective-permute-done.24 = bf16[128,3200]{1,0:T(8,128)(2,1)} collective-permute-done((bf16[128,3200]{1,0:T(8,128)(2,1)}, bf16[128,3200]{1,0:T(8,128)(2,1)}, u32[]{:S(2)}, u32[]{:S(2)}) %collective-permute-start.24) | collective-permute-done | bytes 819232 | tf_op jit(solution)/shard_map/ppermute | solution.py:303
  481.6 4.5 collective-permute-start.26
  494.5 18.5 %collective-permute-done.26 = bf16[128,5120]{1,0:T(8,128)(2,1)S(1)} collective-permute-done((bf16[128,5120]{1,0:T(8,128)(2,1)}, bf16[128,5120]{1,0:T(8,128)(2,1)S(1)}, u32[]{:S(2)}, u32[]{:S(2)}) %collective-permute-start.26) | collective-permute-done | bytes 1310752 | tf_op jit(solution)/shard_map/ppermute | solution.py:303
  515.6 17.8 %collective-permute-done.27 = bf16[128,3200]{1,0:T(8,128)(2,1)S(1)} collective-permute-done((bf16[128,3200]{1,0:T(8,128)(2,1)S(1)}, bf16[128,3200]{1,0:T(8,128)(2,1)S(1)}, u32[]{:S(2)}, u32[]{:S(2)}) %collective-permute-start.27) | collective-permute-done | bytes 819232 | tf_op jit(solution)/shard_map/ppermute | solution.py:303
  542.3 32.1 %collective-permute-done.31 = bf16[128,5120]{1,0:T(8,128)(2,1)S(1)} collective-permute-done((bf16[128,5120]{1,0:T(8,128)(2,1)S(1)}, bf16[128,5120]{1,0:T(8,128)(2,1)S(1)}, u32[]{:S(2)}, u32[]{:S(2)}) %collective-permute-start.31) | collective-permute-done | bytes 1310752 | tf_op jit(solution)/shard_map/ppermute | solution.py:303
  (306 shorter events, 183.0 us)
Async XLA Ops:
  7.2 116.6 %all-gather.3.cloned.1.call-start = ((), (), s32[]{:S(2)}) async-start(), calls=%async_computation.5 | async-start | bytes 9437184 | tf_op jit(solution)/shard_map/all_gather | solution.py:502
  9.6 159.4 %all-gather.5.cloned.1.call-start = ((), (), s32[]{:S(2)}) async-start(), calls=%async_computation.6 | async-start | bytes 11796480 | tf_op jit(solution)/shard_map/all_gather | solution.py:502
  11.9 268.8 %reduce-scatter.4.cloned.1.call-start = ((), (), s32[]{:S(2)}) async-start(), calls=%async_computation.7 | async-start | bytes 9437184 | tf_op jit(solution)/shard_map/reduce_scatter | solution.py:506
  15.7 37.1 %collective-permute-start.3 = (bf16[487,1024]{1,0:T(8,128)(2,1)}, bf16[487,1024]{1,0:T(8,128)(2,1)S(1)}, u32[]{:S(2)}, u32[]{:S(2)}) collective-permute-start(bf16[487,1024]{1,0:T(8,128)(2,1)} %get-tuple-element.174), channel_id=1, source_target_pairs={{1,0},{2,1},{3,2},{4,7},{6,5},{7,6},{9,8},{10,9},{11,10},{12,15},{... | collective-permute-start | bytes 2992136 | tf_op jit(solution)/shard_map/ppermute | solution.py:275
  17.0 38.9 %collective-permute-start.2 = (bf16[487,1024]{1,0:T(8,128)(2,1)}, bf16[487,1024]{1,0:T(8,128)(2,1)}, u32[]{:S(2)}, u32[]{:S(2)}) collective-permute-start(bf16[487,1024]{1,0:T(8,128)(2,1)} %get-tuple-element.175), channel_id=1, source_target_pairs={{0,1},{1,2},{3,0},{4,5},{5,6},{6,7},{8,9},{9,10},{11,8},{12,13},{1... | collective-permute-start | bytes 2992136 | tf_op jit(solution)/shard_map/ppermute | solution.py:275
  23.7 29.1 %collective-permute-start.1 = (bf16[128,3200]{1,0:T(8,128)(2,1)}, bf16[128,3200]{1,0:T(8,128)(2,1)}, u32[]{:S(2)}, u32[]{:S(2)}) collective-permute-start(bf16[128,3200]{1,0:T(8,128)(2,1)} %get-tuple-element.184), channel_id=1, source_target_pairs={{0,16},{4,20},{8,24},{12,28},{16,0},{20,4},{24,8},{28,12},{1,17},{... | collective-permute-start | bytes 2457608 | tf_op jit(solution)/shard_map/ppermute | solution.py:306
  25.6 27.2 %collective-permute-start = (bf16[128,3200]{1,0:T(8,128)(2,1)}, bf16[128,3200]{1,0:T(8,128)(2,1)}, u32[]{:S(2)}, u32[]{:S(2)}) collective-permute-start(bf16[128,3200]{1,0:T(8,128)(2,1)} %get-tuple-element.184), channel_id=1, source_target_pairs={{0,8},{4,12},{8,0},{12,4},{16,24},{20,28},{24,16},{28,20},{1,9},{5... | collective-permute-start | bytes 2457608 | tf_op jit(solution)/shard_map/ppermute | solution.py:306
  57.2 38.5 %collective-permute-start.6 = (bf16[487,1024]{1,0:T(8,128)(2,1)S(1)}, bf16[487,1024]{1,0:T(8,128)(2,1)S(1)}, u32[]{:S(2)}, u32[]{:S(2)}) collective-permute-start(bf16[487,1024]{1,0:T(8,128)(2,1)S(1)} %dynamic-slice_bitcast_fusion.2), channel_id=1, source_target_pairs={{0,2},{2,0},{3,1},{4,6},{5,7},{7,5},{8,10},{10,8},{11,9},{12,14},{... | collective-permute-start | bytes 2992136 | tf_op jit(solution)/shard_map/ppermute | solution.py:275
  63.7 20.7 %collective-permute-start.5 = (bf16[64,3200]{1,0:T(8,128)(2,1)S(1)}, bf16[64,3200]{1,0:T(8,128)(2,1)S(1)}, u32[]{:S(2)}, u32[]{:S(2)}) collective-permute-start(bf16[64,3200]{1,0:T(8,128)(2,1)S(1)} %slice.149), channel_id=1, source_target_pairs={{0,16},{4,20},{8,24},{12,28},{16,0},{20,4},{24,8},{28,12},{1,17},{... | collective-permute-start | bytes 1228808 | tf_op jit(solution)/shard_map/ppermute | solution.py:306
  103.6 61.7 %collective-permute-start.9 = (bf16[512,1024]{1,0:T(8,128)(2,1)}, bf16[512,1024]{1,0:T(8,128)(2,1)}, u32[]{:S(2)}, u32[]{:S(2)}) collective-permute-start(bf16[512,1024]{1,0:T(8,128)(2,1)} %param.27), channel_id=1, source_target_pairs={{0,16},{4,20},{8,24},{12,28},{16,0},{20,4},{24,8},{28,12},{1,17},{... | collective-permute-start | bytes 3145736 | tf_op jit(solution)/shard_map/ppermute | solution.py:306
  105.1 60.3 %collective-permute-start.8 = (bf16[512,1024]{1,0:T(8,128)(2,1)}, bf16[512,1024]{1,0:T(8,128)(2,1)}, u32[]{:S(2)}, u32[]{:S(2)}) collective-permute-start(bf16[512,1024]{1,0:T(8,128)(2,1)} %param.27), channel_id=1, source_target_pairs={{0,8},{4,12},{8,0},{12,4},{16,24},{20,28},{24,16},{28,20},{1,9},{5... | collective-permute-start | bytes 3145736 | tf_op jit(solution)/shard_map/ppermute | solution.py:306
  129.7 35.6 %collective-permute-start.12 = (bf16[112,1024]{1,0:T(8,128)(2,1)S(1)}, bf16[112,1024]{1,0:T(8,128)(2,1)S(1)}, u32[]{:S(2)}, u32[]{:S(2)}) collective-permute-start(bf16[112,1024]{1,0:T(8,128)(2,1)S(1)} %get-tuple-element.185), channel_id=1, source_target_pairs={{1,0},{2,1},{3,2},{4,7},{6,5},{7,6},{9,8},{10,9},{11,10},{12,15},{... | collective-permute-start | bytes 688136 | tf_op jit(solution)/shard_map/ppermute | solution.py:275
  131.0 34.3 %collective-permute-start.11 = (bf16[112,1024]{1,0:T(8,128)(2,1)S(1)}, bf16[112,1024]{1,0:T(8,128)(2,1)S(1)}, u32[]{:S(2)}, u32[]{:S(2)}) collective-permute-start(bf16[112,1024]{1,0:T(8,128)(2,1)S(1)} %get-tuple-element.186), channel_id=1, source_target_pairs={{0,2},{2,0},{3,1},{4,6},{5,7},{7,5},{8,10},{10,8},{11,9},{12,14},{... | collective-permute-start | bytes 688136 | tf_op jit(solution)/shard_map/ppermute | solution.py:275
  133.0 32.4 %collective-permute-start.10 = (bf16[112,1024]{1,0:T(8,128)(2,1)S(1)}, bf16[112,1024]{1,0:T(8,128)(2,1)S(1)}, u32[]{:S(2)}, u32[]{:S(2)}) collective-permute-start(bf16[112,1024]{1,0:T(8,128)(2,1)S(1)} %get-tuple-element.187), channel_id=1, source_target_pairs={{0,1},{1,2},{3,0},{4,5},{5,6},{6,7},{8,9},{9,10},{11,8},{12,13},{1... | collective-permute-start | bytes 688136 | tf_op jit(solution)/shard_map/ppermute | solution.py:275
  195.2 150.6 %reduce-scatter.6.cloned.1.call-start = ((), (), s32[]{:S(2)}) async-start(), calls=%async_computation.8 | async-start | bytes 9437184 | tf_op jit(solution)/shard_map/reduce_scatter | solution.py:506
  280.7 31.2 %collective-permute-start.16 = (bf16[512,1024]{1,0:T(8,128)(2,1)}, bf16[512,1024]{1,0:T(8,128)(2,1)}, u32[]{:S(2)}, u32[]{:S(2)}) collective-permute-start(bf16[512,1024]{1,0:T(8,128)(2,1)} %reduce-scatter.4.cloned.1.call-done), channel_id=1, source_target_pairs={{0,1},{3,2},{4,5},{7,6},{8,9},{11,10},{12,13},{15,14},{16,17},{19,... | collective-permute-start | bytes 3145736 | tf_op jit(solution)/shard_map/ppermute | solution.py:303
  296.6 86.7 %all-to-all-start = ((bf16[4,384,1024]{2,1,0:T(8,128)(2,1)}), bf16[4,384,1024]{2,1,0:T(8,128)(2,1)}, u32[]{:S(2)}, u32[]{:S(2)}) async-start(bf16[4,384,1024]{2,1,0:T(8,128)(2,1)} %bitcast.134), calls=%async_computation.2 | async-start | bytes 6291456 | tf_op jit(solution)/shard_map/all_to_all | solution.py:294
  301.2 180.3 %reduce-scatter.8.cloned.1.call-start = ((), (), s32[]{:S(2)}) async-start(), calls=%async_computation.9 | async-start | bytes 11796480 | tf_op jit(solution)/shard_map/reduce_scatter | solution.py:506
  361.1 22.2 %collective-permute-start.20 = (bf16[4,128,3200]{2,1,0:T(8,128)(2,1)S(1)}, bf16[4,128,3200]{2,1,0:T(8,128)(2,1)}, u32[]{:S(2)}, u32[]{:S(2)}) collective-permute-start(bf16[4,128,3200]{2,1,0:T(8,128)(2,1)S(1)} %pad_maximum_fusion.2), channel_id=1, source_target_pairs={{0,4},{4,0},{8,12},{12,8},{16,20},{20,16},{24,28},{28,24},{1,5},{5... | collective-permute-start | bytes 9830408 | tf_op jit(solution)/shard_map/ppermute | solution.py:306
  365.7 72.0 %collective-permute-start.19 = (bf16[512,1024]{1,0:T(8,128)(2,1)}, bf16[512,1024]{1,0:T(8,128)(2,1)}, u32[]{:S(2)}, u32[]{:S(2)}) collective-permute-start(bf16[512,1024]{1,0:T(8,128)(2,1)} %add_convert_fusion.6), channel_id=1, source_target_pairs={{1,2},{2,1},{5,6},{6,5},{9,10},{10,9},{13,14},{14,13},{17,18},{18,... | collective-permute-start | bytes 3145736 | tf_op jit(solution)/shard_map/ppermute | solution.py:303
  367.4 29.4 %collective-permute-start.17 = (bf16[128,4096]{1,0:T(8,128)(2,1)}, bf16[128,4096]{1,0:T(8,128)(2,1)}, u32[]{:S(2)}, u32[]{:S(2)}) collective-permute-start(bf16[128,4096]{1,0:T(8,128)(2,1)} %reduce-scatter.6.cloned.1.call-done), channel_id=1, source_target_pairs={{0,1},{3,2},{4,5},{7,6},{8,9},{11,10},{12,13},{15,14},{16,17},{19,... | collective-permute-start | bytes 3145736 | tf_op jit(solution)/shard_map/ppermute | solution.py:303
  383.3 51.9 %all-to-all-start.1 = ((bf16[4,224,1024]{2,1,0:T(8,128)(2,1)}), bf16[4,224,1024]{2,1,0:T(8,128)(2,1)}, u32[]{:S(2)}, u32[]{:S(2)}) async-start(bf16[4,224,1024]{2,1,0:T(8,128)(2,1)} %pad_maximum_fusion.4), calls=%async_computation.3 | async-start | bytes 3670016 | tf_op jit(solution)/shard_map/all_to_all | solution.py:294
  399.5 38.2 %collective-permute-start.18 = (bf16[128,4096]{1,0:T(8,128)(2,1)}, bf16[128,4096]{1,0:T(8,128)(2,1)}, u32[]{:S(2)}, u32[]{:S(2)}) collective-permute-start(bf16[128,4096]{1,0:T(8,128)(2,1)} %add_convert_fusion.7), channel_id=1, source_target_pairs={{1,2},{2,1},{5,6},{6,5},{9,10},{10,9},{13,14},{14,13},{17,18},{18,... | collective-permute-start | bytes 3145736 | tf_op jit(solution)/shard_map/ppermute | solution.py:303
  406.1 36.4 %collective-permute-start.23 = (bf16[128,3200]{1,0:T(8,128)(2,1)}, bf16[128,3200]{1,0:T(8,128)(2,1)}, u32[]{:S(2)}, u32[]{:S(2)}) collective-permute-start(bf16[128,3200]{1,0:T(8,128)(2,1)} %get-tuple-element.170), channel_id=1, source_target_pairs={{0,24},{4,28},{8,16},{12,20},{16,8},{20,12},{24,0},{28,4},{1,25},{... | collective-permute-start | bytes 2457608 | tf_op jit(solution)/shard_map/ppermute | solution.py:306
  408.6 47.2 %collective-permute-start.22 = (bf16[128,3200]{1,0:T(8,128)(2,1)}, bf16[128,3200]{1,0:T(8,128)(2,1)}, u32[]{:S(2)}, u32[]{:S(2)}) collective-permute-start(bf16[128,3200]{1,0:T(8,128)(2,1)} %get-tuple-element.171), channel_id=1, source_target_pairs={{0,16},{4,20},{8,24},{12,28},{16,0},{20,4},{24,8},{28,12},{1,17},{... | collective-permute-start | bytes 2457608 | tf_op jit(solution)/shard_map/ppermute | solution.py:306
  409.1 46.9 %collective-permute-start.21 = (bf16[128,3200]{1,0:T(8,128)(2,1)S(1)}, bf16[128,3200]{1,0:T(8,128)(2,1)}, u32[]{:S(2)}, u32[]{:S(2)}) collective-permute-start(bf16[128,3200]{1,0:T(8,128)(2,1)S(1)} %get-tuple-element.172), channel_id=1, source_target_pairs={{0,8},{4,12},{8,0},{12,4},{16,24},{20,28},{24,16},{28,20},{1,9},{5... | collective-permute-start | bytes 2457608 | tf_op jit(solution)/shard_map/ppermute | solution.py:306
  459.2 22.4 %collective-permute-start.24 = (bf16[128,3200]{1,0:T(8,128)(2,1)}, bf16[128,3200]{1,0:T(8,128)(2,1)}, u32[]{:S(2)}, u32[]{:S(2)}) collective-permute-start(bf16[128,3200]{1,0:T(8,128)(2,1)} %fusion.41), channel_id=1, source_target_pairs={{0,1},{3,2},{4,5},{7,6},{8,9},{11,10},{12,13},{15,14},{16,17},{19,... | collective-permute-start | bytes 2457608 | tf_op jit(solution)/shard_map/ppermute | solution.py:303
  467.2 69.4 %collective-permute-start.28 = (bf16[512,1024]{1,0:T(8,128)(2,1)S(1)}, bf16[512,1024]{1,0:T(8,128)(2,1)}, u32[]{:S(2)}, u32[]{:S(2)}) collective-permute-start(bf16[512,1024]{1,0:T(8,128)(2,1)S(1)} %add_convert_fusion.5), channel_id=1, source_target_pairs={{1,0},{2,3},{5,4},{6,7},{9,8},{10,11},{13,12},{14,15},{17,16},{18,... | collective-permute-start | bytes 3145736 | tf_op jit(solution)/shard_map/ppermute | solution.py:303
  481.6 31.4 %collective-permute-start.26 = (bf16[128,5120]{1,0:T(8,128)(2,1)}, bf16[128,5120]{1,0:T(8,128)(2,1)S(1)}, u32[]{:S(2)}, u32[]{:S(2)}) collective-permute-start(bf16[128,5120]{1,0:T(8,128)(2,1)} %reduce-scatter.8.cloned.1.call-done), channel_id=1, source_target_pairs={{0,1},{3,2},{4,5},{7,6},{8,9},{11,10},{12,13},{15,14},{16,17},{19,... | collective-permute-start | bytes 3932168 | tf_op jit(solution)/shard_map/ppermute | solution.py:303
  490.1 46.4 %collective-permute-start.29 = (bf16[128,4096]{1,0:T(8,128)(2,1)S(1)}, bf16[128,4096]{1,0:T(8,128)(2,1)S(1)}, u32[]{:S(2)}, u32[]{:S(2)}) collective-permute-start(bf16[128,4096]{1,0:T(8,128)(2,1)S(1)} %add_convert_fusion.4), channel_id=1, source_target_pairs={{1,0},{2,3},{5,4},{6,7},{9,8},{10,11},{13,12},{14,15},{17,16},{18,... | collective-permute-start | bytes 3145736 | tf_op jit(solution)/shard_map/ppermute | solution.py:303
  514.8 21.7 %collective-permute-start.30 = (bf16[128,5120]{1,0:T(8,128)(2,1)S(1)}, bf16[128,5120]{1,0:T(8,128)(2,1)S(1)}, u32[]{:S(2)}, u32[]{:S(2)}) collective-permute-start(bf16[128,5120]{1,0:T(8,128)(2,1)S(1)} %add_convert_fusion.3), channel_id=1, source_target_pairs={{1,2},{2,1},{5,6},{6,5},{9,10},{10,9},{13,14},{14,13},{17,18},{18,... | collective-permute-start | bytes 3932168 | tf_op jit(solution)/shard_map/ppermute | solution.py:303
  536.9 37.6 %collective-permute-start.31 = (bf16[128,5120]{1,0:T(8,128)(2,1)S(1)}, bf16[128,5120]{1,0:T(8,128)(2,1)S(1)}, u32[]{:S(2)}, u32[]{:S(2)}) collective-permute-start(bf16[128,5120]{1,0:T(8,128)(2,1)S(1)} %add_convert_fusion.2), channel_id=1, source_target_pairs={{1,0},{2,3},{5,4},{6,7},{9,8},{10,11},{13,12},{14,15},{17,16},{18,... | collective-permute-start | bytes 3932168 | tf_op jit(solution)/shard_map/ppermute | solution.py:303
  (70 other events, 472.0 us)
Sparse Core Ops, SparseCore 0:
  10.5 76.2 all-gather.2
  89.2 78.1 all-gather.4
  195.3 71.2 reduce-scatter.3
  270.3 71.2 reduce-scatter.5
  345.0 108.8 reduce-scatter.7

commit v6 on v5

--- a/solution.py
+++ b/solution.py
@@ -676,7 +676,6 @@
     if swift:
         last_core, leaving = tied(last_core, leaving)
         last_own, last_near = grid.fold_chips(last_kept, last_core)
-        inner_sum, inner_in = grid.hop_two(inner_sum, inner_in)
     leaving = grid.hand_back(leaving)
     if swift:
         inner_in, outer_in, grad_encoded, leaving, *last_near = tied(
@@ -685,10 +684,11 @@
         part_last = plus_all(last_own, last_near)
         last_sum, last_in = grid.hop_one(part_last)
         outer_sum, outer_in = grid.hop_three(outer_sum, outer_in)
-        inner_sum, inner_in = grid.hop_three(inner_sum, inner_in)
-        last_in, part_middle = tied(last_in, part_middle)
+        inner_sum, inner_in = grid.hop_two(inner_sum, inner_in)
+        last_in, inner_in, part_middle = tied(last_in, inner_in, part_middle)
         middle_sum, middle_in = grid.hop_one(part_middle)
         last_sum, last_in = grid.hop_two(last_sum, last_in)
+        inner_sum, inner_in = grid.hop_three(inner_sum, inner_in)
         last_in, middle_in = tied(last_in, middle_in)
         middle_sum, middle_in = grid.hop_two(middle_sum, middle_in)
         last_sum, last_in = grid.hop_three(last_sum, last_in)

time: 587 us -> 579 us (0.986)
  waiting for transfers between devices: 193 us -> 176 us
    ppermute x14, waiting for transfers between devices: 64.2 us -> 54.9 us  [flip(): lax.ppermute(values, 'fsdp', [(f, f ^ bits) for f in range(self.fsdp)])]
    unnamed x140 -> x138, local copies, waits for them, and re-layouts: 28.6 us -> 29.7 us
  transfers between devices with their start and end apart: 39 -> 39, of which waited for: 16 -> 15; matrix products, arithmetic and copies ran while one was open for 29% -> 30% of each run, Pallas kernels for 14% -> 14%
where the time goes in v6:
time: 579 us; the launch traced here: 571 us
  waiting for transfers between devices  176 us (30%)
  matrix products  110 us (19%)
  starting transfers between devices  88.3 us (15%)
  Pallas kernels  82 us (14%)
  local copies, waits for them, and re-layouts  51.3 us (9%)
  other arithmetic  47.7 us (8%)
  between operations  15.5 us (3%)
    ppermute x12, waiting for transfers between devices, chain(): return lax.ppermute(values, AXES, pairs)  85.2 us
    ppermute x14, waiting for transfers between devices, flip(): lax.ppermute(values, 'fsdp', [(f, f ^ bits) for f in range(self.fsdp)])  54.9 us
    dot_general x7, matrix products, product_back(): lax.dot_general(incoming, weight, (((1,), (1,)), ((), ())), preferred_ele...  47.6 us
    pallas_call x2, Pallas kernels, attend_back(): pl.pallas_call(kernel, grid=(pairs,), in_specs=specs, out_specs=out_specs...  44 us
    ppermute x12, starting transfers between devices, chain(): return lax.ppermute(values, AXES, pairs)  34 us
    dot_general x7, matrix products, weight_grad(): lax.dot_general(operand, incoming, (((0,), (0,)), ((), ())), preferred_el...  32.8 us
    dot_general x7, matrix products, product(): return jnp.dot(first, second, preferred_element_type=F32)  29.8 us
    unnamed x138, local copies, waits for them, and re-layouts  29.7 us
  transfers between devices with their start and end apart: 39, of which 15 were waited for; matrix products, arithmetic and copies ran while one was open for 30% of the time, Pallas kernels for 14%

profile of v6, /device:TPU:0, one launch (start us, length us, event | category | flops | bytes accessed | tf_op | source)
XLA Modules:
  0.0 570.7 jit_solution(2267722873079935021)
XLA Ops:
  17.0 5.6 collective-permute-start.2
  27.1 25.7 %collective-permute-done.1 = bf16[128,3200]{1,0:T(8,128)(2,1)} collective-permute-done((bf16[128,3200]{1,0:T(8,128)(2,1)}, bf16[128,3200]{1,0:T(8,128)(2,1)}, u32[]{:S(2)}, u32[]{:S(2)}) %collective-permute-start.1) | collective-permute-done | bytes 819232 | tf_op jit(solution)/shard_map/ppermute | solution.py:306
  57.2 4.4 collective-permute-start.6
  66.8 17.6 %collective-permute-done.5 = bf16[64,3200]{1,0:T(8,128)(2,1)S(1)} collective-permute-done((bf16[64,3200]{1,0:T(8,128)(2,1)S(1)}, bf16[64,3200]{1,0:T(8,128)(2,1)S(1)}, u32[]{:S(2)}, u32[]{:S(2)}) %collective-permute-start.5) | collective-permute-done | bytes 409632 | tf_op jit(solution)/shard_map/ppermute | solution.py:306
  84.8 10.9 %collective-permute-done.6.refs_2_ = bf16[487,1024]{1,0:T(8,128)(2,1)S(1)} collective-permute-done((bf16[487,1024]{1,0:T(8,128)(2,1)S(1)}, bf16[487,1024]{1,0:T(8,128)(2,1)S(1)}, u32[]{:S(2)}, u32[]{:S(2)}) %collective-permute-start.6) | collective-permute-done | bytes 997408 | tf_op jit(solution)/shard_map/ppermute | solution.py:275
  113.4 8.7 %attend_causal.1 = (bf16[448,1024]{1,0:T(8,128)(2,1)S(1)}, f32[8,1,896]{2,1,0:T(1,128)S(1)}) custom-call(bf16[448,3072]{1,0:T(8,128)(2,1)S(1)} %multiply_convert_fusion.1.refs_0_.refs_1_.refs_2_, bf16[448,3072]{1,0:T(8,128)(2,1)S(1)} %multiply_convert_fusion.1.refs_0_.refs_1_.refs_2_, bf16[448,3072]{1,0:T(8,128)(2,1)S(1)} %multiply_convert_fusion.1.refs_0_.refs_1_.refs_2_, ...), custom_call_target="tpu_custom_call" | custom-call | flops 3288334336 | bytes 3670016 | tf_op jit(solution)/shard_map/attend_causal/pallas_call | solution.py:156
  137.1 7.2 %add_convert_fusion.refs_1_.refs_2_ = bf16[1536,2048]{1,0:T(8,128)(2,1)S(1)} fusion(bf16[1536,1024]{1,0:T(8,128)(2,1)S(1)} %copy-done.11, f32[2048]{0:T(1024)S(1)} %concatenate.52, bf16[1024,4096]{1,0:T(8,128)(2,1)S(1)} %copy-done.55), kind=kOutput, calls=%fused_computation | convolution fusion | flops 6448742400 | bytes 13639680 | tf_op jit(solution)/shard_map/dot_general | solution.py:211
  144.3 20.9 %attend_cross.1 = (bf16[448,1024]{1,0:T(8,128)(2,1)S(1)}, f32[8,1,896]{2,1,0:T(1,128)S(1)}) custom-call(bf16[448,1024]{1,0:T(8,128)(2,1)S(1)} %multiply_convert_fusion.2.refs_0_, bf16[1536,2048]{1,0:T(8,128)(2,1)S(1)} %add_convert_fusion.refs_1_.refs_2_, bf16[1536,2048]{1,0:T(8,128)(2,1)S(1)} %add_convert_fusion.refs_1_.refs_2_), custom_call_target="tpu_custom_call" | custom-call | flops 11274289152 | bytes 8126464 | tf_op jit(solution)/shard_map/attend_cross/pallas_call | solution.py:156
  174.9 7.1 %multiply_convert_fusion = (bf16[448,4096]{1,0:T(8,128)(2,1)S(1)}, f32[448,4096]{1,0:T(8,128)}) fusion(f32[4096]{0:T(1024)S(1)} %convert.78, bf16[1024,5120]{1,0:T(8,128)(2,1)S(1)} %copy-done.54, f32[448,1024]{1,0:T(8,128)S(1)} %get-tuple-element.209, f32[1024]{0:T(1024)S(1)} %bitcast.160, f32[1024]{0:T(1024)S(1)} %bitcast.150, f32[448]{0:T(512)S(1)} %add_rsqrt_fusion, ...), kind=kOutput, calls=%fused_computation.13 | convolution fusion | flops 3771400192 | bytes 21262336 | tf_op jit(solution)/shard_map/dot_general | solution.py:211
  187.9 6.9 %convolution_convert_fusion.1 = bf16[4096,1024]{1,0:T(8,128)(2,1)} fusion(bf16[448,4096]{1,0:T(8,128)(2,1)S(1)} %get-tuple-element.132, bf16[448,1024]{1,0:T(8,128)(2,1)S(1)} %place.3), kind=kOutput, calls=%fused_computation.3 | convolution fusion | flops 3762290688 | bytes 12976128 | tf_op jit(solution)/shard_map/dot_general | solution.py:221
  195.2 11.6 %reduce-scatter.6.cloned.1.call-start = ((), (), s32[]{:S(2)}) async-start(), calls=%async_computation.8 | async-start | bytes 9437184 | tf_op jit(solution)/shard_map/reduce_scatter | solution.py:506
  206.8 5.1 assemble.3
  212.0 10.3 %fusion.70 = (bf16[4096]{0:T(1024)(128)(2,1)S(1)}, bf16[448,4096]{1,0:T(8,128)(2,1)S(1)}) fusion(f32[448,4096]{1,0:T(8,128)} %get-tuple-element.211, f32[4096]{0:T(1024)S(1)} %convert.78, bf16[448,1024]{1,0:T(8,128)(2,1)S(1)} %place.3, bf16[4096,1024]{1,0:T(8,128)(2,1)S(1)} %assemble.3), kind=kOutput, calls=%fused_computation.169 | convolution fusion | flops 3780112384 | bytes 20340736 | tf_op jit(solution)/shard_map/dot_general | solution.py:215
  224.2 7.3 %convolution_convert_fusion = bf16[1024,4096]{1,0:T(8,128)(2,1)} fusion(bf16[448,4096]{1,0:T(8,128)(2,1)S(1)} %get-tuple-element.113, f32[448,1024]{1,0:T(8,128)S(1)} %copy-done.26, f32[1024]{0:T(1024)S(1)} %bitcast.161, f32[1024]{0:T(1024)S(1)} %bitcast.151, f32[448]{0:T(512)S(1)} %add_rsqrt_fusion, f32[448]{0:T(512)S(1)} %broadcast_multiply_fusion.6), kind=kOutput, calls=%fused_computation.2 | convolution fusion | flops 3764584448 | bytes 13905408 | tf_op jit(solution)/shard_map/dot_general | solution.py:221
  231.6 8.4 %multiply_reduce_fusion = (bf16[1024]{0:T(1024)(128)(2,1)S(1)}, f32[448]{0:T(512)S(1)}, f32[448]{0:T(512)S(1)}, bf16[1024]{0:T(1024)(128)(2,1)S(1)}, f32[448,1024]{1,0:T(8,128)S(1)}) fusion(f32[448,1024]{1,0:T(8,128)S(1)} %copy-done.26, f32[448]{0:T(512)S(1)} %add_rsqrt_fusion, f32[448]{0:T(512)S(1)} %broadcast_multiply_fusion.6, f32[1024]{0:T(1024)S(1)} %bitcast.152, ...), kind=kOutput, calls=%fused_computation.71 | convolution fusion | flops 3762222080 | bytes 15744000 | tf_op jit(solution)/shard_map/dot_general | solution.py:215
  245.5 31.9 %attend_cross_back.1 = (bf16[448,1024]{1,0:T(8,128)(2,1)S(1)}, bf16[1536,2048]{1,0:T(8,128)(2,1)S(1)}) custom-call(bf16[448,1024]{1,0:T(8,128)(2,1)S(1)} %copy-done.20, bf16[1536,2048]{1,0:T(8,128)(2,1)} %copy-done.21, bf16[1536,2048]{1,0:T(8,128)(2,1)} %copy-done.21, bf16[448,1024]{1,0:T(8,128)(2,1)S(1)} %copy-done.18, ...), custom_call_target="tpu_custom_call" | custom-call | flops 28185722880 | bytes 16252928 | tf_op jit(solution)/shard_map/attend_cross_back/pallas_call | solution.py:194
  285.3 11.5 %convolution_convert_fusion.4 = bf16[1536,1024]{1,0:T(8,128)(2,1)} fusion(bf16[1536,2048]{1,0:T(8,128)(2,1)} %copy-done.6, bf16[1024,4096]{1,0:T(8,128)(2,1)} %all-gather.3.cloned.1.call-done), kind=kOutput, calls=%fused_computation.20 | convolution fusion | flops 6444023808 | bytes 13631488 | tf_op jit(solution)/shard_map/dot_general | solution.py:215
  296.8 4.6 all-to-all-start
  301.5 10.6 %convolution_convert_fusion.3.refs_3_ = bf16[1024,2048]{1,0:T(8,128)(2,1)S(1)} fusion(bf16[1536,1024]{1,0:T(8,128)(2,1)} %copy-done.10, bf16[1536,2048]{1,0:T(8,128)(2,1)} %copy-done.6), kind=kOutput, calls=%fused_computation.19 | convolution fusion | flops 6444548096 | bytes 13631488 | tf_op jit(solution)/shard_map/dot_general | solution.py:221
  332.3 12.1 %attend_causal_back.1 = bf16[448,3072]{1,0:T(8,128)(2,1)S(1)} custom-call(bf16[448,3072]{1,0:T(8,128)(2,1)S(1)} %copy-done.13, bf16[448,3072]{1,0:T(8,128)(2,1)S(1)} %copy-done.13, bf16[448,3072]{1,0:T(8,128)(2,1)S(1)} %copy-done.13, bf16[448,1024]{1,0:T(8,128)(2,1)S(1)} %copy-done.16, bf16[448,1024]{1,0:T(8,128)(2,1)S(1)} %fusion.48.refs_4_, ...), custom_call_target="tpu_custom_call" | custom-call | flops 8220835840 | bytes 7340032 | tf_op jit(solution)/shard_map/attend_causal_back/pallas_call | solution.py:194
  348.5 7.8 %fusion.32 = (f32[448]{0:T(512)S(1)}, bf16[1024]{0:T(1024)(128)(2,1)S(1)}, f32[448]{0:T(512)S(1)}, bf16[1024]{0:T(1024)(128)(2,1)S(1)}, f32[448,1024]{1,0:T(8,128)S(1)}) fusion(bf16[448,1024]{1,0:T(8,128)(2,1)S(1)} %copy-done.3, f32[1024]{0:T(1024)S(1)} %bitcast.140, f32[448]{0:T(512)S(1)} %copy-done.44, f32[448]{0:T(512)S(1)} %copy-done.40, ...), kind=kOutput, calls=%fused_computation.62 | convolution fusion | flops 2823156736 | bytes 11811840 | tf_op jit(solution)/shard_map/dot_general | solution.py:215
  372.6 4.9 all-to-all-start.1
  382.1 6.9 %collective-permute-start.17 = (bf16[128,4096]{1,0:T(8,128)(2,1)}, bf16[128,4096]{1,0:T(8,128)(2,1)}, u32[]{:S(2)}, u32[]{:S(2)}) collective-permute-start(bf16[128,4096]{1,0:T(8,128)(2,1)} %reduce-scatter.6.cloned.1.call-done), channel_id=1, source_target_pairs={{0,1},{3,2},{4,5},{7,6},{8,9},{11,10},{12,13},{15,14},{16,17},{19,... | collective-permute-start | bytes 3145736 | tf_op jit(solution)/shard_map/ppermute | solution.py:303
  399.8 21.4 %all-to-all-done.1 = bf16[4,224,1024]{2,1,0:T(8,128)(2,1)} async-done(((bf16[4,224,1024]{2,1,0:T(8,128)(2,1)}), bf16[4,224,1024]{2,1,0:T(8,128)(2,1)}, u32[]{:S(2)}, u32[]{:S(2)}) %all-to-all-start.1) | async-done | bytes 1835040 | tf_op jit(solution)/shard_map/all_to_all | solution.py:294
  423.7 6.0 %collective-permute-done.17 = bf16[128,4096]{1,0:T(8,128)(2,1)} collective-permute-done((bf16[128,4096]{1,0:T(8,128)(2,1)}, bf16[128,4096]{1,0:T(8,128)(2,1)}, u32[]{:S(2)}, u32[]{:S(2)}) %collective-permute-start.17) | collective-permute-done | bytes 1048608 | tf_op jit(solution)/shard_map/ppermute | solution.py:303
  429.7 8.7 %collective-permute-done.21 = bf16[128,3200]{1,0:T(8,128)(2,1)} collective-permute-done((bf16[128,3200]{1,0:T(8,128)(2,1)}, bf16[128,3200]{1,0:T(8,128)(2,1)}, u32[]{:S(2)}, u32[]{:S(2)}) %collective-permute-start.21) | collective-permute-done | bytes 819232 | tf_op jit(solution)/shard_map/ppermute | solution.py:306
  446.1 8.3 %collective-permute-start.23 = (bf16[128,3200]{1,0:T(8,128)(2,1)}, bf16[128,3200]{1,0:T(8,128)(2,1)}, u32[]{:S(2)}, u32[]{:S(2)}) collective-permute-start(bf16[128,3200]{1,0:T(8,128)(2,1)} %fusion.41), channel_id=1, source_target_pairs={{0,1},{3,2},{4,5},{7,6},{8,9},{11,10},{12,13},{15,14},{16,17},{19,... | collective-permute-start | bytes 2457608 | tf_op jit(solution)/shard_map/ppermute | solution.py:303
  460.7 9.1 %collective-permute-done.23 = bf16[128,3200]{1,0:T(8,128)(2,1)} collective-permute-done((bf16[128,3200]{1,0:T(8,128)(2,1)}, bf16[128,3200]{1,0:T(8,128)(2,1)}, u32[]{:S(2)}, u32[]{:S(2)}) %collective-permute-start.23) | collective-permute-done | bytes 819232 | tf_op jit(solution)/shard_map/ppermute | solution.py:303
  469.8 4.5 collective-permute-start.26
  479.9 21.0 %collective-permute-done.26 = bf16[128,5120]{1,0:T(8,128)(2,1)S(1)} collective-permute-done((bf16[128,5120]{1,0:T(8,128)(2,1)}, bf16[128,5120]{1,0:T(8,128)(2,1)S(1)}, u32[]{:S(2)}, u32[]{:S(2)}) %collective-permute-start.26) | collective-permute-done | bytes 1310752 | tf_op jit(solution)/shard_map/ppermute | solution.py:303
  503.4 18.3 %collective-permute-done.27 = bf16[128,3200]{1,0:T(8,128)(2,1)S(1)} collective-permute-done((bf16[128,3200]{1,0:T(8,128)(2,1)S(1)}, bf16[128,3200]{1,0:T(8,128)(2,1)S(1)}, u32[]{:S(2)}, u32[]{:S(2)}) %collective-permute-start.27) | collective-permute-done | bytes 819232 | tf_op jit(solution)/shard_map/ppermute | solution.py:303
  530.7 30.8 %collective-permute-done.31 = bf16[128,5120]{1,0:T(8,128)(2,1)S(1)} collective-permute-done((bf16[128,5120]{1,0:T(8,128)(2,1)S(1)}, bf16[128,5120]{1,0:T(8,128)(2,1)S(1)}, u32[]{:S(2)}, u32[]{:S(2)}) %collective-permute-start.31) | collective-permute-done | bytes 1310752 | tf_op jit(solution)/shard_map/ppermute | solution.py:303
  (304 shorter events, 179.3 us)
Async XLA Ops:
  7.2 116.5 %all-gather.3.cloned.1.call-start = ((), (), s32[]{:S(2)}) async-start(), calls=%async_computation.5 | async-start | bytes 9437184 | tf_op jit(solution)/shard_map/all_gather | solution.py:502
  9.6 159.4 %all-gather.5.cloned.1.call-start = ((), (), s32[]{:S(2)}) async-start(), calls=%async_computation.6 | async-start | bytes 11796480 | tf_op jit(solution)/shard_map/all_gather | solution.py:502
  11.9 269.1 %reduce-scatter.4.cloned.1.call-start = ((), (), s32[]{:S(2)}) async-start(), calls=%async_computation.7 | async-start | bytes 9437184 | tf_op jit(solution)/shard_map/reduce_scatter | solution.py:506
  15.7 37.1 %collective-permute-start.3 = (bf16[487,1024]{1,0:T(8,128)(2,1)}, bf16[487,1024]{1,0:T(8,128)(2,1)S(1)}, u32[]{:S(2)}, u32[]{:S(2)}) collective-permute-start(bf16[487,1024]{1,0:T(8,128)(2,1)} %get-tuple-element.176), channel_id=1, source_target_pairs={{1,0},{2,1},{3,2},{4,7},{6,5},{7,6},{9,8},{10,9},{11,10},{12,15},{... | collective-permute-start | bytes 2992136 | tf_op jit(solution)/shard_map/ppermute | solution.py:275
  17.0 38.9 %collective-permute-start.2 = (bf16[487,1024]{1,0:T(8,128)(2,1)}, bf16[487,1024]{1,0:T(8,128)(2,1)}, u32[]{:S(2)}, u32[]{:S(2)}) collective-permute-start(bf16[487,1024]{1,0:T(8,128)(2,1)} %get-tuple-element.177), channel_id=1, source_target_pairs={{0,1},{1,2},{3,0},{4,5},{5,6},{6,7},{8,9},{9,10},{11,8},{12,13},{1... | collective-permute-start | bytes 2992136 | tf_op jit(solution)/shard_map/ppermute | solution.py:275
  23.7 29.1 %collective-permute-start.1 = (bf16[128,3200]{1,0:T(8,128)(2,1)}, bf16[128,3200]{1,0:T(8,128)(2,1)}, u32[]{:S(2)}, u32[]{:S(2)}) collective-permute-start(bf16[128,3200]{1,0:T(8,128)(2,1)} %get-tuple-element.186), channel_id=1, source_target_pairs={{0,16},{4,20},{8,24},{12,28},{16,0},{20,4},{24,8},{28,12},{1,17},{... | collective-permute-start | bytes 2457608 | tf_op jit(solution)/shard_map/ppermute | solution.py:306
  25.6 27.2 %collective-permute-start = (bf16[128,3200]{1,0:T(8,128)(2,1)}, bf16[128,3200]{1,0:T(8,128)(2,1)}, u32[]{:S(2)}, u32[]{:S(2)}) collective-permute-start(bf16[128,3200]{1,0:T(8,128)(2,1)} %get-tuple-element.186), channel_id=1, source_target_pairs={{0,8},{4,12},{8,0},{12,4},{16,24},{20,28},{24,16},{28,20},{1,9},{5... | collective-permute-start | bytes 2457608 | tf_op jit(solution)/shard_map/ppermute | solution.py:306
  57.2 38.5 %collective-permute-start.6 = (bf16[487,1024]{1,0:T(8,128)(2,1)S(1)}, bf16[487,1024]{1,0:T(8,128)(2,1)S(1)}, u32[]{:S(2)}, u32[]{:S(2)}) collective-permute-start(bf16[487,1024]{1,0:T(8,128)(2,1)S(1)} %dynamic-slice_bitcast_fusion.2), channel_id=1, source_target_pairs={{0,2},{2,0},{3,1},{4,6},{5,7},{7,5},{8,10},{10,8},{11,9},{12,14},{... | collective-permute-start | bytes 2992136 | tf_op jit(solution)/shard_map/ppermute | solution.py:275
  63.7 20.7 %collective-permute-start.5 = (bf16[64,3200]{1,0:T(8,128)(2,1)S(1)}, bf16[64,3200]{1,0:T(8,128)(2,1)S(1)}, u32[]{:S(2)}, u32[]{:S(2)}) collective-permute-start(bf16[64,3200]{1,0:T(8,128)(2,1)S(1)} %slice.149), channel_id=1, source_target_pairs={{0,16},{4,20},{8,24},{12,28},{16,0},{20,4},{24,8},{28,12},{1,17},{... | collective-permute-start | bytes 1228808 | tf_op jit(solution)/shard_map/ppermute | solution.py:306
  103.6 61.7 %collective-permute-start.9 = (bf16[512,1024]{1,0:T(8,128)(2,1)}, bf16[512,1024]{1,0:T(8,128)(2,1)}, u32[]{:S(2)}, u32[]{:S(2)}) collective-permute-start(bf16[512,1024]{1,0:T(8,128)(2,1)} %param.27), channel_id=1, source_target_pairs={{0,16},{4,20},{8,24},{12,28},{16,0},{20,4},{24,8},{28,12},{1,17},{... | collective-permute-start | bytes 3145736 | tf_op jit(solution)/shard_map/ppermute | solution.py:306
  105.1 60.2 %collective-permute-start.8 = (bf16[512,1024]{1,0:T(8,128)(2,1)}, bf16[512,1024]{1,0:T(8,128)(2,1)}, u32[]{:S(2)}, u32[]{:S(2)}) collective-permute-start(bf16[512,1024]{1,0:T(8,128)(2,1)} %param.27), channel_id=1, source_target_pairs={{0,8},{4,12},{8,0},{12,4},{16,24},{20,28},{24,16},{28,20},{1,9},{5... | collective-permute-start | bytes 3145736 | tf_op jit(solution)/shard_map/ppermute | solution.py:306
  129.7 35.6 %collective-permute-start.12 = (bf16[112,1024]{1,0:T(8,128)(2,1)S(1)}, bf16[112,1024]{1,0:T(8,128)(2,1)S(1)}, u32[]{:S(2)}, u32[]{:S(2)}) collective-permute-start(bf16[112,1024]{1,0:T(8,128)(2,1)S(1)} %get-tuple-element.187), channel_id=1, source_target_pairs={{1,0},{2,1},{3,2},{4,7},{6,5},{7,6},{9,8},{10,9},{11,10},{12,15},{... | collective-permute-start | bytes 688136 | tf_op jit(solution)/shard_map/ppermute | solution.py:275
  131.0 34.3 %collective-permute-start.11 = (bf16[112,1024]{1,0:T(8,128)(2,1)S(1)}, bf16[112,1024]{1,0:T(8,128)(2,1)S(1)}, u32[]{:S(2)}, u32[]{:S(2)}) collective-permute-start(bf16[112,1024]{1,0:T(8,128)(2,1)S(1)} %get-tuple-element.188), channel_id=1, source_target_pairs={{0,2},{2,0},{3,1},{4,6},{5,7},{7,5},{8,10},{10,8},{11,9},{12,14},{... | collective-permute-start | bytes 688136 | tf_op jit(solution)/shard_map/ppermute | solution.py:275
  132.9 32.4 %collective-permute-start.10 = (bf16[112,1024]{1,0:T(8,128)(2,1)S(1)}, bf16[112,1024]{1,0:T(8,128)(2,1)S(1)}, u32[]{:S(2)}, u32[]{:S(2)}) collective-permute-start(bf16[112,1024]{1,0:T(8,128)(2,1)S(1)} %get-tuple-element.189), channel_id=1, source_target_pairs={{0,1},{1,2},{3,0},{4,5},{5,6},{6,7},{8,9},{9,10},{11,8},{12,13},{1... | collective-permute-start | bytes 688136 | tf_op jit(solution)/shard_map/ppermute | solution.py:275
  195.2 150.8 %reduce-scatter.6.cloned.1.call-start = ((), (), s32[]{:S(2)}) async-start(), calls=%async_computation.8 | async-start | bytes 9437184 | tf_op jit(solution)/shard_map/reduce_scatter | solution.py:506
  281.1 31.1 %collective-permute-start.16 = (bf16[512,1024]{1,0:T(8,128)(2,1)}, bf16[512,1024]{1,0:T(8,128)(2,1)}, u32[]{:S(2)}, u32[]{:S(2)}) collective-permute-start(bf16[512,1024]{1,0:T(8,128)(2,1)} %reduce-scatter.4.cloned.1.call-done), channel_id=1, source_target_pairs={{0,1},{3,2},{4,5},{7,6},{8,9},{11,10},{12,13},{15,14},{16,17},{19,... | collective-permute-start | bytes 3145736 | tf_op jit(solution)/shard_map/ppermute | solution.py:303
  296.8 75.8 %all-to-all-start = ((bf16[4,384,1024]{2,1,0:T(8,128)(2,1)}), bf16[4,384,1024]{2,1,0:T(8,128)(2,1)}, u32[]{:S(2)}, u32[]{:S(2)}) async-start(bf16[4,384,1024]{2,1,0:T(8,128)(2,1)} %bitcast.134), calls=%async_computation.2 | async-start | bytes 6291456 | tf_op jit(solution)/shard_map/all_to_all | solution.py:294
  301.4 168.4 %reduce-scatter.8.cloned.1.call-start = ((), (), s32[]{:S(2)}) async-start(), calls=%async_computation.9 | async-start | bytes 11796480 | tf_op jit(solution)/shard_map/reduce_scatter | solution.py:506
  372.6 48.6 %all-to-all-start.1 = ((bf16[4,224,1024]{2,1,0:T(8,128)(2,1)}), bf16[4,224,1024]{2,1,0:T(8,128)(2,1)}, u32[]{:S(2)}, u32[]{:S(2)}) async-start(bf16[4,224,1024]{2,1,0:T(8,128)(2,1)} %pad_maximum_fusion.4), calls=%async_computation.3 | async-start | bytes 3670016 | tf_op jit(solution)/shard_map/all_to_all | solution.py:294
  380.4 43.3 %collective-permute-start.18 = (bf16[512,1024]{1,0:T(8,128)(2,1)}, bf16[512,1024]{1,0:T(8,128)(2,1)}, u32[]{:S(2)}, u32[]{:S(2)}) collective-permute-start(bf16[512,1024]{1,0:T(8,128)(2,1)} %add_convert_fusion.7), channel_id=1, source_target_pairs={{1,2},{2,1},{5,6},{6,5},{9,10},{10,9},{13,14},{14,13},{17,18},{18,... | collective-permute-start | bytes 3145736 | tf_op jit(solution)/shard_map/ppermute | solution.py:303
  382.1 47.7 %collective-permute-start.17 = (bf16[128,4096]{1,0:T(8,128)(2,1)}, bf16[128,4096]{1,0:T(8,128)(2,1)}, u32[]{:S(2)}, u32[]{:S(2)}) collective-permute-start(bf16[128,4096]{1,0:T(8,128)(2,1)} %reduce-scatter.6.cloned.1.call-done), channel_id=1, source_target_pairs={{0,1},{3,2},{4,5},{7,6},{8,9},{11,10},{12,13},{15,14},{16,17},{19,... | collective-permute-start | bytes 3145736 | tf_op jit(solution)/shard_map/ppermute | solution.py:303
  394.5 35.2 %collective-permute-start.22 = (bf16[128,3200]{1,0:T(8,128)(2,1)}, bf16[128,3200]{1,0:T(8,128)(2,1)S(1)}, u32[]{:S(2)}, u32[]{:S(2)}) collective-permute-start(bf16[128,3200]{1,0:T(8,128)(2,1)} %get-tuple-element.172), channel_id=1, source_target_pairs={{0,24},{4,28},{8,16},{12,20},{16,8},{20,12},{24,0},{28,4},{1,25},{... | collective-permute-start | bytes 2457608 | tf_op jit(solution)/shard_map/ppermute | solution.py:306
  396.5 42.0 %collective-permute-start.21 = (bf16[128,3200]{1,0:T(8,128)(2,1)}, bf16[128,3200]{1,0:T(8,128)(2,1)}, u32[]{:S(2)}, u32[]{:S(2)}) collective-permute-start(bf16[128,3200]{1,0:T(8,128)(2,1)} %get-tuple-element.173), channel_id=1, source_target_pairs={{0,16},{4,20},{8,24},{12,28},{16,0},{20,4},{24,8},{28,12},{1,17},{... | collective-permute-start | bytes 2457608 | tf_op jit(solution)/shard_map/ppermute | solution.py:306
  397.4 41.4 %collective-permute-start.20 = (bf16[128,3200]{1,0:T(8,128)(2,1)}, bf16[128,3200]{1,0:T(8,128)(2,1)}, u32[]{:S(2)}, u32[]{:S(2)}) collective-permute-start(bf16[128,3200]{1,0:T(8,128)(2,1)} %get-tuple-element.174), channel_id=1, source_target_pairs={{0,8},{4,12},{8,0},{12,4},{16,24},{20,28},{24,16},{28,20},{1,9},{5... | collective-permute-start | bytes 2457608 | tf_op jit(solution)/shard_map/ppermute | solution.py:306
  441.6 28.2 %collective-permute-start.24 = (bf16[128,4096]{1,0:T(8,128)(2,1)}, bf16[128,4096]{1,0:T(8,128)(2,1)}, u32[]{:S(2)}, u32[]{:S(2)}) collective-permute-start(bf16[128,4096]{1,0:T(8,128)(2,1)} %add_convert_fusion.6), channel_id=1, source_target_pairs={{1,2},{2,1},{5,6},{6,5},{9,10},{10,9},{13,14},{14,13},{17,18},{18,... | collective-permute-start | bytes 3145736 | tf_op jit(solution)/shard_map/ppermute | solution.py:303
  446.1 23.7 %collective-permute-start.23 = (bf16[128,3200]{1,0:T(8,128)(2,1)}, bf16[128,3200]{1,0:T(8,128)(2,1)}, u32[]{:S(2)}, u32[]{:S(2)}) collective-permute-start(bf16[128,3200]{1,0:T(8,128)(2,1)} %fusion.41), channel_id=1, source_target_pairs={{0,1},{3,2},{4,5},{7,6},{8,9},{11,10},{12,13},{15,14},{16,17},{19,... | collective-permute-start | bytes 2457608 | tf_op jit(solution)/shard_map/ppermute | solution.py:303
  456.4 68.5 %collective-permute-start.28 = (bf16[512,1024]{1,0:T(8,128)(2,1)S(1)}, bf16[512,1024]{1,0:T(8,128)(2,1)}, u32[]{:S(2)}, u32[]{:S(2)}) collective-permute-start(bf16[512,1024]{1,0:T(8,128)(2,1)S(1)} %add_convert_fusion.5), channel_id=1, source_target_pairs={{1,0},{2,3},{5,4},{6,7},{9,8},{10,11},{13,12},{14,15},{17,16},{18,... | collective-permute-start | bytes 3145736 | tf_op jit(solution)/shard_map/ppermute | solution.py:303
  469.8 31.1 %collective-permute-start.26 = (bf16[128,5120]{1,0:T(8,128)(2,1)}, bf16[128,5120]{1,0:T(8,128)(2,1)S(1)}, u32[]{:S(2)}, u32[]{:S(2)}) collective-permute-start(bf16[128,5120]{1,0:T(8,128)(2,1)} %reduce-scatter.8.cloned.1.call-done), channel_id=1, source_target_pairs={{0,1},{3,2},{4,5},{7,6},{8,9},{11,10},{12,13},{15,14},{16,17},{19,... | collective-permute-start | bytes 3932168 | tf_op jit(solution)/shard_map/ppermute | solution.py:303
  478.6 46.3 %collective-permute-start.29 = (bf16[128,4096]{1,0:T(8,128)(2,1)S(1)}, bf16[128,4096]{1,0:T(8,128)(2,1)S(1)}, u32[]{:S(2)}, u32[]{:S(2)}) collective-permute-start(bf16[128,4096]{1,0:T(8,128)(2,1)S(1)} %add_convert_fusion.4), channel_id=1, source_target_pairs={{1,0},{2,3},{5,4},{6,7},{9,8},{10,11},{13,12},{14,15},{17,16},{18,... | collective-permute-start | bytes 3145736 | tf_op jit(solution)/shard_map/ppermute | solution.py:303
  501.1 20.6 %collective-permute-start.27 = (bf16[128,3200]{1,0:T(8,128)(2,1)S(1)}, bf16[128,3200]{1,0:T(8,128)(2,1)S(1)}, u32[]{:S(2)}, u32[]{:S(2)}) collective-permute-start(bf16[128,3200]{1,0:T(8,128)(2,1)S(1)} %add_convert_fusion.11), channel_id=1, source_target_pairs={{1,0},{2,3},{5,4},{6,7},{9,8},{10,11},{13,12},{14,15},{17,16},{18,... | collective-permute-start | bytes 2457608 | tf_op jit(solution)/shard_map/ppermute | solution.py:303
  502.7 22.2 %collective-permute-start.30 = (bf16[128,5120]{1,0:T(8,128)(2,1)S(1)}, bf16[128,5120]{1,0:T(8,128)(2,1)S(1)}, u32[]{:S(2)}, u32[]{:S(2)}) collective-permute-start(bf16[128,5120]{1,0:T(8,128)(2,1)S(1)} %add_convert_fusion.3), channel_id=1, source_target_pairs={{1,2},{2,1},{5,6},{6,5},{9,10},{10,9},{13,14},{14,13},{17,18},{18,... | collective-permute-start | bytes 3932168 | tf_op jit(solution)/shard_map/ppermute | solution.py:303
  525.2 36.3 %collective-permute-start.31 = (bf16[128,5120]{1,0:T(8,128)(2,1)S(1)}, bf16[128,5120]{1,0:T(8,128)(2,1)S(1)}, u32[]{:S(2)}, u32[]{:S(2)}) collective-permute-start(bf16[128,5120]{1,0:T(8,128)(2,1)S(1)} %add_convert_fusion.2), channel_id=1, source_target_pairs={{1,0},{2,3},{5,4},{6,7},{9,8},{10,11},{13,12},{14,15},{17,16},{18,... | collective-permute-start | bytes 3932168 | tf_op jit(solution)/shard_map/ppermute | solution.py:303
  (69 other events, 445.1 us)
Sparse Core Ops, SparseCore 0:
  10.5 76.2 all-gather.2
  89.2 78.1 all-gather.4
  195.4 71.2 reduce-scatter.3
  270.4 71.2 reduce-scatter.5
  345.0 107.6 reduce-scatter.7

commit v7 on v6

--- a/solution.py
+++ b/solution.py
@@ -515,8 +515,10 @@
         first_shard = jnp.concatenate([self_qkv, small], axis=1)
         first_widths = (self_qkv.shape[1], shard)
         first_x, first_y = grid.flip(first_shard, 2), grid.flip(first_shard, 4)
-    full_self_out, full_cross_q, full_cross_kv = gathered(self_out, cross_q, cross_kv)
-    full_cross_out, full_inner = gathered(cross_out, mlp_in)
+    full_self_out, full_cross_q, full_cross_kv, full_cross_out = gathered(
+        self_out, cross_q, cross_kv, cross_out
+    )
+    (full_inner,) = gathered(mlp_in)
     if swift:
         first_x, first_y, pieces[1], pieces[3], tokens_in = tied(
             first_x, first_y, pieces[1], pieces[3], tokens_in

time: 579 us -> 583 us (level)
  waiting for transfers between devices: 176 us -> 192 us
  starting transfers between devices: 88.3 us -> 74.4 us
    reduce_scatter x3, starting transfers between devices: 11.6 us -> 0.59 us  [scattered(): return lax.psum_scatter(member, 'fsdp', scatter_dimension=0, tiled=True)]
    ppermute x14, waiting for transfers between devices: 54.9 us -> 63.8 us  [flip(): lax.ppermute(values, 'fsdp', [(f, f ^ bits) for f in range(self.fsdp)])]
    reduce_scatter x3, waiting for transfers between devices: 0.02 us -> 7.89 us  [scattered(): return lax.psum_scatter(member, 'fsdp', scatter_dimension=0, tiled=True)]
    unnamed x138 -> x136, local copies, waits for them, and re-layouts: 29.7 us -> 30 us
  transfers between devices with their start and end apart: 39 -> 39, of which waited for: 15 -> 16; matrix products, arithmetic and copies ran while one was open for 30% -> 30% of each run, Pallas kernels for 14% -> 14%
where the time goes in v7:
time: 583 us; the launch traced here: 575 us
  waiting for transfers between devices  192 us (33%)
  matrix products  110 us (19%)
  Pallas kernels  80.9 us (14%)
  starting transfers between devices  74.4 us (13%)
  local copies, waits for them, and re-layouts  53.2 us (9%)
  other arithmetic  48 us (8%)
  between operations  15.7 us (3%)
    ppermute x12, waiting for transfers between devices, chain(): return lax.ppermute(values, AXES, pairs)  87.5 us
    ppermute x14, waiting for transfers between devices, flip(): lax.ppermute(values, 'fsdp', [(f, f ^ bits) for f in range(self.fsdp)])  63.8 us
    dot_general x7, matrix products, product_back(): lax.dot_general(incoming, weight, (((1,), (1,)), ((), ())), preferred_ele...  48.1 us
    pallas_call x2, Pallas kernels, attend_back(): pl.pallas_call(kernel, grid=(pairs,), in_specs=specs, out_specs=out_specs...  43.9 us
    dot_general x7, matrix products, weight_grad(): lax.dot_general(operand, incoming, (((0,), (0,)), ((), ())), preferred_el...  32.3 us
    ppermute x12, starting transfers between devices, chain(): return lax.ppermute(values, AXES, pairs)  31.8 us
    dot_general x7, matrix products, product(): return jnp.dot(first, second, preferred_element_type=F32)  30.1 us
    unnamed x136, local copies, waits for them, and re-layouts  30 us
  transfers between devices with their start and end apart: 39, of which 16 were waited for; matrix products, arithmetic and copies ran while one was open for 30% of the time, Pallas kernels for 14%

profile of v7, /device:TPU:0, one launch (start us, length us, event | category | flops | bytes accessed | tf_op | source)
XLA Modules:
  0.0 574.7 jit_solution(17345119897664131293)
XLA Ops:
  17.8 5.6 collective-permute-start.2
  27.9 28.0 %collective-permute-done.1 = bf16[128,3200]{1,0:T(8,128)(2,1)} collective-permute-done((bf16[128,3200]{1,0:T(8,128)(2,1)}, bf16[128,3200]{1,0:T(8,128)(2,1)}, u32[]{:S(2)}, u32[]{:S(2)}) %collective-permute-start.1) | collective-permute-done | bytes 819232 | tf_op jit(solution)/shard_map/ppermute | solution.py:306
  58.3 4.4 collective-permute-start.6
  67.8 17.6 %collective-permute-done.5 = bf16[64,3200]{1,0:T(8,128)(2,1)S(1)} collective-permute-done((bf16[64,3200]{1,0:T(8,128)(2,1)S(1)}, bf16[64,3200]{1,0:T(8,128)(2,1)S(1)}, u32[]{:S(2)}, u32[]{:S(2)}) %collective-permute-start.5) | collective-permute-done | bytes 409632 | tf_op jit(solution)/shard_map/ppermute | solution.py:306
  86.9 9.5 %collective-permute-done.6.refs_2_ = bf16[487,1024]{1,0:T(8,128)(2,1)S(1)} collective-permute-done((bf16[487,1024]{1,0:T(8,128)(2,1)S(1)}, bf16[487,1024]{1,0:T(8,128)(2,1)S(1)}, u32[]{:S(2)}, u32[]{:S(2)}) %collective-permute-start.6) | collective-permute-done | bytes 997408 | tf_op jit(solution)/shard_map/ppermute | solution.py:275
  113.9 8.8 %attend_causal.1 = (bf16[448,1024]{1,0:T(8,128)(2,1)S(1)}, f32[8,1,896]{2,1,0:T(1,128)S(1)}) custom-call(bf16[448,3072]{1,0:T(8,128)(2,1)S(1)} %multiply_convert_fusion.1.refs_0_.refs_1_.refs_2_, bf16[448,3072]{1,0:T(8,128)(2,1)S(1)} %multiply_convert_fusion.1.refs_0_.refs_1_.refs_2_, bf16[448,3072]{1,0:T(8,128)(2,1)S(1)} %multiply_convert_fusion.1.refs_0_.refs_1_.refs_2_, ...), custom_call_target="tpu_custom_call" | custom-call | flops 3288334336 | bytes 3670016 | tf_op jit(solution)/shard_map/attend_causal/pallas_call | solution.py:156
  138.6 7.2 %add_convert_fusion.refs_1_.refs_2_ = bf16[1536,2048]{1,0:T(8,128)(2,1)S(1)} fusion(bf16[1536,1024]{1,0:T(8,128)(2,1)S(1)} %copy-done.11, f32[2048]{0:T(1024)S(1)} %concatenate.49, bf16[1024,5120]{1,0:T(8,128)(2,1)S(1)} %copy-done.54), kind=kOutput, calls=%fused_computation | convolution fusion | flops 6448742400 | bytes 13639680 | tf_op jit(solution)/shard_map/dot_general | solution.py:211
  145.8 20.9 %attend_cross.1 = (bf16[448,1024]{1,0:T(8,128)(2,1)S(1)}, f32[8,1,896]{2,1,0:T(1,128)S(1)}) custom-call(bf16[448,1024]{1,0:T(8,128)(2,1)S(1)} %multiply_convert_fusion.2.refs_0_, bf16[1536,2048]{1,0:T(8,128)(2,1)S(1)} %add_convert_fusion.refs_1_.refs_2_, bf16[1536,2048]{1,0:T(8,128)(2,1)S(1)} %add_convert_fusion.refs_1_.refs_2_), custom_call_target="tpu_custom_call" | custom-call | flops 11274289152 | bytes 8126464 | tf_op jit(solution)/shard_map/attend_cross/pallas_call | solution.py:156
  173.3 9.6 %multiply_convert_fusion = (bf16[448,4096]{1,0:T(8,128)(2,1)S(1)}, f32[448,4096]{1,0:T(8,128)}) fusion(f32[4096]{0:T(1024)S(1)} %convert.78, bf16[1024,4096]{1,0:T(8,128)(2,1)} %all-gather.5.cloned.1.call-done, f32[448,1024]{1,0:T(8,128)} %copy-done.25, f32[1024]{0:T(1024)S(1)} %bitcast.162, f32[1024]{0:T(1024)S(1)} %bitcast.152, f32[448]{0:T(512)S(1)} %add_rsqrt_fusion, ...), kind=kOutput, calls=%fused_computation.9 | convolution fusion | flops 3771400192 | bytes 21261824 | tf_op jit(solution)/shard_map/dot_general | solution.py:211
  189.5 6.8 %convolution_convert_fusion.1 = bf16[4096,1024]{1,0:T(8,128)(2,1)} fusion(bf16[448,4096]{1,0:T(8,128)(2,1)S(1)} %get-tuple-element.132, bf16[448,1024]{1,0:T(8,128)(2,1)S(1)} %place.3), kind=kOutput, calls=%fused_computation.3 | convolution fusion | flops 3762290688 | bytes 12976128 | tf_op jit(solution)/shard_map/dot_general | solution.py:221
  201.5 10.8 %fusion.67 = (bf16[4096]{0:T(1024)(128)(2,1)S(1)}, bf16[448,4096]{1,0:T(8,128)(2,1)S(1)}) fusion(f32[448,4096]{1,0:T(8,128)} %get-tuple-element.211, f32[4096]{0:T(1024)S(1)} %convert.78, bf16[448,1024]{1,0:T(8,128)(2,1)S(1)} %place.3, bf16[4096,1024]{1,0:T(8,128)(2,1)S(1)} %assemble.3), kind=kOutput, calls=%fused_computation.165 | convolution fusion | flops 3780112384 | bytes 20340736 | tf_op jit(solution)/shard_map/dot_general | solution.py:215
  214.2 7.2 %convolution_convert_fusion = bf16[1024,4096]{1,0:T(8,128)(2,1)} fusion(bf16[448,4096]{1,0:T(8,128)(2,1)S(1)} %get-tuple-element.113, f32[448,1024]{1,0:T(8,128)S(1)} %copy-done.26, f32[1024]{0:T(1024)S(1)} %bitcast.163, f32[1024]{0:T(1024)S(1)} %bitcast.153, f32[448]{0:T(512)S(1)} %add_rsqrt_fusion, f32[448]{0:T(512)S(1)} %broadcast_multiply_fusion.6), kind=kOutput, calls=%fused_computation.2 | convolution fusion | flops 3764584448 | bytes 13905408 | tf_op jit(solution)/shard_map/dot_general | solution.py:221
  221.7 8.4 %multiply_reduce_fusion = (bf16[1024]{0:T(1024)(128)(2,1)S(1)}, f32[448]{0:T(512)S(1)}, f32[448]{0:T(512)S(1)}, bf16[1024]{0:T(1024)(128)(2,1)S(1)}, f32[448,1024]{1,0:T(8,128)S(1)}) fusion(f32[448,1024]{1,0:T(8,128)S(1)} %copy-done.26, f32[448]{0:T(512)S(1)} %add_rsqrt_fusion, f32[448]{0:T(512)S(1)} %broadcast_multiply_fusion.6, f32[1024]{0:T(1024)S(1)} %bitcast.154, ...), kind=kOutput, calls=%fused_computation.67 | convolution fusion | flops 3762222080 | bytes 15744000 | tf_op jit(solution)/shard_map/dot_general | solution.py:215
  235.5 31.9 %attend_cross_back.1 = (bf16[448,1024]{1,0:T(8,128)(2,1)S(1)}, bf16[1536,2048]{1,0:T(8,128)(2,1)S(1)}) custom-call(bf16[448,1024]{1,0:T(8,128)(2,1)S(1)} %copy-done.20, bf16[1536,2048]{1,0:T(8,128)(2,1)} %copy-done.21, bf16[1536,2048]{1,0:T(8,128)(2,1)} %copy-done.21, bf16[448,1024]{1,0:T(8,128)(2,1)S(1)} %copy-done.18, ...), custom_call_target="tpu_custom_call" | custom-call | flops 28185722880 | bytes 16252928 | tf_op jit(solution)/shard_map/attend_cross_back/pallas_call | solution.py:194
  270.0 4.9 collective-permute-start.16
  274.9 11.8 %convolution_convert_fusion.4 = bf16[1536,1024]{1,0:T(8,128)(2,1)} fusion(bf16[1536,2048]{1,0:T(8,128)(2,1)} %copy-done.6, bf16[1024,5120]{1,0:T(8,128)(2,1)} %all-gather.3.cloned.1.call-done), kind=kOutput, calls=%fused_computation.16 | convolution fusion | flops 6444023808 | bytes 13631488 | tf_op jit(solution)/shard_map/dot_general | solution.py:215
  286.7 4.7 all-to-all-start
  291.4 10.1 %convolution_convert_fusion.3.refs_3_ = bf16[1024,2048]{1,0:T(8,128)(2,1)S(1)} fusion(bf16[1536,1024]{1,0:T(8,128)(2,1)} %copy-done.10, bf16[1536,2048]{1,0:T(8,128)(2,1)} %copy-done.6), kind=kOutput, calls=%fused_computation.15 | convolution fusion | flops 6444548096 | bytes 13631488 | tf_op jit(solution)/shard_map/dot_general | solution.py:221
  321.7 12.1 %attend_causal_back.1 = bf16[448,3072]{1,0:T(8,128)(2,1)S(1)} custom-call(bf16[448,3072]{1,0:T(8,128)(2,1)S(1)} %copy-done.13, bf16[448,3072]{1,0:T(8,128)(2,1)S(1)} %copy-done.13, bf16[448,3072]{1,0:T(8,128)(2,1)S(1)} %copy-done.13, bf16[448,1024]{1,0:T(8,128)(2,1)S(1)} %copy-done.16, bf16[448,1024]{1,0:T(8,128)(2,1)S(1)} %fusion.44.refs_4_, ...), custom_call_target="tpu_custom_call" | custom-call | flops 8220835840 | bytes 7340032 | tf_op jit(solution)/shard_map/attend_causal_back/pallas_call | solution.py:194
  335.4 7.9 %reduce-scatter.6.cloned.1.call-done = bf16[128,4096]{1,0:T(8,128)(2,1)} async-done(((bf16[1024,4096]{1,0:T(8,128)(2,1)}), bf16[128,4096]{1,0:T(8,128)(2,1)}) %reduce-scatter.6.cloned.1.call-update) | async-done | bytes 1048592 | tf_op jit(solution)/shard_map/reduce_scatter | solution.py:506
  345.6 7.4 %fusion.28 = (f32[448]{0:T(512)S(1)}, bf16[1024]{0:T(1024)(128)(2,1)S(1)}, f32[448]{0:T(512)S(1)}, bf16[1024]{0:T(1024)(128)(2,1)S(1)}, f32[448,1024]{1,0:T(8,128)S(1)}) fusion(bf16[448,1024]{1,0:T(8,128)(2,1)S(1)} %copy-done.3, f32[1024]{0:T(1024)S(1)} %bitcast.142, f32[448]{0:T(512)S(1)} %copy-done.44, f32[448]{0:T(512)S(1)} %copy-done.40, ...), kind=kOutput, calls=%fused_computation.58 | convolution fusion | flops 2823156736 | bytes 11811840 | tf_op jit(solution)/shard_map/dot_general | solution.py:215
  371.2 4.4 all-to-all-start.1
  380.4 6.6 %collective-permute-start.17 = (bf16[128,4096]{1,0:T(8,128)(2,1)}, bf16[128,4096]{1,0:T(8,128)(2,1)}, u32[]{:S(2)}, u32[]{:S(2)}) collective-permute-start(bf16[128,4096]{1,0:T(8,128)(2,1)} %reduce-scatter.6.cloned.1.call-done), channel_id=1, source_target_pairs={{0,1},{3,2},{4,5},{7,6},{8,9},{11,10},{12,13},{15,14},{16,17},{19,... | collective-permute-start | bytes 3145736 | tf_op jit(solution)/shard_map/ppermute | solution.py:303
  397.9 21.7 %all-to-all-done.1 = bf16[4,224,1024]{2,1,0:T(8,128)(2,1)} async-done(((bf16[4,224,1024]{2,1,0:T(8,128)(2,1)}), bf16[4,224,1024]{2,1,0:T(8,128)(2,1)}, u32[]{:S(2)}, u32[]{:S(2)}) %all-to-all-start.1) | async-done | bytes 1835040 | tf_op jit(solution)/shard_map/all_to_all | solution.py:294
  422.1 6.1 %collective-permute-done.17 = bf16[128,4096]{1,0:T(8,128)(2,1)} collective-permute-done((bf16[128,4096]{1,0:T(8,128)(2,1)}, bf16[128,4096]{1,0:T(8,128)(2,1)}, u32[]{:S(2)}, u32[]{:S(2)}) %collective-permute-start.17) | collective-permute-done | bytes 1048608 | tf_op jit(solution)/shard_map/ppermute | solution.py:303
  428.2 14.3 %collective-permute-done.21 = bf16[128,3200]{1,0:T(8,128)(2,1)} collective-permute-done((bf16[128,3200]{1,0:T(8,128)(2,1)}, bf16[128,3200]{1,0:T(8,128)(2,1)}, u32[]{:S(2)}, u32[]{:S(2)}) %collective-permute-start.21) | collective-permute-done | bytes 819232 | tf_op jit(solution)/shard_map/ppermute | solution.py:306
  450.3 5.7 collective-permute-start.23
  462.3 10.0 %collective-permute-done.23 = bf16[128,3200]{1,0:T(8,128)(2,1)} collective-permute-done((bf16[128,3200]{1,0:T(8,128)(2,1)}, bf16[128,3200]{1,0:T(8,128)(2,1)}, u32[]{:S(2)}, u32[]{:S(2)}) %collective-permute-start.23) | collective-permute-done | bytes 819232 | tf_op jit(solution)/shard_map/ppermute | solution.py:303
  472.4 4.5 collective-permute-start.26
  482.4 21.4 %collective-permute-done.26 = bf16[128,5120]{1,0:T(8,128)(2,1)S(1)} collective-permute-done((bf16[128,5120]{1,0:T(8,128)(2,1)}, bf16[128,5120]{1,0:T(8,128)(2,1)S(1)}, u32[]{:S(2)}, u32[]{:S(2)}) %collective-permute-start.26) | collective-permute-done | bytes 1310752 | tf_op jit(solution)/shard_map/ppermute | solution.py:303
  506.4 17.9 %collective-permute-done.27 = bf16[128,3200]{1,0:T(8,128)(2,1)S(1)} collective-permute-done((bf16[128,3200]{1,0:T(8,128)(2,1)S(1)}, bf16[128,3200]{1,0:T(8,128)(2,1)S(1)}, u32[]{:S(2)}, u32[]{:S(2)}) %collective-permute-start.27) | collective-permute-done | bytes 819232 | tf_op jit(solution)/shard_map/ppermute | solution.py:303
  533.3 32.0 %collective-permute-done.31 = bf16[128,5120]{1,0:T(8,128)(2,1)S(1)} collective-permute-done((bf16[128,5120]{1,0:T(8,128)(2,1)S(1)}, bf16[128,5120]{1,0:T(8,128)(2,1)S(1)}, u32[]{:S(2)}, u32[]{:S(2)}) %collective-permute-start.31) | collective-permute-done | bytes 1310752 | tf_op jit(solution)/shard_map/ppermute | solution.py:303
  (301 shorter events, 178.7 us)
Async XLA Ops:
  7.2 117.1 %all-gather.3.cloned.1.call-start = ((), (), s32[]{:S(2)}) async-start(), calls=%async_computation.5 | async-start | bytes 11796480 | tf_op jit(solution)/shard_map/all_gather | solution.py:502
  9.7 163.6 %all-gather.5.cloned.1.call-start = ((), (), s32[]{:S(2)}) async-start(), calls=%async_computation.6 | async-start | bytes 9437184 | tf_op jit(solution)/shard_map/all_gather | solution.py:502
  10.5 259.5 %reduce-scatter.4.cloned.1.call-start = ((), (), s32[]{:S(2)}) async-start(), calls=%async_computation.7 | async-start | bytes 9437184 | tf_op jit(solution)/shard_map/reduce_scatter | solution.py:506
  16.5 39.4 %collective-permute-start.3 = (bf16[487,1024]{1,0:T(8,128)(2,1)}, bf16[487,1024]{1,0:T(8,128)(2,1)S(1)}, u32[]{:S(2)}, u32[]{:S(2)}) collective-permute-start(bf16[487,1024]{1,0:T(8,128)(2,1)} %get-tuple-element.176), channel_id=1, source_target_pairs={{1,0},{2,1},{3,2},{4,7},{6,5},{7,6},{9,8},{10,9},{11,10},{12,15},{... | collective-permute-start | bytes 2992136 | tf_op jit(solution)/shard_map/ppermute | solution.py:275
  17.8 38.9 %collective-permute-start.2 = (bf16[487,1024]{1,0:T(8,128)(2,1)}, bf16[487,1024]{1,0:T(8,128)(2,1)}, u32[]{:S(2)}, u32[]{:S(2)}) collective-permute-start(bf16[487,1024]{1,0:T(8,128)(2,1)} %get-tuple-element.177), channel_id=1, source_target_pairs={{0,1},{1,2},{3,0},{4,5},{5,6},{6,7},{8,9},{9,10},{11,8},{12,13},{1... | collective-permute-start | bytes 2992136 | tf_op jit(solution)/shard_map/ppermute | solution.py:275
  24.4 31.5 %collective-permute-start.1 = (bf16[128,3200]{1,0:T(8,128)(2,1)}, bf16[128,3200]{1,0:T(8,128)(2,1)}, u32[]{:S(2)}, u32[]{:S(2)}) collective-permute-start(bf16[128,3200]{1,0:T(8,128)(2,1)} %get-tuple-element.186), channel_id=1, source_target_pairs={{0,16},{4,20},{8,24},{12,28},{16,0},{20,4},{24,8},{28,12},{1,17},{... | collective-permute-start | bytes 2457608 | tf_op jit(solution)/shard_map/ppermute | solution.py:306
  26.4 29.5 %collective-permute-start = (bf16[128,3200]{1,0:T(8,128)(2,1)}, bf16[128,3200]{1,0:T(8,128)(2,1)}, u32[]{:S(2)}, u32[]{:S(2)}) collective-permute-start(bf16[128,3200]{1,0:T(8,128)(2,1)} %get-tuple-element.186), channel_id=1, source_target_pairs={{0,8},{4,12},{8,0},{12,4},{16,24},{20,28},{24,16},{28,20},{1,9},{5... | collective-permute-start | bytes 2457608 | tf_op jit(solution)/shard_map/ppermute | solution.py:306
  58.3 38.2 %collective-permute-start.6 = (bf16[487,1024]{1,0:T(8,128)(2,1)S(1)}, bf16[487,1024]{1,0:T(8,128)(2,1)S(1)}, u32[]{:S(2)}, u32[]{:S(2)}) collective-permute-start(bf16[487,1024]{1,0:T(8,128)(2,1)S(1)} %dynamic-slice_bitcast_fusion.2), channel_id=1, source_target_pairs={{0,2},{2,0},{3,1},{4,6},{5,7},{7,5},{8,10},{10,8},{11,9},{12,14},{... | collective-permute-start | bytes 2992136 | tf_op jit(solution)/shard_map/ppermute | solution.py:275
  64.8 20.7 %collective-permute-start.5 = (bf16[64,3200]{1,0:T(8,128)(2,1)S(1)}, bf16[64,3200]{1,0:T(8,128)(2,1)S(1)}, u32[]{:S(2)}, u32[]{:S(2)}) collective-permute-start(bf16[64,3200]{1,0:T(8,128)(2,1)S(1)} %slice.149), channel_id=1, source_target_pairs={{0,16},{4,20},{8,24},{12,28},{16,0},{20,4},{24,8},{28,12},{1,17},{... | collective-permute-start | bytes 1228808 | tf_op jit(solution)/shard_map/ppermute | solution.py:306
  66.4 20.6 %collective-permute-start.4 = (bf16[64,3200]{1,0:T(8,128)(2,1)S(1)}, bf16[64,3200]{1,0:T(8,128)(2,1)S(1)}, u32[]{:S(2)}, u32[]{:S(2)}) collective-permute-start(bf16[64,3200]{1,0:T(8,128)(2,1)S(1)} %slice.148), channel_id=1, source_target_pairs={{0,8},{4,12},{8,0},{12,4},{16,24},{20,28},{24,16},{28,20},{1,9},{5... | collective-permute-start | bytes 1228808 | tf_op jit(solution)/shard_map/ppermute | solution.py:306
  104.2 62.6 %collective-permute-start.9 = (bf16[512,1024]{1,0:T(8,128)(2,1)}, bf16[512,1024]{1,0:T(8,128)(2,1)}, u32[]{:S(2)}, u32[]{:S(2)}) collective-permute-start(bf16[512,1024]{1,0:T(8,128)(2,1)} %param.27), channel_id=1, source_target_pairs={{0,16},{4,20},{8,24},{12,28},{16,0},{20,4},{24,8},{28,12},{1,17},{... | collective-permute-start | bytes 3145736 | tf_op jit(solution)/shard_map/ppermute | solution.py:306
  105.7 61.1 %collective-permute-start.8 = (bf16[512,1024]{1,0:T(8,128)(2,1)}, bf16[512,1024]{1,0:T(8,128)(2,1)}, u32[]{:S(2)}, u32[]{:S(2)}) collective-permute-start(bf16[512,1024]{1,0:T(8,128)(2,1)} %param.27), channel_id=1, source_target_pairs={{0,8},{4,12},{8,0},{12,4},{16,24},{20,28},{24,16},{28,20},{1,9},{5... | collective-permute-start | bytes 3145736 | tf_op jit(solution)/shard_map/ppermute | solution.py:306
  131.2 35.6 %collective-permute-start.12 = (bf16[112,1024]{1,0:T(8,128)(2,1)S(1)}, bf16[112,1024]{1,0:T(8,128)(2,1)S(1)}, u32[]{:S(2)}, u32[]{:S(2)}) collective-permute-start(bf16[112,1024]{1,0:T(8,128)(2,1)S(1)} %get-tuple-element.187), channel_id=1, source_target_pairs={{1,0},{2,1},{3,2},{4,7},{6,5},{7,6},{9,8},{10,9},{11,10},{12,15},{... | collective-permute-start | bytes 688136 | tf_op jit(solution)/shard_map/ppermute | solution.py:275
  132.5 34.3 %collective-permute-start.11 = (bf16[112,1024]{1,0:T(8,128)(2,1)S(1)}, bf16[112,1024]{1,0:T(8,128)(2,1)S(1)}, u32[]{:S(2)}, u32[]{:S(2)}) collective-permute-start(bf16[112,1024]{1,0:T(8,128)(2,1)S(1)} %get-tuple-element.188), channel_id=1, source_target_pairs={{0,2},{2,0},{3,1},{4,6},{5,7},{7,5},{8,10},{10,8},{11,9},{12,14},{... | collective-permute-start | bytes 688136 | tf_op jit(solution)/shard_map/ppermute | solution.py:275
  135.0 31.9 %collective-permute-start.10 = (bf16[112,1024]{1,0:T(8,128)(2,1)S(1)}, bf16[112,1024]{1,0:T(8,128)(2,1)S(1)}, u32[]{:S(2)}, u32[]{:S(2)}) collective-permute-start(bf16[112,1024]{1,0:T(8,128)(2,1)S(1)} %get-tuple-element.189), channel_id=1, source_target_pairs={{0,1},{1,2},{3,0},{4,5},{5,6},{6,7},{8,9},{9,10},{11,8},{12,13},{1... | collective-permute-start | bytes 688136 | tf_op jit(solution)/shard_map/ppermute | solution.py:275
  196.8 146.4 %reduce-scatter.6.cloned.1.call-start = ((), (), s32[]{:S(2)}) async-start(), calls=%async_computation.8 | async-start | bytes 9437184 | tf_op jit(solution)/shard_map/reduce_scatter | solution.py:506
  270.0 31.6 %collective-permute-start.16 = (bf16[512,1024]{1,0:T(8,128)(2,1)}, bf16[512,1024]{1,0:T(8,128)(2,1)}, u32[]{:S(2)}, u32[]{:S(2)}) collective-permute-start(bf16[512,1024]{1,0:T(8,128)(2,1)} %reduce-scatter.4.cloned.1.call-done), channel_id=1, source_target_pairs={{0,1},{3,2},{4,5},{7,6},{8,9},{11,10},{12,13},{15,14},{16,17},{19,... | collective-permute-start | bytes 3145736 | tf_op jit(solution)/shard_map/ppermute | solution.py:303
  286.7 84.5 %all-to-all-start = ((bf16[4,384,1024]{2,1,0:T(8,128)(2,1)}), bf16[4,384,1024]{2,1,0:T(8,128)(2,1)}, u32[]{:S(2)}, u32[]{:S(2)}) async-start(bf16[4,384,1024]{2,1,0:T(8,128)(2,1)} %bitcast.136), calls=%async_computation.2 | async-start | bytes 6291456 | tf_op jit(solution)/shard_map/all_to_all | solution.py:294
  291.4 181.0 %reduce-scatter.8.cloned.1.call-start = ((), (), s32[]{:S(2)}) async-start(), calls=%async_computation.9 | async-start | bytes 11796480 | tf_op jit(solution)/shard_map/reduce_scatter | solution.py:506
  371.2 48.3 %all-to-all-start.1 = ((bf16[4,224,1024]{2,1,0:T(8,128)(2,1)}), bf16[4,224,1024]{2,1,0:T(8,128)(2,1)}, u32[]{:S(2)}, u32[]{:S(2)}) async-start(bf16[4,224,1024]{2,1,0:T(8,128)(2,1)} %pad_maximum_fusion.4), calls=%async_computation.3 | async-start | bytes 3670016 | tf_op jit(solution)/shard_map/all_to_all | solution.py:294
  378.8 43.3 %collective-permute-start.18 = (bf16[512,1024]{1,0:T(8,128)(2,1)}, bf16[512,1024]{1,0:T(8,128)(2,1)}, u32[]{:S(2)}, u32[]{:S(2)}) collective-permute-start(bf16[512,1024]{1,0:T(8,128)(2,1)} %add_convert_fusion.7), channel_id=1, source_target_pairs={{1,2},{2,1},{5,6},{6,5},{9,10},{10,9},{13,14},{14,13},{17,18},{18,... | collective-permute-start | bytes 3145736 | tf_op jit(solution)/shard_map/ppermute | solution.py:303
  380.4 47.8 %collective-permute-start.17 = (bf16[128,4096]{1,0:T(8,128)(2,1)}, bf16[128,4096]{1,0:T(8,128)(2,1)}, u32[]{:S(2)}, u32[]{:S(2)}) collective-permute-start(bf16[128,4096]{1,0:T(8,128)(2,1)} %reduce-scatter.6.cloned.1.call-done), channel_id=1, source_target_pairs={{0,1},{3,2},{4,5},{7,6},{8,9},{11,10},{12,13},{15,14},{16,17},{19,... | collective-permute-start | bytes 3145736 | tf_op jit(solution)/shard_map/ppermute | solution.py:303
  392.5 35.7 %collective-permute-start.22 = (bf16[128,3200]{1,0:T(8,128)(2,1)}, bf16[128,3200]{1,0:T(8,128)(2,1)S(1)}, u32[]{:S(2)}, u32[]{:S(2)}) collective-permute-start(bf16[128,3200]{1,0:T(8,128)(2,1)} %get-tuple-element.172), channel_id=1, source_target_pairs={{0,24},{4,28},{8,16},{12,20},{16,8},{20,12},{24,0},{28,4},{1,25},{... | collective-permute-start | bytes 2457608 | tf_op jit(solution)/shard_map/ppermute | solution.py:306
  393.1 49.4 %collective-permute-start.21 = (bf16[128,3200]{1,0:T(8,128)(2,1)}, bf16[128,3200]{1,0:T(8,128)(2,1)}, u32[]{:S(2)}, u32[]{:S(2)}) collective-permute-start(bf16[128,3200]{1,0:T(8,128)(2,1)} %get-tuple-element.173), channel_id=1, source_target_pairs={{0,16},{4,20},{8,24},{12,28},{16,0},{20,4},{24,8},{28,12},{1,17},{... | collective-permute-start | bytes 2457608 | tf_op jit(solution)/shard_map/ppermute | solution.py:306
  394.5 48.0 %collective-permute-start.20 = (bf16[128,3200]{1,0:T(8,128)(2,1)}, bf16[128,3200]{1,0:T(8,128)(2,1)}, u32[]{:S(2)}, u32[]{:S(2)}) collective-permute-start(bf16[128,3200]{1,0:T(8,128)(2,1)} %get-tuple-element.174), channel_id=1, source_target_pairs={{0,8},{4,12},{8,0},{12,4},{16,24},{20,28},{24,16},{28,20},{1,9},{5... | collective-permute-start | bytes 2457608 | tf_op jit(solution)/shard_map/ppermute | solution.py:306
  445.2 27.2 %collective-permute-start.24 = (bf16[128,4096]{1,0:T(8,128)(2,1)}, bf16[128,4096]{1,0:T(8,128)(2,1)}, u32[]{:S(2)}, u32[]{:S(2)}) collective-permute-start(bf16[128,4096]{1,0:T(8,128)(2,1)} %add_convert_fusion.6), channel_id=1, source_target_pairs={{1,2},{2,1},{5,6},{6,5},{9,10},{10,9},{13,14},{14,13},{17,18},{18,... | collective-permute-start | bytes 3145736 | tf_op jit(solution)/shard_map/ppermute | solution.py:303
  450.3 22.1 %collective-permute-start.23 = (bf16[128,3200]{1,0:T(8,128)(2,1)}, bf16[128,3200]{1,0:T(8,128)(2,1)}, u32[]{:S(2)}, u32[]{:S(2)}) collective-permute-start(bf16[128,3200]{1,0:T(8,128)(2,1)} %fusion.37), channel_id=1, source_target_pairs={{0,1},{3,2},{4,5},{7,6},{8,9},{11,10},{12,13},{15,14},{16,17},{19,... | collective-permute-start | bytes 2457608 | tf_op jit(solution)/shard_map/ppermute | solution.py:303
  458.0 69.5 %collective-permute-start.28 = (bf16[512,1024]{1,0:T(8,128)(2,1)S(1)}, bf16[512,1024]{1,0:T(8,128)(2,1)}, u32[]{:S(2)}, u32[]{:S(2)}) collective-permute-start(bf16[512,1024]{1,0:T(8,128)(2,1)S(1)} %add_convert_fusion.5), channel_id=1, source_target_pairs={{1,0},{2,3},{5,4},{6,7},{9,8},{10,11},{13,12},{14,15},{17,16},{18,... | collective-permute-start | bytes 3145736 | tf_op jit(solution)/shard_map/ppermute | solution.py:303
  472.4 31.4 %collective-permute-start.26 = (bf16[128,5120]{1,0:T(8,128)(2,1)}, bf16[128,5120]{1,0:T(8,128)(2,1)S(1)}, u32[]{:S(2)}, u32[]{:S(2)}) collective-permute-start(bf16[128,5120]{1,0:T(8,128)(2,1)} %reduce-scatter.8.cloned.1.call-done), channel_id=1, source_target_pairs={{0,1},{3,2},{4,5},{7,6},{8,9},{11,10},{12,13},{15,14},{16,17},{19,... | collective-permute-start | bytes 3932168 | tf_op jit(solution)/shard_map/ppermute | solution.py:303
  481.1 46.4 %collective-permute-start.29 = (bf16[128,4096]{1,0:T(8,128)(2,1)S(1)}, bf16[128,4096]{1,0:T(8,128)(2,1)S(1)}, u32[]{:S(2)}, u32[]{:S(2)}) collective-permute-start(bf16[128,4096]{1,0:T(8,128)(2,1)S(1)} %add_convert_fusion.4), channel_id=1, source_target_pairs={{1,0},{2,3},{5,4},{6,7},{9,8},{10,11},{13,12},{14,15},{17,16},{18,... | collective-permute-start | bytes 3145736 | tf_op jit(solution)/shard_map/ppermute | solution.py:303
  505.7 21.9 %collective-permute-start.30 = (bf16[128,5120]{1,0:T(8,128)(2,1)S(1)}, bf16[128,5120]{1,0:T(8,128)(2,1)S(1)}, u32[]{:S(2)}, u32[]{:S(2)}) collective-permute-start(bf16[128,5120]{1,0:T(8,128)(2,1)S(1)} %add_convert_fusion.3), channel_id=1, source_target_pairs={{1,2},{2,1},{5,6},{6,5},{9,10},{10,9},{13,14},{14,13},{17,18},{18,... | collective-permute-start | bytes 3932168 | tf_op jit(solution)/shard_map/ppermute | solution.py:303
  527.9 37.4 %collective-permute-start.31 = (bf16[128,5120]{1,0:T(8,128)(2,1)S(1)}, bf16[128,5120]{1,0:T(8,128)(2,1)S(1)}, u32[]{:S(2)}, u32[]{:S(2)}) collective-permute-start(bf16[128,5120]{1,0:T(8,128)(2,1)S(1)} %add_convert_fusion.2), channel_id=1, source_target_pairs={{1,0},{2,3},{5,4},{6,7},{9,8},{10,11},{13,12},{14,15},{17,16},{18,... | collective-permute-start | bytes 3932168 | tf_op jit(solution)/shard_map/ppermute | solution.py:303
  (68 other events, 511.8 us)
Sparse Core Ops, SparseCore 0:
  10.5 87.6 all-gather.2
  100.1 69.8 all-gather.4
  197.0 71.2 reduce-scatter.3
  271.9 71.2 reduce-scatter.5
  346.6 118.5 reduce-scatter.7
